TPU v7x, 128 devices: a whole 4x4x4 slice. The times are simulated.
128 devices in a mesh: req: 128 (over y, x, z, core).
Axes of the slice: x: 4, y: 4, z: 4, core: 2. Of those that a mesh axis runs over, the one named last changes fastest.
Arguments:
- prefill_hidden: bfloat16 [32768, 1280], P('req'), may hold values from -6 to 6
- decode_hidden: bfloat16 [256, 1280], P('req'), may hold values from -6 to 6
- attn_gain: float32 [1280], replicated, may hold values from 0.1 to 1.9
- w_qkv: bfloat16 [1280, 1920], replicated
- w_out: bfloat16 [1280, 1280], replicated, may hold values from -0.15625 to 0.15625
- ffn_gain: float32 [1280], replicated, may hold values from 0.1 to 1.9
- w_gate_up: bfloat16 [128, 1280, 448], P('req'), as said below
- w_down: bfloat16 [128, 224, 1280], P('req'), as said below
- key_value_cache: bfloat16 [512, 1024, 640], P('req'), may hold values from -6 to 6
- cache_len: int32 [512], P('req'), may hold values from 64 to 1024, as said below
- slot_of_request: int32 [256], replicated, may hold values from 0 to 511, as said below
- held_hidden: bfloat16 [131072, 1280], P('req'), may hold values from -6 to 6
- recomputed_index: int32 [131072], P('req'), may hold values from 0 to 4095, as said below
- recomp_count: int32 [128], P('req'), may hold values from 512 to 1024, as said below
Outputs:
- prefill_out: bfloat16 [32768, 1280], P('req')
- decode_out: bfloat16 [256, 1280], P('req')
Inputs may be any that keep to these rules, and one draw needn't show every extreme that they name: `slot_of_request`: distinct slot numbers; slot s belongs to device s div 4; some device holds 4 requests. `cache_len`: some slot that holds a request has length 1024. `recomputed_index`: within one device's list the entries are distinct. Only the first recomp_count[d] entries of device d's list are live; some device has 1024. `w_gate_up`: copy n equals copy n mod 16. `w_down`: copy n equals copy n mod 16.
All inputs are finite; a program needn't handle non-finite values.
Results may differ from a plain program's by a relative error of at most 0.015.
Values may be sent and summed in bfloat16 or wider, within the bound.
No kernel may reach another device: no remote copies, remote signals or barrier semaphores. Data moves between devices by JAX's collectives and lax.ppermute only.
A program may use at most 192 MiB of HBM per device.

v0:
```python
import jax
import jax.numpy as jnp
from jax import lax
from jax.sharding import PartitionSpec as P

QUERY_HEADS = 20
KEY_VALUE_HEADS = 5
HEAD_SIZE = 64
FF = 3584
GROUP = 16
PREFILL_TOKENS = 1024


eps = 1e-05
theta = 10000.0
masked_score = -1e30


def partner(shard, axis, apart):
    return lax.ppermute(shard, axis, [(i, i ^ 1 << apart) for i in range(lax.axis_size(axis))])


def rms_scale(value_rows, gain):
    as_float = value_rows.astype(jnp.float32)
    return as_float * lax.rsqrt(jnp.mean(as_float * as_float, axis=-1, keepdims=True) + eps) * gain


def apply_rotary(heads, token_positions):
    half = heads.shape[-1] // 2
    frequency = theta ** (-(jnp.arange(half).astype(jnp.float32) * 2.0 / heads.shape[-1]))
    angle = token_positions.astype(jnp.float32)[:, None] * frequency[None, :]
    cosine = jnp.cos(angle)[:, None, :]
    sine = jnp.sin(angle)[:, None, :]
    first = heads[..., :half]
    second = heads[..., half:]
    return jnp.concatenate(
        [first * cosine - second * sine, second * cosine + first * sine], axis=-1
    )


def attend(query, key_rows, value_rows, mask):
    query_len = query.shape[0]
    heads_kv = key_rows.shape[1]
    group = query.shape[1] // heads_kv
    query_groups = jnp.transpose(query.reshape(query_len, heads_kv, group, HEAD_SIZE), (1, 0, 2, 3))
    key_heads = jnp.transpose(key_rows, (1, 0, 2))
    value_heads = jnp.transpose(value_rows, (1, 0, 2))

    def one_head(inputs):
        query_head, key_head, value_head = inputs
        scores = jnp.einsum(
            "qgd,kd->gqk", query_head, key_head, preferred_element_type=jnp.float32
        ) * HEAD_SIZE ** (-0.5)
        scores = jnp.where(mask[None], scores, masked_score)
        top = jnp.max(scores, axis=-1, keepdims=True)
        weights = jnp.where(mask[None], jnp.exp(scores - top), 0.0)
        total = jnp.sum(weights, axis=-1)
        mixed = jnp.einsum(
            "gqk,kd->qgd",
            weights.astype(jnp.bfloat16),
            value_head,
            preferred_element_type=jnp.float32,
        )
        return (mixed / jnp.transpose(total)[..., None]).astype(jnp.bfloat16)

    mixed_heads = lax.map(one_head, (query_groups, key_heads, value_heads))
    return jnp.transpose(mixed_heads, (1, 0, 2, 3)).reshape(query_len, QUERY_HEADS * HEAD_SIZE)


def body(
    prefill_hidden,
    decode_hidden,
    attn_gain,
    w_qkv,
    w_out,
    ffn_gain,
    w_gate_up,
    w_down,
    key_value_cache,
    cache_len,
    slot_of_request,
    held_hidden,
    recomputed_index,
    recomp_count,
):
    query_width = QUERY_HEADS * HEAD_SIZE
    key_value_width = KEY_VALUE_HEADS * HEAD_SIZE
    share = FF // GROUP
    frequency_levels = GROUP.bit_length() - 1
    device_index = lax.axis_index("req")
    row_total = prefill_hidden.shape[0]
    decode_rows = decode_hidden.shape[0]
    slot_number = key_value_cache.shape[0]
    slot_cache_size = key_value_cache.shape[1]
    group_span = PREFILL_TOKENS // row_total
    group_rank = device_index % group_span
    normed = rms_scale(prefill_hidden, attn_gain).astype(jnp.bfloat16)
    projected_rows = jnp.dot(normed, w_qkv, preferred_element_type=jnp.float32)
    token_positions = jnp.arange(row_total, dtype=jnp.int32) * group_span + group_rank
    query_rot = apply_rotary(
        projected_rows[:, :query_width].reshape(row_total, QUERY_HEADS, HEAD_SIZE), token_positions
    ).reshape(row_total, query_width)
    key_rot = apply_rotary(
        projected_rows[:, query_width : query_width + key_value_width].reshape(
            row_total, KEY_VALUE_HEADS, HEAD_SIZE
        ),
        token_positions,
    ).reshape(row_total, key_value_width)
    packed = jnp.concatenate(
        [query_rot, key_rot, projected_rows[:, query_width + key_value_width :]], axis=1
    ).astype(jnp.bfloat16)
    normed_decode = rms_scale(decode_hidden, attn_gain).astype(jnp.bfloat16)
    decode_projected = jnp.dot(normed_decode, w_qkv, preferred_element_type=jnp.float32).astype(
        jnp.bfloat16
    )
    normed_held = rms_scale(held_hidden, attn_gain).astype(jnp.bfloat16)
    kept_key_value = jnp.dot(
        normed_held, w_qkv[:, query_width:], preferred_element_type=jnp.float32
    )
    kept_keys = apply_rotary(
        kept_key_value[:, :key_value_width].reshape(-1, KEY_VALUE_HEADS, HEAD_SIZE),
        recomputed_index % slot_cache_size,
    ).reshape(-1, key_value_width)
    recomputed = jnp.concatenate([kept_keys, kept_key_value[:, key_value_width:]], axis=1).astype(
        jnp.bfloat16
    )
    live_entry = jnp.arange(recomputed_index.shape[0], dtype=jnp.int32) < recomp_count[0]
    target = jnp.where(live_entry, recomputed_index, slot_number * slot_cache_size)
    flat_cache = key_value_cache.reshape(slot_number * slot_cache_size, 2 * key_value_width)
    slot_cache = (
        flat_cache.at[target]
        .set(recomputed, mode="drop")
        .reshape(slot_number, slot_cache_size, 2 * key_value_width)
    )
    block_keys = packed[:, query_width:]
    for bit in range(group_span.bit_length() - 1):
        other = partner(block_keys, "req", bit)
        upper_side = device_index // 2**bit % 2 == 1
        block_keys = jnp.concatenate(
            [jnp.where(upper_side, other, block_keys), jnp.where(upper_side, block_keys, other)],
            axis=0,
        )
    key_order = jnp.arange(group_span * row_total, dtype=jnp.int32)
    key_place = key_order % row_total * group_span + key_order // row_total
    prefill_mask = key_place[None, :] <= token_positions[:, None]
    prefill_mixed = attend(
        packed[:, :query_width].reshape(row_total, QUERY_HEADS, HEAD_SIZE),
        block_keys[:, :key_value_width].reshape(-1, KEY_VALUE_HEADS, HEAD_SIZE),
        block_keys[:, key_value_width:].reshape(-1, KEY_VALUE_HEADS, HEAD_SIZE),
        prefill_mask,
    )
    slot_ids = device_index * slot_number + jnp.arange(slot_number, dtype=jnp.int32)
    owned = slot_of_request[None, :] == slot_ids[:, None]
    live_slot = jnp.any(owned, axis=1)
    owned_bf = owned.astype(jnp.bfloat16)
    my_slots = lax.dynamic_slice_in_dim(slot_of_request, device_index * decode_rows, decode_rows, 0)
    every_row = lax.all_gather(decode_projected, "req", axis=0, tiled=True)
    arriving_rows = jnp.dot(owned_bf, every_row, preferred_element_type=jnp.float32).astype(
        jnp.bfloat16
    )
    decoding_query = apply_rotary(
        arriving_rows[:, :query_width]
        .astype(jnp.float32)
        .reshape(slot_number, QUERY_HEADS, HEAD_SIZE),
        cache_len,
    ).astype(jnp.bfloat16)
    newest_key = apply_rotary(
        arriving_rows[:, query_width : query_width + key_value_width]
        .astype(jnp.float32)
        .reshape(slot_number, KEY_VALUE_HEADS, HEAD_SIZE),
        cache_len,
    ).astype(jnp.bfloat16)
    newest_value = arriving_rows[:, query_width + key_value_width :].reshape(
        slot_number, KEY_VALUE_HEADS, HEAD_SIZE
    )
    query_groups = decoding_query.reshape(
        slot_number, KEY_VALUE_HEADS, QUERY_HEADS // KEY_VALUE_HEADS, HEAD_SIZE
    )
    slot_cache_keys = slot_cache[:, :, :key_value_width].reshape(
        slot_number, slot_cache_size, KEY_VALUE_HEADS, HEAD_SIZE
    )
    slot_cache_values = slot_cache[:, :, key_value_width:].reshape(
        slot_number, slot_cache_size, KEY_VALUE_HEADS, HEAD_SIZE
    )
    cache_scores = jnp.einsum(
        "shgd,skhd->shgk", query_groups, slot_cache_keys, preferred_element_type=jnp.float32
    ) * HEAD_SIZE ** (-0.5)
    own_score = jnp.einsum(
        "shgd,shd->shg", query_groups, newest_key, preferred_element_type=jnp.float32
    ) * HEAD_SIZE ** (-0.5)
    cache_mask = (jnp.arange(slot_cache_size, dtype=jnp.int32)[None, :] < cache_len[:, None])[
        :, None, None, :
    ]
    cache_scores = jnp.where(cache_mask, cache_scores, masked_score)
    top = jnp.maximum(jnp.max(cache_scores, axis=-1), own_score)
    cache_weight = jnp.where(cache_mask, jnp.exp(cache_scores - top[..., None]), 0.0)
    own_weight = jnp.exp(own_score - top)
    total = jnp.sum(cache_weight, axis=-1) + own_weight
    mixed = jnp.einsum(
        "shgk,skhd->shgd",
        cache_weight.astype(jnp.bfloat16),
        slot_cache_values,
        preferred_element_type=jnp.float32,
    )
    mixed = mixed + jnp.einsum(
        "shg,shd->shgd",
        own_weight.astype(jnp.bfloat16),
        newest_value,
        preferred_element_type=jnp.float32,
    )
    slot_mixed = (mixed / total[..., None]).reshape(slot_number, query_width).astype(jnp.bfloat16)
    slot_mixed = jnp.where(live_slot[:, None], slot_mixed, jnp.zeros_like(slot_mixed))
    every_result = lax.all_gather(slot_mixed, "req", axis=0, tiled=True)
    decode_mixed = jnp.take(every_result, my_slots, axis=0)
    hidden_all = jnp.concatenate([prefill_hidden, decode_hidden], axis=0)
    mixed_all = jnp.concatenate([prefill_mixed, decode_mixed], axis=0)
    projection = jnp.dot(mixed_all, w_out, preferred_element_type=jnp.float32)
    resid = (hidden_all.astype(jnp.float32) + projection).astype(jnp.bfloat16)
    normed_ffn = rms_scale(resid, ffn_gain).astype(jnp.bfloat16)
    gathered = normed_ffn
    for bit in range(frequency_levels):
        other = partner(gathered, "req", bit)
        upper_side = device_index // 2**bit % 2 == 1
        gathered = jnp.concatenate(
            [jnp.where(upper_side, other, gathered), jnp.where(upper_side, gathered, other)], axis=0
        )
    gated = jnp.dot(gathered, w_gate_up[0], preferred_element_type=jnp.float32)
    act = (jax.nn.silu(gated[:, :share]) * gated[:, share:]).astype(jnp.bfloat16)
    partial_value = jnp.dot(act, w_down[0], preferred_element_type=jnp.float32)
    for bit in range(frequency_levels - 1, -1, -1):
        half_rows = partial_value.shape[0] // 2
        lower_half = partial_value[:half_rows]
        upper_half = partial_value[half_rows:]
        upper_side = device_index // 2**bit % 2 == 1
        keep = jnp.where(upper_side, upper_half, lower_half)
        outgoing_terms = jnp.where(upper_side, lower_half, upper_half)
        partial_value = keep + partner(outgoing_terms.astype(jnp.bfloat16), "req", bit).astype(
            outgoing_terms.dtype
        )
    result = (resid.astype(jnp.float32) + partial_value).astype(jnp.bfloat16)
    return (result[:row_total], result[row_total:])


def solution(mesh):
    return jax.shard_map(
        body,
        mesh=mesh,
        in_specs=(
            P("req", None),
            P("req", None),
            P(),
            P(),
            P(),
            P(),
            P("req", None, None),
            P("req", None, None),
            P("req", None, None),
            P("req"),
            P(),
            P("req", None),
            P("req"),
            P("req"),
        ),
        out_specs=(P("req", None), P("req", None)),
        check_vma=False,
    )
```

profile of v0, /device:TPU:0, one launch (start us, length us, event | category | flops | bytes accessed | tf_op | source)
XLA Modules:
  0.0 686.6 jit_solution(7722171845229420843)
XLA Ops:
  7.2 5.4 copy.93
  14.0 4.2 fusion.84
  20.9 1.9 copy.50
  24.7 1.7 copy.51
  26.5 1.8 pad_maximum_fusion.8
  31.5 3.2 fusion.68
  34.7 41.9 %all-gather = bf16[128,2,1920]{2,1,0:T(2,128)(2,1)} all-gather(bf16[1,2,1920]{2,1,0:T(2,128)(2,1)S(1)} %fusion.68), channel_id=1, replica_groups=mesh['req'=128] {'req'}, dimensions={0}, use_global_device_ids=true | all-gather | bytes 990720 | tf_op jit(solution)/shard_map/all_gather | solution.py:157
  76.5 3.3 reshape.351
  80.7 1.5 convolution_convert_fusion
  82.9 2.3 fusion.58
  85.2 3.5 fusion.62
  96.2 1.5 subtract_convert_fusion.4
  99.1 1.5 subtract_convert_fusion
  102.0 2.4 copy.59
  104.4 11.6 %scatter_fusion = bf16[4096,640]{1,0:T(8,128)(2,1)} fusion(bf16[4096,640]{1,0:T(8,128)(2,1)} %bitcast.132, s32[1024]{0:T(1024)S(1)} %copy-done.28, bf16[1024,640]{1,0:T(8,128)(2,1)} %copy.59), kind=kCustom, calls=%fused_computation.1 | custom fusion | bytes 3936256 | tf_op jit(solution)/shard_map/scatter | solution.py:132
  116.0 7.2 %fusion.134 = (bf16[4,1024,320]{2,1,0:T(8,128)(2,1)}, bf16[4,1024,320]{2,1,0:T(8,128)(2,1)}) fusion(bf16[4,1024,640]{2,1,0:T(8,128)(2,1)} %bitcast.133), kind=kLoop, calls=%fused_computation.197 | loop fusion | bytes 10485760 | tf_op jit(solution)/shard_map/slice | solution.py:179
  123.2 4.6 copy.60
  128.8 2.4 fusion.135
  132.8 4.5 copy.61
  137.3 2.6 fusion.79
  140.1 1.4 select_bitcast_fusion
  146.3 2.5 slice.153
  148.7 2.8 copy.54
  152.8 1.5 subtract_convert_fusion.1
  155.1 6.6 collective-permute-done.1
  161.8 1.3 broadcast_select_fusion.8
  163.1 1.6 pad_maximum_fusion.4
  164.7 2.2 copy.53
  166.9 2.3 copy.52
  169.2 36.6 %while.11 = (s32[]{:T(128)}, bf16[5,256,4,64]{1,3,2,0:T(8,128)(2,1)}, bf16[5,1024,64]{1,2,0:T(8,128)(2,1)}, bf16[5,1024,64]{1,2,0:T(8,128)(2,1)}, bf16[5,256,4,6...) while((s32[]{:T(128)}, bf16[5,256,4,64]{1,3,2,0:T(8,128)(2,1)}, ...), condition=%wide.region_4.5_spmd.clone, body=%wide.region_1.0_spmd.clone.sunk | while | flops 275121152 | bytes 5520477 | solution.py:66
  169.4 4.3 fusion.153
  173.7 2.8 fusion.154
  176.7 4.3 fusion.153
  181.1 2.8 fusion.154
  184.1 4.3 fusion.153
  188.4 2.8 fusion.154
  191.4 4.3 fusion.153
  195.7 2.8 fusion.154
  198.7 4.3 fusion.153
  203.0 2.8 fusion.154
  205.8 3.4 reshape.353
  209.2 2.2 gather_fusion
  212.4 2.6 multiply_reduce_fusion
  215.4 2.1 collective-permute-done.2
  219.3 30.1 %collective-permute-done.3 = bf16[516,1280]{1,0:T(8,128)(2,1)S(1)} collective-permute-done((bf16[516,1280]{1,0:T(8,128)(2,1)S(1)}, bf16[516,1280]{1,0:T(8,128)(2,1)S(1)}, u32[]{:S(2)}, u32[]{:S(2)}) %collective-permute-start.3) | collective-permute-done | bytes 1320992 | tf_op jit(solution)/shard_map/ppermute | solution.py:20
  250.0 2.1 pad_maximum_fusion.1
  252.3 2.3 collective-permute-start.4
  254.6 58.0 %collective-permute-done.4 = bf16[1032,1280]{1,0:T(8,128)(2,1)} collective-permute-done((bf16[1032,1280]{1,0:T(8,128)(2,1)}, bf16[1032,1280]{1,0:T(8,128)(2,1)}, u32[]{:S(2)}, u32[]{:S(2)}) %collective-permute-start.4) | collective-permute-done | bytes 2641952 | tf_op jit(solution)/shard_map/ppermute | solution.py:20
  312.6 3.1 broadcast_select_fusion.3
  315.8 2.9 pad_maximum_fusion
  318.9 1.4 collective-permute-start.5
  320.3 113.3 %collective-permute-done.5 = bf16[2064,1280]{1,0:T(8,128)(2,1)} collective-permute-done((bf16[2064,1280]{1,0:T(8,128)(2,1)}, bf16[2064,1280]{1,0:T(8,128)(2,1)}, u32[]{:S(2)}, u32[]{:S(2)}) %collective-permute-start.5) | collective-permute-done | bytes 5283872 | tf_op jit(solution)/shard_map/ppermute | solution.py:20
  433.6 8.5 %broadcast_select_fusion.1 = (bf16[2064,1280]{1,0:T(8,128)(2,1)S(1)}, bf16[2064,1280]{1,0:T(8,128)(2,1)S(1)}) fusion(bf16[2064,1280]{1,0:T(8,128)(2,1)} %collective-permute-done.5, pred[]{:T(512)S(6)} %eq.52, bf16[1032,1280]{1,0:T(8,128)(2,1)} %copy-done.2, bf16[1032,1280]{1,0:T(8,128)(2,1)S(1)} %get-tuple-element.73), kind=kLoop, calls=%fused_computation.47 | loop fusion | flops 15851520 | bytes 21135360 | tf_op jit(solution)/shard_map/jit(_where)/select_n | solution.py:225
  442.1 10.8 %fusion.54 = f32[4128,448]{0,1:T(8,128)} fusion(bf16[2064,1280]{1,0:T(8,128)(2,1)S(1)} %get-tuple-element.72, bf16[2064,1280]{1,0:T(8,128)(2,1)S(1)} %get-tuple-element.71, bf16[1,1280,448]{1,2,0:T(8,128)(2,1)S(1)} %copy-done.39), kind=kOutput, calls=%fused_computation.35 | convolution fusion | flops 4755456000 | bytes 19111936 | tf_op jit(solution)/shard_map/dot_general | solution.py:227
  452.9 6.1 fusion.69
  459.0 3.1 select_convert_fusion
  463.4 112.2 %collective-permute-done.6 = bf16[2064,1280]{1,0:T(8,128)(2,1)S(1)} collective-permute-done((bf16[2064,1280]{1,0:T(8,128)(2,1)}, bf16[2064,1280]{1,0:T(8,128)(2,1)S(1)}, u32[]{:S(2)}, u32[]{:S(2)}) %collective-permute-start.6) | collective-permute-done | bytes 5283872 | tf_op jit(solution)/shard_map/ppermute | solution.py:20
  575.7 5.0 convert_add_fusion
  580.7 4.5 select_convert_fusion.1
  585.2 2.4 collective-permute-start.7
  587.6 55.0 %collective-permute-done.7 = bf16[1032,1280]{1,0:T(8,128)(2,1)S(1)} collective-permute-done((bf16[1032,1280]{1,0:T(8,128)(2,1)S(1)}, bf16[1032,1280]{1,0:T(8,128)(2,1)S(1)}, u32[]{:S(2)}, u32[]{:S(2)}) %collective-permute-start.7) | collective-permute-done | bytes 2641952 | tf_op jit(solution)/shard_map/ppermute | solution.py:20
  642.6 4.9 convert_add_fusion.1
  649.0 25.6 %collective-permute-done.8 = bf16[516,1280]{1,0:T(8,128)(2,1)S(1)} collective-permute-done((bf16[516,1280]{1,0:T(8,128)(2,1)S(1)}, bf16[516,1280]{1,0:T(8,128)(2,1)S(1)}, u32[]{:S(2)}, u32[]{:S(2)}) %collective-permute-start.8) | collective-permute-done | bytes 1320992 | tf_op jit(solution)/shard_map/ppermute | solution.py:20
  675.5 2.1 collective-permute-done.9
  (155 shorter events, 40.5 us)
Async XLA Ops:
  7.2 205.3 %copy-start = (bf16[1280,1280]{1,0:T(8,128)(2,1)S(1)}, bf16[1280,1280]{1,0:T(8,128)(2,1)}, u32[]{:S(2)}) copy-start(bf16[1280,1280]{1,0:T(8,128)(2,1)} %param.20) | copy-start | bytes 9830404
  7.2 6.8 copy-start.29
  7.2 198.7 %all-gather.4.cloned.1.call-start = ((), (), s32[]{:S(2)}) async-start(), calls=%async_computation | async-start | bytes 1320960 | tf_op jit(solution)/shard_map/all_gather | solution.py:213
  12.7 10.1 %copy-start.33 = (f32[32]{0:T(128)}, f32[32]{0:T(128)S(1)}, u32[]{:S(2)}) copy-start(f32[32]{0:T(128)S(1)} %negate_power_fusion) | copy-start | bytes 388
  18.2 1.3 copy-start.13
  18.2 13.1 %copy-start.26 = (bf16[2,1280]{1,0:T(2,128)(2,1)S(1)}, bf16[2,1280]{1,0:T(2,128)(2,1)}, u32[]{:S(2)}) copy-start(bf16[2,1280]{1,0:T(2,128)(2,1)} %param.17) | copy-start | bytes 15364
  23.0 11.7 %copy-start.16 = (f32[256,32]{0,1:T(8,128)}, f32[256,32]{0,1:T(8,128)S(1)}, u32[]{:S(2)}) copy-start(f32[256,32]{0,1:T(8,128)S(1)} %get-tuple-element.106) | copy-start | bytes 98308
  28.2 113.2 %collective-permute-start = (bf16[256,640]{1,0:T(8,128)(2,1)}, bf16[256,640]{1,0:T(8,128)(2,1)}, u32[]{:S(2)}, u32[]{:S(2)}) collective-permute-start(bf16[256,640]{1,0:T(8,128)(2,1)} %pad_maximum_fusion.8), channel_id=1, source_target_pairs={{0,1},{1,0},{2,3},{3,2},{4,5},{5,4},{6,7},{7,6},{8,9},{9,8},{10,11... | collective-permute-start | bytes 983048 | tf_op jit(solution)/shard_map/ppermute | solution.py:20
  34.6 45.2 %copy-start.31 = (s32[256]{0:T(256)S(1)}, s32[256]{0:T(256)}, u32[]{:S(2)}) copy-start(s32[256]{0:T(256)} %param.26) | copy-start | bytes 3076
  34.7 45.2 %copy-start.36 = (s32[4]{0:T(128)S(1)}, s32[4]{0:T(128)}, u32[]{:S(2)}) copy-start(s32[4]{0:T(128)} %iota_add_fusion) | copy-start | bytes 52
  76.5 8.6 %copy-start.30 = (f32[1280]{0:T(1024)S(1)}, f32[1280]{0:T(1024)}, u32[]{:S(2)}) copy-start(f32[1280]{0:T(1024)} %param.18) | copy-start | bytes 15364
  79.9 5.3 copy-start.12
  88.7 2.8 copy-start.34
  88.7 2.8 copy-start.38
  88.7 3.5 copy-start.35
  96.2 4.5 copy-start.11
  100.7 3.7 copy-start.28
  123.2 4.6 copy-start.24
  123.2 4.6 copy-start.25
  123.2 5.6 copy-start.20
  127.8 4.1 copy-start.21
  131.2 0.7 copy-start.14
  132.8 4.5 copy-start.22
  140.0 5.6 copy-start.32
  142.7 0.7 copy-start.7
  142.7 1.6 copy-start.9
  144.4 17.4 %collective-permute-start.1 = (bf16[512,640]{1,0:T(8,128)(2,1)}, bf16[512,640]{1,0:T(8,128)(2,1)}, u32[]{:S(2)}, u32[]{:S(2)}) collective-permute-start(bf16[512,640]{1,0:T(8,128)(2,1)} %pad_maximum_fusion.5), channel_id=1, source_target_pairs={{0,2},{1,3},{2,0},{3,1},{4,6},{5,7},{6,4},{7,5},{8,10},{9,11},{10,... | collective-permute-start | bytes 1966088 | tf_op jit(solution)/shard_map/ppermute | solution.py:20
  146.2 6.5 copy-start.17
  151.6 10.2 %copy-start.8 = (bf16[256,640]{1,0:T(8,128)(2,1)S(1)}, bf16[256,640]{1,0:T(8,128)(2,1)}, u32[]{:S(2)}) copy-start(bf16[256,640]{1,0:T(8,128)(2,1)} %copy-done.7) | copy-start | bytes 983044
  151.6 10.2 %copy-start.10 = (bf16[256,640]{1,0:T(8,128)(2,1)S(1)}, bf16[256,640]{1,0:T(8,128)(2,1)}, u32[]{:S(2)}) copy-start(bf16[256,640]{1,0:T(8,128)(2,1)} %copy-done.9) | copy-start | bytes 983044
  163.1 6.1 copy-start.18
  163.1 6.1 copy-start.19
  205.8 5.6 copy-start.37
  205.8 6.6 copy-start.27
  212.4 2.6 copy-start.23
  215.0 2.8 copy-start.3
  215.3 2.2 collective-permute-start.2
  218.0 31.3 %collective-permute-start.3 = (bf16[516,1280]{1,0:T(8,128)(2,1)S(1)}, bf16[516,1280]{1,0:T(8,128)(2,1)S(1)}, u32[]{:S(2)}, u32[]{:S(2)}) collective-permute-start(bf16[516,1280]{1,0:T(8,128)(2,1)S(1)} %pad_maximum_fusion.2), channel_id=1, source_target_pairs={{0,2},{1,3},{2,0},{3,1},{4,6},{5,7},{6,4},{7,5},{8,10},{9,11},{10,... | collective-permute-start | bytes 3962888 | tf_op jit(solution)/shard_map/ppermute | solution.py:20
  249.9 2.2 copy-start.5
  249.9 2.4 copy-start.6
  252.3 60.3 %collective-permute-start.4 = (bf16[1032,1280]{1,0:T(8,128)(2,1)}, bf16[1032,1280]{1,0:T(8,128)(2,1)}, u32[]{:S(2)}, u32[]{:S(2)}) collective-permute-start(bf16[1032,1280]{1,0:T(8,128)(2,1)} %pad_maximum_fusion.1), channel_id=1, source_target_pairs={{0,4},{1,5},{2,6},{3,7},{4,0},{5,1},{6,2},{7,3},{8,12},{9,13},{10,... | collective-permute-start | bytes 7925768 | tf_op jit(solution)/shard_map/ppermute | solution.py:20
  315.7 3.1 copy-start.2
  318.9 114.7 %collective-permute-start.5 = (bf16[2064,1280]{1,0:T(8,128)(2,1)}, bf16[2064,1280]{1,0:T(8,128)(2,1)}, u32[]{:S(2)}, u32[]{:S(2)}) collective-permute-start(bf16[2064,1280]{1,0:T(8,128)(2,1)} %pad_maximum_fusion), channel_id=1, source_target_pairs={{0,8},{1,9},{2,10},{3,11},{4,12},{5,13},{6,14},{7,15},{8,0},{9,1},... | collective-permute-start | bytes 15851528 | tf_op jit(solution)/shard_map/ppermute | solution.py:20
  320.3 121.8 %copy-start.39 = (bf16[1,1280,448]{1,2,0:T(8,128)(2,1)S(1)}, bf16[1,1280,448]{1,2,0:T(8,128)(2,1)}, u32[]{:S(2)}) copy-start(bf16[1,1280,448]{1,2,0:T(8,128)(2,1)} %param.22) | copy-start | bytes 3440644
  442.1 10.8 %copy-start.15 = (bf16[1,224,1280]{2,1,0:T(8,128)(2,1)S(1)}, bf16[1,224,1280]{2,1,0:T(8,128)(2,1)}, u32[]{:S(2)}) copy-start(bf16[1,224,1280]{2,1,0:T(8,128)(2,1)} %param.23) | copy-start | bytes 1720324
  462.2 113.5 %collective-permute-start.6 = (bf16[2064,1280]{1,0:T(8,128)(2,1)}, bf16[2064,1280]{1,0:T(8,128)(2,1)S(1)}, u32[]{:S(2)}, u32[]{:S(2)}) collective-permute-start(bf16[2064,1280]{1,0:T(8,128)(2,1)} %select_convert_fusion), channel_id=1, source_target_pairs={{0,8},{1,9},{2,10},{3,11},{4,12},{5,13},{6,14},{7,15},{8,0},{9,1},... | collective-permute-start | bytes 15851528 | tf_op jit(solution)/shard_map/ppermute | solution.py:20
  585.2 57.3 %collective-permute-start.7 = (bf16[1032,1280]{1,0:T(8,128)(2,1)S(1)}, bf16[1032,1280]{1,0:T(8,128)(2,1)S(1)}, u32[]{:S(2)}, u32[]{:S(2)}) collective-permute-start(bf16[1032,1280]{1,0:T(8,128)(2,1)S(1)} %select_convert_fusion.1), channel_id=1, source_target_pairs={{0,4},{1,5},{2,6},{3,7},{4,0},{5,1},{6,2},{7,3},{8,12},{9,13},{10,... | collective-permute-start | bytes 7925768 | tf_op jit(solution)/shard_map/ppermute | solution.py:20
  647.8 26.8 %collective-permute-start.8 = (bf16[516,1280]{1,0:T(8,128)(2,1)S(1)}, bf16[516,1280]{1,0:T(8,128)(2,1)S(1)}, u32[]{:S(2)}, u32[]{:S(2)}) collective-permute-start(bf16[516,1280]{1,0:T(8,128)(2,1)S(1)} %select_convert_fusion.2), channel_id=1, source_target_pairs={{0,2},{1,3},{2,0},{3,1},{4,6},{5,7},{6,4},{7,5},{8,10},{9,11},{10,... | collective-permute-start | bytes 3962888 | tf_op jit(solution)/shard_map/ppermute | solution.py:20
  675.2 2.4 copy-start.4
  675.2 4.3 copy-start.1
  675.4 2.2 collective-permute-start.9
Sparse Core Ops, SparseCore 0:
  141.6 62.0 all-gather.3
where the time goes:
time: 693 us; the launch traced here: 687 us
  waiting for transfers between devices  405 us (58%)
  matrix products  73.4 us (11%)
  other arithmetic  70 us (10%)
  local copies, waits for them, and re-layouts  69.5 us (10%)
  blocking collectives  41.9 us (6%)
  between operations  15.5 us (2%)
  starting transfers between devices  11.3 us (2%)
    ppermute x10, waiting for transfers between devices, partner(): lax.ppermute(shard, axis, [(i, i ^ 1 << apart) for i in range(lax.axis_si...  405 us
    all_gather x1, blocking collectives, body(): every_row = lax.all_gather(decode_projected, 'req', axis=0, tiled=True)  41.9 us
    sub x5, matrix products, one_head(): weights = jnp.where(mask[None], jnp.exp(scores - top), 0.0)  21.5 us
    unnamed x83, local copies, waits for them, and re-layouts  15.3 us
    dot_general x5, matrix products, one_head(): jnp.einsum('gqk,kd->qgd', weights.astype(jnp.bfloat16), value_head, prefe...  14 us
  transfers between devices with their start and end apart: 11, of which 9 were waited for; matrix products, arithmetic and copies ran while one was open for 18% of the time, Pallas kernels for 0%

commit v1 on v0

v1 whole, which is shorter than its diff:
```python
import functools

import jax
import jax.numpy as jnp
from jax import lax
from jax.experimental import pallas as pl
from jax.experimental.pallas import tpu as pltpu
from jax.sharding import PartitionSpec as P

WIDTH = 1280
QUERY_HEADS = 20
HEAD = 64
QW = 1280
KVW = 640
SHARE = 224
GROUP = 16
SIDE = 4
SLOTS = 4
POSITIONS = 1024
ROWS = 256
HALF = 144
EPS = 1e-05
THETA = 10000.0
NEG = -1e30
F32 = jnp.float32
BF = jnp.bfloat16
NT = (((1,), (1,)), ((), ()))
VMEM_LIMIT = 56 << 20


def place(y, x, z, core):
    return (((y % SIDE) * SIDE + x % SIDE) * SIDE + z % SIDE) * 2 + core


def moves(step):
    pairs = []
    for y in range(SIDE):
        for x in range(SIDE):
            for z in range(SIDE):
                for core in range(2):
                    pairs.append((place(y, x, z, core), place(*step(y, x, z, core))))
    return pairs


def send(array, step):
    return lax.ppermute(array, "req", moves(step))


def other_core(y, x, z, core):
    return y, x, z, 1 - core


def next_x(y, x, z, core):
    return y, x + 1, z, core


def last_x(y, x, z, core):
    return y, x - 1, z, core


def pair_z(y, x, z, core):
    return y, x, z ^ 1, core


def norm_rows(rows, gain):
    rows = rows.astype(F32)
    mean = jnp.mean(rows * rows, axis=-1, keepdims=True)
    return (rows * lax.rsqrt(mean + EPS) * gain).astype(BF)


def lanes(shape):
    return lax.broadcasted_iota(jnp.int32, shape, len(shape) - 1)


def sublanes(shape):
    return lax.broadcasted_iota(jnp.int32, shape, len(shape) - 2)


def rope_tables(position, frequency):
    angle = position * frequency
    sine = jnp.sin(angle)
    low = lanes(angle.shape) % HEAD < HEAD // 2
    return jnp.cos(angle), jnp.where(low, -sine, sine)


def rope(chunk, cosine, sine):
    low = lanes(chunk.shape) % HEAD < HEAD // 2
    other = jnp.where(low, pltpu.roll(chunk, 96, 1), pltpu.roll(chunk, 32, 1))
    return chunk * cosine + other * sine


def pack_kernel(gate_up_ref, down_ref, packed_ref):
    packed_ref[: 2 * SHARE, :] = gate_up_ref[...].astype(F32).T.astype(BF)
    packed_ref[2 * SHARE :, :] = down_ref[...]


def pack_weights(w_gate_up, w_down):
    return pl.pallas_call(
        pack_kernel,
        out_shape=jax.ShapeDtypeStruct((3 * SHARE, WIDTH), BF),
        grid=(1,),
        in_specs=[
            pl.BlockSpec((None, WIDTH, 2 * SHARE), lambda i: (0, 0, 0)),
            pl.BlockSpec((None, SHARE, WIDTH), lambda i: (0, 0, 0)),
        ],
        out_specs=pl.BlockSpec((3 * SHARE, WIDTH), lambda i: (0, 0)),
        compiler_params=pltpu.CompilerParams(vmem_limit_bytes=VMEM_LIMIT),
        cost_estimate=pl.CostEstimate(flops=10**8, transcendentals=0, bytes_accessed=3500000),
        name="pack",
    )(w_gate_up, w_down)


def qkv_kernel(rank_ref, hidden_ref, gain_ref, freq_ref, w_ref, query_ref, kv_ref, normed, cos, sin):
    step = pl.program_id(0)

    @pl.when(step == 0)
    def _():
        normed[...] = norm_rows(hidden_ref[...], gain_ref[...])
        position = (sublanes((ROWS, 128)) * 4 + rank_ref[0]).astype(F32)
        cos[...], sin[...] = rope_tables(position, freq_ref[...])

    projected = jnp.dot(normed[...], w_ref[...], preferred_element_type=F32)
    chunks = [projected[:, i * 128 : (i + 1) * 128] for i in range(5)]

    @pl.when(step < 2)
    def _():
        for i in range(5):
            roped = rope(chunks[i], cos[...], sin[...]).astype(BF)
            query_ref[:, i * 128 : (i + 1) * 128] = roped * jnp.asarray(0.125, BF)

    @pl.when(step == 2)
    def _():
        low = lanes((ROWS, 128)) < HEAD
        first = rope(chunks[0], cos[...], sin[...])
        second = rope(chunks[1], cos[...], sin[...])
        third = jnp.where(low, rope(chunks[2], cos[...], sin[...]), chunks[2])
        swap = lambda value: pltpu.roll(value, 64, 1)
        out = [
            jnp.where(low, first, third),
            jnp.where(low, swap(first), swap(chunks[3])),
            jnp.where(low, second, chunks[3]),
            jnp.where(low, swap(second), swap(chunks[4])),
            jnp.where(low, third, chunks[4]),
        ]
        for i in range(5):
            kv_ref[:, i * 128 : (i + 1) * 128] = out[i].astype(BF)


def prefill_qkv(rank, hidden, gain, freq, w_qkv):
    return pl.pallas_call(
        qkv_kernel,
        out_shape=(
            jax.ShapeDtypeStruct((ROWS, QW), BF),
            jax.ShapeDtypeStruct((ROWS, KVW), BF),
        ),
        grid=(3,),
        in_specs=[
            pl.BlockSpec(memory_space=pltpu.SMEM),
            pl.BlockSpec((ROWS, WIDTH), lambda j: (0, 0)),
            pl.BlockSpec((1, WIDTH), lambda j: (0, 0)),
            pl.BlockSpec((1, 128), lambda j: (0, 0)),
            pl.BlockSpec((WIDTH, KVW), lambda j: (0, j)),
        ],
        out_specs=(
            pl.BlockSpec((ROWS, KVW), lambda j: (0, jnp.minimum(j, 1))),
            pl.BlockSpec((ROWS, KVW), lambda j: (0, 0)),
        ),
        scratch_shapes=[
            pltpu.VMEM((ROWS, WIDTH), BF),
            pltpu.VMEM((ROWS, 128), F32),
            pltpu.VMEM((ROWS, 128), F32),
        ],
        compiler_params=pltpu.CompilerParams(vmem_limit_bytes=VMEM_LIMIT),
        cost_estimate=pl.CostEstimate(flops=4 * 10**9, transcendentals=0, bytes_accessed=7000000),
        name="prefill_qkv",
    )(rank, hidden, gain, freq, w_qkv)


def column(row):
    return jnp.broadcast_to(row, (128, 128)).T


def held_kernel(index_ref, hidden_ref, gain_ref, freq_ref, w_ref, out_ref):
    step = pl.program_id(0)
    normed = norm_rows(hidden_ref[...], gain_ref[...])
    projected = jnp.dot(normed, w_ref[...], preferred_element_type=F32)
    position = (index_ref[pl.ds(step * 2, 2), :] % POSITIONS).astype(F32)
    position = jnp.concatenate([column(position[0:1]), column(position[1:2])], axis=0)
    cosine, sine = rope_tables(position, freq_ref[...])
    low = lanes((256, 128)) < HEAD
    for i in range(5):
        chunk = projected[:, i * 128 : (i + 1) * 128]
        if i < 2:
            chunk = rope(chunk, cosine, sine)
        elif i == 2:
            chunk = jnp.where(low, rope(chunk, cosine, sine), chunk)
        out_ref[:, i * 128 : (i + 1) * 128] = chunk.astype(BF)


def held_rows(index, hidden, gain, freq, w_qkv):
    rows = hidden.shape[0]
    return pl.pallas_call(
        held_kernel,
        out_shape=jax.ShapeDtypeStruct((rows, KVW), BF),
        grid=(rows // 256,),
        in_specs=[
            pl.BlockSpec((8, 128), lambda i: (0, 0)),
            pl.BlockSpec((256, WIDTH), lambda i: (i, 0)),
            pl.BlockSpec((1, WIDTH), lambda i: (0, 0)),
            pl.BlockSpec((1, 128), lambda i: (0, 0)),
            pl.BlockSpec((WIDTH, KVW), lambda i: (0, 2)),
        ],
        out_specs=pl.BlockSpec((256, KVW), lambda i: (i, 0)),
        compiler_params=pltpu.CompilerParams(vmem_limit_bytes=VMEM_LIMIT),
        cost_estimate=pl.CostEstimate(flops=6 * 10**9, transcendentals=0, bytes_accessed=7000000),
        name="held",
    )(index, hidden, gain, freq, w_qkv)


def decode_kernel(
    device_ref,
    length_ref,
    count_ref,
    slot_ref,
    index_ref,
    rows_ref,
    gain_ref,
    freq_ref,
    w_ref,
    cache_ref,
    held_ref,
    out_ref,
    spread,
    query,
    fresh_key,
    fresh_value,
    over,
    result,
):
    step = pl.program_id(0)
    first_slot = device_ref[0] * SLOTS
    index_rows = [index_ref[i : i + 1, :] for i in range(8)]

    @pl.when(step == 0)
    def _():
        spread[...] = (
            sublanes((QW, 384)) % HEAD == lanes((QW, 384)) % HEAD
        ).astype(F32).astype(BF)
        wanted = jnp.broadcast_to(slot_ref[...], (8, 256))
        slot = sublanes((8, 256))
        chosen = ((wanted == first_slot + slot) & (slot < SLOTS)).astype(F32).astype(BF)
        rows = jnp.dot(chosen, rows_ref[...], preferred_element_type=F32)
        normed = norm_rows(rows, gain_ref[...])
        projected = jnp.dot(normed, w_ref[...], preferred_element_type=F32)
        projected = projected.astype(BF).astype(F32)
        row = sublanes((8, 128))
        position = jnp.zeros((8, 128), F32)
        for j in range(SLOTS):
            position = jnp.where(row == j, length_ref[j].astype(F32), position)
        cosine, sine = rope_tables(position, freq_ref[...])
        chunks = [projected[:, i * 128 : (i + 1) * 128] for i in range(15)]
        roped = [rope(chunks[i], cosine, sine).astype(BF) for i in range(13)]
        whole = jnp.concatenate(roped[:10], axis=1).astype(F32) * 0.125
        head_of = sublanes((32, QW))
        keep = lanes((32, QW)) // HEAD == head_of
        group = sublanes((32, 384))
        block = (lanes((32, 384)) // HEAD == group // 4) & (group < QUERY_HEADS)
        for j in range(SLOTS):
            placed = jnp.where(keep, jnp.broadcast_to(whole[j : j + 1], (32, QW)), 0.0)
            turned = jnp.dot(placed.astype(BF), spread[...], preferred_element_type=F32)
            query[j * 32 : (j + 1) * 32, :] = jnp.where(block, turned, 0.0).astype(BF)
        fresh_key[...] = jnp.concatenate(roped[10:13], axis=1).astype(F32)
        fresh_value[...] = jnp.concatenate(chunks[12:15], axis=1)
        counts = jnp.zeros((32, 128), F32)
        for i in range(8):
            entry = i * 128 + lanes((32, 128))
            live = entry < count_ref[0]
            upper = jnp.broadcast_to(index_rows[i] // 128, (32, 128)) == sublanes((32, 128))
            upper = (upper & live).astype(F32).astype(BF)
            lower = jnp.broadcast_to(index_rows[i] % 128, (128, 128)) == sublanes((128, 128))
            lower = lower.astype(F32).astype(BF)
            counts = counts + lax.dot_general(upper, lower, NT, preferred_element_type=F32)
        over[...] = counts

    length = length_ref[step]
    queries = query[pl.ds(pl.multiple_of(step * 32, 32), 32), :]
    taken = over[pl.ds(pl.multiple_of(step * 8, 8), 8), :]
    taken = jnp.concatenate([taken[i : i + 1, :] for i in range(8)], axis=1)
    cache_live = (lanes((1, POSITIONS)) < length) & (taken < 0.5)
    index = jnp.concatenate(index_rows, axis=1)
    held_live = (
        (lanes((1, 1024)) < count_ref[0])
        & (index // POSITIONS == step)
        & (index % POSITIONS < length)
    )
    cache_score = lax.dot_general(queries, cache_ref[:, :384], NT, preferred_element_type=F32)
    held_score = lax.dot_general(queries, held_ref[:, :384], NT, preferred_element_type=F32)
    own_score = jnp.sum(
        queries.astype(F32) * fresh_key[pl.ds(step, 1), :], axis=-1, keepdims=True
    )
    cache_live = jnp.broadcast_to(cache_live, cache_score.shape)
    held_live = jnp.broadcast_to(held_live, held_score.shape)
    cache_score = jnp.where(cache_live, cache_score, NEG)
    held_score = jnp.where(held_live, held_score, NEG)
    top = jnp.maximum(
        jnp.maximum(
            jnp.max(cache_score, axis=-1, keepdims=True), jnp.max(held_score, axis=-1, keepdims=True)
        ),
        own_score,
    )
    cache_weight = jnp.where(cache_live, jnp.exp(cache_score - top), 0.0)
    held_weight = jnp.where(held_live, jnp.exp(held_score - top), 0.0)
    own_weight = jnp.exp(own_score - top)
    total = (
        jnp.sum(cache_weight, axis=-1, keepdims=True)
        + jnp.sum(held_weight, axis=-1, keepdims=True)
        + own_weight
    )
    mixed = jnp.dot(cache_weight.astype(BF), cache_ref[:, 256:], preferred_element_type=F32)
    mixed += jnp.dot(held_weight.astype(BF), held_ref[:, 256:], preferred_element_type=F32)
    mixed += own_weight.astype(BF).astype(F32) * fresh_value[pl.ds(step, 1), :]
    group = sublanes((32, 384))
    block = (lanes((32, 384)) // HEAD == group // 4 + 1) & (group < QUERY_HEADS)
    mixed = jnp.where(block, mixed / total, 0.0).astype(BF)
    turned = lax.dot_general(mixed, spread[...], NT, preferred_element_type=F32)
    keep = lanes((32, QW)) // HEAD == sublanes((32, QW))
    result[pl.ds(step, 1), :] = jnp.sum(jnp.where(keep, turned, 0.0), axis=0, keepdims=True)

    @pl.when(step == SLOTS - 1)
    def _():
        wanted = jnp.broadcast_to(slot_ref[...], (8, 256))
        slot = sublanes((8, 256))
        chosen = ((wanted == first_slot + slot) & (slot < SLOTS)).astype(F32).astype(BF)
        good = jnp.where(sublanes((8, QW)) < SLOTS, result[...], 0.0).astype(BF)
        out_ref[...] = lax.dot_general(
            chosen, good, (((0,), (0,)), ((), ())), preferred_element_type=F32
        ).astype(BF)


def decode_attention(
    device, length, count, slots, index, rows, gain, freq, w_qkv, cache, held
):
    smem = pl.BlockSpec(memory_space=pltpu.SMEM)
    full = lambda shape: pl.BlockSpec(shape, lambda j: (0,) * len(shape))
    return pl.pallas_call(
        decode_kernel,
        out_shape=jax.ShapeDtypeStruct((256, QW), BF),
        grid=(SLOTS,),
        in_specs=[
            smem,
            smem,
            smem,
            full((1, 256)),
            full((8, 128)),
            full((256, WIDTH)),
            full((1, WIDTH)),
            full((1, 128)),
            full((WIDTH, QW + KVW)),
            pl.BlockSpec((None, POSITIONS, KVW), lambda j: (j, 0, 0)),
            full((1024, KVW)),
        ],
        out_specs=full((256, QW)),
        scratch_shapes=[
            pltpu.VMEM((QW, 384), BF),
            pltpu.VMEM((128, 384), BF),
            pltpu.VMEM((8, 384), F32),
            pltpu.VMEM((8, 384), F32),
            pltpu.VMEM((32, 128), F32),
            pltpu.VMEM((8, QW), F32),
        ],
        compiler_params=pltpu.CompilerParams(vmem_limit_bytes=VMEM_LIMIT),
        cost_estimate=pl.CostEstimate(flops=8 * 10**9, transcendentals=0, bytes_accessed=13000000),
        name="decode",
    )(device, length, count, slots, index, rows, gain, freq, w_qkv, cache, held)


def attention_kernel(
    rank_ref,
    query_ref,
    own_ref,
    core_ref,
    zed_ref,
    far_ref,
    w_ref,
    hidden_ref,
    decode_ref,
    back_ref,
    gain_ref,
    resid_ref,
    normed_ref,
    lower_ref,
    upper_ref,
    total,
    decode_mixed,
    mask,
):
    group = pl.program_id(0)

    @pl.when(group == 0)
    def _():
        total[...] = jnp.zeros_like(total)
        source = lanes((32, 256)) % 2
        row = sublanes((32, 256))
        pick = ((row == 0) & (source == 0)) | ((row == 16) & (source == 1))
        pick = pick.astype(F32).astype(BF)
        decode_mixed[...] = jnp.dot(
            pick, back_ref[...], preferred_element_type=F32
        ).astype(BF)
        rank = rank_ref[0]
        row = sublanes((128, 128))
        col = lanes((128, 128))
        for piece in range(4):
            other = rank ^ piece
            bound = jnp.where(other <= rank, 0, 1)
            mask[:, piece * 128 : (piece + 1) * 128] = jnp.where(col + bound <= row, 0.0, NEG)

    pieces = [own_ref, core_ref, zed_ref, far_ref]
    keys = jnp.concatenate(
        [ref[h * 128 : (h + 1) * 128, :] for h in range(2) for ref in pieces], axis=0
    )
    low = lanes((1024, 128)) < HEAD
    wide = keys.astype(F32)
    values = jnp.where(low, pltpu.roll(wide, 64, 1), wide).astype(BF)
    values = jnp.concatenate([values, jnp.ones((1024, 128), BF)], axis=1)
    low = lanes((128, 128)) < HEAD
    blocked = mask[...]
    mixed = []
    for tile in range(2):
        heads = []
        for pair in range(2):
            two = query_ref[tile * 128 : (tile + 1) * 128, pair * 128 : (pair + 1) * 128].astype(F32)
            heads.append(jnp.where(low, two, 0.0).astype(BF))
            heads.append(jnp.where(low, pltpu.roll(two, 64, 1), 0.0).astype(BF))
        out = []
        for head in heads:
            count = 512 * (tile + 1)
            score = lax.dot_general(head, keys[:count], NT, preferred_element_type=F32)
            if tile == 0:
                score = score + blocked
            else:
                score = jnp.concatenate([score[:, :512], score[:, 512:] + blocked], axis=1)
            top = jnp.max(score, axis=-1, keepdims=True)
            weight = jnp.exp(score - top).astype(BF)
            both = jnp.dot(weight, values[:count], preferred_element_type=F32)
            out.append(both[:, :128] / both[:, 128:])
        mixed.append(
            jnp.concatenate(
                [jnp.where(low, out[0], out[1]), jnp.where(low, out[2], out[3])], axis=1
            ).astype(BF)
        )
    extra = decode_mixed[:, pl.ds(pl.multiple_of(group * 256, 256), 256)]
    rows = jnp.concatenate([mixed[0], extra[:16], mixed[1], extra[16:]], axis=0)
    total[...] += jnp.dot(rows, w_ref[...], preferred_element_type=F32)

    @pl.when(group == 4)
    def _():
        first = sublanes((16, WIDTH)) == 0
        single = decode_ref[...].astype(F32)
        for part in range(2):
            alone = jnp.where(first, jnp.broadcast_to(single[part : part + 1], (16, WIDTH)), 0.0)
            hidden = jnp.concatenate(
                [hidden_ref[part * 128 : (part + 1) * 128, :].astype(F32), alone], axis=0
            )
            resid = (hidden + total[part * HALF : (part + 1) * HALF, :]).astype(BF)
            normed = norm_rows(resid, gain_ref[...])
            resid_ref[part * HALF : (part + 1) * HALF, :] = resid
            normed_ref[part * HALF : (part + 1) * HALF, :] = normed
            (lower_ref, upper_ref)[part][...] = normed


def attention(rank, query, own, core, zed, far, w_out, hidden, decode, back, gain):
    full = lambda shape: pl.BlockSpec(shape, lambda g: (0,) * len(shape))
    side = pl.BlockSpec((ROWS, 128), lambda g: (0, g))
    return pl.pallas_call(
        attention_kernel,
        out_shape=(
            jax.ShapeDtypeStruct((2 * HALF, WIDTH), BF),
            jax.ShapeDtypeStruct((2 * HALF, WIDTH), BF),
            jax.ShapeDtypeStruct((HALF, WIDTH), BF),
            jax.ShapeDtypeStruct((HALF, WIDTH), BF),
        ),
        grid=(5,),
        in_specs=[
            pl.BlockSpec(memory_space=pltpu.SMEM),
            pl.BlockSpec((ROWS, 256), lambda g: (0, g)),
            side,
            side,
            side,
            side,
            pl.BlockSpec((256, WIDTH), lambda g: (g, 0)),
            full((ROWS, WIDTH)),
            full((2, WIDTH)),
            full((256, WIDTH)),
            full((1, WIDTH)),
        ],
        out_specs=(
            full((2 * HALF, WIDTH)),
            full((2 * HALF, WIDTH)),
            full((HALF, WIDTH)),
            full((HALF, WIDTH)),
        ),
        scratch_shapes=[
            pltpu.VMEM((2 * HALF, WIDTH), F32),
            pltpu.VMEM((32, WIDTH), BF),
            pltpu.VMEM((128, 512), F32),
        ],
        compiler_params=pltpu.CompilerParams(vmem_limit_bytes=VMEM_LIMIT),
        cost_estimate=pl.CostEstimate(flops=12 * 10**9, transcendentals=0, bytes_accessed=8000000),
        name="attention",
    )(rank, query, own, core, zed, far, w_out, hidden, decode, back, gain)


def feed_kernel(mine_ref, other_ref, w_ref, mine_out, other_out, total):
    step = pl.program_id(0)
    rows = jnp.concatenate([mine_ref[...], other_ref[...]], axis=0)
    gate = lax.dot_general(rows, w_ref[:SHARE, :], NT, preferred_element_type=F32)
    up = lax.dot_general(rows, w_ref[SHARE : 2 * SHARE, :], NT, preferred_element_type=F32)
    act = (gate / (1.0 + jnp.exp(-gate)) * up).astype(BF)
    down = jnp.dot(act, w_ref[2 * SHARE :, :], preferred_element_type=F32)

    @pl.when(step == 0)
    def _():
        total[...] = down

    @pl.when((step > 0) & (step < SIDE - 1))
    def _():
        total[...] += down

    @pl.when(step == SIDE - 1)
    def _():
        done = total[...] + down
        mine_out[...] = done[: 2 * HALF]
        other_out[...] = done[2 * HALF :].astype(BF)


def feed_forward(mine, other, weights, name):
    full = pl.BlockSpec((2 * HALF, WIDTH), lambda i: (0, 0))
    return pl.pallas_call(
        feed_kernel,
        out_shape=(
            jax.ShapeDtypeStruct((2 * HALF, WIDTH), F32),
            jax.ShapeDtypeStruct((2 * HALF, WIDTH), BF),
        ),
        grid=(SIDE,),
        in_specs=[
            full,
            full,
            pl.BlockSpec((None, 3 * SHARE, WIDTH), lambda i: (i, 0, 0)),
        ],
        out_specs=(full, full),
        scratch_shapes=[pltpu.VMEM((4 * HALF, WIDTH), F32)],
        compiler_params=pltpu.CompilerParams(vmem_limit_bytes=VMEM_LIMIT),
        cost_estimate=pl.CostEstimate(flops=6 * 10**9, transcendentals=0, bytes_accessed=11000000),
        name=name,
    )(mine, other, weights)


def add_kernel(mine_ref, other_ref, first_ref, second_ref):
    whole = mine_ref[...] + other_ref[...].astype(F32)
    first_ref[...] = whole[:HALF].astype(BF)
    second_ref[...] = whole[HALF:].astype(BF)


def add_halves(mine, other):
    half = jax.ShapeDtypeStruct((HALF, WIDTH), BF)
    return pl.pallas_call(
        add_kernel,
        out_shape=(half, half),
        compiler_params=pltpu.CompilerParams(vmem_limit_bytes=VMEM_LIMIT),
        cost_estimate=pl.CostEstimate(flops=10**6, transcendentals=0, bytes_accessed=3000000),
        name="add",
    )(mine, other)


def final_kernel(resid_ref, mine_ref, other_ref, first_ref, second_ref, prefill_ref, decode_ref):
    decode = []
    for part, ref in ((0, first_ref), (1, second_ref)):
        cut = slice(part * HALF, (part + 1) * HALF)
        whole = resid_ref[cut, :].astype(F32) + (
            mine_ref[cut, :] + other_ref[cut, :].astype(F32) + ref[...].astype(F32)
        )
        prefill_ref[part * 128 : (part + 1) * 128, :] = whole[:128].astype(BF)
        decode.append(whole[128:129])
    decode_ref[...] = jnp.concatenate(decode, axis=0).astype(BF)


def final_sum(resid, mine, other, first, second):
    return pl.pallas_call(
        final_kernel,
        out_shape=(
            jax.ShapeDtypeStruct((ROWS, WIDTH), BF),
            jax.ShapeDtypeStruct((2, WIDTH), BF),
        ),
        compiler_params=pltpu.CompilerParams(vmem_limit_bytes=VMEM_LIMIT),
        cost_estimate=pl.CostEstimate(flops=10**6, transcendentals=0, bytes_accessed=5000000),
        name="final",
    )(resid, mine, other, first, second)


def body(
    prefill_hidden,
    decode_hidden,
    attn_gain,
    w_qkv,
    w_out,
    ffn_gain,
    w_gate_up,
    w_down,
    key_value_cache,
    cache_len,
    slot_of_request,
    held_hidden,
    recomputed_index,
    recomp_count,
):
    device = lax.axis_index("req").astype(jnp.int32).reshape(1)
    rank = device % 4
    gain = attn_gain.reshape(1, WIDTH)
    gain2 = ffn_gain.reshape(1, WIDTH)
    half = HEAD // 2
    frequency = THETA ** (-(jnp.arange(half).astype(F32) * 2.0 / HEAD))
    freq = jnp.tile(frequency, 4).reshape(1, 128)
    index = recomputed_index.reshape(8, 128)

    packed = pack_weights(w_gate_up, w_down)
    columns = [
        [place(y, x, z, core) for z in range(SIDE)]
        for y in range(SIDE)
        for x in range(SIDE)
        for core in range(2)
    ]
    weights = lax.all_gather(packed, "req", axis_index_groups=columns)

    total = 2 * SIDE**3
    spread = jnp.broadcast_to(decode_hidden[None], (total, 2, WIDTH))
    every_row = lax.all_to_all(spread, "req", 0, 0).reshape(256, WIDTH)

    query, kv = prefill_qkv(rank, prefill_hidden, gain, freq, w_qkv)
    zed = send(kv, pair_z)
    core = send(kv, other_core)
    held = held_rows(index, held_hidden, gain, freq, w_qkv)
    far = send(zed, other_core)

    outgoing = decode_attention(
        device,
        cache_len,
        recomp_count,
        slot_of_request.reshape(1, 256),
        index,
        every_row,
        gain,
        freq,
        w_qkv,
        key_value_cache,
        held,
    )
    back = lax.all_to_all(outgoing.reshape(total, 2, WIDTH), "req", 0, 0).reshape(256, WIDTH)

    resid, normed, lower, upper = attention(
        rank, query, kv, core, zed, far, w_out, prefill_hidden, decode_hidden, back, gain2
    )
    from_last = send(lower, next_x)
    from_next = send(upper, last_x)
    across = send(normed, other_core)
    mine, given = feed_forward(normed, across, weights, "feed_own")
    given = send(given, other_core)
    guests = jnp.concatenate([from_last, from_next], axis=0)
    guests_across = send(guests, other_core)
    guest_mine, guest_given = feed_forward(guests, guests_across, weights, "feed_guest")
    guest_given = send(guest_given, other_core)
    to_last, to_next = add_halves(guest_mine, guest_given)
    first = send(to_last, last_x)
    second = send(to_next, next_x)
    return final_sum(resid, mine, given, first, second)


def solution(mesh):
    return jax.shard_map(
        body,
        mesh=mesh,
        in_specs=(
            P("req", None),
            P("req", None),
            P(),
            P(),
            P(),
            P(),
            P("req", None, None),
            P("req", None, None),
            P("req", None, None),
            P("req"),
            P(),
            P("req", None),
            P("req"),
            P("req"),
        ),
        out_specs=(P("req", None), P("req", None)),
        check_vma=False,
    )
```

time: 693 us -> 164 us (0.24)
  waiting for transfers between devices: 405 us -> 32.5 us
  matrix products: 73.4 us -> 0 us
  other arithmetic: 70 us -> 0.01 us
  Pallas kernels: 0 us -> 69.7 us
  local copies, waits for them, and re-layouts: 69.5 us -> 15.4 us
  blocking collectives: 41.9 us -> 0 us
  starting transfers between devices: 11.3 us -> 30.5 us
    ppermute x10 -> x11, waiting for transfers between devices: 405 us -> 18.6 us  [send(): return lax.ppermute(array, 'req', moves(step))]
    pallas_call x0 -> x9, Pallas kernels: none -> 69.7 us  [the longest x2 20.4 us: feed_forward(): pl.pallas_call(feed_kernel, out_shape=(jax.ShapeDtypeStruct((2 * HALF, WI...]
    dot_general x15 -> x0, matrix products: 51.9 us -> none  [the longest x5 14 us: one_head(): jnp.einsum('gqk,kd->qgd', weights.astype(jnp.bfloat16), value_head, prefe...]
    all_gather x1 -> x0, blocking collectives: 41.9 us -> none  [body(): every_row = lax.all_gather(decode_projected, 'req', axis=0, tiled=True)]
    slice x14 -> x0, local copies, waits for them, and re-layouts: 32.4 us -> none  [the longest x2 11.8 us: body(): slot_cache[:, :, :key_value_width]]
    sub x5 -> x0, matrix products: 21.5 us -> none  [one_head(): weights = jnp.where(mask[None], jnp.exp(scores - top), 0.0)]
    all_to_all x0 -> x2, starting transfers between devices: none -> 21.2 us  [the longest x1 11.1 us: body(): every_row = lax.all_to_all(spread, 'req', 0, 0).reshape(256, WIDTH)]
    select_n x7 -> x0, other arithmetic: 15.2 us -> none  [the longest x4 12.5 us: body(): jnp.where(upper_side, other, gathered)]
  transfers between devices with their start and end apart: 11 -> 14, of which waited for: 9 -> 4; matrix products, arithmetic and copies ran while one was open for 18% -> 5% of each run, Pallas kernels for 0% -> 39%
where the time goes in v1:
time: 164 us; the launch traced here: 163 us
  Pallas kernels  69.7 us (42%)
  waiting for transfers between devices  32.5 us (20%)
  starting transfers between devices  30.5 us (19%)
  local copies, waits for them, and re-layouts  15.4 us (9%)
  between operations  14.8 us (9%)
    pallas_call x2, Pallas kernels, feed_forward(): pl.pallas_call(feed_kernel, out_shape=(jax.ShapeDtypeStruct((2 * HALF, WI...  20.4 us
    ppermute x11, waiting for transfers between devices, send(): return lax.ppermute(array, 'req', moves(step))  18.6 us
    all_to_all x1, waiting for transfers between devices, body(): lax.all_to_all(outgoing.reshape(total, 2, WIDTH), 'req', 0, 0)  13.9 us
    pallas_call x1, Pallas kernels, attention(): pl.pallas_call(attention_kernel, out_shape=(jax.ShapeDtypeStruct((2 * HAL...  13.6 us
    pallas_call x1, Pallas kernels, decode_attention(): pl.pallas_call(decode_kernel, out_shape=jax.ShapeDtypeStruct((256, QW), B...  12.5 us
    all_to_all x1, starting transfers between devices, body(): every_row = lax.all_to_all(spread, 'req', 0, 0).reshape(256, WIDTH)  11.1 us
    all_to_all x1, starting transfers between devices, body(): lax.all_to_all(outgoing.reshape(total, 2, WIDTH), 'req', 0, 0)  10 us
    ppermute x11, starting transfers between devices, send(): return lax.ppermute(array, 'req', moves(step))  9.25 us
  transfers between devices with their start and end apart: 14, of which 4 were waited for; matrix products, arithmetic and copies ran while one was open for 5% of the time, Pallas kernels for 39%

profile of v1, /device:TPU:0, one launch (start us, length us, event | category | flops | bytes accessed | tf_op | source)
XLA Modules:
  0.0 162.9 jit_solution(2752650716372657261)
XLA Ops:
  7.2 0.0 all-gather.3.cloned.1.call-start
  7.2 2.4 %copy.16.gate_up_ref = bf16[1,1280,448]{2,1,0:T(8,128)(2,1)} copy(bf16[1,1280,448]{1,2,0:T(8,128)(2,1)} %param.20) | data formatting | bytes 2293760 | tf_op args[6]
  9.6 3.1 %pack.1 = bf16[672,1280]{1,0:T(8,128)(2,1)} custom-call(bf16[1,1280,448]{2,1,0:T(8,128)(2,1)} %copy.16.gate_up_ref, bf16[1,224,1280]{2,1,0:T(8,128)(2,1)} %down_ref.1), custom_call_target="tpu_custom_call" | custom-call | flops 100000000 | bytes 3500000 | tf_op jit(solution)/shard_map/pack/pallas_call | solution.py:98
  12.8 0.0 copy-start.7
  12.8 0.0 copy-start.5
  12.8 0.0 all-gather.3.cloned.1.call-update
  12.8 0.7 copy-done.7
  13.5 1.2 broadcast_in_dim.2
  14.7 11.1 %all-to-all-start = ((bf16[128,2,1280]{2,1,0:T(2,128)(2,1)}), bf16[128,2,1280]{2,1,0:T(2,128)(2,1)S(1)}, u32[]{:S(2)}, u32[]{:S(2)}) async-start(bf16[128,2,1280]{2,1,0:T(2,128)(2,1)} %broadcast_in_dim.2), calls=%async_computation | async-start | bytes 1310720 | tf_op jit(solution)/shard_map/all_to_all | solution.py:636
  25.8 0.0 copy-done.5
  25.8 0.6 reshape.39.gain_ref
  26.4 0.6 reshape_tile.7.freq_ref
  27.1 7.1 %prefill_qkv.1 = (bf16[256,1280]{1,0:T(8,128)(2,1)}, bf16[256,640]{1,0:T(8,128)(2,1)}) custom-call(s32[1]{0:T(128)S(6)} %select_n.7.rank_ref, bf16[256,1280]{1,0:T(8,128)(2,1)} %hidden_ref.5, f32[1,1280]{1,0:T(1,128)} %reshape.39.gain_ref, f32[1,128]{1,0:T(1,128)} %reshape_tile.7.freq_ref, bf16[1280,1920]{1,0:T(8,128)(2,1)} %w_ref.6), custom_call_target="tpu_custom_call" | custom-call | flops 4000000000 | bytes 7000000 | tf_op jit(solution)/shard_map/prefill_qkv/pallas_call | solution.py:150
  34.2 1.1 collective-permute-start.1
  35.9 7.3 %held.1.held_ref = bf16[1024,640]{1,0:T(8,128)(2,1)} custom-call(s32[8,128]{1,0:T(8,128)} %bitcast.6, bf16[1024,1280]{1,0:T(8,128)(2,1)} %hidden_ref.4, f32[1,1280]{1,0:T(1,128)} %reshape.39.gain_ref, f32[1,128]{1,0:T(1,128)} %reshape_tile.7.freq_ref, bf16[1280,1920]{1,0:T(8,128)(2,1)} %w_ref.6), custom_call_target="tpu_custom_call" | custom-call | flops 6000000000 | bytes 7000000 | tf_op jit(solution)/shard_map/held/pallas_call | solution.py:202
  43.2 0.0 all-to-all-done
  43.2 1.1 reshape.42.rows_ref
  44.3 12.5 %decode.1 = bf16[256,1280]{1,0:T(8,128)(2,1)} custom-call(s32[1]{0:T(128)} %bitcast.device_ref, s32[4]{0:T(128)} %length_ref.1, s32[1]{0:T(128)S(6)} %copy.18.count_ref, s32[1,256]{1,0:T(1,128)} %bitcast.8, s32[8,128]{1,0:T(8,128)} %bitcast.7, bf16[256,1280]{1,0:T(8,128)(2,1)} %reshape.42.rows_ref, f32[1,1280]{1,0:T(1,128)} %reshape.39.gain_ref, ...), custom_call_target="tpu_custom_call" | custom-call | flops 8000000000 | bytes 13000000 | tf_op jit(solution)/shard_map/decode/pallas_call | solution.py:345
  56.8 2.7 %reshape.43 = bf16[128,2,1280]{2,1,0:T(2,128)(2,1)} reshape(bf16[256,1280]{1,0:T(8,128)(2,1)} %decode.1) | data formatting | bytes 1310720 | tf_op jit(solution)/shard_map/reshape | solution.py:657
  59.5 10.0 %all-to-all-start.1 = ((bf16[128,2,1280]{2,1,0:T(2,128)(2,1)}), bf16[128,2,1280]{2,1,0:T(2,128)(2,1)S(1)}, u32[]{:S(2)}, u32[]{:S(2)}) async-start(bf16[128,2,1280]{2,1,0:T(2,128)(2,1)} %reshape.43), calls=%async_computation.1 | async-start | bytes 1310720 | tf_op jit(solution)/shard_map/all_to_all | solution.py:657
  69.5 0.0 copy-done.10
  69.5 0.1 collective-permute-start
  69.6 0.0 collective-permute-done.1.zed_ref
  69.7 0.0 copy-start.11
  69.7 0.5 collective-permute-start.2
  70.1 0.0 copy-done.6
  70.1 0.6 reshape.45.gain_ref
  70.7 13.9 %all-to-all-done.1 = bf16[128,2,1280]{2,1,0:T(2,128)(2,1)S(1)} async-done(((bf16[128,2,1280]{2,1,0:T(2,128)(2,1)}), bf16[128,2,1280]{2,1,0:T(2,128)(2,1)S(1)}, u32[]{:S(2)}, u32[]{:S(2)}) %all-to-all-start.1) | async-done | bytes 655392 | tf_op jit(solution)/shard_map/all_to_all | solution.py:657
  84.7 1.1 reshape.44.back_ref
  85.8 0.0 collective-permute-done.core_ref
  85.8 0.0 collective-permute-done.2.far_ref
  85.8 0.0 copy-start.13
  85.8 0.0 copy-done.11
  85.8 0.7 copy-done.12
  86.5 0.2 copy-done.13
  86.7 13.6 %attention.1 = (bf16[288,1280]{1,0:T(8,128)(2,1)}, bf16[288,1280]{1,0:T(8,128)(2,1)}, bf16[144,1280]{1,0:T(8,128)(2,1)}, bf16[144,1280]{1,0:T(8,128)(2,1)}) custom-call(s32[1]{0:T(128)S(6)} %select_n.7.rank_ref, bf16[256,1280]{1,0:T(8,128)(2,1)} %get-tuple-element.14.query_ref, bf16[256,640]{1,0:T(8,128)(2,1)} %get-tuple-element.15.own_ref, ...), custom_call_target="tpu_custom_call" | custom-call | flops 12000000000 | bytes 8000000 | tf_op jit(solution)/shard_map/attention/pallas_call | solution.py:474
  100.3 0.6 collective-permute-start.5
  101.0 2.6 %collective-permute-start.6 = (bf16[144,1280]{1,0:T(8,128)(2,1)}, bf16[144,1280]{1,0:T(8,128)(2,1)S(1)}, u32[]{:S(2)}, u32[]{:S(2)}) collective-permute-start(bf16[144,1280]{1,0:T(8,128)(2,1)} %get-tuple-element.21), channel_id=1, source_target_pairs={{0,24},{1,25},{2,26},{3,27},{4,28},{5,29},{6,30},{7,31},{8,0},{9,1... | collective-permute-start | bytes 1105928 | tf_op jit(solution)/shard_map/ppermute | solution.py:46
  103.6 8.0 %collective-permute-done.5 = bf16[144,1280]{1,0:T(8,128)(2,1)S(1)} collective-permute-done((bf16[144,1280]{1,0:T(8,128)(2,1)}, bf16[144,1280]{1,0:T(8,128)(2,1)S(1)}, u32[]{:S(2)}, u32[]{:S(2)}) %collective-permute-start.5) | collective-permute-done | bytes 368672 | tf_op jit(solution)/shard_map/ppermute | solution.py:46
  111.5 0.0 collective-permute-done.6
  111.6 0.0 copy-start.4
  111.6 0.1 collective-permute-start.7
  111.7 0.5 collective-permute-start.3
  112.2 1.8 %collective-permute-done.7.other_ref = bf16[288,1280]{1,0:T(8,128)(2,1)S(1)} collective-permute-done((bf16[288,1280]{1,0:T(8,128)(2,1)S(1)}, bf16[288,1280]{1,0:T(8,128)(2,1)S(1)}, u32[]{:S(2)}, u32[]{:S(2)}) %collective-permute-start.7) | collective-permute-done | bytes 737312 | tf_op jit(solution)/shard_map/ppermute | solution.py:46
  114.0 0.0 copy-done.4
  114.0 0.9 copy-done.9
  114.9 10.1 %feed_guest.1 = (f32[288,1280]{1,0:T(8,128)}, bf16[288,1280]{1,0:T(8,128)(2,1)}) custom-call(bf16[288,1280]{1,0:T(8,128)(2,1)} %copy-done.4, bf16[288,1280]{1,0:T(8,128)(2,1)} %copy-done.9, bf16[4,672,1280]{2,1,0:T(8,128)(2,1)} %bitcast.4), custom_call_target="tpu_custom_call" | custom-call | flops 6000000000 | bytes 11000000 | tf_op jit(solution)/shard_map/feed_guest/pallas_call | solution.py:538
  125.0 0.1 collective-permute-start.8
  125.2 0.0 collective-permute-done.3.other_ref
  125.2 0.9 copy-done.8
  126.1 10.3 %feed_own.1 = (f32[288,1280]{1,0:T(8,128)}, bf16[288,1280]{1,0:T(8,128)(2,1)}) custom-call(bf16[288,1280]{1,0:T(8,128)(2,1)} %get-tuple-element.17.mine_ref, bf16[288,1280]{1,0:T(8,128)(2,1)} %copy-done.8, bf16[4,672,1280]{2,1,0:T(8,128)(2,1)} %bitcast.5), custom_call_target="tpu_custom_call" | custom-call | flops 6000000000 | bytes 11000000 | tf_op jit(solution)/shard_map/feed_own/pallas_call | solution.py:538
  136.3 0.4 collective-permute-start.4
  136.7 0.0 collective-permute-done.8.other_ref
  136.7 0.9 copy-done.1
  137.6 2.5 %add.8 = (bf16[144,1280]{1,0:T(8,128)(2,1)}, bf16[144,1280]{1,0:T(8,128)(2,1)}) custom-call(f32[288,1280]{1,0:T(8,128)} %get-tuple-element.22.mine_ref, bf16[288,1280]{1,0:T(8,128)(2,1)} %copy-done.1), custom_call_target="tpu_custom_call" | custom-call | flops 1000000 | bytes 3000000 | tf_op jit(solution)/shard_map/add/pallas_call | solution.py:566
  140.0 0.0 collective-permute-start.10
  140.0 3.2 %collective-permute-start.9 = (bf16[144,1280]{1,0:T(8,128)(2,1)}, bf16[144,1280]{1,0:T(8,128)(2,1)S(1)}, u32[]{:S(2)}, u32[]{:S(2)}) collective-permute-start(bf16[144,1280]{1,0:T(8,128)(2,1)} %get-tuple-element.24), channel_id=1, source_target_pairs={{0,24},{1,25},{2,26},{3,27},{4,28},{5,29},{6,30},{7,31},{8,0},{9,1... | collective-permute-start | bytes 1105928 | tf_op jit(solution)/shard_map/ppermute | solution.py:46
  143.3 0.0 collective-permute-done.4.other_ref
  143.3 8.8 %collective-permute-done.10.second_ref = bf16[144,1280]{1,0:T(8,128)(2,1)S(1)} collective-permute-done((bf16[144,1280]{1,0:T(8,128)(2,1)}, bf16[144,1280]{1,0:T(8,128)(2,1)S(1)}, u32[]{:S(2)}, u32[]{:S(2)}) %collective-permute-start.10) | collective-permute-done | bytes 368672 | tf_op jit(solution)/shard_map/ppermute | solution.py:46
  152.1 0.0 collective-permute-done.9.first_ref
  152.1 0.0 copy-done
  152.1 0.7 copy-done.2
  152.8 0.1 copy-done.3
  153.0 3.1 %final.1 = (bf16[256,1280]{1,0:T(8,128)(2,1)}, bf16[2,1280]{1,0:T(2,128)(2,1)}) custom-call(bf16[288,1280]{1,0:T(8,128)(2,1)} %get-tuple-element.16.resid_ref, f32[288,1280]{1,0:T(8,128)} %get-tuple-element.18.mine_ref, bf16[288,1280]{1,0:T(8,128)(2,1)} %copy-done, bf16[144,1280]{1,0:T(8,128)(2,1)} %copy-done.3, bf16[144,1280]{1,0:T(8,128)(2,1)} %copy-done.2), custom_call_target="tpu_custom_call" | custom-call | flops 1000000 | bytes 5000000 | tf_op jit(solution)/shard_map/final/pallas_call | solution.py:588
  (14 shorter events, 0.1 us)
Async XLA Ops:
  7.2 106.9 %all-gather.3.cloned.1.call-start = ((), (), s32[]{:S(2)}) async-start(), calls=%async_computation.2 | async-start | bytes 8601600 | tf_op jit(solution)/shard_map/all_gather | solution.py:632
  12.8 0.7 copy-start.7
  12.8 13.0 %copy-start.5 = (f32[1280]{0:T(1024)S(1)}, f32[1280]{0:T(1024)}, u32[]{:S(2)}) copy-start(f32[1280]{0:T(1024)} %param.16) | copy-start | bytes 15364
  14.7 28.5 %all-to-all-start = ((bf16[128,2,1280]{2,1,0:T(2,128)(2,1)}), bf16[128,2,1280]{2,1,0:T(2,128)(2,1)S(1)}, u32[]{:S(2)}, u32[]{:S(2)}) async-start(bf16[128,2,1280]{2,1,0:T(2,128)(2,1)} %broadcast_in_dim.2), calls=%async_computation | async-start | bytes 1310720 | tf_op jit(solution)/shard_map/all_to_all | solution.py:636
  34.2 35.5 %collective-permute-start.1 = (bf16[256,640]{1,0:T(8,128)(2,1)}, bf16[256,640]{1,0:T(8,128)(2,1)S(1)}, u32[]{:S(2)}, u32[]{:S(2)}) collective-permute-start(bf16[256,640]{1,0:T(8,128)(2,1)} %get-tuple-element.15.own_ref), channel_id=1, source_target_pairs={{0,2},{1,3},{2,0},{3,1},{4,6},{5,7},{6,4},{7,5},{8,10},{9,11},{10,... | collective-permute-start | bytes 983048 | tf_op jit(solution)/shard_map/ppermute | solution.py:46
  56.8 12.7 %copy-start.10 = (bf16[256,640]{1,0:T(8,128)(2,1)S(1)}, bf16[256,640]{1,0:T(8,128)(2,1)}, u32[]{:S(2)}) copy-start(bf16[256,640]{1,0:T(8,128)(2,1)} %get-tuple-element.15.own_ref) | copy-start | bytes 983044
  56.8 13.4 %copy-start.6 = (f32[1280]{0:T(1024)S(1)}, f32[1280]{0:T(1024)}, u32[]{:S(2)}) copy-start(f32[1280]{0:T(1024)} %param.19) | copy-start | bytes 15364
  59.5 25.2 %all-to-all-start.1 = ((bf16[128,2,1280]{2,1,0:T(2,128)(2,1)}), bf16[128,2,1280]{2,1,0:T(2,128)(2,1)S(1)}, u32[]{:S(2)}, u32[]{:S(2)}) async-start(bf16[128,2,1280]{2,1,0:T(2,128)(2,1)} %reshape.43), calls=%async_computation.1 | async-start | bytes 1310720 | tf_op jit(solution)/shard_map/all_to_all | solution.py:657
  69.5 16.2 %collective-permute-start = (bf16[256,640]{1,0:T(8,128)(2,1)S(1)}, bf16[256,640]{1,0:T(8,128)(2,1)S(1)}, u32[]{:S(2)}, u32[]{:S(2)}) collective-permute-start(bf16[256,640]{1,0:T(8,128)(2,1)S(1)} %copy-done.10), channel_id=1, source_target_pairs={{0,1},{1,0},{2,3},{3,2},{4,5},{5,4},{6,7},{7,6},{8,9},{9,8},{10,11... | collective-permute-start | bytes 983048 | tf_op jit(solution)/shard_map/ppermute | solution.py:46
  69.7 16.1 %copy-start.11 = (bf16[256,640]{1,0:T(8,128)(2,1)}, bf16[256,640]{1,0:T(8,128)(2,1)S(1)}, u32[]{:S(2)}) copy-start(bf16[256,640]{1,0:T(8,128)(2,1)S(1)} %collective-permute-done.1.zed_ref) | copy-start | bytes 983044
  69.7 16.1 %collective-permute-start.2 = (bf16[256,640]{1,0:T(8,128)(2,1)S(1)}, bf16[256,640]{1,0:T(8,128)(2,1)S(1)}, u32[]{:S(2)}, u32[]{:S(2)}) collective-permute-start(bf16[256,640]{1,0:T(8,128)(2,1)S(1)} %collective-permute-done.1.zed_ref), channel_id=1, source_target_pairs={{0,1},{1,0},{2,3},{3,2},{4,5},{5,4},{6,7},{7,6},{8,9},{9,8},{10,11... | collective-permute-start | bytes 983048 | tf_op jit(solution)/shard_map/ppermute | solution.py:46
  85.8 0.8 copy-start.12
  85.8 0.9 copy-start.13
  100.3 11.2 %collective-permute-start.5 = (bf16[144,1280]{1,0:T(8,128)(2,1)}, bf16[144,1280]{1,0:T(8,128)(2,1)S(1)}, u32[]{:S(2)}, u32[]{:S(2)}) collective-permute-start(bf16[144,1280]{1,0:T(8,128)(2,1)} %get-tuple-element.20), channel_id=1, source_target_pairs={{0,8},{1,9},{2,10},{3,11},{4,12},{5,13},{6,14},{7,15},{8,16},{9,17... | collective-permute-start | bytes 1105928 | tf_op jit(solution)/shard_map/ppermute | solution.py:46
  101.0 10.6 %collective-permute-start.6 = (bf16[144,1280]{1,0:T(8,128)(2,1)}, bf16[144,1280]{1,0:T(8,128)(2,1)S(1)}, u32[]{:S(2)}, u32[]{:S(2)}) collective-permute-start(bf16[144,1280]{1,0:T(8,128)(2,1)} %get-tuple-element.21), channel_id=1, source_target_pairs={{0,24},{1,25},{2,26},{3,27},{4,28},{5,29},{6,30},{7,31},{8,0},{9,1... | collective-permute-start | bytes 1105928 | tf_op jit(solution)/shard_map/ppermute | solution.py:46
  111.6 2.4 %copy-start.4 = (bf16[288,1280]{1,0:T(8,128)(2,1)}, bf16[288,1280]{1,0:T(8,128)(2,1)S(1)}, u32[]{:S(2)}) copy-start(bf16[288,1280]{1,0:T(8,128)(2,1)S(1)} %constant_dynamic-update-slice_fusion.mine_ref) | copy-start | bytes 2211844
  111.6 2.4 %collective-permute-start.7 = (bf16[288,1280]{1,0:T(8,128)(2,1)S(1)}, bf16[288,1280]{1,0:T(8,128)(2,1)S(1)}, u32[]{:S(2)}, u32[]{:S(2)}) collective-permute-start(bf16[288,1280]{1,0:T(8,128)(2,1)S(1)} %constant_dynamic-update-slice_fusion.mine_ref), channel_id=1, source_target_pairs={{0,1},{1,0},{2,3},{3,2},{4,5},{5,4},{6,7},{7,6},{8,9},{9,8},{10,11... | collective-permute-start | bytes 2211848 | tf_op jit(solution)/shard_map/ppermute | solution.py:46
  111.7 13.5 %collective-permute-start.3 = (bf16[288,1280]{1,0:T(8,128)(2,1)}, bf16[288,1280]{1,0:T(8,128)(2,1)S(1)}, u32[]{:S(2)}, u32[]{:S(2)}) collective-permute-start(bf16[288,1280]{1,0:T(8,128)(2,1)} %get-tuple-element.17.mine_ref), channel_id=1, source_target_pairs={{0,1},{1,0},{2,3},{3,2},{4,5},{5,4},{6,7},{7,6},{8,9},{9,8},{10,11... | collective-permute-start | bytes 2211848 | tf_op jit(solution)/shard_map/ppermute | solution.py:46
  114.0 0.9 copy-start.9
  125.0 11.7 %collective-permute-start.8 = (bf16[288,1280]{1,0:T(8,128)(2,1)}, bf16[288,1280]{1,0:T(8,128)(2,1)S(1)}, u32[]{:S(2)}, u32[]{:S(2)}) collective-permute-start(bf16[288,1280]{1,0:T(8,128)(2,1)} %get-tuple-element.23), channel_id=1, source_target_pairs={{0,1},{1,0},{2,3},{3,2},{4,5},{5,4},{6,7},{7,6},{8,9},{9,8},{10,11... | collective-permute-start | bytes 2211848 | tf_op jit(solution)/shard_map/ppermute | solution.py:46
  125.2 0.9 copy-start.8
  136.3 7.0 %collective-permute-start.4 = (bf16[288,1280]{1,0:T(8,128)(2,1)}, bf16[288,1280]{1,0:T(8,128)(2,1)S(1)}, u32[]{:S(2)}, u32[]{:S(2)}) collective-permute-start(bf16[288,1280]{1,0:T(8,128)(2,1)} %get-tuple-element.19), channel_id=1, source_target_pairs={{0,1},{1,0},{2,3},{3,2},{4,5},{5,4},{6,7},{7,6},{8,9},{9,8},{10,11... | collective-permute-start | bytes 2211848 | tf_op jit(solution)/shard_map/ppermute | solution.py:46
  136.7 0.9 copy-start.1
  140.0 12.1 %collective-permute-start.10 = (bf16[144,1280]{1,0:T(8,128)(2,1)}, bf16[144,1280]{1,0:T(8,128)(2,1)S(1)}, u32[]{:S(2)}, u32[]{:S(2)}) collective-permute-start(bf16[144,1280]{1,0:T(8,128)(2,1)} %get-tuple-element.25), channel_id=1, source_target_pairs={{0,8},{1,9},{2,10},{3,11},{4,12},{5,13},{6,14},{7,15},{8,16},{9,17... | collective-permute-start | bytes 1105928 | tf_op jit(solution)/shard_map/ppermute | solution.py:46
  140.0 12.1 %collective-permute-start.9 = (bf16[144,1280]{1,0:T(8,128)(2,1)}, bf16[144,1280]{1,0:T(8,128)(2,1)S(1)}, u32[]{:S(2)}, u32[]{:S(2)}) collective-permute-start(bf16[144,1280]{1,0:T(8,128)(2,1)} %get-tuple-element.24), channel_id=1, source_target_pairs={{0,24},{1,25},{2,26},{3,27},{4,28},{5,29},{6,30},{7,31},{8,0},{9,1... | collective-permute-start | bytes 1105928 | tf_op jit(solution)/shard_map/ppermute | solution.py:46
  143.3 8.8 %copy-start = (bf16[288,1280]{1,0:T(8,128)(2,1)}, bf16[288,1280]{1,0:T(8,128)(2,1)S(1)}, u32[]{:S(2)}) copy-start(bf16[288,1280]{1,0:T(8,128)(2,1)S(1)} %collective-permute-done.4.other_ref) | copy-start | bytes 2211844
  152.1 0.7 copy-start.2
  152.1 0.9 copy-start.3
Sparse Core Ops, SparseCore 0:
  12.9 92.5 all-gather.2

commit v2 on v1

v2 whole, which is shorter than its diff:
```python
import functools

import jax
import jax.numpy as jnp
import numpy as np
from jax import lax
from jax.experimental import pallas as pl
from jax.experimental.pallas import tpu as pltpu
from jax.sharding import PartitionSpec as P

WIDTH = 1280
QUERY_HEADS = 20
HEAD = 64
QW = 1280
KVW = 640
SHARE = 224
GROUP = 16
SIDE = 4
SLOTS = 4
POSITIONS = 1024
ROWS = 256
HALF = 144
EPS = 1e-05
THETA = 10000.0
NEG = -1e30
F32 = jnp.float32
BF = jnp.bfloat16
NT = (((1,), (1,)), ((), ()))
VMEM_LIMIT = 56 << 20


def place(y, x, z, core):
    return (((y % SIDE) * SIDE + x % SIDE) * SIDE + z % SIDE) * 2 + core


def moves(step):
    pairs = []
    for y in range(SIDE):
        for x in range(SIDE):
            for z in range(SIDE):
                for core in range(2):
                    pairs.append((place(y, x, z, core), place(*step(y, x, z, core))))
    return pairs


def send(array, step):
    return lax.ppermute(array, "req", moves(step))


def other_core(y, x, z, core):
    return y, x, z, 1 - core


def next_x(y, x, z, core):
    return y, x + 1, z, core


def last_x(y, x, z, core):
    return y, x - 1, z, core


def next_z(y, x, z, core):
    return y, x, z + 1, core


def last_z(y, x, z, core):
    return y, x, z - 1, core


def pair_z(y, x, z, core):
    return y, x, z ^ 1, core


def norm_rows(rows, gain):
    rows = rows.astype(F32)
    mean = jnp.mean(rows * rows, axis=-1, keepdims=True)
    return (rows * lax.rsqrt(mean + EPS) * gain).astype(BF)


def lanes(shape):
    return lax.broadcasted_iota(jnp.int32, shape, len(shape) - 1)


def sublanes(shape):
    return lax.broadcasted_iota(jnp.int32, shape, len(shape) - 2)


def rope_tables(position, frequency):
    angle = position * frequency
    sine = jnp.sin(angle)
    low = lanes(angle.shape) % HEAD < HEAD // 2
    return jnp.cos(angle), jnp.where(low, -sine, sine)


def rope(chunk, cosine, sine):
    low = lanes(chunk.shape) % HEAD < HEAD // 2
    other = jnp.where(low, pltpu.roll(chunk, 96, 1), pltpu.roll(chunk, 32, 1))
    return chunk * cosine + other * sine


def qkv_kernel(rank_ref, hidden_ref, gain_ref, freq_ref, w_ref, query_ref, kv_ref, normed, cos, sin):
    step = pl.program_id(0)

    @pl.when(step == 0)
    def _():
        normed[...] = norm_rows(hidden_ref[...], gain_ref[...])
        position = (sublanes((ROWS, 128)) * 4 + rank_ref[0]).astype(F32)
        cos[...], sin[...] = rope_tables(position, freq_ref[...])

    projected = jnp.dot(normed[...], w_ref[...], preferred_element_type=F32)
    chunks = [projected[:, i * 128 : (i + 1) * 128] for i in range(5)]

    @pl.when(step < 2)
    def _():
        for i in range(5):
            roped = rope(chunks[i], cos[...], sin[...]).astype(BF)
            query_ref[:, i * 128 : (i + 1) * 128] = roped * jnp.asarray(0.125, BF)

    @pl.when(step == 2)
    def _():
        low = lanes((ROWS, 128)) < HEAD
        first = rope(chunks[0], cos[...], sin[...])
        second = rope(chunks[1], cos[...], sin[...])
        third = jnp.where(low, rope(chunks[2], cos[...], sin[...]), chunks[2])
        swap = lambda value: pltpu.roll(value, 64, 1)
        out = [
            jnp.where(low, first, third),
            jnp.where(low, swap(first), swap(chunks[3])),
            jnp.where(low, second, chunks[3]),
            jnp.where(low, swap(second), swap(chunks[4])),
            jnp.where(low, third, chunks[4]),
        ]
        for i in range(5):
            kv_ref[:, i * 128 : (i + 1) * 128] = out[i].astype(BF)


def prefill_qkv(rank, hidden, gain, freq, w_qkv):
    return pl.pallas_call(
        qkv_kernel,
        out_shape=(
            jax.ShapeDtypeStruct((ROWS, QW), BF),
            jax.ShapeDtypeStruct((ROWS, KVW), BF),
        ),
        grid=(3,),
        in_specs=[
            pl.BlockSpec(memory_space=pltpu.SMEM),
            pl.BlockSpec((ROWS, WIDTH), lambda j: (0, 0)),
            pl.BlockSpec((1, WIDTH), lambda j: (0, 0)),
            pl.BlockSpec((1, 128), lambda j: (0, 0)),
            pl.BlockSpec((WIDTH, KVW), lambda j: (0, j)),
        ],
        out_specs=(
            pl.BlockSpec((ROWS, KVW), lambda j: (0, jnp.minimum(j, 1))),
            pl.BlockSpec((ROWS, KVW), lambda j: (0, 0)),
        ),
        scratch_shapes=[
            pltpu.VMEM((ROWS, WIDTH), BF),
            pltpu.VMEM((ROWS, 128), F32),
            pltpu.VMEM((ROWS, 128), F32),
        ],
        compiler_params=pltpu.CompilerParams(vmem_limit_bytes=VMEM_LIMIT),
        cost_estimate=pl.CostEstimate(flops=4 * 10**9, transcendentals=0, bytes_accessed=7000000),
        name="prefill_qkv",
    )(rank, hidden, gain, freq, w_qkv)


def column(row):
    return jnp.broadcast_to(row, (128, 128)).T


def decode_kernel(
    device_ref,
    length_ref,
    count_ref,
    slot_ref,
    index_ref,
    rows_ref,
    gain_ref,
    freq_ref,
    w_ref,
    cache_ref,
    hidden_ref,
    out_ref,
    held_ref,
    spread,
    query,
    fresh_key,
    fresh_value,
    over,
    result,
):
    tick = pl.program_id(0)
    step = tick - SLOTS
    first_slot = device_ref[0] * SLOTS

    @pl.when(tick < SLOTS)
    def _():
        normed = norm_rows(hidden_ref[...], gain_ref[...])
        projected = jnp.dot(normed, w_ref[:, QW:], preferred_element_type=F32)
        position = (index_ref[pl.ds(tick * 2, 2), :] % POSITIONS).astype(F32)
        position = jnp.concatenate([column(position[0:1]), column(position[1:2])], axis=0)
        cosine, sine = rope_tables(position, freq_ref[...])
        low = lanes((256, 128)) < HEAD
        rows = pl.ds(pl.multiple_of(tick * 256, 256), 256)
        for i in range(5):
            chunk = projected[:, i * 128 : (i + 1) * 128]
            if i < 2:
                chunk = rope(chunk, cosine, sine)
            elif i == 2:
                chunk = jnp.where(low, rope(chunk, cosine, sine), chunk)
            held_ref[rows, i * 128 : (i + 1) * 128] = chunk.astype(BF)

    index_rows = [index_ref[i : i + 1, :] for i in range(8)]

    @pl.when(step == 0)
    def _():
        spread[...] = (
            sublanes((QW, 384)) % HEAD == lanes((QW, 384)) % HEAD
        ).astype(F32).astype(BF)
        wanted = jnp.broadcast_to(slot_ref[...], (8, 256))
        slot = sublanes((8, 256))
        chosen = ((wanted == first_slot + slot) & (slot < SLOTS)).astype(F32).astype(BF)
        rows = jnp.dot(chosen, rows_ref[...], preferred_element_type=F32)
        normed = norm_rows(rows, gain_ref[...])
        projected = jnp.dot(normed, w_ref[...], preferred_element_type=F32)
        projected = projected.astype(BF).astype(F32)
        row = sublanes((8, 128))
        position = jnp.zeros((8, 128), F32)
        for j in range(SLOTS):
            position = jnp.where(row == j, length_ref[j].astype(F32), position)
        cosine, sine = rope_tables(position, freq_ref[...])
        chunks = [projected[:, i * 128 : (i + 1) * 128] for i in range(15)]
        roped = [rope(chunks[i], cosine, sine).astype(BF) for i in range(13)]
        whole = jnp.concatenate(roped[:10], axis=1).astype(F32) * 0.125
        head_of = sublanes((32, QW))
        keep = lanes((32, QW)) // HEAD == head_of
        group = sublanes((32, 384))
        block = (lanes((32, 384)) // HEAD == group // 4) & (group < QUERY_HEADS)
        for j in range(SLOTS):
            placed = jnp.where(keep, jnp.broadcast_to(whole[j : j + 1], (32, QW)), 0.0)
            turned = jnp.dot(placed.astype(BF), spread[...], preferred_element_type=F32)
            query[j * 32 : (j + 1) * 32, :] = jnp.where(block, turned, 0.0).astype(BF)
        fresh_key[...] = jnp.concatenate(roped[10:13], axis=1).astype(F32)
        fresh_value[...] = jnp.concatenate(chunks[12:15], axis=1)
        counts = jnp.zeros((32, 128), F32)
        for i in range(8):
            entry = i * 128 + lanes((32, 128))
            live = entry < count_ref[0]
            upper = jnp.broadcast_to(index_rows[i] // 128, (32, 128)) == sublanes((32, 128))
            upper = (upper & live).astype(F32).astype(BF)
            lower = jnp.broadcast_to(index_rows[i] % 128, (128, 128)) == sublanes((128, 128))
            lower = lower.astype(F32).astype(BF)
            counts = counts + lax.dot_general(upper, lower, NT, preferred_element_type=F32)
        over[...] = counts

    @pl.when(step >= 0)
    def _():
        length = length_ref[step]
        queries = query[pl.ds(pl.multiple_of(step * 32, 32), 32), :]
        taken = over[pl.ds(pl.multiple_of(step * 8, 8), 8), :]
        taken = jnp.concatenate([taken[i : i + 1, :] for i in range(8)], axis=1)
        cache_live = (lanes((1, POSITIONS)) < length) & (taken < 0.5)
        index = jnp.concatenate(index_rows, axis=1)
        held_live = (
            (lanes((1, 1024)) < count_ref[0])
            & (index // POSITIONS == step)
            & (index % POSITIONS < length)
        )
        cache_score = lax.dot_general(queries, cache_ref[:, :384], NT, preferred_element_type=F32)
        held_score = lax.dot_general(queries, held_ref[:, :384], NT, preferred_element_type=F32)
        own_score = jnp.sum(
            queries.astype(F32) * fresh_key[pl.ds(step, 1), :], axis=-1, keepdims=True
        )
        cache_live = jnp.broadcast_to(cache_live, cache_score.shape)
        held_live = jnp.broadcast_to(held_live, held_score.shape)
        cache_score = jnp.where(cache_live, cache_score, NEG)
        held_score = jnp.where(held_live, held_score, NEG)
        top = jnp.maximum(
            jnp.maximum(
                jnp.max(cache_score, axis=-1, keepdims=True), jnp.max(held_score, axis=-1, keepdims=True)
            ),
            own_score,
        )
        cache_weight = jnp.where(cache_live, jnp.exp(cache_score - top), 0.0)
        held_weight = jnp.where(held_live, jnp.exp(held_score - top), 0.0)
        own_weight = jnp.exp(own_score - top)
        total = (
            jnp.sum(cache_weight, axis=-1, keepdims=True)
            + jnp.sum(held_weight, axis=-1, keepdims=True)
            + own_weight
        )
        mixed = jnp.dot(cache_weight.astype(BF), cache_ref[:, 256:], preferred_element_type=F32)
        mixed += jnp.dot(held_weight.astype(BF), held_ref[:, 256:], preferred_element_type=F32)
        mixed += own_weight.astype(BF).astype(F32) * fresh_value[pl.ds(step, 1), :]
        group = sublanes((32, 384))
        block = (lanes((32, 384)) // HEAD == group // 4 + 1) & (group < QUERY_HEADS)
        mixed = jnp.where(block, mixed / total, 0.0).astype(BF)
        turned = lax.dot_general(mixed, spread[...], NT, preferred_element_type=F32)
        keep = lanes((32, QW)) // HEAD == sublanes((32, QW))
        result[pl.ds(step, 1), :] = jnp.sum(jnp.where(keep, turned, 0.0), axis=0, keepdims=True)

    @pl.when(step == SLOTS - 1)
    def _():
        wanted = jnp.broadcast_to(slot_ref[...], (8, 256))
        slot = sublanes((8, 256))
        chosen = ((wanted == first_slot + slot) & (slot < SLOTS)).astype(F32).astype(BF)
        good = jnp.where(sublanes((8, QW)) < SLOTS, result[...], 0.0).astype(BF)
        out_ref[...] = lax.dot_general(
            chosen, good, (((0,), (0,)), ((), ())), preferred_element_type=F32
        ).astype(BF)


def decode_attention(
    device, length, count, slots, index, rows, gain, freq, w_qkv, cache, hidden
):
    smem = pl.BlockSpec(memory_space=pltpu.SMEM)
    full = lambda shape: pl.BlockSpec(shape, lambda j: (0,) * len(shape))
    return pl.pallas_call(
        decode_kernel,
        out_shape=jax.ShapeDtypeStruct((256, QW), BF),
        grid=(2 * SLOTS,),
        in_specs=[
            smem,
            smem,
            smem,
            full((1, 256)),
            full((8, 128)),
            full((256, WIDTH)),
            full((1, WIDTH)),
            full((1, 128)),
            full((WIDTH, QW + KVW)),
            pl.BlockSpec((None, POSITIONS, KVW), lambda j: (jnp.maximum(j - SLOTS, 0), 0, 0)),
            pl.BlockSpec((256, WIDTH), lambda j: (jnp.minimum(j, SLOTS - 1), 0)),
        ],
        out_specs=full((256, QW)),
        scratch_shapes=[
            pltpu.VMEM((1024, KVW), BF),
            pltpu.VMEM((QW, 384), BF),
            pltpu.VMEM((128, 384), BF),
            pltpu.VMEM((8, 384), F32),
            pltpu.VMEM((8, 384), F32),
            pltpu.VMEM((32, 128), F32),
            pltpu.VMEM((8, QW), F32),
        ],
        compiler_params=pltpu.CompilerParams(vmem_limit_bytes=VMEM_LIMIT),
        cost_estimate=pl.CostEstimate(flops=12 * 10**9, transcendentals=0, bytes_accessed=15000000),
        name="decode",
    )(device, length, count, slots, index, rows, gain, freq, w_qkv, cache, hidden)


def attention_kernel(
    rank_ref,
    query_ref,
    own_ref,
    core_ref,
    zed_ref,
    far_ref,
    w_ref,
    hidden_ref,
    gain_ref,
    resid_ref,
    lower_ref,
    upper_ref,
    total,
    mask,
):
    group = pl.program_id(0)

    @pl.when(group == 0)
    def _():
        total[...] = jnp.zeros_like(total)
        rank = rank_ref[0]
        row = sublanes((128, 128))
        col = lanes((128, 128))
        for piece in range(4):
            other = rank ^ piece
            bound = jnp.where(other <= rank, 0, 1)
            mask[:, piece * 128 : (piece + 1) * 128] = jnp.where(col + bound <= row, 0.0, NEG)

    pieces = [own_ref, core_ref, zed_ref, far_ref]
    keys = jnp.concatenate(
        [ref[h * 128 : (h + 1) * 128, :] for h in range(2) for ref in pieces], axis=0
    )
    low = lanes((1024, 128)) < HEAD
    wide = keys.astype(F32)
    values = jnp.where(low, pltpu.roll(wide, 64, 1), wide).astype(BF)
    values = jnp.concatenate([values, jnp.ones((1024, 128), BF)], axis=1)
    low = lanes((128, 128)) < HEAD
    blocked = mask[...]
    mixed = []
    for tile in range(2):
        heads = []
        for pair in range(2):
            two = query_ref[tile * 128 : (tile + 1) * 128, pair * 128 : (pair + 1) * 128].astype(F32)
            heads.append(jnp.where(low, two, 0.0).astype(BF))
            heads.append(jnp.where(low, pltpu.roll(two, 64, 1), 0.0).astype(BF))
        out = []
        for head in heads:
            count = 512 * (tile + 1)
            score = lax.dot_general(head, keys[:count], NT, preferred_element_type=F32)
            if tile == 0:
                score = score + blocked
            else:
                score = jnp.concatenate([score[:, :512], score[:, 512:] + blocked], axis=1)
            top = jnp.max(score, axis=-1, keepdims=True)
            weight = jnp.exp(score - top).astype(BF)
            both = jnp.dot(weight, values[:count], preferred_element_type=F32)
            out.append(both[:, :128] / both[:, 128:])
        mixed.append(
            jnp.concatenate(
                [jnp.where(low, out[0], out[1]), jnp.where(low, out[2], out[3])], axis=1
            ).astype(BF)
        )
    rows = jnp.concatenate(mixed, axis=0)
    total[...] += jnp.dot(rows, w_ref[...], preferred_element_type=F32)

    @pl.when(group == 4)
    def _():
        for part in range(2):
            cut = slice(part * 128, (part + 1) * 128)
            resid = (hidden_ref[cut, :].astype(F32) + total[cut, :]).astype(BF)
            resid_ref[cut, :] = resid
            (lower_ref, upper_ref)[part][:128, :] = norm_rows(resid, gain_ref[...])


def attention(rank, query, own, core, zed, far, w_out, hidden, gain):
    full = lambda shape: pl.BlockSpec(shape, lambda g: (0,) * len(shape))
    side = pl.BlockSpec((ROWS, 128), lambda g: (0, g))
    return pl.pallas_call(
        attention_kernel,
        out_shape=(
            jax.ShapeDtypeStruct((ROWS, WIDTH), BF),
            jax.ShapeDtypeStruct((HALF, WIDTH), BF),
            jax.ShapeDtypeStruct((HALF, WIDTH), BF),
        ),
        grid=(5,),
        in_specs=[
            pl.BlockSpec(memory_space=pltpu.SMEM),
            pl.BlockSpec((ROWS, 256), lambda g: (0, g)),
            side,
            side,
            side,
            side,
            pl.BlockSpec((256, WIDTH), lambda g: (g, 0)),
            full((ROWS, WIDTH)),
            full((1, WIDTH)),
        ],
        out_specs=(
            full((ROWS, WIDTH)),
            full((HALF, WIDTH)),
            full((HALF, WIDTH)),
        ),
        scratch_shapes=[
            pltpu.VMEM((ROWS, WIDTH), F32),
            pltpu.VMEM((128, 512), F32),
        ],
        compiler_params=pltpu.CompilerParams(vmem_limit_bytes=VMEM_LIMIT),
        cost_estimate=pl.CostEstimate(flops=12 * 10**9, transcendentals=0, bytes_accessed=8000000),
        name="attention",
    )(rank, query, own, core, zed, far, w_out, hidden, gain)


def decode_rows_kernel(back_ref, w_ref, decode_ref, gain_ref, lower_in, upper_in, resid_ref, lower_ref, upper_ref):
    del lower_in, upper_in
    source = lanes((32, 256)) % 2
    row = sublanes((32, 256))
    pick = ((row == 0) & (source == 0)) | ((row == 16) & (source == 1))
    pick = pick.astype(F32).astype(BF)
    mixed = jnp.dot(pick, back_ref[...], preferred_element_type=F32).astype(BF)
    projection = jnp.dot(mixed, w_ref[...], preferred_element_type=F32)
    first = sublanes((16, WIDTH)) == 0
    single = decode_ref[...].astype(F32)
    for part in range(2):
        cut = slice(part * 16, (part + 1) * 16)
        alone = jnp.where(first, jnp.broadcast_to(single[part : part + 1], (16, WIDTH)), 0.0)
        resid = (alone + projection[cut]).astype(BF)
        resid_ref[cut, :] = resid
        (lower_ref, upper_ref)[part][...] = norm_rows(resid, gain_ref[...])


def decode_rows(back, w_out, decode, gain, lower, upper):
    full = lambda shape: pl.BlockSpec(shape, lambda g: (0,) * len(shape))
    tail = pl.BlockSpec((16, WIDTH), lambda g: (8, 0))
    return pl.pallas_call(
        decode_rows_kernel,
        out_shape=(
            jax.ShapeDtypeStruct((32, WIDTH), BF),
            jax.ShapeDtypeStruct((HALF, WIDTH), BF),
            jax.ShapeDtypeStruct((HALF, WIDTH), BF),
        ),
        grid=(1,),
        in_specs=[
            full((256, WIDTH)),
            full((WIDTH, WIDTH)),
            full((2, WIDTH)),
            full((1, WIDTH)),
            tail,
            tail,
        ],
        out_specs=(full((32, WIDTH)), tail, tail),
        input_output_aliases={4: 1, 5: 2},
        compiler_params=pltpu.CompilerParams(vmem_limit_bytes=VMEM_LIMIT),
        cost_estimate=pl.CostEstimate(flops=10**8, transcendentals=0, bytes_accessed=4000000),
        name="decode_rows",
    )(back, w_out, decode, gain, lower, upper)


def feed_kernel(*refs):
    pieces, gate_ups, downs = refs[:4], refs[4:8], refs[8:12]
    mine_out, other_out, rows, gate_up, down, act, row_sem, gate_sem, down_sem = refs[12:]
    row_copies = [
        pltpu.make_async_copy(pieces[i], rows.at[pl.ds(i * HALF, HALF)], row_sem.at[i])
        for i in range(4)
    ]
    gate_copies = [
        pltpu.make_async_copy(gate_ups[k].at[0], gate_up.at[k], gate_sem.at[k]) for k in range(4)
    ]
    down_copies = [
        pltpu.make_async_copy(downs[k].at[0], down.at[pl.ds(k * SHARE, SHARE)], down_sem.at[k])
        for k in range(4)
    ]
    for copy in row_copies + gate_copies + down_copies:
        copy.start()
    for copy in row_copies:
        copy.wait()
    for k in range(4):
        gate_copies[k].wait()
        gate = lax.dot_general(
            rows[...], gate_up[k, :SHARE, :], NT, preferred_element_type=F32
        )
        up = lax.dot_general(rows[...], gate_up[k, SHARE:, :], NT, preferred_element_type=F32)
        act[:, k * SHARE : (k + 1) * SHARE] = (gate / (1.0 + jnp.exp(-gate)) * up).astype(BF)
    for copy in down_copies:
        copy.wait()
    mine_out[...] = jnp.dot(
        act[: 2 * HALF], down[...], preferred_element_type=F32
    ).astype(BF)
    other_out[...] = jnp.dot(
        act[2 * HALF :], down[...], preferred_element_type=F32
    ).astype(BF)


def feed_forward(pieces, gate_ups, downs, name):
    whole = jax.ShapeDtypeStruct((2 * HALF, WIDTH), BF)
    return pl.pallas_call(
        feed_kernel,
        out_shape=(whole, whole),
        in_specs=[pl.BlockSpec(memory_space=pl.ANY)] * 12,
        scratch_shapes=[
            pltpu.VMEM((4 * HALF, WIDTH), BF),
            pltpu.VMEM((4, 2 * SHARE, WIDTH), BF),
            pltpu.VMEM((4 * SHARE, WIDTH), BF),
            pltpu.VMEM((4 * HALF, 4 * SHARE), BF),
            pltpu.SemaphoreType.DMA((4,)),
            pltpu.SemaphoreType.DMA((4,)),
            pltpu.SemaphoreType.DMA((4,)),
        ],
        compiler_params=pltpu.CompilerParams(vmem_limit_bytes=VMEM_LIMIT),
        cost_estimate=pl.CostEstimate(flops=6 * 10**9, transcendentals=0, bytes_accessed=11000000),
        name=name,
    )(*pieces, *gate_ups, *downs)


def add_kernel(mine_ref, other_ref, out_ref):
    out_ref[...] = (mine_ref[...].astype(F32) + other_ref[...].astype(F32)).astype(BF)


def add_half(mine, other, part):
    block = pl.BlockSpec((HALF, WIDTH), lambda i: (part, 0))
    return pl.pallas_call(
        add_kernel,
        out_shape=jax.ShapeDtypeStruct((HALF, WIDTH), BF),
        grid=(1,),
        in_specs=[block, block],
        out_specs=pl.BlockSpec((HALF, WIDTH), lambda i: (0, 0)),
        compiler_params=pltpu.CompilerParams(vmem_limit_bytes=VMEM_LIMIT),
        cost_estimate=pl.CostEstimate(flops=10**6, transcendentals=0, bytes_accessed=1000000),
        name=("add_first", "add_second")[part],
    )(mine, other)


def start_kernel(resid_ref, extra_ref, mine_ref, other_ref, out_ref):
    for part in range(2):
        cut = slice(part * HALF, part * HALF + 128)
        out_ref[cut, :] = resid_ref[part * 128 : (part + 1) * 128, :].astype(F32) + (
            mine_ref[cut, :].astype(F32) + other_ref[cut, :].astype(F32)
        )
        cut = slice(part * HALF + 128, (part + 1) * HALF)
        out_ref[cut, :] = extra_ref[part * 16 : (part + 1) * 16, :].astype(F32) + (
            mine_ref[cut, :].astype(F32) + other_ref[cut, :].astype(F32)
        )


def start_sum(resid, extra, mine, other):
    return pl.pallas_call(
        start_kernel,
        out_shape=jax.ShapeDtypeStruct((2 * HALF, WIDTH), F32),
        compiler_params=pltpu.CompilerParams(vmem_limit_bytes=VMEM_LIMIT),
        cost_estimate=pl.CostEstimate(flops=10**6, transcendentals=0, bytes_accessed=5000000),
        name="start_sum",
    )(resid, extra, mine, other)


def final_kernel(start_ref, first_ref, second_ref, prefill_ref, decode_ref):
    decode = []
    for part, ref in ((0, first_ref), (1, second_ref)):
        whole = start_ref[part * HALF : (part + 1) * HALF, :] + ref[...].astype(F32)
        prefill_ref[part * 128 : (part + 1) * 128, :] = whole[:128].astype(BF)
        decode.append(whole[128:129])
    decode_ref[...] = jnp.concatenate(decode, axis=0).astype(BF)


def final_sum(start, first, second):
    return pl.pallas_call(
        final_kernel,
        out_shape=(
            jax.ShapeDtypeStruct((ROWS, WIDTH), BF),
            jax.ShapeDtypeStruct((2, WIDTH), BF),
        ),
        compiler_params=pltpu.CompilerParams(vmem_limit_bytes=VMEM_LIMIT),
        cost_estimate=pl.CostEstimate(flops=10**6, transcendentals=0, bytes_accessed=4000000),
        name="final",
    )(start, first, second)


def body(
    prefill_hidden,
    decode_hidden,
    attn_gain,
    w_qkv,
    w_out,
    ffn_gain,
    w_gate_up,
    w_down,
    key_value_cache,
    cache_len,
    slot_of_request,
    held_hidden,
    recomputed_index,
    recomp_count,
):
    device = lax.axis_index("req").astype(jnp.int32).reshape(1)
    rank = device % 4
    gain = attn_gain.reshape(1, WIDTH)
    gain2 = ffn_gain.reshape(1, WIDTH)
    exponent = np.arange(HEAD // 2) * (2.0 / HEAD)
    freq = jnp.asarray(np.tile(THETA**-exponent, 4).reshape(1, 128), F32)
    index = recomputed_index.reshape(8, 128)

    gate_up = jnp.swapaxes(w_gate_up, 1, 2)
    gate_below = send(gate_up, next_z)
    gate_above = send(gate_up, last_z)
    down_below = send(w_down, next_z)
    down_above = send(w_down, last_z)
    gate_far = send(gate_above, last_z)
    down_far = send(down_below, next_z)
    gate_ups = (gate_up, gate_below, gate_above, gate_far)
    downs = (w_down, down_below, down_above, down_far)

    total = 2 * SIDE**3
    spread = jnp.broadcast_to(decode_hidden[None], (total, 2, WIDTH))
    every_row = lax.all_to_all(spread, "req", 0, 0).reshape(256, WIDTH)

    query, kv = prefill_qkv(rank, prefill_hidden, gain, freq, w_qkv)
    zed = send(kv, pair_z)
    core = send(kv, other_core)
    far = send(zed, other_core)

    outgoing = decode_attention(
        device,
        cache_len,
        recomp_count,
        slot_of_request.reshape(1, 256),
        index,
        every_row,
        gain,
        freq,
        w_qkv,
        key_value_cache,
        held_hidden,
    )
    back = lax.all_to_all(outgoing.reshape(total, 2, WIDTH), "req", 0, 0).reshape(256, WIDTH)

    resid, lower, upper = attention(
        rank, query, kv, core, zed, far, w_out, prefill_hidden, gain2
    )
    extra, lower, upper = decode_rows(back, w_out, decode_hidden, gain2, lower, upper)
    from_last = send(lower, next_x)
    from_next = send(upper, last_x)
    lower_across = send(lower, other_core)
    upper_across = send(upper, other_core)
    mine, given = feed_forward(
        (lower, upper, lower_across, upper_across), gate_ups, downs, "feed_own"
    )
    from_last, from_next, mine, given = lax.optimization_barrier(
        (from_last, from_next, mine, given)
    )
    last_across = send(from_last, other_core)
    next_across = send(from_next, other_core)
    given = send(given, other_core)
    guest_mine, guest_given = feed_forward(
        (from_last, from_next, last_across, next_across), gate_ups, downs, "feed_guest"
    )
    guest_given = send(guest_given, other_core)
    first = send(add_half(guest_mine, guest_given, 0), last_x)
    second = send(add_half(guest_mine, guest_given, 1), next_x)
    start = start_sum(resid, extra, mine, given)
    return final_sum(start, first, second)


def solution(mesh):
    return jax.shard_map(
        body,
        mesh=mesh,
        in_specs=(
            P("req", None),
            P("req", None),
            P(),
            P(),
            P(),
            P(),
            P("req", None, None),
            P("req", None, None),
            P("req", None, None),
            P("req"),
            P(),
            P("req", None),
            P("req"),
            P("req"),
        ),
        out_specs=(P("req", None), P("req", None)),
        check_vma=False,
    )
```

time: 164 us -> 158 us (0.963)
  between operations: 14.8 us -> 1.46 us
  starting transfers between devices: 30.5 us -> 39.9 us
  local copies, waits for them, and re-layouts: 15.4 us -> 11.4 us
  waiting for transfers between devices: 32.5 us -> 34.8 us
    ppermute x11 -> x19, waiting for transfers between devices: 18.6 us -> 34.8 us  [send(): return lax.ppermute(array, 'req', moves(step))]
    all_to_all x1, waiting for transfers between devices: 13.9 us -> 0.01 us  [body(): lax.all_to_all(outgoing.reshape(total, 2, WIDTH), 'req', 0, 0)]
    ppermute x11 -> x19, starting transfers between devices: 9.25 us -> 19.5 us  [send(): return lax.ppermute(array, 'req', moves(step))]
    pallas_call x1, Pallas kernels: 12.5 us -> 17.5 us  [decode_attention(): pl.pallas_call(decode_kernel, out_shape=jax.ShapeDtypeStruct((256, QW), B...]
    pallas_call x6 -> x7, Pallas kernels: 46.9 us -> 42.3 us  [the longest x2 19.3 us: feed_forward(): pl.pallas_call(feed_kernel, out_shape=(whole, whole), in_specs=[pl.BlockS...]
    unnamed x30 -> x32, local copies, waits for them, and re-layouts: 7.48 us -> 3.46 us
  transfers between devices with their start and end apart: 14 -> 21, of which waited for: 4 -> 8; matrix products, arithmetic and copies ran while one was open for 5% -> 4% of each run, Pallas kernels for 39% -> 36%
where the time goes in v2:
time: 158 us; the launch traced here: 157 us
  Pallas kernels  69.5 us (44%)
  starting transfers between devices  39.9 us (25%)
  waiting for transfers between devices  34.8 us (22%)
  local copies, waits for them, and re-layouts  11.4 us (7%)
    ppermute x19, waiting for transfers between devices, send(): return lax.ppermute(array, 'req', moves(step))  34.8 us
    ppermute x19, starting transfers between devices, send(): return lax.ppermute(array, 'req', moves(step))  19.5 us
    pallas_call x2, Pallas kernels, feed_forward(): pl.pallas_call(feed_kernel, out_shape=(whole, whole), in_specs=[pl.BlockS...  19.3 us
    pallas_call x1, Pallas kernels, decode_attention(): pl.pallas_call(decode_kernel, out_shape=jax.ShapeDtypeStruct((256, QW), B...  17.5 us
    pallas_call x1, Pallas kernels, attention(): pl.pallas_call(attention_kernel, out_shape=(jax.ShapeDtypeStruct((ROWS, W...  12.6 us
    all_to_all x1, starting transfers between devices, body(): every_row = lax.all_to_all(spread, 'req', 0, 0).reshape(256, WIDTH)  11.1 us
    all_to_all x1, starting transfers between devices, body(): lax.all_to_all(outgoing.reshape(total, 2, WIDTH), 'req', 0, 0)  9.31 us
    pallas_call x1, Pallas kernels, prefill_qkv(): pl.pallas_call(qkv_kernel, out_shape=(jax.ShapeDtypeStruct((ROWS, QW), BF...  7.11 us
  transfers between devices with their start and end apart: 21, of which 8 were waited for; matrix products, arithmetic and copies ran while one was open for 4% of the time, Pallas kernels for 36%

profile of v2, /device:TPU:0, one launch (start us, length us, event | category | flops | bytes accessed | tf_op | source)
XLA Modules:
  0.0 157.0 jit_solution(14094274930260037423)
XLA Ops:
  0.6 1.9 %broadcast_in_dim.2 = bf16[128,2,1280]{2,1,0:T(2,128)(2,1)} broadcast(bf16[2,1280]{1,0:T(2,128)(2,1)} %decode_ref.1), dimensions={1,2} | broadcast | bytes 660480 | tf_op jit(solution)/shard_map/broadcast_in_dim | solution.py:661
  2.5 11.1 %all-to-all-start = ((bf16[128,2,1280]{2,1,0:T(2,128)(2,1)}), bf16[128,2,1280]{2,1,0:T(2,128)(2,1)S(1)}, u32[]{:S(2)}, u32[]{:S(2)}) async-start(bf16[128,2,1280]{2,1,0:T(2,128)(2,1)} %broadcast_in_dim.2), calls=%async_computation | async-start | bytes 1310720 | tf_op jit(solution)/shard_map/all_to_all | solution.py:662
  13.7 0.6 reshape.32.gain_ref
  14.3 7.1 %prefill_qkv.1 = (bf16[256,1280]{1,0:T(8,128)(2,1)}, bf16[256,640]{1,0:T(8,128)(2,1)}) custom-call(s32[1]{0:T(128)S(6)} %select_n.7.rank_ref, bf16[256,1280]{1,0:T(8,128)(2,1)} %hidden_ref.4, f32[1,1280]{1,0:T(1,128)} %reshape.32.gain_ref, f32[1,128]{1,0:T(1,128)} %constant.25.clone.freq_ref, bf16[1280,1920]{1,0:T(8,128)(2,1)} %w_ref.6), custom_call_target="tpu_custom_call" | custom-call | flops 4000000000 | bytes 7000000 | tf_op jit(solution)/shard_map/prefill_qkv/pallas_call | solution.py:138
  21.4 1.1 collective-permute-start.1
  22.5 2.3 %collective-permute-start.8 = (bf16[1,448,1280]{2,1,0:T(8,128)(2,1)S(1)}, bf16[1,448,1280]{2,1,0:T(8,128)(2,1)S(1)}, u32[]{:S(2)}, u32[]{:S(2)}) collective-permute-start(bf16[1,448,1280]{2,1,0:T(8,128)(2,1)S(1)} %bitcast.6), channel_id=1, source_target_pairs={{0,6},{1,7},{2,0},{3,1},{4,2},{5,3},{6,4},{7,5},{8,14},{9,15},{10,... | collective-permute-start | bytes 3440648 | tf_op jit(solution)/shard_map/ppermute | solution.py:47
  24.8 0.0 collective-permute-start
  24.8 0.0 collective-permute-start.7
  24.8 0.9 collective-permute-start.10
  25.7 0.6 reshape.33.gain_ref
  27.0 5.8 %collective-permute-done.1.zed_ref = bf16[256,640]{1,0:T(8,128)(2,1)} collective-permute-done((bf16[256,640]{1,0:T(8,128)(2,1)}, bf16[256,640]{1,0:T(8,128)(2,1)}, u32[]{:S(2)}, u32[]{:S(2)}) %collective-permute-start.1) | collective-permute-done | bytes 327712 | tf_op jit(solution)/shard_map/ppermute | solution.py:47
  32.8 0.0 collective-permute-start.2
  32.8 0.0 all-to-all-done
  32.8 1.1 reshape.36.rows_ref
  33.9 17.5 %decode.1 = bf16[256,1280]{1,0:T(8,128)(2,1)} custom-call(s32[1]{0:T(128)} %bitcast.device_ref, s32[4]{0:T(128)} %length_ref.1, s32[1]{0:T(128)S(6)} %copy.21.count_ref, s32[1,256]{1,0:T(1,128)} %bitcast.9, s32[8,128]{1,0:T(8,128)} %bitcast.8, bf16[256,1280]{1,0:T(8,128)(2,1)} %reshape.36.rows_ref, f32[1,1280]{1,0:T(1,128)} %reshape.32.gain_ref, ...), custom_call_target="tpu_custom_call" | custom-call | flops 12000000000 | bytes 15000000 | tf_op jit(solution)/shard_map/decode/pallas_call | solution.py:318
  51.5 2.7 %reshape.37 = bf16[128,2,1280]{2,1,0:T(2,128)(2,1)} reshape(bf16[256,1280]{1,0:T(8,128)(2,1)} %decode.1) | data formatting | bytes 1310720 | tf_op jit(solution)/shard_map/reshape | solution.py:682
  54.2 9.3 %all-to-all-start.1 = ((bf16[128,2,1280]{2,1,0:T(2,128)(2,1)}), bf16[128,2,1280]{2,1,0:T(2,128)(2,1)S(1)}, u32[]{:S(2)}, u32[]{:S(2)}) async-start(bf16[128,2,1280]{2,1,0:T(2,128)(2,1)} %reshape.37), calls=%async_computation.1 | async-start | bytes 1310720 | tf_op jit(solution)/shard_map/all_to_all | solution.py:682
  63.5 0.0 collective-permute-done.core_ref
  63.5 2.9 %collective-permute-start.11 = (bf16[1,224,1280]{2,1,0:T(8,128)(2,1)S(1)}, bf16[1,224,1280]{2,1,0:T(8,128)(2,1)}, u32[]{:S(2)}, u32[]{:S(2)}) collective-permute-start(bf16[1,224,1280]{2,1,0:T(8,128)(2,1)S(1)} %copy-done.9), channel_id=1, source_target_pairs={{0,6},{1,7},{2,0},{3,1},{4,2},{5,3},{6,4},{7,5},{8,14},{9,15},{10,... | collective-permute-start | bytes 1720328 | tf_op jit(solution)/shard_map/ppermute | solution.py:47
  66.4 7.6 %collective-permute-done.10.refs_9_ = bf16[1,224,1280]{2,1,0:T(8,128)(2,1)} collective-permute-done((bf16[1,224,1280]{2,1,0:T(8,128)(2,1)S(1)}, bf16[1,224,1280]{2,1,0:T(8,128)(2,1)}, u32[]{:S(2)}, u32[]{:S(2)}) %collective-permute-start.10) | collective-permute-done | bytes 573472 | tf_op jit(solution)/shard_map/ppermute | solution.py:47
  74.0 2.6 %collective-permute-start.12 = (bf16[1,224,1280]{2,1,0:T(8,128)(2,1)}, bf16[1,224,1280]{2,1,0:T(8,128)(2,1)}, u32[]{:S(2)}, u32[]{:S(2)}) collective-permute-start(bf16[1,224,1280]{2,1,0:T(8,128)(2,1)} %collective-permute-done.10.refs_9_), channel_id=1, source_target_pairs={{0,2},{1,3},{2,4},{3,5},{4,6},{5,7},{6,0},{7,1},{8,10},{9,11},{10,... | collective-permute-start | bytes 1720328 | tf_op jit(solution)/shard_map/ppermute | solution.py:47
  76.6 0.0 collective-permute-done.8.refs_6_
  76.6 2.1 %collective-permute-start.9 = (bf16[1,448,1280]{2,1,0:T(8,128)(2,1)S(1)}, bf16[1,448,1280]{2,1,0:T(8,128)(2,1)}, u32[]{:S(2)}, u32[]{:S(2)}) collective-permute-start(bf16[1,448,1280]{2,1,0:T(8,128)(2,1)S(1)} %collective-permute-done.8.refs_6_), channel_id=1, source_target_pairs={{0,6},{1,7},{2,0},{3,1},{4,2},{5,3},{6,4},{7,5},{8,14},{9,15},{10,... | collective-permute-start | bytes 3440648 | tf_op jit(solution)/shard_map/ppermute | solution.py:47
  78.7 0.0 collective-permute-done.2.far_ref
  78.7 12.6 %attention.1 = (bf16[256,1280]{1,0:T(8,128)(2,1)}, bf16[144,1280]{1,0:T(8,128)(2,1)}, bf16[144,1280]{1,0:T(8,128)(2,1)}) custom-call(s32[1]{0:T(128)S(6)} %select_n.7.rank_ref, bf16[256,1280]{1,0:T(8,128)(2,1)} %get-tuple-element.18.query_ref, bf16[256,640]{1,0:T(8,128)(2,1)} %get-tuple-element.19.own_ref, bf16[256,640]{1,0:T(8,128)(2,1)} %collective-permute-done.core_ref, ...), custom_call_target="tpu_custom_call" | custom-call | flops 12000000000 | bytes 8000000 | tf_op jit(solution)/shard_map/attention/pallas_call | solution.py:429
  91.3 0.0 all-to-all-done.1
  91.3 1.1 reshape.38.back_ref
  92.4 3.6 %decode_rows.1 = (bf16[32,1280]{1,0:T(8,128)(2,1)}, bf16[144,1280]{1,0:T(8,128)(2,1)}, bf16[144,1280]{1,0:T(8,128)(2,1)}) custom-call(bf16[256,1280]{1,0:T(8,128)(2,1)} %reshape.38.back_ref, bf16[1280,1280]{1,0:T(8,128)(2,1)} %w_ref.7, bf16[2,1280]{1,0:T(2,128)(2,1)} %decode_ref.1, ...), custom_call_target="tpu_custom_call", output_to_operand_aliasing={{1}: (4, {}), {2}: (5, {})} | custom-call | flops 100000000 | bytes 4000000 | tf_op jit(solution)/shard_map/decode_rows/pallas_call | solution.py:484
  96.0 0.0 collective-permute-start.5
  96.0 0.0 collective-permute-done.11.refs_10_
  96.0 0.5 collective-permute-start.6
  96.5 0.0 collective-permute-done.7.refs_5_
  96.5 1.1 collective-permute-start.3
  97.6 0.0 collective-permute-done.12.refs_11_
  97.6 2.2 %collective-permute-start.4 = (bf16[144,1280]{1,0:T(8,128)(2,1)}, bf16[144,1280]{1,0:T(8,128)(2,1)S(1)}, u32[]{:S(2)}, u32[]{:S(2)}) collective-permute-start(bf16[144,1280]{1,0:T(8,128)(2,1)} %get-tuple-element.25.refs_1_), channel_id=1, source_target_pairs={{0,24},{1,25},{2,26},{3,27},{4,28},{5,29},{6,30},{7,31},{8,0},{9,1... | collective-permute-start | bytes 1105928 | tf_op jit(solution)/shard_map/ppermute | solution.py:47
  99.7 0.0 collective-permute-done.5.refs_2_
  99.7 0.0 collective-permute-done.6.refs_3_
  99.8 9.8 %collective-permute-done.9.refs_7_ = bf16[1,448,1280]{2,1,0:T(8,128)(2,1)} collective-permute-done((bf16[1,448,1280]{2,1,0:T(8,128)(2,1)S(1)}, bf16[1,448,1280]{2,1,0:T(8,128)(2,1)}, u32[]{:S(2)}, u32[]{:S(2)}) %collective-permute-start.9) | collective-permute-done | bytes 1146912 | tf_op jit(solution)/shard_map/ppermute | solution.py:47
  109.5 9.6 %feed_own.1 = (bf16[288,1280]{1,0:T(8,128)(2,1)}, bf16[288,1280]{1,0:T(8,128)(2,1)}) custom-call(bf16[144,1280]{1,0:T(8,128)(2,1)} %get-tuple-element.24.refs_0_, bf16[144,1280]{1,0:T(8,128)(2,1)} %get-tuple-element.25.refs_1_, bf16[144,1280]{1,0:T(8,128)(2,1)} %copy-done.12, bf16[144,1280]{1,0:T(8,128)(2,1)} %copy-done.13, bf16[1,448,1280]{2,1,0:T(8,128)(2,1)} %bitcast.4, ...), custom_call_target="tpu_custom_call" | custom-call | flops 6000000000 | bytes 11000000 | tf_op jit(solution)/shard_map/feed_own/pallas_call | solution.py:545
  119.2 0.0 collective-permute-done.3.refs_0_
  119.2 0.0 copy-start.10
  119.2 0.0 collective-permute-done.4.refs_1_
  119.2 0.1 collective-permute-start.14
  119.3 0.5 collective-permute-start.15
  119.8 1.2 collective-permute-done.14.refs_2_
  121.0 0.5 collective-permute-done.15.refs_3_
  121.5 0.2 copy-done.14
  121.7 0.7 copy-done.15
  122.5 9.7 %feed_guest.1 = (bf16[288,1280]{1,0:T(8,128)(2,1)}, bf16[288,1280]{1,0:T(8,128)(2,1)}) custom-call(bf16[144,1280]{1,0:T(8,128)(2,1)} %copy-done.10, bf16[144,1280]{1,0:T(8,128)(2,1)} %copy-done.11, bf16[144,1280]{1,0:T(8,128)(2,1)} %copy-done.14, bf16[144,1280]{1,0:T(8,128)(2,1)} %copy-done.15, bf16[1,448,1280]{2,1,0:T(8,128)(2,1)} %bitcast.5, ...), custom_call_target="tpu_custom_call" | custom-call | flops 6000000000 | bytes 11000000 | tf_op jit(solution)/shard_map/feed_guest/pallas_call | solution.py:545
  132.2 0.2 collective-permute-start.16
  132.4 0.4 collective-permute-start.13
  132.8 1.9 %collective-permute-done.16.other_ref = bf16[288,1280]{1,0:T(8,128)(2,1)S(1)} collective-permute-done((bf16[288,1280]{1,0:T(8,128)(2,1)}, bf16[288,1280]{1,0:T(8,128)(2,1)S(1)}, u32[]{:S(2)}, u32[]{:S(2)}) %collective-permute-start.16) | collective-permute-done | bytes 737312 | tf_op jit(solution)/shard_map/ppermute | solution.py:47
  134.7 0.9 copy-done
  135.6 1.9 %add_first.1 = bf16[144,1280]{1,0:T(8,128)(2,1)} custom-call(bf16[288,1280]{1,0:T(8,128)(2,1)} %get-tuple-element.32.mine_ref, bf16[288,1280]{1,0:T(8,128)(2,1)} %copy-done), custom_call_target="tpu_custom_call" | custom-call | flops 1000000 | bytes 1000000 | tf_op jit(solution)/shard_map/add_first/pallas_call | solution.py:570
  137.5 2.6 %collective-permute-start.17 = (bf16[144,1280]{1,0:T(8,128)(2,1)}, bf16[144,1280]{1,0:T(8,128)(2,1)S(1)}, u32[]{:S(2)}, u32[]{:S(2)}) collective-permute-start(bf16[144,1280]{1,0:T(8,128)(2,1)} %add_first.1), channel_id=1, source_target_pairs={{0,24},{1,25},{2,26},{3,27},{4,28},{5,29},{6,30},{7,31},{8,0},{9,1... | collective-permute-start | bytes 1105928 | tf_op jit(solution)/shard_map/ppermute | solution.py:47
  140.1 1.9 %add_second.1 = bf16[144,1280]{1,0:T(8,128)(2,1)} custom-call(bf16[288,1280]{1,0:T(8,128)(2,1)} %get-tuple-element.32.mine_ref, bf16[288,1280]{1,0:T(8,128)(2,1)} %copy-done), custom_call_target="tpu_custom_call" | custom-call | flops 1000000 | bytes 1000000 | tf_op jit(solution)/shard_map/add_second/pallas_call | solution.py:570
  142.0 0.0 collective-permute-start.18
  142.0 0.0 collective-permute-done.13.other_ref
  142.0 0.9 copy-done.1
  142.9 2.9 %start_sum.1.start_ref = f32[288,1280]{1,0:T(8,128)} custom-call(bf16[256,1280]{1,0:T(8,128)(2,1)} %get-tuple-element.20.resid_ref, bf16[32,1280]{1,0:T(8,128)(2,1)} %get-tuple-element.23.extra_ref, bf16[288,1280]{1,0:T(8,128)(2,1)} %get-tuple-element.28.mine_ref, bf16[288,1280]{1,0:T(8,128)(2,1)} %copy-done.1), custom_call_target="tpu_custom_call" | custom-call | flops 1000000 | bytes 5000000 | tf_op jit(solution)/shard_map/start_sum/pallas_call | solution.py:595
  145.8 2.7 %collective-permute-done.17.first_ref = bf16[144,1280]{1,0:T(8,128)(2,1)S(1)} collective-permute-done((bf16[144,1280]{1,0:T(8,128)(2,1)}, bf16[144,1280]{1,0:T(8,128)(2,1)S(1)}, u32[]{:S(2)}, u32[]{:S(2)}) %collective-permute-start.17) | collective-permute-done | bytes 368672 | tf_op jit(solution)/shard_map/ppermute | solution.py:47
  148.6 5.2 %collective-permute-done.18.second_ref = bf16[144,1280]{1,0:T(8,128)(2,1)S(1)} collective-permute-done((bf16[144,1280]{1,0:T(8,128)(2,1)}, bf16[144,1280]{1,0:T(8,128)(2,1)S(1)}, u32[]{:S(2)}, u32[]{:S(2)}) %collective-permute-start.18) | collective-permute-done | bytes 368672 | tf_op jit(solution)/shard_map/ppermute | solution.py:47
  153.8 0.7 copy-done.3
  154.6 2.5 %final.1 = (bf16[256,1280]{1,0:T(8,128)(2,1)}, bf16[2,1280]{1,0:T(2,128)(2,1)}) custom-call(f32[288,1280]{1,0:T(8,128)} %start_sum.1.start_ref, bf16[144,1280]{1,0:T(8,128)(2,1)} %copy-done.2, bf16[144,1280]{1,0:T(8,128)(2,1)} %copy-done.3), custom_call_target="tpu_custom_call" | custom-call | flops 1000000 | bytes 4000000 | tf_op jit(solution)/shard_map/final/pallas_call | solution.py:614
  (26 shorter events, 0.0 us)
Async XLA Ops:
  0.6 13.1 %copy-start.4 = (f32[1280]{0:T(1024)S(1)}, f32[1280]{0:T(1024)}, u32[]{:S(2)}) copy-start(f32[1280]{0:T(1024)} %param.17) | copy-start | bytes 15364
  2.5 30.3 %all-to-all-start = ((bf16[128,2,1280]{2,1,0:T(2,128)(2,1)}), bf16[128,2,1280]{2,1,0:T(2,128)(2,1)S(1)}, u32[]{:S(2)}, u32[]{:S(2)}) async-start(bf16[128,2,1280]{2,1,0:T(2,128)(2,1)} %broadcast_in_dim.2), calls=%async_computation | async-start | bytes 1310720 | tf_op jit(solution)/shard_map/all_to_all | solution.py:662
  14.3 8.2 %copy-start.6 = (bf16[1,1280,448]{1,2,0:T(8,128)(2,1)S(1)}, bf16[1,1280,448]{1,2,0:T(8,128)(2,1)}, u32[]{:S(2)}) copy-start(bf16[1,1280,448]{1,2,0:T(8,128)(2,1)} %param.21) | copy-start | bytes 3440644
  14.3 10.5 %copy-start.9 = (bf16[1,224,1280]{2,1,0:T(8,128)(2,1)S(1)}, bf16[1,224,1280]{2,1,0:T(8,128)(2,1)}, u32[]{:S(2)}) copy-start(bf16[1,224,1280]{2,1,0:T(8,128)(2,1)} %refs_8_.3) | copy-start | bytes 1720324
  14.3 11.4 %copy-start.5 = (f32[1280]{0:T(1024)S(1)}, f32[1280]{0:T(1024)}, u32[]{:S(2)}) copy-start(f32[1280]{0:T(1024)} %param.20) | copy-start | bytes 15364
  21.4 11.4 %collective-permute-start.1 = (bf16[256,640]{1,0:T(8,128)(2,1)}, bf16[256,640]{1,0:T(8,128)(2,1)}, u32[]{:S(2)}, u32[]{:S(2)}) collective-permute-start(bf16[256,640]{1,0:T(8,128)(2,1)} %get-tuple-element.19.own_ref), channel_id=1, source_target_pairs={{0,2},{1,3},{2,0},{3,1},{4,6},{5,7},{6,4},{7,5},{8,10},{9,11},{10,... | collective-permute-start | bytes 983048 | tf_op jit(solution)/shard_map/ppermute | solution.py:47
  22.5 54.1 %collective-permute-start.8 = (bf16[1,448,1280]{2,1,0:T(8,128)(2,1)S(1)}, bf16[1,448,1280]{2,1,0:T(8,128)(2,1)S(1)}, u32[]{:S(2)}, u32[]{:S(2)}) collective-permute-start(bf16[1,448,1280]{2,1,0:T(8,128)(2,1)S(1)} %bitcast.6), channel_id=1, source_target_pairs={{0,6},{1,7},{2,0},{3,1},{4,2},{5,3},{6,4},{7,5},{8,14},{9,15},{10,... | collective-permute-start | bytes 3440648 | tf_op jit(solution)/shard_map/ppermute | solution.py:47
  24.8 38.7 %collective-permute-start = (bf16[256,640]{1,0:T(8,128)(2,1)}, bf16[256,640]{1,0:T(8,128)(2,1)}, u32[]{:S(2)}, u32[]{:S(2)}) collective-permute-start(bf16[256,640]{1,0:T(8,128)(2,1)} %get-tuple-element.19.own_ref), channel_id=1, source_target_pairs={{0,1},{1,0},{2,3},{3,2},{4,5},{5,4},{6,7},{7,6},{8,9},{9,8},{10,11... | collective-permute-start | bytes 983048 | tf_op jit(solution)/shard_map/ppermute | solution.py:47
  24.8 71.7 %collective-permute-start.7 = (bf16[1,448,1280]{2,1,0:T(8,128)(2,1)S(1)}, bf16[1,448,1280]{2,1,0:T(8,128)(2,1)}, u32[]{:S(2)}, u32[]{:S(2)}) collective-permute-start(bf16[1,448,1280]{2,1,0:T(8,128)(2,1)S(1)} %bitcast.7), channel_id=1, source_target_pairs={{0,2},{1,3},{2,4},{3,5},{4,6},{5,7},{6,0},{7,1},{8,10},{9,11},{10,... | collective-permute-start | bytes 3440648 | tf_op jit(solution)/shard_map/ppermute | solution.py:47
  24.8 49.1 %collective-permute-start.10 = (bf16[1,224,1280]{2,1,0:T(8,128)(2,1)S(1)}, bf16[1,224,1280]{2,1,0:T(8,128)(2,1)}, u32[]{:S(2)}, u32[]{:S(2)}) collective-permute-start(bf16[1,224,1280]{2,1,0:T(8,128)(2,1)S(1)} %copy-done.9), channel_id=1, source_target_pairs={{0,2},{1,3},{2,4},{3,5},{4,6},{5,7},{6,0},{7,1},{8,10},{9,11},{10,... | collective-permute-start | bytes 1720328 | tf_op jit(solution)/shard_map/ppermute | solution.py:47
  32.8 45.8 %collective-permute-start.2 = (bf16[256,640]{1,0:T(8,128)(2,1)}, bf16[256,640]{1,0:T(8,128)(2,1)}, u32[]{:S(2)}, u32[]{:S(2)}) collective-permute-start(bf16[256,640]{1,0:T(8,128)(2,1)} %collective-permute-done.1.zed_ref), channel_id=1, source_target_pairs={{0,1},{1,0},{2,3},{3,2},{4,5},{5,4},{6,7},{7,6},{8,9},{9,8},{10,11... | collective-permute-start | bytes 983048 | tf_op jit(solution)/shard_map/ppermute | solution.py:47
  54.2 37.1 %all-to-all-start.1 = ((bf16[128,2,1280]{2,1,0:T(2,128)(2,1)}), bf16[128,2,1280]{2,1,0:T(2,128)(2,1)S(1)}, u32[]{:S(2)}, u32[]{:S(2)}) async-start(bf16[128,2,1280]{2,1,0:T(2,128)(2,1)} %reshape.37), calls=%async_computation.1 | async-start | bytes 1310720 | tf_op jit(solution)/shard_map/all_to_all | solution.py:682
  63.5 32.5 %collective-permute-start.11 = (bf16[1,224,1280]{2,1,0:T(8,128)(2,1)S(1)}, bf16[1,224,1280]{2,1,0:T(8,128)(2,1)}, u32[]{:S(2)}, u32[]{:S(2)}) collective-permute-start(bf16[1,224,1280]{2,1,0:T(8,128)(2,1)S(1)} %copy-done.9), channel_id=1, source_target_pairs={{0,6},{1,7},{2,0},{3,1},{4,2},{5,3},{6,4},{7,5},{8,14},{9,15},{10,... | collective-permute-start | bytes 1720328 | tf_op jit(solution)/shard_map/ppermute | solution.py:47
  74.0 23.6 %collective-permute-start.12 = (bf16[1,224,1280]{2,1,0:T(8,128)(2,1)}, bf16[1,224,1280]{2,1,0:T(8,128)(2,1)}, u32[]{:S(2)}, u32[]{:S(2)}) collective-permute-start(bf16[1,224,1280]{2,1,0:T(8,128)(2,1)} %collective-permute-done.10.refs_9_), channel_id=1, source_target_pairs={{0,2},{1,3},{2,4},{3,5},{4,6},{5,7},{6,0},{7,1},{8,10},{9,11},{10,... | collective-permute-start | bytes 1720328 | tf_op jit(solution)/shard_map/ppermute | solution.py:47
  76.6 14.7 %copy-start.7 = (bf16[1,448,1280]{2,1,0:T(8,128)(2,1)}, bf16[1,448,1280]{2,1,0:T(8,128)(2,1)S(1)}, u32[]{:S(2)}) copy-start(bf16[1,448,1280]{2,1,0:T(8,128)(2,1)S(1)} %collective-permute-done.8.refs_6_) | copy-start | bytes 3440644
  76.6 33.0 %collective-permute-start.9 = (bf16[1,448,1280]{2,1,0:T(8,128)(2,1)S(1)}, bf16[1,448,1280]{2,1,0:T(8,128)(2,1)}, u32[]{:S(2)}, u32[]{:S(2)}) collective-permute-start(bf16[1,448,1280]{2,1,0:T(8,128)(2,1)S(1)} %collective-permute-done.8.refs_6_), channel_id=1, source_target_pairs={{0,6},{1,7},{2,0},{3,1},{4,2},{5,3},{6,4},{7,5},{8,14},{9,15},{10,... | collective-permute-start | bytes 3440648 | tf_op jit(solution)/shard_map/ppermute | solution.py:47
  96.0 3.8 %collective-permute-start.5 = (bf16[144,1280]{1,0:T(8,128)(2,1)}, bf16[144,1280]{1,0:T(8,128)(2,1)S(1)}, u32[]{:S(2)}, u32[]{:S(2)}) collective-permute-start(bf16[144,1280]{1,0:T(8,128)(2,1)} %get-tuple-element.24.refs_0_), channel_id=1, source_target_pairs={{0,1},{1,0},{2,3},{3,2},{4,5},{5,4},{6,7},{7,6},{8,9},{9,8},{10,11... | collective-permute-start | bytes 1105928 | tf_op jit(solution)/shard_map/ppermute | solution.py:47
  96.0 3.8 %collective-permute-start.6 = (bf16[144,1280]{1,0:T(8,128)(2,1)}, bf16[144,1280]{1,0:T(8,128)(2,1)S(1)}, u32[]{:S(2)}, u32[]{:S(2)}) collective-permute-start(bf16[144,1280]{1,0:T(8,128)(2,1)} %get-tuple-element.25.refs_1_), channel_id=1, source_target_pairs={{0,1},{1,0},{2,3},{3,2},{4,5},{5,4},{6,7},{7,6},{8,9},{9,8},{10,11... | collective-permute-start | bytes 1105928 | tf_op jit(solution)/shard_map/ppermute | solution.py:47
  96.5 22.7 %collective-permute-start.3 = (bf16[144,1280]{1,0:T(8,128)(2,1)}, bf16[144,1280]{1,0:T(8,128)(2,1)S(1)}, u32[]{:S(2)}, u32[]{:S(2)}) collective-permute-start(bf16[144,1280]{1,0:T(8,128)(2,1)} %get-tuple-element.24.refs_0_), channel_id=1, source_target_pairs={{0,8},{1,9},{2,10},{3,11},{4,12},{5,13},{6,14},{7,15},{8,16},{9,17... | collective-permute-start | bytes 1105928 | tf_op jit(solution)/shard_map/ppermute | solution.py:47
  97.6 21.6 %collective-permute-start.4 = (bf16[144,1280]{1,0:T(8,128)(2,1)}, bf16[144,1280]{1,0:T(8,128)(2,1)S(1)}, u32[]{:S(2)}, u32[]{:S(2)}) collective-permute-start(bf16[144,1280]{1,0:T(8,128)(2,1)} %get-tuple-element.25.refs_1_), channel_id=1, source_target_pairs={{0,24},{1,25},{2,26},{3,27},{4,28},{5,29},{6,30},{7,31},{8,0},{9,1... | collective-permute-start | bytes 1105928 | tf_op jit(solution)/shard_map/ppermute | solution.py:47
  99.7 9.8 %copy-start.12 = (bf16[144,1280]{1,0:T(8,128)(2,1)}, bf16[144,1280]{1,0:T(8,128)(2,1)S(1)}, u32[]{:S(2)}) copy-start(bf16[144,1280]{1,0:T(8,128)(2,1)S(1)} %collective-permute-done.5.refs_2_) | copy-start | bytes 1105924
  99.7 9.8 %copy-start.13 = (bf16[144,1280]{1,0:T(8,128)(2,1)}, bf16[144,1280]{1,0:T(8,128)(2,1)S(1)}, u32[]{:S(2)}) copy-start(bf16[144,1280]{1,0:T(8,128)(2,1)S(1)} %collective-permute-done.6.refs_3_) | copy-start | bytes 1105924
  119.2 2.3 %copy-start.10 = (bf16[144,1280]{1,0:T(8,128)(2,1)}, bf16[144,1280]{1,0:T(8,128)(2,1)S(1)}, u32[]{:S(2)}) copy-start(bf16[144,1280]{1,0:T(8,128)(2,1)S(1)} %collective-permute-done.3.refs_0_) | copy-start | bytes 1105924
  119.2 2.3 %copy-start.11 = (bf16[144,1280]{1,0:T(8,128)(2,1)}, bf16[144,1280]{1,0:T(8,128)(2,1)S(1)}, u32[]{:S(2)}) copy-start(bf16[144,1280]{1,0:T(8,128)(2,1)S(1)} %collective-permute-done.4.refs_1_) | copy-start | bytes 1105924
  119.2 13.2 %copy-start.8 = (bf16[288,1280]{1,0:T(8,128)(2,1)S(1)}, bf16[288,1280]{1,0:T(8,128)(2,1)}, u32[]{:S(2)}) copy-start(bf16[288,1280]{1,0:T(8,128)(2,1)} %get-tuple-element.29) | copy-start | bytes 2211844
  119.2 1.8 %collective-permute-start.14 = (bf16[144,1280]{1,0:T(8,128)(2,1)S(1)}, bf16[144,1280]{1,0:T(8,128)(2,1)S(1)}, u32[]{:S(2)}, u32[]{:S(2)}) collective-permute-start(bf16[144,1280]{1,0:T(8,128)(2,1)S(1)} %collective-permute-done.3.refs_0_), channel_id=1, source_target_pairs={{0,1},{1,0},{2,3},{3,2},{4,5},{5,4},{6,7},{7,6},{8,9},{9,8},{10,11... | collective-permute-start | bytes 1105928 | tf_op jit(solution)/shard_map/ppermute | solution.py:47
  119.3 2.2 %collective-permute-start.15 = (bf16[144,1280]{1,0:T(8,128)(2,1)S(1)}, bf16[144,1280]{1,0:T(8,128)(2,1)S(1)}, u32[]{:S(2)}, u32[]{:S(2)}) collective-permute-start(bf16[144,1280]{1,0:T(8,128)(2,1)S(1)} %collective-permute-done.4.refs_1_), channel_id=1, source_target_pairs={{0,1},{1,0},{2,3},{3,2},{4,5},{5,4},{6,7},{7,6},{8,9},{9,8},{10,11... | collective-permute-start | bytes 1105928 | tf_op jit(solution)/shard_map/ppermute | solution.py:47
  121.0 0.7 copy-start.14
  121.7 0.7 copy-start.15
  132.2 2.5 %collective-permute-start.16 = (bf16[288,1280]{1,0:T(8,128)(2,1)}, bf16[288,1280]{1,0:T(8,128)(2,1)S(1)}, u32[]{:S(2)}, u32[]{:S(2)}) collective-permute-start(bf16[288,1280]{1,0:T(8,128)(2,1)} %get-tuple-element.33), channel_id=1, source_target_pairs={{0,1},{1,0},{2,3},{3,2},{4,5},{5,4},{6,7},{7,6},{8,9},{9,8},{10,11... | collective-permute-start | bytes 2211848 | tf_op jit(solution)/shard_map/ppermute | solution.py:47
  132.4 9.6 %collective-permute-start.13 = (bf16[288,1280]{1,0:T(8,128)(2,1)S(1)}, bf16[288,1280]{1,0:T(8,128)(2,1)S(1)}, u32[]{:S(2)}, u32[]{:S(2)}) collective-permute-start(bf16[288,1280]{1,0:T(8,128)(2,1)S(1)} %copy-done.8), channel_id=1, source_target_pairs={{0,1},{1,0},{2,3},{3,2},{4,5},{5,4},{6,7},{7,6},{8,9},{9,8},{10,11... | collective-permute-start | bytes 2211848 | tf_op jit(solution)/shard_map/ppermute | solution.py:47
  134.7 0.9 copy-start
  137.5 11.1 %collective-permute-start.17 = (bf16[144,1280]{1,0:T(8,128)(2,1)}, bf16[144,1280]{1,0:T(8,128)(2,1)S(1)}, u32[]{:S(2)}, u32[]{:S(2)}) collective-permute-start(bf16[144,1280]{1,0:T(8,128)(2,1)} %add_first.1), channel_id=1, source_target_pairs={{0,24},{1,25},{2,26},{3,27},{4,28},{5,29},{6,30},{7,31},{8,0},{9,1... | collective-permute-start | bytes 1105928 | tf_op jit(solution)/shard_map/ppermute | solution.py:47
  142.0 11.8 %collective-permute-start.18 = (bf16[144,1280]{1,0:T(8,128)(2,1)}, bf16[144,1280]{1,0:T(8,128)(2,1)S(1)}, u32[]{:S(2)}, u32[]{:S(2)}) collective-permute-start(bf16[144,1280]{1,0:T(8,128)(2,1)} %add_second.1), channel_id=1, source_target_pairs={{0,8},{1,9},{2,10},{3,11},{4,12},{5,13},{6,14},{7,15},{8,16},{9,17... | collective-permute-start | bytes 1105928 | tf_op jit(solution)/shard_map/ppermute | solution.py:47
  142.0 0.9 copy-start.1
  148.6 5.2 %copy-start.2 = (bf16[144,1280]{1,0:T(8,128)(2,1)}, bf16[144,1280]{1,0:T(8,128)(2,1)S(1)}, u32[]{:S(2)}) copy-start(bf16[144,1280]{1,0:T(8,128)(2,1)S(1)} %collective-permute-done.17.first_ref) | copy-start | bytes 1105924
  153.8 0.7 copy-start.3

commit v3 on v2

--- a/solution.py
+++ b/solution.py
@@ -26,7 +26,13 @@
 F32 = jnp.float32
 BF = jnp.bfloat16
 NT = (((1,), (1,)), ((), ()))
-VMEM_LIMIT = 56 << 20
+VMEM_LIMIT = 24 << 20
+
+
+def cost(microseconds):
+    return pl.CostEstimate(
+        flops=int(microseconds * 10**9), transcendentals=0, bytes_accessed=int(microseconds * 3000000)
+    )
 
 
 def place(y, x, z, core):
@@ -47,6 +53,10 @@
     return lax.ppermute(array, "req", moves(step))
 
 
+def in_hbm(*arrays):
+    return [pltpu.with_memory_space_constraint(a, pltpu.MemorySpace.HBM) for a in arrays]
+
+
 def other_core(y, x, z, core):
     return y, x, z, 1 - core
 
@@ -85,17 +95,57 @@
     return lax.broadcasted_iota(jnp.int32, shape, len(shape) - 2)
 
 
+def sine_cosine(angle):
+    turns = jnp.floor(angle * (2.0 / np.pi) + 0.5)
+    rest = angle - turns * 1.5703125
+    rest = rest - turns * 4.837512969970703125e-4
+    rest = rest - turns * 7.54978995489188216e-8
+    square = rest * rest
+    sine = 8.3321608736e-3 + square * -1.9515295891e-4
+    sine = rest + rest * square * (-1.6666654611e-1 + square * sine)
+    cosine = -1.388731625493765e-3 + square * 2.443315711809948e-5
+    cosine = 4.166664568298827e-2 + square * cosine
+    cosine = 1.0 - 0.5 * square + square * square * cosine
+    quarter = turns.astype(jnp.int32) & 3
+    odd = (quarter & 1) == 1
+    out_sine = jnp.where(odd, cosine, sine)
+    out_cosine = jnp.where(odd, sine, cosine)
+    out_sine = jnp.where(quarter >= 2, -out_sine, out_sine)
+    out_cosine = jnp.where((quarter == 1) | (quarter == 2), -out_cosine, out_cosine)
+    return out_sine, out_cosine
+
+
 def rope_tables(position, frequency):
-    angle = position * frequency
-    sine = jnp.sin(angle)
-    low = lanes(angle.shape) % HEAD < HEAD // 2
-    return jnp.cos(angle), jnp.where(low, -sine, sine)
+    sine, cosine = sine_cosine(position * frequency)
+    low = lanes(sine.shape) % HEAD < HEAD // 2
+    return cosine, jnp.where(low, -sine, sine)
 
 
 def rope(chunk, cosine, sine):
     low = lanes(chunk.shape) % HEAD < HEAD // 2
     other = jnp.where(low, pltpu.roll(chunk, 96, 1), pltpu.roll(chunk, 32, 1))
     return chunk * cosine + other * sine
+
+
+def pack_kernel(gate_up_ref, down_ref, packed_ref):
+    packed_ref[: 2 * SHARE, :] = gate_up_ref[...]
+    packed_ref[2 * SHARE :, :] = down_ref[...]
+
+
+def pack_weights(gate_up, down):
+    return pl.pallas_call(
+        pack_kernel,
+        out_shape=jax.ShapeDtypeStruct((3 * SHARE, WIDTH), BF),
+        grid=(2,),
+        in_specs=[
+            pl.BlockSpec((None, 2 * SHARE, WIDTH // 2), lambda i: (0, 0, i)),
+            pl.BlockSpec((None, SHARE, WIDTH // 2), lambda i: (0, 0, i)),
+        ],
+        out_specs=pl.BlockSpec((3 * SHARE, WIDTH // 2), lambda i: (0, i)),
+        compiler_params=pltpu.CompilerParams(vmem_limit_bytes=VMEM_LIMIT),
+        cost_estimate=cost(1.5),
+        name="pack",
+    )(gate_up, down)
 
 
 def qkv_kernel(rank_ref, hidden_ref, gain_ref, freq_ref, w_ref, query_ref, kv_ref, normed, cos, sin):
@@ -159,7 +209,7 @@
             pltpu.VMEM((ROWS, 128), F32),
         ],
         compiler_params=pltpu.CompilerParams(vmem_limit_bytes=VMEM_LIMIT),
-        cost_estimate=pl.CostEstimate(flops=4 * 10**9, transcendentals=0, bytes_accessed=7000000),
+        cost_estimate=cost(7),
         name="prefill_qkv",
     )(rank, hidden, gain, freq, w_qkv)
 
@@ -328,7 +378,9 @@
             full((256, WIDTH)),
             full((1, WIDTH)),
             full((1, 128)),
-            full((WIDTH, QW + KVW)),
+            pl.BlockSpec(
+                (WIDTH, QW + KVW), lambda j: (0, 0), pipeline_mode=pl.Buffered(1)
+            ),
             pl.BlockSpec((None, POSITIONS, KVW), lambda j: (jnp.maximum(j - SLOTS, 0), 0, 0)),
             pl.BlockSpec((256, WIDTH), lambda j: (jnp.minimum(j, SLOTS - 1), 0)),
         ],
@@ -343,7 +395,7 @@
             pltpu.VMEM((8, QW), F32),
         ],
         compiler_params=pltpu.CompilerParams(vmem_limit_bytes=VMEM_LIMIT),
-        cost_estimate=pl.CostEstimate(flops=12 * 10**9, transcendentals=0, bytes_accessed=15000000),
+        cost_estimate=cost(17),
         name="decode",
     )(device, length, count, slots, index, rows, gain, freq, w_qkv, cache, hidden)
 
@@ -455,7 +507,7 @@
             pltpu.VMEM((128, 512), F32),
         ],
         compiler_params=pltpu.CompilerParams(vmem_limit_bytes=VMEM_LIMIT),
-        cost_estimate=pl.CostEstimate(flops=12 * 10**9, transcendentals=0, bytes_accessed=8000000),
+        cost_estimate=cost(12),
         name="attention",
     )(rank, query, own, core, zed, far, w_out, hidden, gain)
 
@@ -500,105 +552,72 @@
         out_specs=(full((32, WIDTH)), tail, tail),
         input_output_aliases={4: 1, 5: 2},
         compiler_params=pltpu.CompilerParams(vmem_limit_bytes=VMEM_LIMIT),
-        cost_estimate=pl.CostEstimate(flops=10**8, transcendentals=0, bytes_accessed=4000000),
+        cost_estimate=cost(3),
         name="decode_rows",
     )(back, w_out, decode, gain, lower, upper)
 
 
 def feed_kernel(*refs):
-    pieces, gate_ups, downs = refs[:4], refs[4:8], refs[8:12]
-    mine_out, other_out, rows, gate_up, down, act, row_sem, gate_sem, down_sem = refs[12:]
-    row_copies = [
-        pltpu.make_async_copy(pieces[i], rows.at[pl.ds(i * HALF, HALF)], row_sem.at[i])
-        for i in range(4)
-    ]
-    gate_copies = [
-        pltpu.make_async_copy(gate_ups[k].at[0], gate_up.at[k], gate_sem.at[k]) for k in range(4)
-    ]
-    down_copies = [
-        pltpu.make_async_copy(downs[k].at[0], down.at[pl.ds(k * SHARE, SHARE)], down_sem.at[k])
-        for k in range(4)
-    ]
-    for copy in row_copies + gate_copies + down_copies:
-        copy.start()
-    for copy in row_copies:
-        copy.wait()
-    for k in range(4):
-        gate_copies[k].wait()
-        gate = lax.dot_general(
-            rows[...], gate_up[k, :SHARE, :], NT, preferred_element_type=F32
-        )
-        up = lax.dot_general(rows[...], gate_up[k, SHARE:, :], NT, preferred_element_type=F32)
+    pieces, packs, far_low, far_high = refs[:2], refs[2:8], refs[8:10], refs[10:12]
+    outs, act = refs[12:14], refs[14]
+    cut = 3 * SHARE // 2
+    rows = jnp.concatenate([ref[...] for ref in pieces], axis=0)
+    downs = []
+    for k in range(8):
+        if k < 6:
+            gate_rows = packs[k][:SHARE, :]
+            up_rows = packs[k][SHARE : 2 * SHARE, :]
+            downs.append(packs[k][2 * SHARE :, :])
+        else:
+            low, high = far_low[k - 6], far_high[k - 6]
+            gate_rows = low[:SHARE, :]
+            up_rows = jnp.concatenate([low[SHARE:, :], high[: 2 * SHARE - cut, :]], axis=0)
+            downs.append(high[2 * SHARE - cut :, :])
+        gate = lax.dot_general(rows, gate_rows, NT, preferred_element_type=F32)
+        up = lax.dot_general(rows, up_rows, NT, preferred_element_type=F32)
         act[:, k * SHARE : (k + 1) * SHARE] = (gate / (1.0 + jnp.exp(-gate)) * up).astype(BF)
-    for copy in down_copies:
-        copy.wait()
-    mine_out[...] = jnp.dot(
-        act[: 2 * HALF], down[...], preferred_element_type=F32
-    ).astype(BF)
-    other_out[...] = jnp.dot(
-        act[2 * HALF :], down[...], preferred_element_type=F32
-    ).astype(BF)
-
-
-def feed_forward(pieces, gate_ups, downs, name):
-    whole = jax.ShapeDtypeStruct((2 * HALF, WIDTH), BF)
+    down = jnp.dot(act[...], jnp.concatenate(downs, axis=0), preferred_element_type=F32)
+    outs[0][...] = down[:HALF].astype(BF)
+    outs[1][...] = down[HALF:].astype(BF)
+
+
+def feed_forward(pieces, weights, name):
+    vmem = pl.BlockSpec(memory_space=pltpu.VMEM)
     return pl.pallas_call(
         feed_kernel,
-        out_shape=(whole, whole),
-        in_specs=[pl.BlockSpec(memory_space=pl.ANY)] * 12,
-        scratch_shapes=[
-            pltpu.VMEM((4 * HALF, WIDTH), BF),
-            pltpu.VMEM((4, 2 * SHARE, WIDTH), BF),
-            pltpu.VMEM((4 * SHARE, WIDTH), BF),
-            pltpu.VMEM((4 * HALF, 4 * SHARE), BF),
-            pltpu.SemaphoreType.DMA((4,)),
-            pltpu.SemaphoreType.DMA((4,)),
-            pltpu.SemaphoreType.DMA((4,)),
-        ],
+        out_shape=(jax.ShapeDtypeStruct((HALF, WIDTH), BF),) * 2,
+        in_specs=[vmem] * 12,
+        out_specs=(vmem,) * 2,
+        scratch_shapes=[pltpu.VMEM((2 * HALF, 8 * SHARE), BF)],
         compiler_params=pltpu.CompilerParams(vmem_limit_bytes=VMEM_LIMIT),
-        cost_estimate=pl.CostEstimate(flops=6 * 10**9, transcendentals=0, bytes_accessed=11000000),
+        cost_estimate=cost(8),
         name=name,
-    )(*pieces, *gate_ups, *downs)
-
-
-def add_kernel(mine_ref, other_ref, out_ref):
-    out_ref[...] = (mine_ref[...].astype(F32) + other_ref[...].astype(F32)).astype(BF)
-
-
-def add_half(mine, other, part):
-    block = pl.BlockSpec((HALF, WIDTH), lambda i: (part, 0))
-    return pl.pallas_call(
-        add_kernel,
-        out_shape=jax.ShapeDtypeStruct((HALF, WIDTH), BF),
-        grid=(1,),
-        in_specs=[block, block],
-        out_specs=pl.BlockSpec((HALF, WIDTH), lambda i: (0, 0)),
-        compiler_params=pltpu.CompilerParams(vmem_limit_bytes=VMEM_LIMIT),
-        cost_estimate=pl.CostEstimate(flops=10**6, transcendentals=0, bytes_accessed=1000000),
-        name=("add_first", "add_second")[part],
-    )(mine, other)
-
-
-def start_kernel(resid_ref, extra_ref, mine_ref, other_ref, out_ref):
+    )(*pieces, *weights)
+
+
+def start_kernel(resid_ref, extra_ref, lower_ref, upper_ref, out_ref):
     for part in range(2):
+        mine_ref = (lower_ref, upper_ref)[part]
         cut = slice(part * HALF, part * HALF + 128)
-        out_ref[cut, :] = resid_ref[part * 128 : (part + 1) * 128, :].astype(F32) + (
-            mine_ref[cut, :].astype(F32) + other_ref[cut, :].astype(F32)
-        )
+        out_ref[cut, :] = resid_ref[part * 128 : (part + 1) * 128, :].astype(F32) + mine_ref[
+            :128, :
+        ].astype(F32)
         cut = slice(part * HALF + 128, (part + 1) * HALF)
-        out_ref[cut, :] = extra_ref[part * 16 : (part + 1) * 16, :].astype(F32) + (
-            mine_ref[cut, :].astype(F32) + other_ref[cut, :].astype(F32)
-        )
-
-
-def start_sum(resid, extra, mine, other):
+        out_ref[cut, :] = extra_ref[part * 16 : (part + 1) * 16, :].astype(F32) + mine_ref[
+            128:, :
+        ].astype(F32)
+
+
+def start_sum(resid, extra, mine):
     return pl.pallas_call(
         start_kernel,
         out_shape=jax.ShapeDtypeStruct((2 * HALF, WIDTH), F32),
+        in_specs=[pl.BlockSpec(memory_space=pltpu.VMEM)] * 4,
+        out_specs=pl.BlockSpec(memory_space=pltpu.VMEM),
         compiler_params=pltpu.CompilerParams(vmem_limit_bytes=VMEM_LIMIT),
-        cost_estimate=pl.CostEstimate(flops=10**6, transcendentals=0, bytes_accessed=5000000),
+        cost_estimate=cost(1.5),
         name="start_sum",
-    )(resid, extra, mine, other)
+    )(resid, extra, *mine)
 
 
 def final_kernel(start_ref, first_ref, second_ref, prefill_ref, decode_ref):
@@ -617,8 +636,9 @@
             jax.ShapeDtypeStruct((ROWS, WIDTH), BF),
             jax.ShapeDtypeStruct((2, WIDTH), BF),
         ),
+        in_specs=[pl.BlockSpec(memory_space=pltpu.VMEM)] * 3,
         compiler_params=pltpu.CompilerParams(vmem_limit_bytes=VMEM_LIMIT),
-        cost_estimate=pl.CostEstimate(flops=10**6, transcendentals=0, bytes_accessed=4000000),
+        cost_estimate=cost(1.5),
         name="final",
     )(start, first, second)
 
@@ -647,25 +667,24 @@
     freq = jnp.asarray(np.tile(THETA**-exponent, 4).reshape(1, 128), F32)
     index = recomputed_index.reshape(8, 128)
 
-    gate_up = jnp.swapaxes(w_gate_up, 1, 2)
-    gate_below = send(gate_up, next_z)
-    gate_above = send(gate_up, last_z)
-    down_below = send(w_down, next_z)
-    down_above = send(w_down, last_z)
-    gate_far = send(gate_above, last_z)
-    down_far = send(down_below, next_z)
-    gate_ups = (gate_up, gate_below, gate_above, gate_far)
-    downs = (w_down, down_below, down_above, down_far)
-
+    w_qkv, w_out, key_value_cache, held_hidden, prefill_hidden = in_hbm(
+        w_qkv, w_out, key_value_cache, held_hidden, prefill_hidden
+    )
     total = 2 * SIDE**3
     spread = jnp.broadcast_to(decode_hidden[None], (total, 2, WIDTH))
     every_row = lax.all_to_all(spread, "req", 0, 0).reshape(256, WIDTH)
 
     query, kv = prefill_qkv(rank, prefill_hidden, gain, freq, w_qkv)
+    query, kv = in_hbm(query, kv)
     zed = send(kv, pair_z)
     core = send(kv, other_core)
-    far = send(zed, other_core)
-
+    gate_up, w_down, query = lax.optimization_barrier(
+        (jnp.swapaxes(w_gate_up, 1, 2), w_down, query)
+    )
+    packed = pack_weights(gate_up, w_down)
+    below = send(packed, next_z)
+    above = send(packed, last_z)
+    packed_core = send(packed, other_core)
     outgoing = decode_attention(
         device,
         cache_len,
@@ -679,32 +698,38 @@
         key_value_cache,
         held_hidden,
     )
+    outgoing, zed, core, below, above, packed_core = lax.optimization_barrier(
+        (outgoing, zed, core, below, above, packed_core)
+    )
+    far = send(zed, other_core)
+    core, zed, far = in_hbm(core, zed, far)
+    cut = 3 * SHARE // 2
+    far_low = send(below[:cut], next_z)
+    far_high = send(above[cut:], last_z)
+    below_core = send(below, other_core)
+    above_core = send(above, other_core)
     back = lax.all_to_all(outgoing.reshape(total, 2, WIDTH), "req", 0, 0).reshape(256, WIDTH)
 
     resid, lower, upper = attention(
         rank, query, kv, core, zed, far, w_out, prefill_hidden, gain2
     )
+    (resid,) = in_hbm(resid)
+    lower, upper, back, far_low, far_high, below_core, above_core = lax.optimization_barrier(
+        (lower, upper, back, far_low, far_high, below_core, above_core)
+    )
+    far_low_core = send(far_low, other_core)
+    far_high_core = send(far_high, other_core)
     extra, lower, upper = decode_rows(back, w_out, decode_hidden, gain2, lower, upper)
     from_last = send(lower, next_x)
     from_next = send(upper, last_x)
-    lower_across = send(lower, other_core)
-    upper_across = send(upper, other_core)
-    mine, given = feed_forward(
-        (lower, upper, lower_across, upper_across), gate_ups, downs, "feed_own"
-    )
-    from_last, from_next, mine, given = lax.optimization_barrier(
-        (from_last, from_next, mine, given)
-    )
-    last_across = send(from_last, other_core)
-    next_across = send(from_next, other_core)
-    given = send(given, other_core)
-    guest_mine, guest_given = feed_forward(
-        (from_last, from_next, last_across, next_across), gate_ups, downs, "feed_guest"
-    )
-    guest_given = send(guest_given, other_core)
-    first = send(add_half(guest_mine, guest_given, 0), last_x)
-    second = send(add_half(guest_mine, guest_given, 1), next_x)
-    start = start_sum(resid, extra, mine, given)
+    weights = (packed, packed_core, below, below_core, above, above_core)
+    weights += (far_low, far_low_core, far_high, far_high_core)
+    mine = feed_forward((lower, upper), weights, "feed_own")
+    from_last, from_next, mine = lax.optimization_barrier((from_last, from_next, mine))
+    guest = feed_forward((from_last, from_next), weights, "feed_guest")
+    first = send(guest[0], last_x)
+    second = send(guest[1], next_x)
+    start = start_sum(resid, extra, mine)
     return final_sum(start, first, second)
 
 

time: 158 us -> 153 us (0.968)
  waiting for transfers between devices: 34.8 us -> 50.6 us
  Pallas kernels: 69.5 us -> 56.6 us
  starting transfers between devices: 39.9 us -> 34.3 us
  local copies, waits for them, and re-layouts: 11.4 us -> 9.31 us
    ppermute x19 -> x16, waiting for transfers between devices: 34.8 us -> 47 us  [send(): return lax.ppermute(array, 'req', moves(step))]
    ppermute x19 -> x16, starting transfers between devices: 19.5 us -> 13.5 us  [send(): return lax.ppermute(array, 'req', moves(step))]
    pallas_call x4 -> x3, Pallas kernels: 23.2 us -> 19 us  [the longest x2 17.5 us: feed_forward(): pl.pallas_call(feed_kernel, out_shape=(jax.ShapeDtypeStruct((HALF, WIDTH)...]
    all_to_all x1, waiting for transfers between devices: 0.01 us -> 3.68 us  [body(): every_row = lax.all_to_all(spread, 'req', 0, 0).reshape(256, WIDTH)]
    slice x0 -> x2, local copies, waits for them, and re-layouts: none -> 3.11 us  [the longest x1 2.14 us: body(): far_low = send(below[:cut], next_z)]
    unnamed x32 -> x24, local copies, waits for them, and re-layouts: 3.46 us -> 0.9 us
    pallas_call x1, Pallas kernels: 17.5 us -> 15.3 us  [decode_attention(): pl.pallas_call(decode_kernel, out_shape=jax.ShapeDtypeStruct((256, QW), B...]
    pallas_call x1, Pallas kernels: 2.93 us -> 1.23 us  [start_sum(): pl.pallas_call(start_kernel, out_shape=jax.ShapeDtypeStruct((2 * HALF, WI...]
  transfers between devices with their start and end apart: 21 -> 18, of which waited for: 8 -> 6; matrix products, arithmetic and copies ran while one was open for 4% -> 4% of each run, Pallas kernels for 36% -> 31%
where the time goes in v3:
time: 153 us; the launch traced here: 152 us
  Pallas kernels  56.6 us (37%)
  waiting for transfers between devices  50.6 us (33%)
  starting transfers between devices  34.3 us (22%)
  local copies, waits for them, and re-layouts  9.31 us (6%)
  between operations  1.59 us (1%)
    ppermute x16, waiting for transfers between devices, send(): return lax.ppermute(array, 'req', moves(step))  47 us
    pallas_call x2, Pallas kernels, feed_forward(): pl.pallas_call(feed_kernel, out_shape=(jax.ShapeDtypeStruct((HALF, WIDTH)...  17.5 us
    pallas_call x1, Pallas kernels, decode_attention(): pl.pallas_call(decode_kernel, out_shape=jax.ShapeDtypeStruct((256, QW), B...  15.3 us
    ppermute x16, starting transfers between devices, send(): return lax.ppermute(array, 'req', moves(step))  13.5 us
    pallas_call x1, Pallas kernels, attention(): pl.pallas_call(attention_kernel, out_shape=(jax.ShapeDtypeStruct((ROWS, W...  11.5 us
    all_to_all x1, starting transfers between devices, body(): every_row = lax.all_to_all(spread, 'req', 0, 0).reshape(256, WIDTH)  11.1 us
    all_to_all x1, starting transfers between devices, body(): lax.all_to_all(outgoing.reshape(total, 2, WIDTH), 'req', 0, 0)  9.72 us
    pallas_call x1, Pallas kernels, prefill_qkv(): pl.pallas_call(qkv_kernel, out_shape=(jax.ShapeDtypeStruct((ROWS, QW), BF...  5.9 us
  transfers between devices with their start and end apart: 18, of which 6 were waited for; matrix products, arithmetic and copies ran while one was open for 4% of the time, Pallas kernels for 31%

profile of v3, /device:TPU:0, one launch (start us, length us, event | category | flops | bytes accessed | tf_op | source)
XLA Modules:
  0.0 152.4 jit_solution(3430358797969824132)
XLA Ops:
  0.6 0.0 copy-start.7
  0.7 1.9 %broadcast_in_dim.2 = bf16[128,2,1280]{2,1,0:T(2,128)(2,1)} broadcast(bf16[2,1280]{1,0:T(2,128)(2,1)} %decode_ref.1), dimensions={1,2} | broadcast | bytes 660480 | tf_op jit(solution)/shard_map/broadcast_in_dim | solution.py:674
  2.5 11.1 %all-to-all-start = ((bf16[128,2,1280]{2,1,0:T(2,128)(2,1)}), bf16[128,2,1280]{2,1,0:T(2,128)(2,1)S(1)}, u32[]{:S(2)}, u32[]{:S(2)}) async-start(bf16[128,2,1280]{2,1,0:T(2,128)(2,1)} %broadcast_in_dim.2), calls=%async_computation | async-start | bytes 1310720 | tf_op jit(solution)/shard_map/all_to_all | solution.py:675
  13.7 0.0 copy-done.10
  13.7 0.0 copy-start.1
  13.7 0.0 copy-start.2
  13.8 5.9 %prefill_qkv.1 = (bf16[256,1280]{1,0:T(8,128)(2,1)S(1)}, bf16[256,640]{1,0:T(8,128)(2,1)S(1)}) custom-call(s32[1]{0:T(128)S(6)} %select_n.7.rank_ref, bf16[256,1280]{1,0:T(8,128)(2,1)} %hidden_ref.5, f32[1,1280]{1,0:T(1,128)S(1)} %reshape.32.gain_ref, f32[1,128]{1,0:T(1,128)S(1)} %copy-done.7, bf16[1280,1920]{1,0:T(8,128)(2,1)} %w_ref.5), custom_call_target="tpu_custom_call" | custom-call | flops 7000000000 | bytes 21000000 | tf_op jit(solution)/shard_map/prefill_qkv/pallas_call | solution.py:188
  19.7 0.0 copy-start.9
  19.7 0.0 copy-start.4
  19.7 0.0 copy-start.5
  19.7 0.0 copy-start.6
  19.7 1.5 %pack.1.refs_2_ = bf16[672,1280]{1,0:T(8,128)(2,1)} custom-call(bf16[1,448,1280]{2,1,0:T(8,128)(2,1)S(1)} %bitcast.4, bf16[1,224,1280]{2,1,0:T(8,128)(2,1)S(1)} %copy-done.2), custom_call_target="tpu_custom_call" | custom-call | flops 1500000000 | bytes 4500000 | tf_op jit(solution)/shard_map/pack/pallas_call | solution.py:136
  21.3 0.0 collective-permute-start.4
  21.3 3.0 %collective-permute-start.3 = (bf16[672,1280]{1,0:T(8,128)(2,1)}, bf16[672,1280]{1,0:T(8,128)(2,1)S(1)}, u32[]{:S(2)}, u32[]{:S(2)}) collective-permute-start(bf16[672,1280]{1,0:T(8,128)(2,1)} %pack.1.refs_2_), channel_id=1, source_target_pairs={{0,6},{1,7},{2,0},{3,1},{4,2},{5,3},{6,4},{7,5},{8,14},{9,15},{10,... | collective-permute-start | bytes 5160968 | tf_op jit(solution)/shard_map/ppermute | solution.py:53
  24.3 0.0 collective-permute-start.2
  24.3 0.1 collective-permute-start.1
  24.3 0.2 collective-permute-start
  25.2 3.7 %all-to-all-done = bf16[128,2,1280]{2,1,0:T(2,128)(2,1)S(1)} async-done(((bf16[128,2,1280]{2,1,0:T(2,128)(2,1)}), bf16[128,2,1280]{2,1,0:T(2,128)(2,1)S(1)}, u32[]{:S(2)}, u32[]{:S(2)}) %all-to-all-start) | async-done | bytes 655392 | tf_op jit(solution)/shard_map/all_to_all | solution.py:675
  28.9 0.2 reshape.35.rows_ref
  29.1 0.0 copy-done.4
  29.2 0.0 copy-start.11
  29.2 15.3 %decode.1 = bf16[256,1280]{1,0:T(8,128)(2,1)S(1)} custom-call(s32[1]{0:T(128)} %bitcast.device_ref, s32[4]{0:T(128)S(1)} %copy-done.6, s32[1]{0:T(128)S(6)} %copy.21.count_ref, s32[1,256]{1,0:T(1,128)S(1)} %bitcast.6, s32[8,128]{1,0:T(8,128)S(1)} %bitcast.5, bf16[256,1280]{1,0:T(8,128)(2,1)S(1)} %reshape.35.rows_ref, f32[1,1280]{1,0:T(1,128)S(1)} %reshape.32.gain_ref, ...), custom_call_target="tpu_custom_call" | custom-call | flops 16999999488 | bytes 51000000 | tf_op jit(solution)/shard_map/decode/pallas_call | solution.py:368
  44.4 0.0 collective-permute-done.1.core_ref
  44.5 25.0 %collective-permute-done.zed_ref = bf16[256,640]{1,0:T(8,128)(2,1)} collective-permute-done((bf16[256,640]{1,0:T(8,128)(2,1)S(1)}, bf16[256,640]{1,0:T(8,128)(2,1)}, u32[]{:S(2)}, u32[]{:S(2)}) %collective-permute-start) | collective-permute-done | bytes 327712 | tf_op jit(solution)/shard_map/ppermute | solution.py:53
  69.4 0.0 collective-permute-done.4.refs_3_
  69.4 0.0 collective-permute-done.3.refs_6_
  69.4 0.0 collective-permute-done.2.refs_4_
  69.4 0.1 collective-permute-start.8
  69.5 0.5 collective-permute-start.9
  70.0 0.1 collective-permute-start.5
  70.1 2.1 %slice.6 = bf16[336,1280]{1,0:T(8,128)(2,1)} slice(bf16[672,1280]{1,0:T(8,128)(2,1)} %collective-permute-done.2.refs_4_), slice={[0:336], [0:1280]} | slice | bytes 1720320 | tf_op jit(solution)/shard_map/slice | solution.py:707
  72.2 1.0 slice.7
  73.2 1.1 reshape.37
  74.3 9.7 %all-to-all-start.1 = ((bf16[128,2,1280]{2,1,0:T(2,128)(2,1)}), bf16[128,2,1280]{2,1,0:T(2,128)(2,1)}, u32[]{:S(2)}, u32[]{:S(2)}) async-start(bf16[128,2,1280]{2,1,0:T(2,128)(2,1)} %reshape.37), calls=%async_computation.1 | async-start | bytes 1310720 | tf_op jit(solution)/shard_map/all_to_all | solution.py:711
  84.1 0.0 copy-start
  84.1 2.8 %collective-permute-start.7 = (bf16[336,1280]{1,0:T(8,128)(2,1)}, bf16[336,1280]{1,0:T(8,128)(2,1)}, u32[]{:S(2)}, u32[]{:S(2)}) collective-permute-start(bf16[336,1280]{1,0:T(8,128)(2,1)} %slice.7), channel_id=1, source_target_pairs={{0,6},{1,7},{2,0},{3,1},{4,2},{5,3},{6,4},{7,5},{8,14},{9,15},{10,... | collective-permute-start | bytes 2580488 | tf_op jit(solution)/shard_map/ppermute | solution.py:53
  86.9 0.0 collective-permute-start.6
  86.9 0.0 collective-permute-done.5.far_ref
  86.9 11.5 %attention.1 = (bf16[256,1280]{1,0:T(8,128)(2,1)S(1)}, bf16[144,1280]{1,0:T(8,128)(2,1)S(1)}, bf16[144,1280]{1,0:T(8,128)(2,1)S(1)}) custom-call(s32[1]{0:T(128)S(6)} %select_n.7.rank_ref, bf16[256,1280]{1,0:T(8,128)(2,1)} %copy-done.9, bf16[256,640]{1,0:T(8,128)(2,1)} %copy-done.3, bf16[256,640]{1,0:T(8,128)(2,1)} %collective-permute-done.1.core_ref, ...), custom_call_target="tpu_custom_call" | custom-call | flops 12000000000 | bytes 36000000 | tf_op jit(solution)/shard_map/attention/pallas_call | solution.py:481
  98.4 0.0 copy-start.8
  98.4 0.8 copy-done.8
  99.2 0.0 all-to-all-done.1
  99.2 2.1 %reshape.38.back_ref = bf16[256,1280]{1,0:T(8,128)(2,1)S(1)} reshape(bf16[128,2,1280]{2,1,0:T(2,128)(2,1)} %all-to-all-done.1) | data formatting | bytes 1310720 | tf_op jit(solution)/shard_map/reshape | solution.py:711
  101.3 10.2 %collective-permute-done.7.refs_10_ = bf16[336,1280]{1,0:T(8,128)(2,1)} collective-permute-done((bf16[336,1280]{1,0:T(8,128)(2,1)}, bf16[336,1280]{1,0:T(8,128)(2,1)}, u32[]{:S(2)}, u32[]{:S(2)}) %collective-permute-start.7) | collective-permute-done | bytes 860192 | tf_op jit(solution)/shard_map/ppermute | solution.py:53
  111.5 2.7 %collective-permute-done.6.refs_8_ = bf16[336,1280]{1,0:T(8,128)(2,1)} collective-permute-done((bf16[336,1280]{1,0:T(8,128)(2,1)}, bf16[336,1280]{1,0:T(8,128)(2,1)}, u32[]{:S(2)}, u32[]{:S(2)}) %collective-permute-start.6) | collective-permute-done | bytes 860192 | tf_op jit(solution)/shard_map/ppermute | solution.py:53
  114.2 0.0 collective-permute-done.8.refs_5_
  114.2 0.0 collective-permute-done.9.refs_7_
  114.2 0.0 collective-permute-start.12
  114.2 0.5 collective-permute-start.13
  114.7 2.8 %decode_rows.1 = (bf16[32,1280]{1,0:T(8,128)(2,1)S(1)}, bf16[144,1280]{1,0:T(8,128)(2,1)S(1)}, bf16[144,1280]{1,0:T(8,128)(2,1)S(1)}) custom-call(bf16[256,1280]{1,0:T(8,128)(2,1)S(1)} %reshape.38.back_ref, bf16[1280,1280]{1,0:T(8,128)(2,1)} %w_ref.7, bf16[2,1280]{1,0:T(2,128)(2,1)S(1)} %copy-done, ...), custom_call_target="tpu_custom_call", output_to_operand_aliasing={{1}: (4, {}), {2}: (5, {})} | custom-call | flops 3000000000 | bytes 9000000 | tf_op jit(solution)/shard_map/decode_rows/pallas_call | solution.py:536
  117.5 1.5 collective-permute-start.10
  118.9 1.8 %collective-permute-start.11 = (bf16[144,1280]{1,0:T(8,128)(2,1)S(1)}, bf16[144,1280]{1,0:T(8,128)(2,1)S(1)}, u32[]{:S(2)}, u32[]{:S(2)}) collective-permute-start(bf16[144,1280]{1,0:T(8,128)(2,1)S(1)} %get-tuple-element.52.refs_1_), channel_id=1, source_target_pairs={{0,24},{1,25},{2,26},{3,27},{4,28},{5,29},{6,30},{7,31},{8,0},{9,1... | collective-permute-start | bytes 1105928 | tf_op jit(solution)/shard_map/ppermute | solution.py:53
  120.8 0.0 collective-permute-done.12.refs_9_
  120.8 0.0 collective-permute-done.13.refs_11_
  120.8 8.7 %feed_own.1 = (bf16[144,1280]{1,0:T(8,128)(2,1)S(1)}, bf16[144,1280]{1,0:T(8,128)(2,1)S(1)}) custom-call(bf16[144,1280]{1,0:T(8,128)(2,1)S(1)} %get-tuple-element.51.refs_0_, bf16[144,1280]{1,0:T(8,128)(2,1)S(1)} %get-tuple-element.52.refs_1_, bf16[672,1280]{1,0:T(8,128)(2,1)} %pack.1.refs_2_, bf16[672,1280]{1,0:T(8,128)(2,1)} %collective-permute-done.4.refs_3_, ...), custom_call_target="tpu_custom_call" | custom-call | flops 8000000000 | bytes 24000000 | tf_op jit(solution)/shard_map/feed_own/pallas_call | solution.py:586
  129.5 0.0 collective-permute-done.10.refs_0_
  129.5 0.0 collective-permute-done.11.refs_1_
  129.5 8.8 %feed_guest.1 = (bf16[144,1280]{1,0:T(8,128)(2,1)S(1)}, bf16[144,1280]{1,0:T(8,128)(2,1)S(1)}) custom-call(bf16[144,1280]{1,0:T(8,128)(2,1)S(1)} %collective-permute-done.10.refs_0_, bf16[144,1280]{1,0:T(8,128)(2,1)S(1)} %collective-permute-done.11.refs_1_, bf16[672,1280]{1,0:T(8,128)(2,1)} %pack.1.refs_2_, ...), custom_call_target="tpu_custom_call" | custom-call | flops 8000000000 | bytes 24000000 | tf_op jit(solution)/shard_map/feed_guest/pallas_call | solution.py:586
  138.3 2.9 %collective-permute-start.14 = (bf16[144,1280]{1,0:T(8,128)(2,1)S(1)}, bf16[144,1280]{1,0:T(8,128)(2,1)S(1)}, u32[]{:S(2)}, u32[]{:S(2)}) collective-permute-start(bf16[144,1280]{1,0:T(8,128)(2,1)S(1)} %get-tuple-element.64), channel_id=1, source_target_pairs={{0,24},{1,25},{2,26},{3,27},{4,28},{5,29},{6,30},{7,31},{8,0},{9,1... | collective-permute-start | bytes 1105928 | tf_op jit(solution)/shard_map/ppermute | solution.py:53
  141.1 0.0 collective-permute-start.15
  141.1 1.2 start_sum.1.start_ref
  142.4 6.0 %collective-permute-done.14.first_ref = bf16[144,1280]{1,0:T(8,128)(2,1)S(1)} collective-permute-done((bf16[144,1280]{1,0:T(8,128)(2,1)S(1)}, bf16[144,1280]{1,0:T(8,128)(2,1)S(1)}, u32[]{:S(2)}, u32[]{:S(2)}) %collective-permute-start.14) | collective-permute-done | bytes 368672 | tf_op jit(solution)/shard_map/ppermute | solution.py:53
  148.4 3.1 %collective-permute-done.15.second_ref = bf16[144,1280]{1,0:T(8,128)(2,1)S(1)} collective-permute-done((bf16[144,1280]{1,0:T(8,128)(2,1)S(1)}, bf16[144,1280]{1,0:T(8,128)(2,1)S(1)}, u32[]{:S(2)}, u32[]{:S(2)}) %collective-permute-start.15) | collective-permute-done | bytes 368672 | tf_op jit(solution)/shard_map/ppermute | solution.py:53
  151.5 1.0 final.1
  (13 shorter events, 0.0 us)
Async XLA Ops:
  0.6 13.1 %copy-start.7 = (f32[1,128]{1,0:T(1,128)S(1)}, f32[1,128]{1,0:T(1,128)}, u32[]{:S(2)}) copy-start(f32[1,128]{1,0:T(1,128)} %constant.25.clone.freq_ref) | copy-start | bytes 1540
  0.6 13.1 %copy-start.10 = (f32[1280]{0:T(1024)S(1)}, f32[1280]{0:T(1024)}, u32[]{:S(2)}) copy-start(f32[1280]{0:T(1024)} %param.17) | copy-start | bytes 15364
  2.5 26.4 %all-to-all-start = ((bf16[128,2,1280]{2,1,0:T(2,128)(2,1)}), bf16[128,2,1280]{2,1,0:T(2,128)(2,1)S(1)}, u32[]{:S(2)}, u32[]{:S(2)}) async-start(bf16[128,2,1280]{2,1,0:T(2,128)(2,1)} %broadcast_in_dim.2), calls=%async_computation | async-start | bytes 1310720 | tf_op jit(solution)/shard_map/all_to_all | solution.py:675
  13.7 6.0 %copy-start.1 = (bf16[1,1280,448]{1,2,0:T(8,128)(2,1)S(1)}, bf16[1,1280,448]{1,2,0:T(8,128)(2,1)}, u32[]{:S(2)}) copy-start(bf16[1,1280,448]{1,2,0:T(8,128)(2,1)} %param.21) | copy-start | bytes 3440644
  13.7 6.0 %copy-start.2 = (bf16[1,224,1280]{2,1,0:T(8,128)(2,1)S(1)}, bf16[1,224,1280]{2,1,0:T(8,128)(2,1)}, u32[]{:S(2)}) copy-start(bf16[1,224,1280]{2,1,0:T(8,128)(2,1)} %down_ref) | copy-start | bytes 1720324
  19.7 1.6 %copy-start.9 = (bf16[256,1280]{1,0:T(8,128)(2,1)}, bf16[256,1280]{1,0:T(8,128)(2,1)S(1)}, u32[]{:S(2)}) copy-start(bf16[256,1280]{1,0:T(8,128)(2,1)S(1)} %get-tuple-element.35.query_ref) | copy-start | bytes 1966084
  19.7 4.7 %copy-start.3 = (bf16[256,640]{1,0:T(8,128)(2,1)}, bf16[256,640]{1,0:T(8,128)(2,1)S(1)}, u32[]{:S(2)}) copy-start(bf16[256,640]{1,0:T(8,128)(2,1)S(1)} %get-tuple-element.36.own_ref) | copy-start | bytes 983044
  19.7 9.4 %copy-start.4 = (s32[1024]{0:T(1024)S(1)}, s32[1024]{0:T(1024)}, u32[]{:S(2)}) copy-start(s32[1024]{0:T(1024)} %param.27) | copy-start | bytes 12292
  19.7 9.4 %copy-start.5 = (s32[256]{0:T(256)S(1)}, s32[256]{0:T(256)}, u32[]{:S(2)}) copy-start(s32[256]{0:T(256)} %param.25) | copy-start | bytes 3076
  19.7 9.4 %copy-start.6 = (s32[4]{0:T(128)S(1)}, s32[4]{0:T(128)}, u32[]{:S(2)}) copy-start(s32[4]{0:T(128)} %length_ref.1) | copy-start | bytes 52
  21.3 48.1 %collective-permute-start.4 = (bf16[672,1280]{1,0:T(8,128)(2,1)}, bf16[672,1280]{1,0:T(8,128)(2,1)}, u32[]{:S(2)}, u32[]{:S(2)}) collective-permute-start(bf16[672,1280]{1,0:T(8,128)(2,1)} %pack.1.refs_2_), channel_id=1, source_target_pairs={{0,1},{1,0},{2,3},{3,2},{4,5},{5,4},{6,7},{7,6},{8,9},{9,8},{10,11... | collective-permute-start | bytes 5160968 | tf_op jit(solution)/shard_map/ppermute | solution.py:53
  21.3 48.1 %collective-permute-start.3 = (bf16[672,1280]{1,0:T(8,128)(2,1)}, bf16[672,1280]{1,0:T(8,128)(2,1)S(1)}, u32[]{:S(2)}, u32[]{:S(2)}) collective-permute-start(bf16[672,1280]{1,0:T(8,128)(2,1)} %pack.1.refs_2_), channel_id=1, source_target_pairs={{0,6},{1,7},{2,0},{3,1},{4,2},{5,3},{6,4},{7,5},{8,14},{9,15},{10,... | collective-permute-start | bytes 5160968 | tf_op jit(solution)/shard_map/ppermute | solution.py:53
  24.3 45.1 %collective-permute-start.2 = (bf16[672,1280]{1,0:T(8,128)(2,1)}, bf16[672,1280]{1,0:T(8,128)(2,1)}, u32[]{:S(2)}, u32[]{:S(2)}) collective-permute-start(bf16[672,1280]{1,0:T(8,128)(2,1)} %pack.1.refs_2_), channel_id=1, source_target_pairs={{0,2},{1,3},{2,4},{3,5},{4,6},{5,7},{6,0},{7,1},{8,10},{9,11},{10,... | collective-permute-start | bytes 5160968 | tf_op jit(solution)/shard_map/ppermute | solution.py:53
  24.3 20.2 %collective-permute-start.1 = (bf16[256,640]{1,0:T(8,128)(2,1)S(1)}, bf16[256,640]{1,0:T(8,128)(2,1)}, u32[]{:S(2)}, u32[]{:S(2)}) collective-permute-start(bf16[256,640]{1,0:T(8,128)(2,1)S(1)} %get-tuple-element.36.own_ref), channel_id=1, source_target_pairs={{0,1},{1,0},{2,3},{3,2},{4,5},{5,4},{6,7},{7,6},{8,9},{9,8},{10,11... | collective-permute-start | bytes 983048 | tf_op jit(solution)/shard_map/ppermute | solution.py:53
  24.3 45.1 %collective-permute-start = (bf16[256,640]{1,0:T(8,128)(2,1)S(1)}, bf16[256,640]{1,0:T(8,128)(2,1)}, u32[]{:S(2)}, u32[]{:S(2)}) collective-permute-start(bf16[256,640]{1,0:T(8,128)(2,1)S(1)} %get-tuple-element.36.own_ref), channel_id=1, source_target_pairs={{0,2},{1,3},{2,0},{3,1},{4,6},{5,7},{6,4},{7,5},{8,10},{9,11},{10,... | collective-permute-start | bytes 983048 | tf_op jit(solution)/shard_map/ppermute | solution.py:53
  29.2 40.9 %copy-start.11 = (f32[1280]{0:T(1024)S(1)}, f32[1280]{0:T(1024)}, u32[]{:S(2)}) copy-start(f32[1280]{0:T(1024)} %param.20) | copy-start | bytes 15364
  69.4 44.7 %collective-permute-start.8 = (bf16[672,1280]{1,0:T(8,128)(2,1)}, bf16[672,1280]{1,0:T(8,128)(2,1)}, u32[]{:S(2)}, u32[]{:S(2)}) collective-permute-start(bf16[672,1280]{1,0:T(8,128)(2,1)} %collective-permute-done.2.refs_4_), channel_id=1, source_target_pairs={{0,1},{1,0},{2,3},{3,2},{4,5},{5,4},{6,7},{7,6},{8,9},{9,8},{10,11... | collective-permute-start | bytes 5160968 | tf_op jit(solution)/shard_map/ppermute | solution.py:53
  69.5 44.7 %collective-permute-start.9 = (bf16[672,1280]{1,0:T(8,128)(2,1)S(1)}, bf16[672,1280]{1,0:T(8,128)(2,1)}, u32[]{:S(2)}, u32[]{:S(2)}) collective-permute-start(bf16[672,1280]{1,0:T(8,128)(2,1)S(1)} %collective-permute-done.3.refs_6_), channel_id=1, source_target_pairs={{0,1},{1,0},{2,3},{3,2},{4,5},{5,4},{6,7},{7,6},{8,9},{9,8},{10,11... | collective-permute-start | bytes 5160968 | tf_op jit(solution)/shard_map/ppermute | solution.py:53
  70.0 16.9 %collective-permute-start.5 = (bf16[256,640]{1,0:T(8,128)(2,1)}, bf16[256,640]{1,0:T(8,128)(2,1)}, u32[]{:S(2)}, u32[]{:S(2)}) collective-permute-start(bf16[256,640]{1,0:T(8,128)(2,1)} %collective-permute-done.zed_ref), channel_id=1, source_target_pairs={{0,1},{1,0},{2,3},{3,2},{4,5},{5,4},{6,7},{7,6},{8,9},{9,8},{10,11... | collective-permute-start | bytes 983048 | tf_op jit(solution)/shard_map/ppermute | solution.py:53
  74.3 24.9 %all-to-all-start.1 = ((bf16[128,2,1280]{2,1,0:T(2,128)(2,1)}), bf16[128,2,1280]{2,1,0:T(2,128)(2,1)}, u32[]{:S(2)}, u32[]{:S(2)}) async-start(bf16[128,2,1280]{2,1,0:T(2,128)(2,1)} %reshape.37), calls=%async_computation.1 | async-start | bytes 1310720 | tf_op jit(solution)/shard_map/all_to_all | solution.py:711
  84.1 30.6 %copy-start = (bf16[2,1280]{1,0:T(2,128)(2,1)S(1)}, bf16[2,1280]{1,0:T(2,128)(2,1)}, u32[]{:S(2)}) copy-start(bf16[2,1280]{1,0:T(2,128)(2,1)} %decode_ref.1) | copy-start | bytes 15364
  84.1 27.4 %collective-permute-start.7 = (bf16[336,1280]{1,0:T(8,128)(2,1)}, bf16[336,1280]{1,0:T(8,128)(2,1)}, u32[]{:S(2)}, u32[]{:S(2)}) collective-permute-start(bf16[336,1280]{1,0:T(8,128)(2,1)} %slice.7), channel_id=1, source_target_pairs={{0,6},{1,7},{2,0},{3,1},{4,2},{5,3},{6,4},{7,5},{8,14},{9,15},{10,... | collective-permute-start | bytes 2580488 | tf_op jit(solution)/shard_map/ppermute | solution.py:53
  86.9 27.3 %collective-permute-start.6 = (bf16[336,1280]{1,0:T(8,128)(2,1)}, bf16[336,1280]{1,0:T(8,128)(2,1)}, u32[]{:S(2)}, u32[]{:S(2)}) collective-permute-start(bf16[336,1280]{1,0:T(8,128)(2,1)} %slice.6), channel_id=1, source_target_pairs={{0,2},{1,3},{2,4},{3,5},{4,6},{5,7},{6,0},{7,1},{8,10},{9,11},{10,... | collective-permute-start | bytes 2580488 | tf_op jit(solution)/shard_map/ppermute | solution.py:53
  98.4 0.8 copy-start.8
  114.2 6.6 %collective-permute-start.12 = (bf16[336,1280]{1,0:T(8,128)(2,1)}, bf16[336,1280]{1,0:T(8,128)(2,1)S(1)}, u32[]{:S(2)}, u32[]{:S(2)}) collective-permute-start(bf16[336,1280]{1,0:T(8,128)(2,1)} %collective-permute-done.6.refs_8_), channel_id=1, source_target_pairs={{0,1},{1,0},{2,3},{3,2},{4,5},{5,4},{6,7},{7,6},{8,9},{9,8},{10,11... | collective-permute-start | bytes 2580488 | tf_op jit(solution)/shard_map/ppermute | solution.py:53
  114.2 6.6 %collective-permute-start.13 = (bf16[336,1280]{1,0:T(8,128)(2,1)}, bf16[336,1280]{1,0:T(8,128)(2,1)S(1)}, u32[]{:S(2)}, u32[]{:S(2)}) collective-permute-start(bf16[336,1280]{1,0:T(8,128)(2,1)} %collective-permute-done.7.refs_10_), channel_id=1, source_target_pairs={{0,1},{1,0},{2,3},{3,2},{4,5},{5,4},{6,7},{7,6},{8,9},{9,8},{10,11... | collective-permute-start | bytes 2580488 | tf_op jit(solution)/shard_map/ppermute | solution.py:53
  117.5 12.0 %collective-permute-start.10 = (bf16[144,1280]{1,0:T(8,128)(2,1)S(1)}, bf16[144,1280]{1,0:T(8,128)(2,1)S(1)}, u32[]{:S(2)}, u32[]{:S(2)}) collective-permute-start(bf16[144,1280]{1,0:T(8,128)(2,1)S(1)} %get-tuple-element.51.refs_0_), channel_id=1, source_target_pairs={{0,8},{1,9},{2,10},{3,11},{4,12},{5,13},{6,14},{7,15},{8,16},{9,17... | collective-permute-start | bytes 1105928 | tf_op jit(solution)/shard_map/ppermute | solution.py:53
  118.9 10.6 %collective-permute-start.11 = (bf16[144,1280]{1,0:T(8,128)(2,1)S(1)}, bf16[144,1280]{1,0:T(8,128)(2,1)S(1)}, u32[]{:S(2)}, u32[]{:S(2)}) collective-permute-start(bf16[144,1280]{1,0:T(8,128)(2,1)S(1)} %get-tuple-element.52.refs_1_), channel_id=1, source_target_pairs={{0,24},{1,25},{2,26},{3,27},{4,28},{5,29},{6,30},{7,31},{8,0},{9,1... | collective-permute-start | bytes 1105928 | tf_op jit(solution)/shard_map/ppermute | solution.py:53
  138.3 10.1 %collective-permute-start.14 = (bf16[144,1280]{1,0:T(8,128)(2,1)S(1)}, bf16[144,1280]{1,0:T(8,128)(2,1)S(1)}, u32[]{:S(2)}, u32[]{:S(2)}) collective-permute-start(bf16[144,1280]{1,0:T(8,128)(2,1)S(1)} %get-tuple-element.64), channel_id=1, source_target_pairs={{0,24},{1,25},{2,26},{3,27},{4,28},{5,29},{6,30},{7,31},{8,0},{9,1... | collective-permute-start | bytes 1105928 | tf_op jit(solution)/shard_map/ppermute | solution.py:53
  141.1 10.3 %collective-permute-start.15 = (bf16[144,1280]{1,0:T(8,128)(2,1)S(1)}, bf16[144,1280]{1,0:T(8,128)(2,1)S(1)}, u32[]{:S(2)}, u32[]{:S(2)}) collective-permute-start(bf16[144,1280]{1,0:T(8,128)(2,1)S(1)} %get-tuple-element.65), channel_id=1, source_target_pairs={{0,8},{1,9},{2,10},{3,11},{4,12},{5,13},{6,14},{7,15},{8,16},{9,17... | collective-permute-start | bytes 1105928 | tf_op jit(solution)/shard_map/ppermute | solution.py:53

commit v4 on v3

--- a/solution.py
+++ b/solution.py
@@ -14,6 +14,7 @@
 QW = 1280
 KVW = 640
 SHARE = 224
+PART = 3 * SHARE // 2
 GROUP = 16
 SIDE = 4
 SLOTS = 4
@@ -127,90 +128,88 @@
     return chunk * cosine + other * sine
 
 
-def pack_kernel(gate_up_ref, down_ref, packed_ref):
-    packed_ref[: 2 * SHARE, :] = gate_up_ref[...]
-    packed_ref[2 * SHARE :, :] = down_ref[...]
+def pack_kernel(gate_up_ref, down_ref, low_ref, high_ref):
+    low_ref[...] = gate_up_ref[:PART, :]
+    high_ref[: 2 * SHARE - PART, :] = gate_up_ref[PART:, :]
+    high_ref[2 * SHARE - PART :, :] = down_ref[...]
 
 
 def pack_weights(gate_up, down):
+    half = jax.ShapeDtypeStruct((PART, WIDTH), BF)
+    block = pl.BlockSpec((PART, WIDTH // 2), lambda i: (0, i))
     return pl.pallas_call(
         pack_kernel,
-        out_shape=jax.ShapeDtypeStruct((3 * SHARE, WIDTH), BF),
+        out_shape=(half, half),
         grid=(2,),
         in_specs=[
             pl.BlockSpec((None, 2 * SHARE, WIDTH // 2), lambda i: (0, 0, i)),
             pl.BlockSpec((None, SHARE, WIDTH // 2), lambda i: (0, 0, i)),
         ],
-        out_specs=pl.BlockSpec((3 * SHARE, WIDTH // 2), lambda i: (0, i)),
+        out_specs=(block, block),
         compiler_params=pltpu.CompilerParams(vmem_limit_bytes=VMEM_LIMIT),
         cost_estimate=cost(1.5),
         name="pack",
     )(gate_up, down)
 
 
-def qkv_kernel(rank_ref, hidden_ref, gain_ref, freq_ref, w_ref, query_ref, kv_ref, normed, cos, sin):
-    step = pl.program_id(0)
-
-    @pl.when(step == 0)
+def kv_kernel(rank_ref, hidden_ref, gain_ref, freq_ref, w_ref, kv_ref):
+    normed = norm_rows(hidden_ref[...], gain_ref[...])
+    position = (sublanes((ROWS, 128)) * 4 + rank_ref[0]).astype(F32)
+    cosine, sine = rope_tables(position, freq_ref[...])
+    projected = jnp.dot(normed, w_ref[...], preferred_element_type=F32)
+    chunks = [projected[:, i * 128 : (i + 1) * 128] for i in range(5)]
+    low = lanes((ROWS, 128)) < HEAD
+    first = rope(chunks[0], cosine, sine)
+    second = rope(chunks[1], cosine, sine)
+    third = jnp.where(low, rope(chunks[2], cosine, sine), chunks[2])
+    swap = lambda value: pltpu.roll(value, 64, 1)
+    out = [
+        jnp.where(low, first, third),
+        jnp.where(low, swap(first), swap(chunks[3])),
+        jnp.where(low, second, chunks[3]),
+        jnp.where(low, swap(second), swap(chunks[4])),
+        jnp.where(low, third, chunks[4]),
+    ]
+    for i in range(5):
+        kv_ref[:, i * 128 : (i + 1) * 128] = out[i].astype(BF)
+
+
+def query_kernel(rank_ref, hidden_ref, gain_ref, freq_ref, w_ref, query_ref, normed, cos, sin):
+    @pl.when(pl.program_id(0) == 0)
     def _():
         normed[...] = norm_rows(hidden_ref[...], gain_ref[...])
         position = (sublanes((ROWS, 128)) * 4 + rank_ref[0]).astype(F32)
         cos[...], sin[...] = rope_tables(position, freq_ref[...])
 
     projected = jnp.dot(normed[...], w_ref[...], preferred_element_type=F32)
-    chunks = [projected[:, i * 128 : (i + 1) * 128] for i in range(5)]
-
-    @pl.when(step < 2)
-    def _():
-        for i in range(5):
-            roped = rope(chunks[i], cos[...], sin[...]).astype(BF)
-            query_ref[:, i * 128 : (i + 1) * 128] = roped * jnp.asarray(0.125, BF)
-
-    @pl.when(step == 2)
-    def _():
-        low = lanes((ROWS, 128)) < HEAD
-        first = rope(chunks[0], cos[...], sin[...])
-        second = rope(chunks[1], cos[...], sin[...])
-        third = jnp.where(low, rope(chunks[2], cos[...], sin[...]), chunks[2])
-        swap = lambda value: pltpu.roll(value, 64, 1)
-        out = [
-            jnp.where(low, first, third),
-            jnp.where(low, swap(first), swap(chunks[3])),
-            jnp.where(low, second, chunks[3]),
-            jnp.where(low, swap(second), swap(chunks[4])),
-            jnp.where(low, third, chunks[4]),
-        ]
-        for i in range(5):
-            kv_ref[:, i * 128 : (i + 1) * 128] = out[i].astype(BF)
-
-
-def prefill_qkv(rank, hidden, gain, freq, w_qkv):
+    for i in range(5):
+        roped = rope(projected[:, i * 128 : (i + 1) * 128], cos[...], sin[...]).astype(BF)
+        query_ref[:, i * 128 : (i + 1) * 128] = roped * jnp.asarray(0.125, BF)
+
+
+def project(rank, hidden, gain, freq, w_qkv, keys):
+    steps = 1 if keys else 2
+    scratch = [
+        pltpu.VMEM((ROWS, WIDTH), BF),
+        pltpu.VMEM((ROWS, 128), F32),
+        pltpu.VMEM((ROWS, 128), F32),
+    ]
     return pl.pallas_call(
-        qkv_kernel,
-        out_shape=(
-            jax.ShapeDtypeStruct((ROWS, QW), BF),
-            jax.ShapeDtypeStruct((ROWS, KVW), BF),
-        ),
-        grid=(3,),
+        kv_kernel if keys else query_kernel,
+        out_shape=jax.ShapeDtypeStruct((ROWS, KVW * steps), BF),
+        grid=(steps,),
         in_specs=[
             pl.BlockSpec(memory_space=pltpu.SMEM),
             pl.BlockSpec((ROWS, WIDTH), lambda j: (0, 0)),
             pl.BlockSpec((1, WIDTH), lambda j: (0, 0)),
             pl.BlockSpec((1, 128), lambda j: (0, 0)),
-            pl.BlockSpec((WIDTH, KVW), lambda j: (0, j)),
+            pl.BlockSpec((WIDTH, KVW), (lambda j: (0, 2)) if keys else (lambda j: (0, j))),
         ],
-        out_specs=(
-            pl.BlockSpec((ROWS, KVW), lambda j: (0, jnp.minimum(j, 1))),
-            pl.BlockSpec((ROWS, KVW), lambda j: (0, 0)),
-        ),
-        scratch_shapes=[
-            pltpu.VMEM((ROWS, WIDTH), BF),
-            pltpu.VMEM((ROWS, 128), F32),
-            pltpu.VMEM((ROWS, 128), F32),
-        ],
+        out_specs=pl.BlockSpec((ROWS, KVW), lambda j: (0, j)),
+        scratch_shapes=[] if keys else scratch,
         compiler_params=pltpu.CompilerParams(vmem_limit_bytes=VMEM_LIMIT),
-        cost_estimate=cost(7),
-        name="prefill_qkv",
+        cost_estimate=cost(3 if keys else 5),
+        name="prefill_kv" if keys else "prefill_query",
     )(rank, hidden, gain, freq, w_qkv)
 
 
@@ -558,41 +557,33 @@
 
 
 def feed_kernel(*refs):
-    pieces, packs, far_low, far_high = refs[:2], refs[2:8], refs[8:10], refs[10:12]
-    outs, act = refs[12:14], refs[14]
-    cut = 3 * SHARE // 2
+    pieces, lows, highs, outs, act = refs[:2], refs[2:10], refs[10:18], refs[18:20], refs[20]
+    cut = 2 * SHARE - PART
     rows = jnp.concatenate([ref[...] for ref in pieces], axis=0)
-    downs = []
     for k in range(8):
-        if k < 6:
-            gate_rows = packs[k][:SHARE, :]
-            up_rows = packs[k][SHARE : 2 * SHARE, :]
-            downs.append(packs[k][2 * SHARE :, :])
-        else:
-            low, high = far_low[k - 6], far_high[k - 6]
-            gate_rows = low[:SHARE, :]
-            up_rows = jnp.concatenate([low[SHARE:, :], high[: 2 * SHARE - cut, :]], axis=0)
-            downs.append(high[2 * SHARE - cut :, :])
+        gate_rows = lows[k][:SHARE, :]
+        up_rows = jnp.concatenate([lows[k][SHARE:, :], highs[k][:cut, :]], axis=0)
         gate = lax.dot_general(rows, gate_rows, NT, preferred_element_type=F32)
         up = lax.dot_general(rows, up_rows, NT, preferred_element_type=F32)
         act[:, k * SHARE : (k + 1) * SHARE] = (gate / (1.0 + jnp.exp(-gate)) * up).astype(BF)
-    down = jnp.dot(act[...], jnp.concatenate(downs, axis=0), preferred_element_type=F32)
+    down = jnp.concatenate([ref[cut:, :] for ref in highs], axis=0)
+    down = jnp.dot(act[...], down, preferred_element_type=F32)
     outs[0][...] = down[:HALF].astype(BF)
     outs[1][...] = down[HALF:].astype(BF)
 
 
-def feed_forward(pieces, weights, name):
+def feed_forward(pieces, lows, highs, name):
     vmem = pl.BlockSpec(memory_space=pltpu.VMEM)
     return pl.pallas_call(
         feed_kernel,
         out_shape=(jax.ShapeDtypeStruct((HALF, WIDTH), BF),) * 2,
-        in_specs=[vmem] * 12,
+        in_specs=[vmem] * 18,
         out_specs=(vmem,) * 2,
         scratch_shapes=[pltpu.VMEM((2 * HALF, 8 * SHARE), BF)],
         compiler_params=pltpu.CompilerParams(vmem_limit_bytes=VMEM_LIMIT),
         cost_estimate=cost(8),
         name=name,
-    )(*pieces, *weights)
+    )(*pieces, *lows, *highs)
 
 
 def start_kernel(resid_ref, extra_ref, lower_ref, upper_ref, out_ref):
@@ -674,17 +665,18 @@
     spread = jnp.broadcast_to(decode_hidden[None], (total, 2, WIDTH))
     every_row = lax.all_to_all(spread, "req", 0, 0).reshape(256, WIDTH)
 
-    query, kv = prefill_qkv(rank, prefill_hidden, gain, freq, w_qkv)
-    query, kv = in_hbm(query, kv)
+    low, high = pack_weights(jnp.swapaxes(w_gate_up, 1, 2), w_down)
+    (kv,) = in_hbm(project(rank, prefill_hidden, gain, freq, w_qkv, True))
     zed = send(kv, pair_z)
     core = send(kv, other_core)
-    gate_up, w_down, query = lax.optimization_barrier(
-        (jnp.swapaxes(w_gate_up, 1, 2), w_down, query)
-    )
-    packed = pack_weights(gate_up, w_down)
-    below = send(packed, next_z)
-    above = send(packed, last_z)
-    packed_core = send(packed, other_core)
+    low, high, kv = lax.optimization_barrier((low, high, kv))
+    below_low = send(low, next_z)
+    above_high = send(high, last_z)
+    below_high = send(high, next_z)
+    above_low = send(low, last_z)
+    low_core = send(low, other_core)
+    high_core = send(high, other_core)
+    (query,) = in_hbm(project(rank, prefill_hidden, gain, freq, w_qkv, False))
     outgoing = decode_attention(
         device,
         cache_len,
@@ -698,35 +690,39 @@
         key_value_cache,
         held_hidden,
     )
-    outgoing, zed, core, below, above, packed_core = lax.optimization_barrier(
-        (outgoing, zed, core, below, above, packed_core)
+    outgoing, zed, core, below_low, above_high, low_core, high_core = lax.optimization_barrier(
+        (outgoing, zed, core, below_low, above_high, low_core, high_core)
     )
     far = send(zed, other_core)
     core, zed, far = in_hbm(core, zed, far)
-    cut = 3 * SHARE // 2
-    far_low = send(below[:cut], next_z)
-    far_high = send(above[cut:], last_z)
-    below_core = send(below, other_core)
-    above_core = send(above, other_core)
+    far_low = send(below_low, next_z)
+    far_high = send(above_high, last_z)
+    below_low_core = send(below_low, other_core)
+    above_high_core = send(above_high, other_core)
     back = lax.all_to_all(outgoing.reshape(total, 2, WIDTH), "req", 0, 0).reshape(256, WIDTH)
 
     resid, lower, upper = attention(
         rank, query, kv, core, zed, far, w_out, prefill_hidden, gain2
     )
     (resid,) = in_hbm(resid)
-    lower, upper, back, far_low, far_high, below_core, above_core = lax.optimization_barrier(
-        (lower, upper, back, far_low, far_high, below_core, above_core)
+    lower, upper, back, below_high, above_low = lax.optimization_barrier(
+        (lower, upper, back, below_high, above_low)
     )
+    below_high_core = send(below_high, other_core)
+    above_low_core = send(above_low, other_core)
+    extra, lower, upper = decode_rows(back, w_out, decode_hidden, gain2, lower, upper)
+    lower, upper, far_low, far_high = lax.optimization_barrier((lower, upper, far_low, far_high))
     far_low_core = send(far_low, other_core)
     far_high_core = send(far_high, other_core)
-    extra, lower, upper = decode_rows(back, w_out, decode_hidden, gain2, lower, upper)
     from_last = send(lower, next_x)
     from_next = send(upper, last_x)
-    weights = (packed, packed_core, below, below_core, above, above_core)
-    weights += (far_low, far_low_core, far_high, far_high_core)
-    mine = feed_forward((lower, upper), weights, "feed_own")
+    lows = (low, low_core, below_low, below_low_core)
+    lows += (above_low, above_low_core, far_low, far_low_core)
+    highs = (high, high_core, below_high, below_high_core)
+    highs += (above_high, above_high_core, far_high, far_high_core)
+    mine = feed_forward((lower, upper), lows, highs, "feed_own")
     from_last, from_next, mine = lax.optimization_barrier((from_last, from_next, mine))
-    guest = feed_forward((from_last, from_next), weights, "feed_guest")
+    guest = feed_forward((from_last, from_next), lows, highs, "feed_guest")
     first = send(guest[0], last_x)
     second = send(guest[1], next_x)
     start = start_sum(resid, extra, mine)

time: 153 us -> 137 us (0.90)
  waiting for transfers between devices: 50.6 us -> 35.1 us
    ppermute x16 -> x21, waiting for transfers between devices: 47 us -> 15.2 us  [send(): return lax.ppermute(array, 'req', moves(step))]
    all_to_all x1, waiting for transfers between devices: 0.01 us -> 12.7 us  [body(): lax.all_to_all(outgoing.reshape(total, 2, WIDTH), 'req', 0, 0)]
    all_to_all x1, waiting for transfers between devices: 3.68 us -> 7.25 us  [body(): every_row = lax.all_to_all(spread, 'req', 0, 0).reshape(256, WIDTH)]
    slice x2 -> x0, local copies, waits for them, and re-layouts: 3.11 us -> none  [the longest x1 2.14 us: body(): far_low = send(below[:cut], next_z)]
    unnamed x24 -> x28, local copies, waits for them, and re-layouts: 0.9 us -> 3.29 us
    ppermute x16 -> x21, starting transfers between devices: 13.5 us -> 15.7 us  [send(): return lax.ppermute(array, 'req', moves(step))]
    all_to_all x1, starting transfers between devices: 9.72 us -> 7.93 us  [body(): lax.all_to_all(outgoing.reshape(total, 2, WIDTH), 'req', 0, 0)]
    pallas_call x2, Pallas kernels: 17.5 us -> 15.7 us  [feed_forward(): pl.pallas_call(feed_kernel, out_shape=(jax.ShapeDtypeStruct((HALF, WIDTH)...]
  transfers between devices with their start and end apart: 18 -> 23, of which waited for: 6 -> 7; matrix products, arithmetic and copies ran while one was open for 4% -> 3% of each run, Pallas kernels for 31% -> 35%
where the time goes in v4:
time: 137 us
  Pallas kernels  56.1 us (41%)
  waiting for transfers between devices  35.1 us (26%)
  starting transfers between devices  34.8 us (25%)
  local copies, waits for them, and re-layouts  9.31 us (7%)
  between operations  1.54 us (1%)
    pallas_call x2, Pallas kernels, feed_forward(): pl.pallas_call(feed_kernel, out_shape=(jax.ShapeDtypeStruct((HALF, WIDTH)...  15.7 us
    ppermute x21, starting transfers between devices, send(): return lax.ppermute(array, 'req', moves(step))  15.7 us
    pallas_call x1, Pallas kernels, decode_attention(): pl.pallas_call(decode_kernel, out_shape=jax.ShapeDtypeStruct((256, QW), B...  15.3 us
    ppermute x21, waiting for transfers between devices, send(): return lax.ppermute(array, 'req', moves(step))  15.2 us
    all_to_all x1, waiting for transfers between devices, body(): lax.all_to_all(outgoing.reshape(total, 2, WIDTH), 'req', 0, 0)  12.7 us
    pallas_call x1, Pallas kernels, attention(): pl.pallas_call(attention_kernel, out_shape=(jax.ShapeDtypeStruct((ROWS, W...  12.4 us
    all_to_all x1, starting transfers between devices, body(): every_row = lax.all_to_all(spread, 'req', 0, 0).reshape(256, WIDTH)  11.1 us
    all_to_all x1, starting transfers between devices, body(): lax.all_to_all(outgoing.reshape(total, 2, WIDTH), 'req', 0, 0)  7.93 us
  transfers between devices with their start and end apart: 23, of which 7 were waited for; matrix products, arithmetic and copies ran while one was open for 3% of the time, Pallas kernels for 35%

profile of v4, /device:TPU:0, one launch (start us, length us, event | category | flops | bytes accessed | tf_op | source)
XLA Modules:
  0.0 136.8 jit_solution(6155055467048743015)
XLA Ops:
  0.6 1.9 %broadcast_in_dim.2 = bf16[128,2,1280]{2,1,0:T(2,128)(2,1)} broadcast(bf16[2,1280]{1,0:T(2,128)(2,1)} %decode_ref.1), dimensions={1,2} | broadcast | bytes 660480 | tf_op jit(solution)/shard_map/broadcast_in_dim | solution.py:665
  2.5 11.1 %all-to-all-start = ((bf16[128,2,1280]{2,1,0:T(2,128)(2,1)}), bf16[128,2,1280]{2,1,0:T(2,128)(2,1)S(1)}, u32[]{:S(2)}, u32[]{:S(2)}) async-start(bf16[128,2,1280]{2,1,0:T(2,128)(2,1)} %broadcast_in_dim.2), calls=%async_computation | async-start | bytes 1310720 | tf_op jit(solution)/shard_map/all_to_all | solution.py:666
  13.7 0.7 reshape.32.gain_ref
  14.4 0.7 copy-done.9
  15.0 2.7 %prefill_kv.1.own_ref = bf16[256,640]{1,0:T(8,128)(2,1)S(1)} custom-call(s32[1]{0:T(128)S(6)} %select_n.7.rank_ref, bf16[256,1280]{1,0:T(8,128)(2,1)} %hidden_ref.7, f32[1,1280]{1,0:T(1,128)S(1)} %reshape.32.gain_ref, f32[1,128]{1,0:T(1,128)S(1)} %copy-done.9, bf16[1280,1920]{1,0:T(8,128)(2,1)} %w_ref.7), custom_call_target="tpu_custom_call" | custom-call | flops 3000000000 | bytes 9000000 | tf_op jit(solution)/shard_map/prefill_kv/pallas_call | solution.py:197
  17.8 0.0 copy-start.13
  17.8 0.1 collective-permute-start.1
  17.9 1.2 collective-permute-start
  19.1 0.0 copy-start.8
  19.1 0.0 copy-start.10
  19.1 0.5 pack.1
  19.6 0.1 collective-permute-start.4
  19.8 1.0 collective-permute-start.2
  20.8 0.1 collective-permute-start.5
  21.5 7.2 %all-to-all-done = bf16[128,2,1280]{2,1,0:T(2,128)(2,1)S(1)} async-done(((bf16[128,2,1280]{2,1,0:T(2,128)(2,1)}), bf16[128,2,1280]{2,1,0:T(2,128)(2,1)S(1)}, u32[]{:S(2)}, u32[]{:S(2)}) %all-to-all-start) | async-done | bytes 655392 | tf_op jit(solution)/shard_map/all_to_all | solution.py:666
  28.8 0.2 reshape.35.rows_ref
  29.0 0.0 collective-permute-done.1.core_ref
  29.0 0.2 collective-permute-start.3
  29.2 15.3 %decode.1 = bf16[256,1280]{1,0:T(8,128)(2,1)S(1)} custom-call(s32[1]{0:T(128)} %bitcast.device_ref, s32[4]{0:T(128)S(1)} %copy-done.8, s32[1]{0:T(128)S(6)} %copy.21.count_ref, s32[1,256]{1,0:T(1,128)S(1)} %bitcast.6, s32[8,128]{1,0:T(8,128)S(1)} %bitcast.5, bf16[256,1280]{1,0:T(8,128)(2,1)S(1)} %reshape.35.rows_ref, f32[1,1280]{1,0:T(1,128)S(1)} %reshape.32.gain_ref, ...), custom_call_target="tpu_custom_call" | custom-call | flops 16999999488 | bytes 51000000 | tf_op jit(solution)/shard_map/decode/pallas_call | solution.py:367
  44.5 0.0 collective-permute-done.zed_ref
  44.5 0.7 collective-permute-start.8
  45.2 0.0 collective-permute-done.4.refs_3_
  45.2 1.4 %collective-permute-start.7 = (bf16[336,1280]{1,0:T(8,128)(2,1)S(1)}, bf16[336,1280]{1,0:T(8,128)(2,1)}, u32[]{:S(2)}, u32[]{:S(2)}) collective-permute-start(bf16[336,1280]{1,0:T(8,128)(2,1)S(1)} %get-tuple-element.41.refs_10_), channel_id=1, source_target_pairs={{0,2},{1,3},{2,4},{3,5},{4,6},{5,7},{6,0},{7,1},{8,10},{9,11},{10,... | collective-permute-start | bytes 2580488 | tf_op jit(solution)/shard_map/ppermute | solution.py:54
  46.6 1.2 collective-permute-done.2.refs_4_
  47.8 0.0 collective-permute-done.5.refs_11_
  47.8 3.3 %collective-permute-done.3.refs_14_ = bf16[336,1280]{1,0:T(8,128)(2,1)S(1)} collective-permute-done((bf16[336,1280]{1,0:T(8,128)(2,1)S(1)}, bf16[336,1280]{1,0:T(8,128)(2,1)S(1)}, u32[]{:S(2)}, u32[]{:S(2)}) %collective-permute-start.3) | collective-permute-done | bytes 860192 | tf_op jit(solution)/shard_map/ppermute | solution.py:54
  51.2 0.9 copy-done.2
  52.1 0.0 collective-permute-start.6
  52.1 3.9 %prefill_query.1.query_ref = bf16[256,1280]{1,0:T(8,128)(2,1)S(1)} custom-call(s32[1]{0:T(128)S(6)} %select_n.7.rank_ref, bf16[256,1280]{1,0:T(8,128)(2,1)} %hidden_ref.7, f32[1,1280]{1,0:T(1,128)S(1)} %reshape.32.gain_ref, f32[1,128]{1,0:T(1,128)S(1)} %copy-done.10, bf16[1280,1920]{1,0:T(8,128)(2,1)} %w_ref.7), custom_call_target="tpu_custom_call" | custom-call | flops 5000000000 | bytes 15000000 | tf_op jit(solution)/shard_map/prefill_query/pallas_call | solution.py:197
  56.0 0.0 copy-start.12
  56.0 0.8 copy-done.12
  56.8 0.5 collective-permute-start.13
  57.3 0.0 collective-permute-start.9
  57.3 1.1 reshape.37
  58.5 7.9 %all-to-all-start.1 = ((bf16[128,2,1280]{2,1,0:T(2,128)(2,1)}), bf16[128,2,1280]{2,1,0:T(2,128)(2,1)}, u32[]{:S(2)}, u32[]{:S(2)}) async-start(bf16[128,2,1280]{2,1,0:T(2,128)(2,1)} %reshape.37), calls=%async_computation.1 | async-start | bytes 1310720 | tf_op jit(solution)/shard_map/all_to_all | solution.py:702
  66.4 0.0 copy-start
  66.4 0.0 collective-permute-done.6.far_ref
  66.4 3.0 %collective-permute-start.10 = (bf16[336,1280]{1,0:T(8,128)(2,1)S(1)}, bf16[336,1280]{1,0:T(8,128)(2,1)}, u32[]{:S(2)}, u32[]{:S(2)}) collective-permute-start(bf16[336,1280]{1,0:T(8,128)(2,1)S(1)} %copy-done.3), channel_id=1, source_target_pairs={{0,6},{1,7},{2,0},{3,1},{4,2},{5,3},{6,4},{7,5},{8,14},{9,15},{10,... | collective-permute-start | bytes 2580488 | tf_op jit(solution)/shard_map/ppermute | solution.py:54
  69.4 12.4 %attention.1 = (bf16[256,1280]{1,0:T(8,128)(2,1)S(1)}, bf16[144,1280]{1,0:T(8,128)(2,1)}, bf16[144,1280]{1,0:T(8,128)(2,1)}) custom-call(s32[1]{0:T(128)S(6)} %select_n.7.rank_ref, bf16[256,1280]{1,0:T(8,128)(2,1)} %copy-done.12, bf16[256,640]{1,0:T(8,128)(2,1)} %copy-done.5, bf16[256,640]{1,0:T(8,128)(2,1)} %collective-permute-done.1.core_ref, ...), custom_call_target="tpu_custom_call" | custom-call | flops 12000000000 | bytes 36000000 | tf_op jit(solution)/shard_map/attention/pallas_call | solution.py:480
  81.8 0.8 copy-done.11
  82.7 12.7 %all-to-all-done.1 = bf16[128,2,1280]{2,1,0:T(2,128)(2,1)} async-done(((bf16[128,2,1280]{2,1,0:T(2,128)(2,1)}), bf16[128,2,1280]{2,1,0:T(2,128)(2,1)}, u32[]{:S(2)}, u32[]{:S(2)}) %all-to-all-start.1) | async-done | bytes 655392 | tf_op jit(solution)/shard_map/all_to_all | solution.py:702
  95.3 2.1 %reshape.38.back_ref = bf16[256,1280]{1,0:T(8,128)(2,1)S(1)} reshape(bf16[128,2,1280]{2,1,0:T(2,128)(2,1)} %all-to-all-done.1) | data formatting | bytes 1310720 | tf_op jit(solution)/shard_map/reshape | solution.py:702
  97.4 0.0 collective-permute-done.8.refs_6_
  97.4 0.2 collective-permute-start.17
  97.6 0.0 collective-permute-done.7.refs_12_
  97.6 0.4 collective-permute-start.14
  98.0 3.4 %decode_rows.1 = (bf16[32,1280]{1,0:T(8,128)(2,1)S(1)}, bf16[144,1280]{1,0:T(8,128)(2,1)}, bf16[144,1280]{1,0:T(8,128)(2,1)}) custom-call(bf16[256,1280]{1,0:T(8,128)(2,1)S(1)} %reshape.38.back_ref, bf16[1280,1280]{1,0:T(8,128)(2,1)} %w_ref.9, bf16[2,1280]{1,0:T(2,128)(2,1)S(1)} %copy-done, ...), custom_call_target="tpu_custom_call", output_to_operand_aliasing={{1}: (4, {}), {2}: (5, {})} | custom-call | flops 3000000000 | bytes 9000000 | tf_op jit(solution)/shard_map/decode_rows/pallas_call | solution.py:535
  101.4 0.0 collective-permute-done.9.refs_8_
  101.4 0.1 collective-permute-start.16
  101.6 0.4 collective-permute-start.15
  101.9 0.0 collective-permute-done.13.refs_5_
  102.0 0.1 collective-permute-start.18
  102.1 0.8 collective-permute-start.11
  102.9 2.5 %collective-permute-start.12 = (bf16[144,1280]{1,0:T(8,128)(2,1)}, bf16[144,1280]{1,0:T(8,128)(2,1)S(1)}, u32[]{:S(2)}, u32[]{:S(2)}) collective-permute-start(bf16[144,1280]{1,0:T(8,128)(2,1)} %get-tuple-element.57.refs_1_), channel_id=1, source_target_pairs={{0,24},{1,25},{2,26},{3,27},{4,28},{5,29},{6,30},{7,31},{8,0},{9,1... | collective-permute-start | bytes 1105928 | tf_op jit(solution)/shard_map/ppermute | solution.py:54
  105.4 1.1 collective-permute-done.18.refs_17_
  106.5 8.0 %feed_own.1 = (bf16[144,1280]{1,0:T(8,128)(2,1)S(1)}, bf16[144,1280]{1,0:T(8,128)(2,1)S(1)}) custom-call(bf16[144,1280]{1,0:T(8,128)(2,1)} %get-tuple-element.56.refs_0_, bf16[144,1280]{1,0:T(8,128)(2,1)} %get-tuple-element.57.refs_1_, bf16[336,1280]{1,0:T(8,128)(2,1)S(1)} %get-tuple-element.40.refs_2_, bf16[336,1280]{1,0:T(8,128)(2,1)} %collective-permute-done.4.refs_3_, ...), custom_call_target="tpu_custom_call" | custom-call | flops 8000000000 | bytes 24000000 | tf_op jit(solution)/shard_map/feed_own/pallas_call | solution.py:577
  114.5 0.0 collective-permute-done.12.refs_1_
  114.5 7.8 %feed_guest.1 = (bf16[144,1280]{1,0:T(8,128)(2,1)S(1)}, bf16[144,1280]{1,0:T(8,128)(2,1)S(1)}) custom-call(bf16[144,1280]{1,0:T(8,128)(2,1)S(1)} %collective-permute-done.11.refs_0_, bf16[144,1280]{1,0:T(8,128)(2,1)S(1)} %collective-permute-done.12.refs_1_, bf16[336,1280]{1,0:T(8,128)(2,1)S(1)} %get-tuple-element.40.refs_2_, ...), custom_call_target="tpu_custom_call" | custom-call | flops 8000000000 | bytes 24000000 | tf_op jit(solution)/shard_map/feed_guest/pallas_call | solution.py:577
  122.3 2.9 %collective-permute-start.19 = (bf16[144,1280]{1,0:T(8,128)(2,1)S(1)}, bf16[144,1280]{1,0:T(8,128)(2,1)S(1)}, u32[]{:S(2)}, u32[]{:S(2)}) collective-permute-start(bf16[144,1280]{1,0:T(8,128)(2,1)S(1)} %get-tuple-element.70), channel_id=1, source_target_pairs={{0,24},{1,25},{2,26},{3,27},{4,28},{5,29},{6,30},{7,31},{8,0},{9,1... | collective-permute-start | bytes 1105928 | tf_op jit(solution)/shard_map/ppermute | solution.py:54
  125.2 0.0 collective-permute-start.20
  125.2 1.2 start_sum.1.start_ref
  126.4 6.5 %collective-permute-done.19.first_ref = bf16[144,1280]{1,0:T(8,128)(2,1)S(1)} collective-permute-done((bf16[144,1280]{1,0:T(8,128)(2,1)S(1)}, bf16[144,1280]{1,0:T(8,128)(2,1)S(1)}, u32[]{:S(2)}, u32[]{:S(2)}) %collective-permute-start.19) | collective-permute-done | bytes 368672 | tf_op jit(solution)/shard_map/ppermute | solution.py:54
  133.0 2.9 %collective-permute-done.20.second_ref = bf16[144,1280]{1,0:T(8,128)(2,1)S(1)} collective-permute-done((bf16[144,1280]{1,0:T(8,128)(2,1)S(1)}, bf16[144,1280]{1,0:T(8,128)(2,1)S(1)}, u32[]{:S(2)}, u32[]{:S(2)}) %collective-permute-start.20) | collective-permute-done | bytes 368672 | tf_op jit(solution)/shard_map/ppermute | solution.py:54
  135.9 1.0 final.1
  (26 shorter events, 0.1 us)
Async XLA Ops:
  2.5 26.3 %all-to-all-start = ((bf16[128,2,1280]{2,1,0:T(2,128)(2,1)}), bf16[128,2,1280]{2,1,0:T(2,128)(2,1)S(1)}, u32[]{:S(2)}, u32[]{:S(2)}) async-start(bf16[128,2,1280]{2,1,0:T(2,128)(2,1)} %broadcast_in_dim.2), calls=%async_computation | async-start | bytes 1310720 | tf_op jit(solution)/shard_map/all_to_all | solution.py:666
  14.4 0.7 copy-start.9
  15.0 4.1 %copy-start.1 = (bf16[1,1280,448]{1,2,0:T(8,128)(2,1)S(1)}, bf16[1,1280,448]{1,2,0:T(8,128)(2,1)}, u32[]{:S(2)}) copy-start(bf16[1,1280,448]{1,2,0:T(8,128)(2,1)} %param.21) | copy-start | bytes 3440644
  15.0 4.1 %copy-start.4 = (bf16[1,224,1280]{2,1,0:T(8,128)(2,1)S(1)}, bf16[1,224,1280]{2,1,0:T(8,128)(2,1)}, u32[]{:S(2)}) copy-start(bf16[1,224,1280]{2,1,0:T(8,128)(2,1)} %down_ref.1) | copy-start | bytes 1720324
  17.8 11.3 %copy-start.5 = (bf16[256,640]{1,0:T(8,128)(2,1)}, bf16[256,640]{1,0:T(8,128)(2,1)S(1)}, u32[]{:S(2)}) copy-start(bf16[256,640]{1,0:T(8,128)(2,1)S(1)} %prefill_kv.1.own_ref) | copy-start | bytes 983044
  17.8 3.7 %copy-start.13 = (f32[1280]{0:T(1024)S(1)}, f32[1280]{0:T(1024)}, u32[]{:S(2)}) copy-start(f32[1280]{0:T(1024)} %param.20) | copy-start | bytes 15364
  17.8 11.3 %collective-permute-start.1 = (bf16[256,640]{1,0:T(8,128)(2,1)S(1)}, bf16[256,640]{1,0:T(8,128)(2,1)}, u32[]{:S(2)}, u32[]{:S(2)}) collective-permute-start(bf16[256,640]{1,0:T(8,128)(2,1)S(1)} %prefill_kv.1.own_ref), channel_id=1, source_target_pairs={{0,1},{1,0},{2,3},{3,2},{4,5},{5,4},{6,7},{7,6},{8,9},{9,8},{10,11... | collective-permute-start | bytes 983048 | tf_op jit(solution)/shard_map/ppermute | solution.py:54
  17.9 26.6 %collective-permute-start = (bf16[256,640]{1,0:T(8,128)(2,1)S(1)}, bf16[256,640]{1,0:T(8,128)(2,1)}, u32[]{:S(2)}, u32[]{:S(2)}) collective-permute-start(bf16[256,640]{1,0:T(8,128)(2,1)S(1)} %prefill_kv.1.own_ref), channel_id=1, source_target_pairs={{0,2},{1,3},{2,0},{3,1},{4,6},{5,7},{6,4},{7,5},{8,10},{9,11},{10,... | collective-permute-start | bytes 983048 | tf_op jit(solution)/shard_map/ppermute | solution.py:54
  19.1 10.1 %copy-start.6 = (s32[1024]{0:T(1024)S(1)}, s32[1024]{0:T(1024)}, u32[]{:S(2)}) copy-start(s32[1024]{0:T(1024)} %param.27) | copy-start | bytes 12292
  19.1 10.1 %copy-start.7 = (s32[256]{0:T(256)S(1)}, s32[256]{0:T(256)}, u32[]{:S(2)}) copy-start(s32[256]{0:T(256)} %param.25) | copy-start | bytes 3076
  19.1 10.1 %copy-start.8 = (s32[4]{0:T(128)S(1)}, s32[4]{0:T(128)}, u32[]{:S(2)}) copy-start(s32[4]{0:T(128)} %length_ref.1) | copy-start | bytes 52
  19.1 10.1 %copy-start.10 = (f32[1,128]{1,0:T(1,128)S(1)}, f32[1,128]{1,0:T(1,128)}, u32[]{:S(2)}) copy-start(f32[1,128]{1,0:T(1,128)} %constant.25.clone.freq_ref) | copy-start | bytes 1540
  19.6 25.6 %collective-permute-start.4 = (bf16[336,1280]{1,0:T(8,128)(2,1)S(1)}, bf16[336,1280]{1,0:T(8,128)(2,1)}, u32[]{:S(2)}, u32[]{:S(2)}) collective-permute-start(bf16[336,1280]{1,0:T(8,128)(2,1)S(1)} %get-tuple-element.40.refs_2_), channel_id=1, source_target_pairs={{0,1},{1,0},{2,3},{3,2},{4,5},{5,4},{6,7},{7,6},{8,9},{9,8},{10,11... | collective-permute-start | bytes 2580488 | tf_op jit(solution)/shard_map/ppermute | solution.py:54
  19.8 28.0 %collective-permute-start.2 = (bf16[336,1280]{1,0:T(8,128)(2,1)S(1)}, bf16[336,1280]{1,0:T(8,128)(2,1)}, u32[]{:S(2)}, u32[]{:S(2)}) collective-permute-start(bf16[336,1280]{1,0:T(8,128)(2,1)S(1)} %get-tuple-element.40.refs_2_), channel_id=1, source_target_pairs={{0,2},{1,3},{2,4},{3,5},{4,6},{5,7},{6,0},{7,1},{8,10},{9,11},{10,... | collective-permute-start | bytes 2580488 | tf_op jit(solution)/shard_map/ppermute | solution.py:54
  20.8 27.1 %collective-permute-start.5 = (bf16[336,1280]{1,0:T(8,128)(2,1)S(1)}, bf16[336,1280]{1,0:T(8,128)(2,1)}, u32[]{:S(2)}, u32[]{:S(2)}) collective-permute-start(bf16[336,1280]{1,0:T(8,128)(2,1)S(1)} %get-tuple-element.41.refs_10_), channel_id=1, source_target_pairs={{0,1},{1,0},{2,3},{3,2},{4,5},{5,4},{6,7},{7,6},{8,9},{9,8},{10,11... | collective-permute-start | bytes 2580488 | tf_op jit(solution)/shard_map/ppermute | solution.py:54
  29.0 22.1 %collective-permute-start.3 = (bf16[336,1280]{1,0:T(8,128)(2,1)S(1)}, bf16[336,1280]{1,0:T(8,128)(2,1)S(1)}, u32[]{:S(2)}, u32[]{:S(2)}) collective-permute-start(bf16[336,1280]{1,0:T(8,128)(2,1)S(1)} %get-tuple-element.41.refs_10_), channel_id=1, source_target_pairs={{0,6},{1,7},{2,0},{3,1},{4,2},{5,3},{6,4},{7,5},{8,14},{9,15},{10,... | collective-permute-start | bytes 2580488 | tf_op jit(solution)/shard_map/ppermute | solution.py:54
  44.5 52.9 %collective-permute-start.8 = (bf16[336,1280]{1,0:T(8,128)(2,1)S(1)}, bf16[336,1280]{1,0:T(8,128)(2,1)}, u32[]{:S(2)}, u32[]{:S(2)}) collective-permute-start(bf16[336,1280]{1,0:T(8,128)(2,1)S(1)} %get-tuple-element.40.refs_2_), channel_id=1, source_target_pairs={{0,6},{1,7},{2,0},{3,1},{4,2},{5,3},{6,4},{7,5},{8,14},{9,15},{10,... | collective-permute-start | bytes 2580488 | tf_op jit(solution)/shard_map/ppermute | solution.py:54
  45.2 52.4 %collective-permute-start.7 = (bf16[336,1280]{1,0:T(8,128)(2,1)S(1)}, bf16[336,1280]{1,0:T(8,128)(2,1)}, u32[]{:S(2)}, u32[]{:S(2)}) collective-permute-start(bf16[336,1280]{1,0:T(8,128)(2,1)S(1)} %get-tuple-element.41.refs_10_), channel_id=1, source_target_pairs={{0,2},{1,3},{2,4},{3,5},{4,6},{5,7},{6,0},{7,1},{8,10},{9,11},{10,... | collective-permute-start | bytes 2580488 | tf_op jit(solution)/shard_map/ppermute | solution.py:54
  51.2 0.9 copy-start.2
  52.1 14.3 %collective-permute-start.6 = (bf16[256,640]{1,0:T(8,128)(2,1)}, bf16[256,640]{1,0:T(8,128)(2,1)}, u32[]{:S(2)}, u32[]{:S(2)}) collective-permute-start(bf16[256,640]{1,0:T(8,128)(2,1)} %collective-permute-done.zed_ref), channel_id=1, source_target_pairs={{0,1},{1,0},{2,3},{3,2},{4,5},{5,4},{6,7},{7,6},{8,9},{9,8},{10,11... | collective-permute-start | bytes 983048 | tf_op jit(solution)/shard_map/ppermute | solution.py:54
  52.1 14.3 %copy-start.3 = (bf16[336,1280]{1,0:T(8,128)(2,1)S(1)}, bf16[336,1280]{1,0:T(8,128)(2,1)}, u32[]{:S(2)}) copy-start(bf16[336,1280]{1,0:T(8,128)(2,1)} %copy-done.2) | copy-start | bytes 2580484
  56.0 0.8 copy-start.12
  56.8 45.1 %collective-permute-start.13 = (bf16[336,1280]{1,0:T(8,128)(2,1)}, bf16[336,1280]{1,0:T(8,128)(2,1)}, u32[]{:S(2)}, u32[]{:S(2)}) collective-permute-start(bf16[336,1280]{1,0:T(8,128)(2,1)} %collective-permute-done.2.refs_4_), channel_id=1, source_target_pairs={{0,1},{1,0},{2,3},{3,2},{4,5},{5,4},{6,7},{7,6},{8,9},{9,8},{10,11... | collective-permute-start | bytes 2580488 | tf_op jit(solution)/shard_map/ppermute | solution.py:54
  57.3 44.1 %collective-permute-start.9 = (bf16[336,1280]{1,0:T(8,128)(2,1)}, bf16[336,1280]{1,0:T(8,128)(2,1)}, u32[]{:S(2)}, u32[]{:S(2)}) collective-permute-start(bf16[336,1280]{1,0:T(8,128)(2,1)} %collective-permute-done.2.refs_4_), channel_id=1, source_target_pairs={{0,2},{1,3},{2,4},{3,5},{4,6},{5,7},{6,0},{7,1},{8,10},{9,11},{10,... | collective-permute-start | bytes 2580488 | tf_op jit(solution)/shard_map/ppermute | solution.py:54
  58.5 36.9 %all-to-all-start.1 = ((bf16[128,2,1280]{2,1,0:T(2,128)(2,1)}), bf16[128,2,1280]{2,1,0:T(2,128)(2,1)}, u32[]{:S(2)}, u32[]{:S(2)}) async-start(bf16[128,2,1280]{2,1,0:T(2,128)(2,1)} %reshape.37), calls=%async_computation.1 | async-start | bytes 1310720 | tf_op jit(solution)/shard_map/all_to_all | solution.py:702
  66.4 31.6 %copy-start = (bf16[2,1280]{1,0:T(2,128)(2,1)S(1)}, bf16[2,1280]{1,0:T(2,128)(2,1)}, u32[]{:S(2)}) copy-start(bf16[2,1280]{1,0:T(2,128)(2,1)} %decode_ref.1) | copy-start | bytes 15364
  66.4 35.1 %collective-permute-start.10 = (bf16[336,1280]{1,0:T(8,128)(2,1)S(1)}, bf16[336,1280]{1,0:T(8,128)(2,1)}, u32[]{:S(2)}, u32[]{:S(2)}) collective-permute-start(bf16[336,1280]{1,0:T(8,128)(2,1)S(1)} %copy-done.3), channel_id=1, source_target_pairs={{0,6},{1,7},{2,0},{3,1},{4,2},{5,3},{6,4},{7,5},{8,14},{9,15},{10,... | collective-permute-start | bytes 2580488 | tf_op jit(solution)/shard_map/ppermute | solution.py:54
  81.8 0.8 copy-start.11
  97.4 4.7 %collective-permute-start.17 = (bf16[336,1280]{1,0:T(8,128)(2,1)S(1)}, bf16[336,1280]{1,0:T(8,128)(2,1)S(1)}, u32[]{:S(2)}, u32[]{:S(2)}) collective-permute-start(bf16[336,1280]{1,0:T(8,128)(2,1)S(1)} %copy-done.3), channel_id=1, source_target_pairs={{0,1},{1,0},{2,3},{3,2},{4,5},{5,4},{6,7},{7,6},{8,9},{9,8},{10,11... | collective-permute-start | bytes 2580488 | tf_op jit(solution)/shard_map/ppermute | solution.py:54
  97.6 5.2 %collective-permute-start.14 = (bf16[336,1280]{1,0:T(8,128)(2,1)}, bf16[336,1280]{1,0:T(8,128)(2,1)S(1)}, u32[]{:S(2)}, u32[]{:S(2)}) collective-permute-start(bf16[336,1280]{1,0:T(8,128)(2,1)} %collective-permute-done.8.refs_6_), channel_id=1, source_target_pairs={{0,1},{1,0},{2,3},{3,2},{4,5},{5,4},{6,7},{7,6},{8,9},{9,8},{10,11... | collective-permute-start | bytes 2580488 | tf_op jit(solution)/shard_map/ppermute | solution.py:54
  101.4 3.9 %collective-permute-start.16 = (bf16[336,1280]{1,0:T(8,128)(2,1)}, bf16[336,1280]{1,0:T(8,128)(2,1)S(1)}, u32[]{:S(2)}, u32[]{:S(2)}) collective-permute-start(bf16[336,1280]{1,0:T(8,128)(2,1)} %collective-permute-done.7.refs_12_), channel_id=1, source_target_pairs={{0,1},{1,0},{2,3},{3,2},{4,5},{5,4},{6,7},{7,6},{8,9},{9,8},{10,11... | collective-permute-start | bytes 2580488 | tf_op jit(solution)/shard_map/ppermute | solution.py:54
  101.6 3.8 %collective-permute-start.15 = (bf16[336,1280]{1,0:T(8,128)(2,1)}, bf16[336,1280]{1,0:T(8,128)(2,1)S(1)}, u32[]{:S(2)}, u32[]{:S(2)}) collective-permute-start(bf16[336,1280]{1,0:T(8,128)(2,1)} %collective-permute-done.9.refs_8_), channel_id=1, source_target_pairs={{0,1},{1,0},{2,3},{3,2},{4,5},{5,4},{6,7},{7,6},{8,9},{9,8},{10,11... | collective-permute-start | bytes 2580488 | tf_op jit(solution)/shard_map/ppermute | solution.py:54
  102.0 4.5 %collective-permute-start.18 = (bf16[336,1280]{1,0:T(8,128)(2,1)}, bf16[336,1280]{1,0:T(8,128)(2,1)S(1)}, u32[]{:S(2)}, u32[]{:S(2)}) collective-permute-start(bf16[336,1280]{1,0:T(8,128)(2,1)} %collective-permute-done.10.refs_16_), channel_id=1, source_target_pairs={{0,1},{1,0},{2,3},{3,2},{4,5},{5,4},{6,7},{7,6},{8,9},{9,8},{10,11... | collective-permute-start | bytes 2580488 | tf_op jit(solution)/shard_map/ppermute | solution.py:54
  102.1 12.4 %collective-permute-start.11 = (bf16[144,1280]{1,0:T(8,128)(2,1)}, bf16[144,1280]{1,0:T(8,128)(2,1)S(1)}, u32[]{:S(2)}, u32[]{:S(2)}) collective-permute-start(bf16[144,1280]{1,0:T(8,128)(2,1)} %get-tuple-element.56.refs_0_), channel_id=1, source_target_pairs={{0,8},{1,9},{2,10},{3,11},{4,12},{5,13},{6,14},{7,15},{8,16},{9,17... | collective-permute-start | bytes 1105928 | tf_op jit(solution)/shard_map/ppermute | solution.py:54
  102.9 11.6 %collective-permute-start.12 = (bf16[144,1280]{1,0:T(8,128)(2,1)}, bf16[144,1280]{1,0:T(8,128)(2,1)S(1)}, u32[]{:S(2)}, u32[]{:S(2)}) collective-permute-start(bf16[144,1280]{1,0:T(8,128)(2,1)} %get-tuple-element.57.refs_1_), channel_id=1, source_target_pairs={{0,24},{1,25},{2,26},{3,27},{4,28},{5,29},{6,30},{7,31},{8,0},{9,1... | collective-permute-start | bytes 1105928 | tf_op jit(solution)/shard_map/ppermute | solution.py:54
  122.3 10.7 %collective-permute-start.19 = (bf16[144,1280]{1,0:T(8,128)(2,1)S(1)}, bf16[144,1280]{1,0:T(8,128)(2,1)S(1)}, u32[]{:S(2)}, u32[]{:S(2)}) collective-permute-start(bf16[144,1280]{1,0:T(8,128)(2,1)S(1)} %get-tuple-element.70), channel_id=1, source_target_pairs={{0,24},{1,25},{2,26},{3,27},{4,28},{5,29},{6,30},{7,31},{8,0},{9,1... | collective-permute-start | bytes 1105928 | tf_op jit(solution)/shard_map/ppermute | solution.py:54
  125.2 10.7 %collective-permute-start.20 = (bf16[144,1280]{1,0:T(8,128)(2,1)S(1)}, bf16[144,1280]{1,0:T(8,128)(2,1)S(1)}, u32[]{:S(2)}, u32[]{:S(2)}) collective-permute-start(bf16[144,1280]{1,0:T(8,128)(2,1)S(1)} %get-tuple-element.71), channel_id=1, source_target_pairs={{0,8},{1,9},{2,10},{3,11},{4,12},{5,13},{6,14},{7,15},{8,16},{9,17... | collective-permute-start | bytes 1105928 | tf_op jit(solution)/shard_map/ppermute | solution.py:54

commit v5 on v4

--- a/solution.py
+++ b/solution.py
@@ -20,7 +20,6 @@
 SLOTS = 4
 POSITIONS = 1024
 ROWS = 256
-HALF = 144
 EPS = 1e-05
 THETA = 10000.0
 NEG = -1e30
@@ -85,7 +84,7 @@
 def norm_rows(rows, gain):
     rows = rows.astype(F32)
     mean = jnp.mean(rows * rows, axis=-1, keepdims=True)
-    return (rows * lax.rsqrt(mean + EPS) * gain).astype(BF)
+    return (rows * lax.rsqrt(mean + EPS) * gain.reshape(1, WIDTH)).astype(BF)
 
 
 def lanes(shape):
@@ -116,7 +115,9 @@
     return out_sine, out_cosine
 
 
-def rope_tables(position, frequency):
+def rope_tables(position):
+    pair = (lanes((1, position.shape[1])) % (HEAD // 2)).astype(F32)
+    frequency = jnp.exp(pair * (-2.0 * np.log(THETA) / HEAD))
     sine, cosine = sine_cosine(position * frequency)
     low = lanes(sine.shape) % HEAD < HEAD // 2
     return cosine, jnp.where(low, -sine, sine)
@@ -152,10 +153,10 @@
     )(gate_up, down)
 
 
-def kv_kernel(rank_ref, hidden_ref, gain_ref, freq_ref, w_ref, kv_ref):
+def kv_kernel(rank_ref, hidden_ref, gain_ref, w_ref, kv_ref):
     normed = norm_rows(hidden_ref[...], gain_ref[...])
     position = (sublanes((ROWS, 128)) * 4 + rank_ref[0]).astype(F32)
-    cosine, sine = rope_tables(position, freq_ref[...])
+    cosine, sine = rope_tables(position)
     projected = jnp.dot(normed, w_ref[...], preferred_element_type=F32)
     chunks = [projected[:, i * 128 : (i + 1) * 128] for i in range(5)]
     low = lanes((ROWS, 128)) < HEAD
@@ -174,12 +175,12 @@
         kv_ref[:, i * 128 : (i + 1) * 128] = out[i].astype(BF)
 
 
-def query_kernel(rank_ref, hidden_ref, gain_ref, freq_ref, w_ref, query_ref, normed, cos, sin):
+def query_kernel(rank_ref, hidden_ref, gain_ref, w_ref, query_ref, normed, cos, sin):
     @pl.when(pl.program_id(0) == 0)
     def _():
         normed[...] = norm_rows(hidden_ref[...], gain_ref[...])
         position = (sublanes((ROWS, 128)) * 4 + rank_ref[0]).astype(F32)
-        cos[...], sin[...] = rope_tables(position, freq_ref[...])
+        cos[...], sin[...] = rope_tables(position)
 
     projected = jnp.dot(normed[...], w_ref[...], preferred_element_type=F32)
     for i in range(5):
@@ -187,7 +188,7 @@
         query_ref[:, i * 128 : (i + 1) * 128] = roped * jnp.asarray(0.125, BF)
 
 
-def project(rank, hidden, gain, freq, w_qkv, keys):
+def project(rank, hidden, gain, w_qkv, keys):
     steps = 1 if keys else 2
     scratch = [
         pltpu.VMEM((ROWS, WIDTH), BF),
@@ -201,16 +202,15 @@
         in_specs=[
             pl.BlockSpec(memory_space=pltpu.SMEM),
             pl.BlockSpec((ROWS, WIDTH), lambda j: (0, 0)),
-            pl.BlockSpec((1, WIDTH), lambda j: (0, 0)),
-            pl.BlockSpec((1, 128), lambda j: (0, 0)),
+            pl.BlockSpec((WIDTH,), lambda j: (0,)),
             pl.BlockSpec((WIDTH, KVW), (lambda j: (0, 2)) if keys else (lambda j: (0, j))),
         ],
         out_specs=pl.BlockSpec((ROWS, KVW), lambda j: (0, j)),
         scratch_shapes=[] if keys else scratch,
         compiler_params=pltpu.CompilerParams(vmem_limit_bytes=VMEM_LIMIT),
-        cost_estimate=cost(3 if keys else 5),
+        cost_estimate=cost(0.1),
         name="prefill_kv" if keys else "prefill_query",
-    )(rank, hidden, gain, freq, w_qkv)
+    )(rank, hidden, gain, w_qkv)
 
 
 def column(row):
@@ -225,7 +225,6 @@
     index_ref,
     rows_ref,
     gain_ref,
-    freq_ref,
     w_ref,
     cache_ref,
     hidden_ref,
@@ -248,7 +247,7 @@
         projected = jnp.dot(normed, w_ref[:, QW:], preferred_element_type=F32)
         position = (index_ref[pl.ds(tick * 2, 2), :] % POSITIONS).astype(F32)
         position = jnp.concatenate([column(position[0:1]), column(position[1:2])], axis=0)
-        cosine, sine = rope_tables(position, freq_ref[...])
+        cosine, sine = rope_tables(position)
         low = lanes((256, 128)) < HEAD
         rows = pl.ds(pl.multiple_of(tick * 256, 256), 256)
         for i in range(5):
@@ -277,7 +276,7 @@
         position = jnp.zeros((8, 128), F32)
         for j in range(SLOTS):
             position = jnp.where(row == j, length_ref[j].astype(F32), position)
-        cosine, sine = rope_tables(position, freq_ref[...])
+        cosine, sine = rope_tables(position)
         chunks = [projected[:, i * 128 : (i + 1) * 128] for i in range(15)]
         roped = [rope(chunks[i], cosine, sine).astype(BF) for i in range(13)]
         whole = jnp.concatenate(roped[:10], axis=1).astype(F32) * 0.125
@@ -360,7 +359,7 @@
 
 
 def decode_attention(
-    device, length, count, slots, index, rows, gain, freq, w_qkv, cache, hidden
+    device, length, count, slots, index, rows, gain, w_qkv, cache, hidden
 ):
     smem = pl.BlockSpec(memory_space=pltpu.SMEM)
     full = lambda shape: pl.BlockSpec(shape, lambda j: (0,) * len(shape))
@@ -375,8 +374,7 @@
             full((1, 256)),
             full((8, 128)),
             full((256, WIDTH)),
-            full((1, WIDTH)),
-            full((1, 128)),
+            full((WIDTH,)),
             pl.BlockSpec(
                 (WIDTH, QW + KVW), lambda j: (0, 0), pipeline_mode=pl.Buffered(1)
             ),
@@ -396,7 +394,7 @@
         compiler_params=pltpu.CompilerParams(vmem_limit_bytes=VMEM_LIMIT),
         cost_estimate=cost(17),
         name="decode",
-    )(device, length, count, slots, index, rows, gain, freq, w_qkv, cache, hidden)
+    )(device, length, count, slots, index, rows, gain, w_qkv, cache, hidden)
 
 
 def attention_kernel(
@@ -471,7 +469,7 @@
             cut = slice(part * 128, (part + 1) * 128)
             resid = (hidden_ref[cut, :].astype(F32) + total[cut, :]).astype(BF)
             resid_ref[cut, :] = resid
-            (lower_ref, upper_ref)[part][:128, :] = norm_rows(resid, gain_ref[...])
+            (lower_ref, upper_ref)[part][...] = norm_rows(resid, gain_ref[...])
 
 
 def attention(rank, query, own, core, zed, far, w_out, hidden, gain):
@@ -481,8 +479,8 @@
         attention_kernel,
         out_shape=(
             jax.ShapeDtypeStruct((ROWS, WIDTH), BF),
-            jax.ShapeDtypeStruct((HALF, WIDTH), BF),
-            jax.ShapeDtypeStruct((HALF, WIDTH), BF),
+            jax.ShapeDtypeStruct((ROWS // 2, WIDTH), BF),
+            jax.ShapeDtypeStruct((ROWS // 2, WIDTH), BF),
         ),
         grid=(5,),
         in_specs=[
@@ -494,144 +492,110 @@
             side,
             pl.BlockSpec((256, WIDTH), lambda g: (g, 0)),
             full((ROWS, WIDTH)),
-            full((1, WIDTH)),
+            full((WIDTH,)),
         ],
         out_specs=(
             full((ROWS, WIDTH)),
-            full((HALF, WIDTH)),
-            full((HALF, WIDTH)),
+            full((ROWS // 2, WIDTH)),
+            full((ROWS // 2, WIDTH)),
         ),
         scratch_shapes=[
             pltpu.VMEM((ROWS, WIDTH), F32),
             pltpu.VMEM((128, 512), F32),
         ],
         compiler_params=pltpu.CompilerParams(vmem_limit_bytes=VMEM_LIMIT),
-        cost_estimate=cost(12),
+        cost_estimate=cost(0.1),
         name="attention",
     )(rank, query, own, core, zed, far, w_out, hidden, gain)
 
 
-def decode_rows_kernel(back_ref, w_ref, decode_ref, gain_ref, lower_in, upper_in, resid_ref, lower_ref, upper_ref):
-    del lower_in, upper_in
-    source = lanes((32, 256)) % 2
-    row = sublanes((32, 256))
-    pick = ((row == 0) & (source == 0)) | ((row == 16) & (source == 1))
-    pick = pick.astype(F32).astype(BF)
-    mixed = jnp.dot(pick, back_ref[...], preferred_element_type=F32).astype(BF)
-    projection = jnp.dot(mixed, w_ref[...], preferred_element_type=F32)
-    first = sublanes((16, WIDTH)) == 0
+def decode_rows_kernel(back_ref, w_ref, decode_ref, gain_ref, resid_ref, normed_ref):
+    mixed = jnp.sum(back_ref[...].astype(F32), axis=0)
+    mixed = jnp.concatenate([mixed, jnp.zeros((14, WIDTH), F32)], axis=0).astype(BF)
     single = decode_ref[...].astype(F32)
-    for part in range(2):
-        cut = slice(part * 16, (part + 1) * 16)
-        alone = jnp.where(first, jnp.broadcast_to(single[part : part + 1], (16, WIDTH)), 0.0)
-        resid = (alone + projection[cut]).astype(BF)
-        resid_ref[cut, :] = resid
-        (lower_ref, upper_ref)[part][...] = norm_rows(resid, gain_ref[...])
-
-
-def decode_rows(back, w_out, decode, gain, lower, upper):
-    full = lambda shape: pl.BlockSpec(shape, lambda g: (0,) * len(shape))
-    tail = pl.BlockSpec((16, WIDTH), lambda g: (8, 0))
+    hidden = jnp.concatenate([single, jnp.zeros((14, WIDTH), F32)], axis=0)
+    resid = (hidden + jnp.dot(mixed, w_ref[...], preferred_element_type=F32)).astype(BF)
+    resid_ref[...] = resid
+    normed_ref[...] = norm_rows(resid, gain_ref[...])
+
+
+def decode_rows(back, w_out, decode, gain):
+    vmem = pl.BlockSpec(memory_space=pltpu.VMEM)
     return pl.pallas_call(
         decode_rows_kernel,
-        out_shape=(
-            jax.ShapeDtypeStruct((32, WIDTH), BF),
-            jax.ShapeDtypeStruct((HALF, WIDTH), BF),
-            jax.ShapeDtypeStruct((HALF, WIDTH), BF),
-        ),
-        grid=(1,),
-        in_specs=[
-            full((256, WIDTH)),
-            full((WIDTH, WIDTH)),
-            full((2, WIDTH)),
-            full((1, WIDTH)),
-            tail,
-            tail,
-        ],
-        out_specs=(full((32, WIDTH)), tail, tail),
-        input_output_aliases={4: 1, 5: 2},
+        out_shape=(jax.ShapeDtypeStruct((16, WIDTH), BF),) * 2,
+        in_specs=[vmem] * 4,
+        out_specs=(vmem,) * 2,
         compiler_params=pltpu.CompilerParams(vmem_limit_bytes=VMEM_LIMIT),
         cost_estimate=cost(3),
         name="decode_rows",
-    )(back, w_out, decode, gain, lower, upper)
-
-
-def feed_kernel(*refs):
-    pieces, lows, highs, outs, act = refs[:2], refs[2:10], refs[10:18], refs[18:20], refs[20]
+    )(back, w_out, decode, gain)
+
+
+def hidden_units(rows, lows, highs, act):
     cut = 2 * SHARE - PART
-    rows = jnp.concatenate([ref[...] for ref in pieces], axis=0)
-    for k in range(8):
+    for k in range(len(lows)):
         gate_rows = lows[k][:SHARE, :]
         up_rows = jnp.concatenate([lows[k][SHARE:, :], highs[k][:cut, :]], axis=0)
         gate = lax.dot_general(rows, gate_rows, NT, preferred_element_type=F32)
         up = lax.dot_general(rows, up_rows, NT, preferred_element_type=F32)
         act[:, k * SHARE : (k + 1) * SHARE] = (gate / (1.0 + jnp.exp(-gate)) * up).astype(BF)
     down = jnp.concatenate([ref[cut:, :] for ref in highs], axis=0)
-    down = jnp.dot(act[...], down, preferred_element_type=F32)
-    outs[0][...] = down[:HALF].astype(BF)
-    outs[1][...] = down[HALF:].astype(BF)
-
-
-def feed_forward(pieces, lows, highs, name):
+    return jnp.dot(act[...], down, preferred_element_type=F32)
+
+
+def first_kernel(*refs):
+    rows = jnp.concatenate([refs[0][...], refs[1][...]], axis=0)
+    refs[6][...] = hidden_units(rows, refs[2:4], refs[4:6], refs[7])
+
+
+def second_kernel(*refs):
+    rows = jnp.concatenate([refs[0][...], refs[1][...]], axis=0)
+    down = hidden_units(rows, refs[2:8], refs[8:14], refs[17])
+    refs[16][...] = refs[15][...].astype(F32) + (refs[14][...] + down)
+
+
+def guest_kernel(*refs):
+    rows = jnp.concatenate([ref[...] for ref in refs[:4]], axis=0)
+    down = hidden_units(rows, refs[4:12], refs[12:20], refs[23]).astype(BF)
+    for ref, start, stop in zip(refs[20:23], (0, 144, 272), (144, 272, 288)):
+        ref[...] = down[start:stop]
+
+
+def feed_forward(kernel, inputs, outputs, rows, shares, time, name):
     vmem = pl.BlockSpec(memory_space=pltpu.VMEM)
     return pl.pallas_call(
-        feed_kernel,
-        out_shape=(jax.ShapeDtypeStruct((HALF, WIDTH), BF),) * 2,
-        in_specs=[vmem] * 18,
-        out_specs=(vmem,) * 2,
-        scratch_shapes=[pltpu.VMEM((2 * HALF, 8 * SHARE), BF)],
+        kernel,
+        out_shape=outputs,
+        in_specs=[vmem] * len(inputs),
+        out_specs=(vmem,) * len(outputs),
+        scratch_shapes=[pltpu.VMEM((rows, shares * SHARE), BF)],
         compiler_params=pltpu.CompilerParams(vmem_limit_bytes=VMEM_LIMIT),
-        cost_estimate=cost(8),
+        cost_estimate=cost(time),
         name=name,
-    )(*pieces, *lows, *highs)
-
-
-def start_kernel(resid_ref, extra_ref, lower_ref, upper_ref, out_ref):
-    for part in range(2):
-        mine_ref = (lower_ref, upper_ref)[part]
-        cut = slice(part * HALF, part * HALF + 128)
-        out_ref[cut, :] = resid_ref[part * 128 : (part + 1) * 128, :].astype(F32) + mine_ref[
-            :128, :
-        ].astype(F32)
-        cut = slice(part * HALF + 128, (part + 1) * HALF)
-        out_ref[cut, :] = extra_ref[part * 16 : (part + 1) * 16, :].astype(F32) + mine_ref[
-            128:, :
-        ].astype(F32)
-
-
-def start_sum(resid, extra, mine):
-    return pl.pallas_call(
-        start_kernel,
-        out_shape=jax.ShapeDtypeStruct((2 * HALF, WIDTH), F32),
-        in_specs=[pl.BlockSpec(memory_space=pltpu.VMEM)] * 4,
-        out_specs=pl.BlockSpec(memory_space=pltpu.VMEM),
-        compiler_params=pltpu.CompilerParams(vmem_limit_bytes=VMEM_LIMIT),
-        cost_estimate=cost(1.5),
-        name="start_sum",
-    )(resid, extra, *mine)
-
-
-def final_kernel(start_ref, first_ref, second_ref, prefill_ref, decode_ref):
-    decode = []
+    )(*inputs)
+
+
+def final_kernel(start_ref, extra_ref, mine_ref, first_ref, second_ref, prefill_ref, decode_ref):
     for part, ref in ((0, first_ref), (1, second_ref)):
-        whole = start_ref[part * HALF : (part + 1) * HALF, :] + ref[...].astype(F32)
-        prefill_ref[part * 128 : (part + 1) * 128, :] = whole[:128].astype(BF)
-        decode.append(whole[128:129])
-    decode_ref[...] = jnp.concatenate(decode, axis=0).astype(BF)
-
-
-def final_sum(start, first, second):
+        cut = slice(part * 128, (part + 1) * 128)
+        prefill_ref[cut, :] = (start_ref[cut, :] + ref[:128, :].astype(F32)).astype(BF)
+    alone = mine_ref[...].astype(F32) + first_ref[128:, :].astype(F32)
+    decode_ref[...] = (extra_ref[...].astype(F32) + alone)[:2].astype(BF)
+
+
+def final_sum(start, extra, mine, first, second):
     return pl.pallas_call(
         final_kernel,
         out_shape=(
             jax.ShapeDtypeStruct((ROWS, WIDTH), BF),
             jax.ShapeDtypeStruct((2, WIDTH), BF),
         ),
-        in_specs=[pl.BlockSpec(memory_space=pltpu.VMEM)] * 3,
+        in_specs=[pl.BlockSpec(memory_space=pltpu.VMEM)] * 5,
         compiler_params=pltpu.CompilerParams(vmem_limit_bytes=VMEM_LIMIT),
-        cost_estimate=cost(1.5),
+        cost_estimate=cost(1),
         name="final",
-    )(start, first, second)
+    )(start, extra, mine, first, second)
 
 
 def body(
@@ -652,12 +616,10 @@
 ):
     device = lax.axis_index("req").astype(jnp.int32).reshape(1)
     rank = device % 4
-    gain = attn_gain.reshape(1, WIDTH)
-    gain2 = ffn_gain.reshape(1, WIDTH)
-    exponent = np.arange(HEAD // 2) * (2.0 / HEAD)
-    freq = jnp.asarray(np.tile(THETA**-exponent, 4).reshape(1, 128), F32)
+    gain, gain2 = attn_gain, ffn_gain
     index = recomputed_index.reshape(8, 128)
 
+    w_all = w_out
     w_qkv, w_out, key_value_cache, held_hidden, prefill_hidden = in_hbm(
         w_qkv, w_out, key_value_cache, held_hidden, prefill_hidden
     )
@@ -666,7 +628,7 @@
     every_row = lax.all_to_all(spread, "req", 0, 0).reshape(256, WIDTH)
 
     low, high = pack_weights(jnp.swapaxes(w_gate_up, 1, 2), w_down)
-    (kv,) = in_hbm(project(rank, prefill_hidden, gain, freq, w_qkv, True))
+    (kv,) = in_hbm(project(rank, prefill_hidden, gain, w_qkv, True))
     zed = send(kv, pair_z)
     core = send(kv, other_core)
     low, high, kv = lax.optimization_barrier((low, high, kv))
@@ -676,7 +638,8 @@
     above_low = send(low, last_z)
     low_core = send(low, other_core)
     high_core = send(high, other_core)
-    (query,) = in_hbm(project(rank, prefill_hidden, gain, freq, w_qkv, False))
+    (query,) = in_hbm(project(rank, prefill_hidden, gain, w_qkv, False))
+    every_row, query = lax.optimization_barrier((every_row, query))
     outgoing = decode_attention(
         device,
         cache_len,
@@ -685,7 +648,6 @@
         index,
         every_row,
         gain,
-        freq,
         w_qkv,
         key_value_cache,
         held_hidden,
@@ -699,34 +661,60 @@
     far_high = send(above_high, last_z)
     below_low_core = send(below_low, other_core)
     above_high_core = send(above_high, other_core)
-    back = lax.all_to_all(outgoing.reshape(total, 2, WIDTH), "req", 0, 0).reshape(256, WIDTH)
+    back = lax.all_to_all(outgoing.reshape(total, 2, WIDTH), "req", 0, 0)
 
     resid, lower, upper = attention(
         rank, query, kv, core, zed, far, w_out, prefill_hidden, gain2
     )
-    (resid,) = in_hbm(resid)
-    lower, upper, back, below_high, above_low = lax.optimization_barrier(
-        (lower, upper, back, below_high, above_low)
-    )
+    from_last = send(lower, next_x)
+    from_next = send(upper, last_x)
+    (mine,) = feed_forward(
+        first_kernel,
+        (lower, upper, low, low_core, high, high_core),
+        (jax.ShapeDtypeStruct((ROWS, WIDTH), F32),),
+        ROWS,
+        2,
+        0.1,
+        "feed_first",
+    )
+    mine, back = lax.optimization_barrier((mine, back))
+    extra, alone = decode_rows(back, w_all, decode_hidden, gain2)
+    alone, far_low, far_high, from_last, from_next, below_high, above_low = (
+        lax.optimization_barrier(
+            (alone, far_low, far_high, from_last, from_next, below_high, above_low)
+        )
+    )
+    far_low_core = send(far_low, other_core)
+    far_high_core = send(far_high, other_core)
     below_high_core = send(below_high, other_core)
     above_low_core = send(above_low, other_core)
-    extra, lower, upper = decode_rows(back, w_out, decode_hidden, gain2, lower, upper)
-    lower, upper, far_low, far_high = lax.optimization_barrier((lower, upper, far_low, far_high))
-    far_low_core = send(far_low, other_core)
-    far_high_core = send(far_high, other_core)
-    from_last = send(lower, next_x)
-    from_next = send(upper, last_x)
-    lows = (low, low_core, below_low, below_low_core)
-    lows += (above_low, above_low_core, far_low, far_low_core)
-    highs = (high, high_core, below_high, below_high_core)
-    highs += (above_high, above_high_core, far_high, far_high_core)
-    mine = feed_forward((lower, upper), lows, highs, "feed_own")
-    from_last, from_next, mine = lax.optimization_barrier((from_last, from_next, mine))
-    guest = feed_forward((from_last, from_next), lows, highs, "feed_guest")
-    first = send(guest[0], last_x)
-    second = send(guest[1], next_x)
-    start = start_sum(resid, extra, mine)
-    return final_sum(start, first, second)
+    guest = send(alone, next_x)
+    lows = (low, low_core)
+    highs = (high, high_core)
+    lows_far = (below_low, below_low_core, above_low, above_low_core, far_low, far_low_core)
+    highs_far = (below_high, below_high_core, above_high, above_high_core, far_high, far_high_core)
+    to_last, to_next, alone = feed_forward(
+        guest_kernel,
+        (from_last, guest, from_next, alone) + lows + lows_far + highs + highs_far,
+        tuple(jax.ShapeDtypeStruct((n, WIDTH), BF) for n in (144, 128, 16)),
+        ROWS + 32,
+        8,
+        8,
+        "feed_guest",
+    )
+    to_last, to_next, mine = lax.optimization_barrier((to_last, to_next, mine))
+    first = send(to_last, last_x)
+    second = send(to_next, next_x)
+    (start,) = feed_forward(
+        second_kernel,
+        (lower, upper) + lows_far + highs_far + (mine, resid),
+        (jax.ShapeDtypeStruct((ROWS, WIDTH), F32),),
+        ROWS,
+        6,
+        6,
+        "feed_second",
+    )
+    return final_sum(start, extra, alone, first, second)
 
 
 def solution(mesh):

time: 137 us -> 143 us (1.044); the launches traced: 137 us -> 141 us
  starting transfers between devices: 34.8 us -> 39.2 us
  local copies, waits for them, and re-layouts: 9.31 us -> 13.1 us
  waiting for transfers between devices: 35.1 us -> 31.9 us
    all_to_all x1, waiting for transfers between devices: 12.7 us -> 0.01 us  [body(): back = lax.all_to_all(outgoing.reshape(total, 2, WIDTH), 'req', 0, 0)]
    ppermute x21 -> x22, waiting for transfers between devices: 15.2 us -> 26.2 us  [send(): return lax.ppermute(array, 'req', moves(step))]
    unnamed x28 -> x60, local copies, waits for them, and re-layouts: 3.29 us -> 8.08 us
    reshape x4 -> x1, local copies, waits for them, and re-layouts: 3.91 us -> 1.11 us  [body(): back = lax.all_to_all(outgoing.reshape(total, 2, WIDTH), 'req', 0, 0)]
    ppermute x21 -> x22, starting transfers between devices: 15.7 us -> 18.2 us  [send(): return lax.ppermute(array, 'req', moves(step))]
    reshape x1, local copies, waits for them, and re-layouts: 0.25 us -> 2.7 us  [body(): every_row = lax.all_to_all(spread, 'req', 0, 0).reshape(256, WIDTH)]
    all_to_all x1, waiting for transfers between devices: 7.25 us -> 5.78 us  [body(): every_row = lax.all_to_all(spread, 'req', 0, 0).reshape(256, WIDTH)]
  transfers between devices with their start and end apart: 23 -> 24, of which waited for: 7 -> 7; matrix products, arithmetic and copies ran while one was open for 3% -> 4% of each run, Pallas kernels for 35% -> 30%
where the time goes in v5:
time: 143 us; the launch traced here: 141 us
  Pallas kernels  55.2 us (39%)
  starting transfers between devices  39.2 us (27%)
  waiting for transfers between devices  31.9 us (22%)
  local copies, waits for them, and re-layouts  13.1 us (9%)
  between operations  1.67 us (1%)
    ppermute x22, waiting for transfers between devices, send(): return lax.ppermute(array, 'req', moves(step))  26.2 us
    ppermute x22, starting transfers between devices, send(): return lax.ppermute(array, 'req', moves(step))  18.2 us
    pallas_call x3, Pallas kernels, feed_forward(): pl.pallas_call(kernel, out_shape=outputs, in_specs=[vmem] * len(inputs),...  16.7 us
    pallas_call x1, Pallas kernels, decode_attention(): pl.pallas_call(decode_kernel, out_shape=jax.ShapeDtypeStruct((256, QW), B...  15.2 us
    pallas_call x1, Pallas kernels, attention(): pl.pallas_call(attention_kernel, out_shape=(jax.ShapeDtypeStruct((ROWS, W...  12.4 us
    all_to_all x1, starting transfers between devices, body(): every_row = lax.all_to_all(spread, 'req', 0, 0).reshape(256, WIDTH)  11.7 us
    all_to_all x1, starting transfers between devices, body(): back = lax.all_to_all(outgoing.reshape(total, 2, WIDTH), 'req', 0, 0)  9.3 us
    unnamed x60, local copies, waits for them, and re-layouts  8.08 us
  transfers between devices with their start and end apart: 24, of which 7 were waited for; matrix products, arithmetic and copies ran while one was open for 4% of the time, Pallas kernels for 30%

profile of v5, /device:TPU:0, one launch (start us, length us, event | category | flops | bytes accessed | tf_op | source)
XLA Modules:
  0.0 141.1 jit_solution(11435476091976368029)
XLA Ops:
  0.7 1.2 copy-done.21
  1.9 1.1 copy-done.24
  3.0 0.5 pack.1
  3.5 0.2 copy-done.18
  3.7 3.2 %prefill_kv.1.own_ref = bf16[256,640]{1,0:T(8,128)(2,1)S(1)} custom-call(s32[1]{0:T(128)S(6)} %select_n.7.rank_ref, bf16[256,1280]{1,0:T(8,128)(2,1)} %hidden_ref.7, f32[1280]{0:T(1024)S(1)} %copy-done.18, bf16[1280,1920]{1,0:T(8,128)(2,1)} %w_ref.7), custom_call_target="tpu_custom_call" | custom-call | flops 100000000 | bytes 300000 | tf_op jit(solution)/shard_map/prefill_kv/pallas_call | solution.py:198
  6.9 0.1 collective-permute-start.4
  7.0 1.2 broadcast_in_dim.2
  8.2 11.7 %all-to-all-start = ((bf16[128,2,1280]{2,1,0:T(2,128)(2,1)}), bf16[128,2,1280]{2,1,0:T(2,128)(2,1)}, u32[]{:S(2)}, u32[]{:S(2)}) async-start(bf16[128,2,1280]{2,1,0:T(2,128)(2,1)} %broadcast_in_dim.2), calls=%async_computation | async-start | bytes 1310720 | tf_op jit(solution)/shard_map/all_to_all | solution.py:628
  19.9 0.1 collective-permute-start.1
  20.0 1.2 collective-permute-start
  21.2 2.3 %collective-permute-start.13 = (bf16[336,1280]{1,0:T(8,128)(2,1)S(1)}, bf16[336,1280]{1,0:T(8,128)(2,1)}, u32[]{:S(2)}, u32[]{:S(2)}) collective-permute-start(bf16[336,1280]{1,0:T(8,128)(2,1)S(1)} %get-tuple-element.41.refs_2_.refs_4_), channel_id=1, source_target_pairs={{0,6},{1,7},{2,0},{3,1},{4,2},{5,3},{6,4},{7,5},{8,14},{9,15},{10,... | collective-permute-start | bytes 2580488 | tf_op jit(solution)/shard_map/ppermute | solution.py:53
  23.5 0.0 collective-permute-start.2
  24.2 0.0 copy-start.25
  24.2 0.0 copy-start.26
  24.2 0.0 copy-start.27
  24.2 3.8 %prefill_query.1.query_ref = bf16[256,1280]{1,0:T(8,128)(2,1)S(1)} custom-call(s32[1]{0:T(128)S(6)} %select_n.7.rank_ref, bf16[256,1280]{1,0:T(8,128)(2,1)} %hidden_ref.7, f32[1280]{0:T(1024)S(1)} %copy-done.18, bf16[1280,1920]{1,0:T(8,128)(2,1)} %w_ref.7), custom_call_target="tpu_custom_call" | custom-call | flops 100000000 | bytes 300000 | tf_op jit(solution)/shard_map/prefill_query/pallas_call | solution.py:198
  28.0 0.0 copy-start.1
  28.1 0.8 copy-done.1
  28.9 5.8 %all-to-all-done = bf16[128,2,1280]{2,1,0:T(2,128)(2,1)} async-done(((bf16[128,2,1280]{2,1,0:T(2,128)(2,1)}), bf16[128,2,1280]{2,1,0:T(2,128)(2,1)}, u32[]{:S(2)}, u32[]{:S(2)}) %all-to-all-start) | async-done | bytes 655392 | tf_op jit(solution)/shard_map/all_to_all | solution.py:628
  34.7 2.7 %reshape.23.rows_ref = bf16[256,1280]{1,0:T(8,128)(2,1)} reshape(bf16[128,2,1280]{2,1,0:T(2,128)(2,1)} %all-to-all-done) | data formatting | bytes 1310720 | tf_op jit(solution)/shard_map/reshape | solution.py:628
  37.4 0.3 collective-permute-start.12
  37.7 0.0 collective-permute-done.zed_ref
  37.7 0.0 collective-permute-start.5
  37.7 0.0 collective-permute-done.4.refs_3_.refs_5_
  37.7 3.0 %collective-permute-start.3 = (bf16[336,1280]{1,0:T(8,128)(2,1)S(1)}, bf16[336,1280]{1,0:T(8,128)(2,1)}, u32[]{:S(2)}, u32[]{:S(2)}) collective-permute-start(bf16[336,1280]{1,0:T(8,128)(2,1)S(1)} %get-tuple-element.42.refs_4_.refs_12_), channel_id=1, source_target_pairs={{0,6},{1,7},{2,0},{3,1},{4,2},{5,3},{6,4},{7,5},{8,14},{9,15},{10,... | collective-permute-start | bytes 2580488 | tf_op jit(solution)/shard_map/ppermute | solution.py:53
  40.8 1.1 copy-done.17
  41.8 15.2 %decode.1 = bf16[256,1280]{1,0:T(8,128)(2,1)S(1)} custom-call(s32[1]{0:T(128)} %bitcast.device_ref, s32[4]{0:T(128)S(1)} %copy-done.27, s32[1]{0:T(128)S(6)} %copy.16.count_ref, s32[1,256]{1,0:T(1,128)S(1)} %bitcast.6, s32[8,128]{1,0:T(8,128)S(1)} %bitcast.5, bf16[256,1280]{1,0:T(8,128)(2,1)S(1)} %copy-done.17, f32[1280]{0:T(1024)S(1)} %copy-done.18, ...), custom_call_target="tpu_custom_call" | custom-call | flops 16999999488 | bytes 51000000 | tf_op jit(solution)/shard_map/decode/pallas_call | solution.py:366
  57.1 0.0 copy-start.19
  57.1 0.0 collective-permute-done.5.refs_5_.refs_13_
  57.1 0.9 copy-done.14
  58.0 15.3 %collective-permute-done.3.refs_16_.refs_10_ = bf16[336,1280]{1,0:T(8,128)(2,1)} collective-permute-done((bf16[336,1280]{1,0:T(8,128)(2,1)S(1)}, bf16[336,1280]{1,0:T(8,128)(2,1)}, u32[]{:S(2)}, u32[]{:S(2)}) %collective-permute-start.3) | collective-permute-done | bytes 860192 | tf_op jit(solution)/shard_map/ppermute | solution.py:53
  73.3 1.1 reshape.26
  74.4 9.3 %all-to-all-start.1 = ((bf16[128,2,1280]{2,1,0:T(2,128)(2,1)}), bf16[128,2,1280]{2,1,0:T(2,128)(2,1)}, u32[]{:S(2)}, u32[]{:S(2)}) async-start(bf16[128,2,1280]{2,1,0:T(2,128)(2,1)} %reshape.26), calls=%async_computation.1 | async-start | bytes 1310720 | tf_op jit(solution)/shard_map/all_to_all | solution.py:664
  83.8 1.3 collective-permute-start.8
  85.0 2.2 %collective-permute-start.9 = (bf16[336,1280]{1,0:T(8,128)(2,1)}, bf16[336,1280]{1,0:T(8,128)(2,1)}, u32[]{:S(2)}, u32[]{:S(2)}) collective-permute-start(bf16[336,1280]{1,0:T(8,128)(2,1)} %collective-permute-done.3.refs_16_.refs_10_), channel_id=1, source_target_pairs={{0,6},{1,7},{2,0},{3,1},{4,2},{5,3},{6,4},{7,5},{8,14},{9,15},{10,... | collective-permute-start | bytes 2580488 | tf_op jit(solution)/shard_map/ppermute | solution.py:53
  87.3 0.0 collective-permute-done.6.far_ref
  87.3 0.0 collective-permute-start.7
  87.3 0.7 copy-done.29
  88.0 12.4 %attention.1 = (bf16[256,1280]{1,0:T(8,128)(2,1)S(1)}, bf16[128,1280]{1,0:T(8,128)(2,1)}, bf16[128,1280]{1,0:T(8,128)(2,1)}) custom-call(s32[1]{0:T(128)S(6)} %select_n.7.rank_ref, bf16[256,1280]{1,0:T(8,128)(2,1)} %copy-done.1, bf16[256,640]{1,0:T(8,128)(2,1)} %copy-done.2, bf16[256,640]{1,0:T(8,128)(2,1)} %copy-done.28, ...), custom_call_target="tpu_custom_call" | custom-call | flops 100000000 | bytes 300000 | tf_op jit(solution)/shard_map/attention/pallas_call | solution.py:478
  100.4 0.8 copy-done.22
  101.2 0.0 collective-permute-done.13.refs_8_.refs_4_
  101.2 1.1 collective-permute-start.10
  102.3 2.1 %collective-permute-start.11 = (bf16[128,1280]{1,0:T(8,128)(2,1)}, bf16[128,1280]{1,0:T(8,128)(2,1)}, u32[]{:S(2)}, u32[]{:S(2)}) collective-permute-start(bf16[128,1280]{1,0:T(8,128)(2,1)} %get-tuple-element.46.refs_1_), channel_id=1, source_target_pairs={{0,24},{1,25},{2,26},{3,27},{4,28},{5,29},{6,30},{7,31},{8,0},{9,1... | collective-permute-start | bytes 983048 | tf_op jit(solution)/shard_map/ppermute | solution.py:53
  104.5 2.6 %feed_first.1.refs_14_ = f32[256,1280]{1,0:T(8,128)S(1)} custom-call(bf16[128,1280]{1,0:T(8,128)(2,1)} %get-tuple-element.45.refs_0_, bf16[128,1280]{1,0:T(8,128)(2,1)} %get-tuple-element.46.refs_1_, bf16[336,1280]{1,0:T(8,128)(2,1)S(1)} %copy-done.6, bf16[336,1280]{1,0:T(8,128)(2,1)S(1)} %copy-done.12, bf16[336,1280]{1,0:T(8,128)(2,1)S(1)} %copy-done.9, ...), custom_call_target="tpu_custom_call" | custom-call | flops 100000000 | bytes 300000 | tf_op jit(solution)/shard_map/feed_first/pallas_call | solution.py:567
  107.1 1.1 copy-done.3
  108.1 0.0 all-to-all-done.1.back_ref
  108.2 4.0 %collective-permute-done.10.refs_0_ = bf16[128,1280]{1,0:T(8,128)(2,1)} collective-permute-done((bf16[128,1280]{1,0:T(8,128)(2,1)}, bf16[128,1280]{1,0:T(8,128)(2,1)}, u32[]{:S(2)}, u32[]{:S(2)}) %collective-permute-start.10) | collective-permute-done | bytes 327712 | tf_op jit(solution)/shard_map/ppermute | solution.py:53
  112.1 2.3 %decode_rows.1 = (bf16[16,1280]{1,0:T(8,128)(2,1)S(1)}, bf16[16,1280]{1,0:T(8,128)(2,1)S(1)}) custom-call(bf16[128,2,1280]{2,1,0:T(2,128)(2,1)} %all-to-all-done.1.back_ref, bf16[1280,1280]{1,0:T(8,128)(2,1)S(1)} %copy-done, bf16[2,1280]{1,0:T(2,128)(2,1)S(1)} %copy-done.20, f32[1280]{0:T(1024)S(1)} %copy-done.19), custom_call_target="tpu_custom_call" | custom-call | flops 3000000000 | bytes 9000000 | tf_op jit(solution)/shard_map/decode_rows/pallas_call | solution.py:524
  114.5 0.0 collective-permute-done.11.refs_2_
  114.5 0.0 collective-permute-done.9.refs_18_.refs_12_
  114.5 0.0 copy-start.23
  114.5 0.6 collective-permute-start.14
  115.1 0.1 collective-permute-start.15
  115.2 0.4 collective-permute-start.16
  115.6 0.1 collective-permute-start.18
  115.7 5.2 %collective-permute-done.19.refs_1_ = bf16[16,1280]{1,0:T(8,128)(2,1)S(1)} collective-permute-done((bf16[16,1280]{1,0:T(8,128)(2,1)S(1)}, bf16[16,1280]{1,0:T(8,128)(2,1)S(1)}, u32[]{:S(2)}, u32[]{:S(2)}) %collective-permute-start.19) | collective-permute-done | bytes 40992 | tf_op jit(solution)/shard_map/ppermute | solution.py:53
  120.9 0.1 collective-permute-done.18.refs_19_.refs_13_
  121.0 7.7 %feed_guest.1 = (bf16[144,1280]{1,0:T(8,128)(2,1)S(1)}, bf16[128,1280]{1,0:T(8,128)(2,1)S(1)}, bf16[16,1280]{1,0:T(8,128)(2,1)S(1)}) custom-call(bf16[128,1280]{1,0:T(8,128)(2,1)} %collective-permute-done.10.refs_0_, bf16[16,1280]{1,0:T(8,128)(2,1)S(1)} %collective-permute-done.19.refs_1_, bf16[128,1280]{1,0:T(8,128)(2,1)} %collective-permute-done.11.refs_2_, ...), custom_call_target="tpu_custom_call" | custom-call | flops 8000000000 | bytes 24000000 | tf_op jit(solution)/shard_map/feed_guest/pallas_call | solution.py:567
  128.7 0.1 collective-permute-start.21
  128.8 3.2 %collective-permute-start.20 = (bf16[144,1280]{1,0:T(8,128)(2,1)S(1)}, bf16[144,1280]{1,0:T(8,128)(2,1)S(1)}, u32[]{:S(2)}, u32[]{:S(2)}) collective-permute-start(bf16[144,1280]{1,0:T(8,128)(2,1)S(1)} %get-tuple-element.68), channel_id=1, source_target_pairs={{0,24},{1,25},{2,26},{3,27},{4,28},{5,29},{6,30},{7,31},{8,0},{9,1... | collective-permute-start | bytes 1105928 | tf_op jit(solution)/shard_map/ppermute | solution.py:53
  132.1 6.5 %feed_second.1.start_ref = f32[256,1280]{1,0:T(8,128)S(1)} custom-call(bf16[128,1280]{1,0:T(8,128)(2,1)} %get-tuple-element.45.refs_0_, bf16[128,1280]{1,0:T(8,128)(2,1)} %get-tuple-element.46.refs_1_, bf16[336,1280]{1,0:T(8,128)(2,1)} %collective-permute-done.2.refs_6_.refs_2_, bf16[336,1280]{1,0:T(8,128)(2,1)} %collective-permute-done.7.refs_7_.refs_3_, ...), custom_call_target="tpu_custom_call" | custom-call | flops 6000000000 | bytes 18000000 | tf_op jit(solution)/shard_map/feed_second/pallas_call | solution.py:567
  138.5 1.5 %collective-permute-done.21.second_ref = bf16[128,1280]{1,0:T(8,128)(2,1)S(1)} collective-permute-done((bf16[128,1280]{1,0:T(8,128)(2,1)S(1)}, bf16[128,1280]{1,0:T(8,128)(2,1)S(1)}, u32[]{:S(2)}, u32[]{:S(2)}) %collective-permute-start.21) | collective-permute-done | bytes 327712 | tf_op jit(solution)/shard_map/ppermute | solution.py:53
  140.0 0.1 collective-permute-done.20.first_ref
  140.2 1.0 final.1
  (57 shorter events, 0.1 us)
Async XLA Ops:
  0.6 1.3 copy-start.21
  1.9 1.1 copy-start.24
  3.0 0.7 copy-start.18
  3.7 19.8 %copy-start.5 = (bf16[336,1280]{1,0:T(8,128)(2,1)}, bf16[336,1280]{1,0:T(8,128)(2,1)S(1)}, u32[]{:S(2)}) copy-start(bf16[336,1280]{1,0:T(8,128)(2,1)S(1)} %get-tuple-element.41.refs_2_.refs_4_) | copy-start | bytes 2580484
  3.7 34.0 %copy-start.8 = (bf16[336,1280]{1,0:T(8,128)(2,1)}, bf16[336,1280]{1,0:T(8,128)(2,1)S(1)}, u32[]{:S(2)}) copy-start(bf16[336,1280]{1,0:T(8,128)(2,1)S(1)} %get-tuple-element.42.refs_4_.refs_12_) | copy-start | bytes 2580484
  3.7 3.3 %copy-start.20 = (bf16[2,1280]{1,0:T(2,128)(2,1)S(1)}, bf16[2,1280]{1,0:T(2,128)(2,1)}, u32[]{:S(2)}) copy-start(bf16[2,1280]{1,0:T(2,128)(2,1)} %decode_ref.1) | copy-start | bytes 15364
  6.9 21.1 %copy-start.2 = (bf16[256,640]{1,0:T(8,128)(2,1)}, bf16[256,640]{1,0:T(8,128)(2,1)S(1)}, u32[]{:S(2)}) copy-start(bf16[256,640]{1,0:T(8,128)(2,1)S(1)} %prefill_kv.1.own_ref) | copy-start | bytes 983044
  6.9 30.8 %collective-permute-start.4 = (bf16[336,1280]{1,0:T(8,128)(2,1)S(1)}, bf16[336,1280]{1,0:T(8,128)(2,1)S(1)}, u32[]{:S(2)}, u32[]{:S(2)}) collective-permute-start(bf16[336,1280]{1,0:T(8,128)(2,1)S(1)} %get-tuple-element.41.refs_2_.refs_4_), channel_id=1, source_target_pairs={{0,1},{1,0},{2,3},{3,2},{4,5},{5,4},{6,7},{7,6},{8,9},{9,8},{10,11... | collective-permute-start | bytes 2580488 | tf_op jit(solution)/shard_map/ppermute | solution.py:53
  8.2 26.5 %all-to-all-start = ((bf16[128,2,1280]{2,1,0:T(2,128)(2,1)}), bf16[128,2,1280]{2,1,0:T(2,128)(2,1)}, u32[]{:S(2)}, u32[]{:S(2)}) async-start(bf16[128,2,1280]{2,1,0:T(2,128)(2,1)} %broadcast_in_dim.2), calls=%async_computation | async-start | bytes 1310720 | tf_op jit(solution)/shard_map/all_to_all | solution.py:628
  19.9 17.5 %collective-permute-start.1 = (bf16[256,640]{1,0:T(8,128)(2,1)S(1)}, bf16[256,640]{1,0:T(8,128)(2,1)S(1)}, u32[]{:S(2)}, u32[]{:S(2)}) collective-permute-start(bf16[256,640]{1,0:T(8,128)(2,1)S(1)} %prefill_kv.1.own_ref), channel_id=1, source_target_pairs={{0,1},{1,0},{2,3},{3,2},{4,5},{5,4},{6,7},{7,6},{8,9},{9,8},{10,11... | collective-permute-start | bytes 983048 | tf_op jit(solution)/shard_map/ppermute | solution.py:53
  20.0 17.7 %collective-permute-start = (bf16[256,640]{1,0:T(8,128)(2,1)S(1)}, bf16[256,640]{1,0:T(8,128)(2,1)}, u32[]{:S(2)}, u32[]{:S(2)}) collective-permute-start(bf16[256,640]{1,0:T(8,128)(2,1)S(1)} %prefill_kv.1.own_ref), channel_id=1, source_target_pairs={{0,2},{1,3},{2,0},{3,1},{4,6},{5,7},{6,4},{7,5},{8,10},{9,11},{10,... | collective-permute-start | bytes 983048 | tf_op jit(solution)/shard_map/ppermute | solution.py:53
  21.2 80.0 %collective-permute-start.13 = (bf16[336,1280]{1,0:T(8,128)(2,1)S(1)}, bf16[336,1280]{1,0:T(8,128)(2,1)}, u32[]{:S(2)}, u32[]{:S(2)}) collective-permute-start(bf16[336,1280]{1,0:T(8,128)(2,1)S(1)} %get-tuple-element.41.refs_2_.refs_4_), channel_id=1, source_target_pairs={{0,6},{1,7},{2,0},{3,1},{4,2},{5,3},{6,4},{7,5},{8,14},{9,15},{10,... | collective-permute-start | bytes 2580488 | tf_op jit(solution)/shard_map/ppermute | solution.py:53
  23.5 33.6 %collective-permute-start.2 = (bf16[336,1280]{1,0:T(8,128)(2,1)S(1)}, bf16[336,1280]{1,0:T(8,128)(2,1)}, u32[]{:S(2)}, u32[]{:S(2)}) collective-permute-start(bf16[336,1280]{1,0:T(8,128)(2,1)S(1)} %get-tuple-element.41.refs_2_.refs_4_), channel_id=1, source_target_pairs={{0,2},{1,3},{2,4},{3,5},{4,6},{5,7},{6,0},{7,1},{8,10},{9,11},{10,... | collective-permute-start | bytes 2580488 | tf_op jit(solution)/shard_map/ppermute | solution.py:53
  24.2 16.6 %copy-start.25 = (s32[1024]{0:T(1024)S(1)}, s32[1024]{0:T(1024)}, u32[]{:S(2)}) copy-start(s32[1024]{0:T(1024)} %param.26) | copy-start | bytes 12292
  24.2 16.6 %copy-start.26 = (s32[256]{0:T(256)S(1)}, s32[256]{0:T(256)}, u32[]{:S(2)}) copy-start(s32[256]{0:T(256)} %param.24) | copy-start | bytes 3076
  24.2 16.6 %copy-start.27 = (s32[4]{0:T(128)S(1)}, s32[4]{0:T(128)}, u32[]{:S(2)}) copy-start(s32[4]{0:T(128)} %length_ref.1) | copy-start | bytes 52
  28.0 0.8 copy-start.1
  37.4 3.4 %copy-start.28 = (bf16[256,640]{1,0:T(8,128)(2,1)}, bf16[256,640]{1,0:T(8,128)(2,1)S(1)}, u32[]{:S(2)}) copy-start(bf16[256,640]{1,0:T(8,128)(2,1)S(1)} %collective-permute-done.1.core_ref) | copy-start | bytes 983044
  37.4 64.9 %collective-permute-start.12 = (bf16[336,1280]{1,0:T(8,128)(2,1)S(1)}, bf16[336,1280]{1,0:T(8,128)(2,1)}, u32[]{:S(2)}, u32[]{:S(2)}) collective-permute-start(bf16[336,1280]{1,0:T(8,128)(2,1)S(1)} %get-tuple-element.42.refs_4_.refs_12_), channel_id=1, source_target_pairs={{0,2},{1,3},{2,4},{3,5},{4,6},{5,7},{6,0},{7,1},{8,10},{9,11},{10,... | collective-permute-start | bytes 2580488 | tf_op jit(solution)/shard_map/ppermute | solution.py:53
  37.7 19.4 %collective-permute-start.5 = (bf16[336,1280]{1,0:T(8,128)(2,1)S(1)}, bf16[336,1280]{1,0:T(8,128)(2,1)S(1)}, u32[]{:S(2)}, u32[]{:S(2)}) collective-permute-start(bf16[336,1280]{1,0:T(8,128)(2,1)S(1)} %get-tuple-element.42.refs_4_.refs_12_), channel_id=1, source_target_pairs={{0,1},{1,0},{2,3},{3,2},{4,5},{5,4},{6,7},{7,6},{8,9},{9,8},{10,11... | collective-permute-start | bytes 2580488 | tf_op jit(solution)/shard_map/ppermute | solution.py:53
  37.7 19.4 %copy-start.11 = (bf16[336,1280]{1,0:T(8,128)(2,1)}, bf16[336,1280]{1,0:T(8,128)(2,1)S(1)}, u32[]{:S(2)}) copy-start(bf16[336,1280]{1,0:T(8,128)(2,1)S(1)} %collective-permute-done.4.refs_3_.refs_5_) | copy-start | bytes 2580484
  37.7 35.6 %collective-permute-start.3 = (bf16[336,1280]{1,0:T(8,128)(2,1)S(1)}, bf16[336,1280]{1,0:T(8,128)(2,1)}, u32[]{:S(2)}, u32[]{:S(2)}) collective-permute-start(bf16[336,1280]{1,0:T(8,128)(2,1)S(1)} %get-tuple-element.42.refs_4_.refs_12_), channel_id=1, source_target_pairs={{0,6},{1,7},{2,0},{3,1},{4,2},{5,3},{6,4},{7,5},{8,14},{9,15},{10,... | collective-permute-start | bytes 2580488 | tf_op jit(solution)/shard_map/ppermute | solution.py:53
  40.7 1.1 copy-start.17
  57.1 30.9 %copy-start.19 = (f32[1280]{0:T(1024)S(1)}, f32[1280]{0:T(1024)}, u32[]{:S(2)}) copy-start(f32[1280]{0:T(1024)} %gain_ref.9) | copy-start | bytes 15364
  57.1 0.9 copy-start.14
  73.3 14.0 %collective-permute-start.6 = (bf16[256,640]{1,0:T(8,128)(2,1)}, bf16[256,640]{1,0:T(8,128)(2,1)S(1)}, u32[]{:S(2)}, u32[]{:S(2)}) collective-permute-start(bf16[256,640]{1,0:T(8,128)(2,1)} %collective-permute-done.zed_ref), channel_id=1, source_target_pairs={{0,1},{1,0},{2,3},{3,2},{4,5},{5,4},{6,7},{7,6},{8,9},{9,8},{10,11... | collective-permute-start | bytes 983048 | tf_op jit(solution)/shard_map/ppermute | solution.py:53
  74.4 33.7 %all-to-all-start.1 = ((bf16[128,2,1280]{2,1,0:T(2,128)(2,1)}), bf16[128,2,1280]{2,1,0:T(2,128)(2,1)}, u32[]{:S(2)}, u32[]{:S(2)}) async-start(bf16[128,2,1280]{2,1,0:T(2,128)(2,1)} %reshape.26), calls=%async_computation.1 | async-start | bytes 1310720 | tf_op jit(solution)/shard_map/all_to_all | solution.py:664
  83.7 20.7 %copy-start.6 = (bf16[336,1280]{1,0:T(8,128)(2,1)S(1)}, bf16[336,1280]{1,0:T(8,128)(2,1)}, u32[]{:S(2)}) copy-start(bf16[336,1280]{1,0:T(8,128)(2,1)} %copy-done.5) | copy-start | bytes 2580484
  83.7 20.7 %copy-start.9 = (bf16[336,1280]{1,0:T(8,128)(2,1)S(1)}, bf16[336,1280]{1,0:T(8,128)(2,1)}, u32[]{:S(2)}) copy-start(bf16[336,1280]{1,0:T(8,128)(2,1)} %copy-done.8) | copy-start | bytes 2580484
  83.7 20.7 %copy-start.12 = (bf16[336,1280]{1,0:T(8,128)(2,1)S(1)}, bf16[336,1280]{1,0:T(8,128)(2,1)}, u32[]{:S(2)}) copy-start(bf16[336,1280]{1,0:T(8,128)(2,1)} %copy-done.11) | copy-start | bytes 2580484
  83.8 20.7 %copy-start.15 = (bf16[336,1280]{1,0:T(8,128)(2,1)S(1)}, bf16[336,1280]{1,0:T(8,128)(2,1)}, u32[]{:S(2)}) copy-start(bf16[336,1280]{1,0:T(8,128)(2,1)} %copy-done.14) | copy-start | bytes 2580484
  83.8 30.7 %collective-permute-start.8 = (bf16[336,1280]{1,0:T(8,128)(2,1)}, bf16[336,1280]{1,0:T(8,128)(2,1)}, u32[]{:S(2)}, u32[]{:S(2)}) collective-permute-start(bf16[336,1280]{1,0:T(8,128)(2,1)} %collective-permute-done.2.refs_6_.refs_2_), channel_id=1, source_target_pairs={{0,2},{1,3},{2,4},{3,5},{4,6},{5,7},{6,0},{7,1},{8,10},{9,11},{10,... | collective-permute-start | bytes 2580488 | tf_op jit(solution)/shard_map/ppermute | solution.py:53
  85.0 29.4 %collective-permute-start.9 = (bf16[336,1280]{1,0:T(8,128)(2,1)}, bf16[336,1280]{1,0:T(8,128)(2,1)}, u32[]{:S(2)}, u32[]{:S(2)}) collective-permute-start(bf16[336,1280]{1,0:T(8,128)(2,1)} %collective-permute-done.3.refs_16_.refs_10_), channel_id=1, source_target_pairs={{0,6},{1,7},{2,0},{3,1},{4,2},{5,3},{6,4},{7,5},{8,14},{9,15},{10,... | collective-permute-start | bytes 2580488 | tf_op jit(solution)/shard_map/ppermute | solution.py:53
  87.3 0.7 copy-start.29
  87.3 28.3 %collective-permute-start.7 = (bf16[336,1280]{1,0:T(8,128)(2,1)}, bf16[336,1280]{1,0:T(8,128)(2,1)}, u32[]{:S(2)}, u32[]{:S(2)}) collective-permute-start(bf16[336,1280]{1,0:T(8,128)(2,1)} %collective-permute-done.2.refs_6_.refs_2_), channel_id=1, source_target_pairs={{0,1},{1,0},{2,3},{3,2},{4,5},{5,4},{6,7},{7,6},{8,9},{9,8},{10,11... | collective-permute-start | bytes 2580488 | tf_op jit(solution)/shard_map/ppermute | solution.py:53
  100.4 0.8 copy-start.22
  101.2 10.9 %collective-permute-start.10 = (bf16[128,1280]{1,0:T(8,128)(2,1)}, bf16[128,1280]{1,0:T(8,128)(2,1)}, u32[]{:S(2)}, u32[]{:S(2)}) collective-permute-start(bf16[128,1280]{1,0:T(8,128)(2,1)} %get-tuple-element.45.refs_0_), channel_id=1, source_target_pairs={{0,8},{1,9},{2,10},{3,11},{4,12},{5,13},{6,14},{7,15},{8,16},{9,17... | collective-permute-start | bytes 983048 | tf_op jit(solution)/shard_map/ppermute | solution.py:53
  102.3 9.8 %copy-start = (bf16[1280,1280]{1,0:T(8,128)(2,1)S(1)}, bf16[1280,1280]{1,0:T(8,128)(2,1)}, u32[]{:S(2)}) copy-start(bf16[1280,1280]{1,0:T(8,128)(2,1)} %w_ref.9) | copy-start | bytes 9830404
  102.3 12.2 %collective-permute-start.11 = (bf16[128,1280]{1,0:T(8,128)(2,1)}, bf16[128,1280]{1,0:T(8,128)(2,1)}, u32[]{:S(2)}, u32[]{:S(2)}) collective-permute-start(bf16[128,1280]{1,0:T(8,128)(2,1)} %get-tuple-element.46.refs_1_), channel_id=1, source_target_pairs={{0,24},{1,25},{2,26},{3,27},{4,28},{5,29},{6,30},{7,31},{8,0},{9,1... | collective-permute-start | bytes 983048 | tf_op jit(solution)/shard_map/ppermute | solution.py:53
  107.0 1.1 copy-start.3
  108.1 12.9 %copy-start.7 = (bf16[336,1280]{1,0:T(8,128)(2,1)S(1)}, bf16[336,1280]{1,0:T(8,128)(2,1)}, u32[]{:S(2)}) copy-start(bf16[336,1280]{1,0:T(8,128)(2,1)} %copy-done.5) | copy-start | bytes 2580484
  108.1 12.9 %copy-start.10 = (bf16[336,1280]{1,0:T(8,128)(2,1)S(1)}, bf16[336,1280]{1,0:T(8,128)(2,1)}, u32[]{:S(2)}) copy-start(bf16[336,1280]{1,0:T(8,128)(2,1)} %copy-done.8) | copy-start | bytes 2580484
  108.2 12.9 %copy-start.13 = (bf16[336,1280]{1,0:T(8,128)(2,1)S(1)}, bf16[336,1280]{1,0:T(8,128)(2,1)}, u32[]{:S(2)}) copy-start(bf16[336,1280]{1,0:T(8,128)(2,1)} %copy-done.11) | copy-start | bytes 2580484
  108.2 12.9 %copy-start.16 = (bf16[336,1280]{1,0:T(8,128)(2,1)S(1)}, bf16[336,1280]{1,0:T(8,128)(2,1)}, u32[]{:S(2)}) copy-start(bf16[336,1280]{1,0:T(8,128)(2,1)} %copy-done.14) | copy-start | bytes 2580484
  112.1 3.6 %collective-permute-start.17 = (bf16[336,1280]{1,0:T(8,128)(2,1)}, bf16[336,1280]{1,0:T(8,128)(2,1)S(1)}, u32[]{:S(2)}, u32[]{:S(2)}) collective-permute-start(bf16[336,1280]{1,0:T(8,128)(2,1)} %collective-permute-done.3.refs_16_.refs_10_), channel_id=1, source_target_pairs={{0,1},{1,0},{2,3},{3,2},{4,5},{5,4},{6,7},{7,6},{8,9},{9,8},{10,11... | collective-permute-start | bytes 2580488 | tf_op jit(solution)/shard_map/ppermute | solution.py:53
  114.5 17.6 %copy-start.4 = (f32[256,1280]{1,0:T(8,128)S(1)}, f32[256,1280]{1,0:T(8,128)}, u32[]{:S(2)}) copy-start(f32[256,1280]{1,0:T(8,128)} %copy-done.3) | copy-start | bytes 3932164
  114.5 17.6 %copy-start.23 = (bf16[256,1280]{1,0:T(8,128)(2,1)S(1)}, bf16[256,1280]{1,0:T(8,128)(2,1)}, u32[]{:S(2)}) copy-start(bf16[256,1280]{1,0:T(8,128)(2,1)} %copy-done.22) | copy-start | bytes 1966084
  114.5 6.4 %collective-permute-start.14 = (bf16[336,1280]{1,0:T(8,128)(2,1)}, bf16[336,1280]{1,0:T(8,128)(2,1)S(1)}, u32[]{:S(2)}, u32[]{:S(2)}) collective-permute-start(bf16[336,1280]{1,0:T(8,128)(2,1)} %collective-permute-done.13.refs_8_.refs_4_), channel_id=1, source_target_pairs={{0,1},{1,0},{2,3},{3,2},{4,5},{5,4},{6,7},{7,6},{8,9},{9,8},{10,11... | collective-permute-start | bytes 2580488 | tf_op jit(solution)/shard_map/ppermute | solution.py:53
  115.1 5.8 %collective-permute-start.15 = (bf16[336,1280]{1,0:T(8,128)(2,1)}, bf16[336,1280]{1,0:T(8,128)(2,1)S(1)}, u32[]{:S(2)}, u32[]{:S(2)}) collective-permute-start(bf16[336,1280]{1,0:T(8,128)(2,1)} %collective-permute-done.8.refs_10_.refs_6_), channel_id=1, source_target_pairs={{0,1},{1,0},{2,3},{3,2},{4,5},{5,4},{6,7},{7,6},{8,9},{9,8},{10,11... | collective-permute-start | bytes 2580488 | tf_op jit(solution)/shard_map/ppermute | solution.py:53
  115.2 5.7 %collective-permute-start.16 = (bf16[336,1280]{1,0:T(8,128)(2,1)}, bf16[336,1280]{1,0:T(8,128)(2,1)S(1)}, u32[]{:S(2)}, u32[]{:S(2)}) collective-permute-start(bf16[336,1280]{1,0:T(8,128)(2,1)} %collective-permute-done.12.refs_14_.refs_8_), channel_id=1, source_target_pairs={{0,1},{1,0},{2,3},{3,2},{4,5},{5,4},{6,7},{7,6},{8,9},{9,8},{10,11... | collective-permute-start | bytes 2580488 | tf_op jit(solution)/shard_map/ppermute | solution.py:53
  115.6 5.4 %collective-permute-start.18 = (bf16[336,1280]{1,0:T(8,128)(2,1)}, bf16[336,1280]{1,0:T(8,128)(2,1)S(1)}, u32[]{:S(2)}, u32[]{:S(2)}) collective-permute-start(bf16[336,1280]{1,0:T(8,128)(2,1)} %collective-permute-done.9.refs_18_.refs_12_), channel_id=1, source_target_pairs={{0,1},{1,0},{2,3},{3,2},{4,5},{5,4},{6,7},{7,6},{8,9},{9,8},{10,11... | collective-permute-start | bytes 2580488 | tf_op jit(solution)/shard_map/ppermute | solution.py:53
  115.7 5.2 %collective-permute-start.19 = (bf16[16,1280]{1,0:T(8,128)(2,1)S(1)}, bf16[16,1280]{1,0:T(8,128)(2,1)S(1)}, u32[]{:S(2)}, u32[]{:S(2)}) collective-permute-start(bf16[16,1280]{1,0:T(8,128)(2,1)S(1)} %get-tuple-element.59.refs_3_), channel_id=1, source_target_pairs={{0,8},{1,9},{2,10},{3,11},{4,12},{5,13},{6,14},{7,15},{8,16},{9,17... | collective-permute-start | bytes 122888 | tf_op jit(solution)/shard_map/ppermute | solution.py:53
  128.7 11.3 %collective-permute-start.21 = (bf16[128,1280]{1,0:T(8,128)(2,1)S(1)}, bf16[128,1280]{1,0:T(8,128)(2,1)S(1)}, u32[]{:S(2)}, u32[]{:S(2)}) collective-permute-start(bf16[128,1280]{1,0:T(8,128)(2,1)S(1)} %get-tuple-element.69), channel_id=1, source_target_pairs={{0,8},{1,9},{2,10},{3,11},{4,12},{5,13},{6,14},{7,15},{8,16},{9,17... | collective-permute-start | bytes 983048 | tf_op jit(solution)/shard_map/ppermute | solution.py:53
  128.8 11.3 %collective-permute-start.20 = (bf16[144,1280]{1,0:T(8,128)(2,1)S(1)}, bf16[144,1280]{1,0:T(8,128)(2,1)S(1)}, u32[]{:S(2)}, u32[]{:S(2)}) collective-permute-start(bf16[144,1280]{1,0:T(8,128)(2,1)S(1)} %get-tuple-element.68), channel_id=1, source_target_pairs={{0,24},{1,25},{2,26},{3,27},{4,28},{5,29},{6,30},{7,31},{8,0},{9,1... | collective-permute-start | bytes 1105928 | tf_op jit(solution)/shard_map/ppermute | solution.py:53

commit v6 on v5

--- a/solution.py
+++ b/solution.py
@@ -208,7 +208,7 @@
         out_specs=pl.BlockSpec((ROWS, KVW), lambda j: (0, j)),
         scratch_shapes=[] if keys else scratch,
         compiler_params=pltpu.CompilerParams(vmem_limit_bytes=VMEM_LIMIT),
-        cost_estimate=cost(0.1),
+        cost_estimate=cost(3 if keys else 0.1),
         name="prefill_kv" if keys else "prefill_query",
     )(rank, hidden, gain, w_qkv)
 
@@ -627,18 +627,17 @@
     spread = jnp.broadcast_to(decode_hidden[None], (total, 2, WIDTH))
     every_row = lax.all_to_all(spread, "req", 0, 0).reshape(256, WIDTH)
 
-    low, high = pack_weights(jnp.swapaxes(w_gate_up, 1, 2), w_down)
+    low, high = pack_weights(*in_hbm(jnp.swapaxes(w_gate_up, 1, 2), w_down))
     (kv,) = in_hbm(project(rank, prefill_hidden, gain, w_qkv, True))
     zed = send(kv, pair_z)
     core = send(kv, other_core)
     low, high, kv = lax.optimization_barrier((low, high, kv))
     below_low = send(low, next_z)
     above_high = send(high, last_z)
+    (query,) = in_hbm(project(rank, prefill_hidden, gain, w_qkv, False))
+    low, high, query = lax.optimization_barrier((low, high, query))
     below_high = send(high, next_z)
     above_low = send(low, last_z)
-    low_core = send(low, other_core)
-    high_core = send(high, other_core)
-    (query,) = in_hbm(project(rank, prefill_hidden, gain, w_qkv, False))
     every_row, query = lax.optimization_barrier((every_row, query))
     outgoing = decode_attention(
         device,
@@ -652,9 +651,11 @@
         key_value_cache,
         held_hidden,
     )
-    outgoing, zed, core, below_low, above_high, low_core, high_core = lax.optimization_barrier(
-        (outgoing, zed, core, below_low, above_high, low_core, high_core)
-    )
+    outgoing, zed, core, below_low, above_high, low, high = lax.optimization_barrier(
+        (outgoing, zed, core, below_low, above_high, low, high)
+    )
+    low_core = send(low, other_core)
+    high_core = send(high, other_core)
     far = send(zed, other_core)
     core, zed, far = in_hbm(core, zed, far)
     far_low = send(below_low, next_z)

time: 143 us -> 134 us (0.937)
  waiting for transfers between devices: 31.9 us -> 24.5 us
    all_to_all x1, waiting for transfers between devices: 5.78 us -> 0.01 us  [body(): every_row = lax.all_to_all(spread, 'req', 0, 0).reshape(256, WIDTH)]
    reshape x1, local copies, waits for them, and re-layouts: 2.7 us -> 0.25 us  [body(): every_row = lax.all_to_all(spread, 'req', 0, 0).reshape(256, WIDTH)]
    ppermute x22, waiting for transfers between devices: 26.2 us -> 24.5 us  [send(): return lax.ppermute(array, 'req', moves(step))]
    reshape x1, local copies, waits for them, and re-layouts: 1.11 us -> 2.61 us  [body(): back = lax.all_to_all(outgoing.reshape(total, 2, WIDTH), 'req', 0, 0)]
    unnamed x60 -> x54, local copies, waits for them, and re-layouts: 8.08 us -> 8.58 us
  transfers between devices with their start and end apart: 24 -> 24, of which waited for: 7 -> 8; matrix products, arithmetic and copies ran while one was open for 4% -> 2% of each run, Pallas kernels for 30% -> 35%
where the time goes in v6:
time: 134 us; the launch traced here: 133 us
  Pallas kernels  55.7 us (42%)
  starting transfers between devices  37.9 us (28%)
  waiting for transfers between devices  24.5 us (18%)
  local copies, waits for them, and re-layouts  13.3 us (10%)
  between operations  1.62 us (1%)
    ppermute x22, waiting for transfers between devices, send(): return lax.ppermute(array, 'req', moves(step))  24.5 us
    ppermute x22, starting transfers between devices, send(): return lax.ppermute(array, 'req', moves(step))  18.3 us
    pallas_call x3, Pallas kernels, feed_forward(): pl.pallas_call(kernel, out_shape=outputs, in_specs=[vmem] * len(inputs),...  16.8 us
    pallas_call x1, Pallas kernels, decode_attention(): pl.pallas_call(decode_kernel, out_shape=jax.ShapeDtypeStruct((256, QW), B...  15.3 us
    pallas_call x1, Pallas kernels, attention(): pl.pallas_call(attention_kernel, out_shape=(jax.ShapeDtypeStruct((ROWS, W...  12.4 us
    all_to_all x1, starting transfers between devices, body(): every_row = lax.all_to_all(spread, 'req', 0, 0).reshape(256, WIDTH)  11.1 us
    unnamed x54, local copies, waits for them, and re-layouts  8.58 us
    all_to_all x1, starting transfers between devices, body(): back = lax.all_to_all(outgoing.reshape(total, 2, WIDTH), 'req', 0, 0)  8.43 us
  transfers between devices with their start and end apart: 24, of which 8 were waited for; matrix products, arithmetic and copies ran while one was open for 2% of the time, Pallas kernels for 35%

profile of v6, /device:TPU:0, one launch (start us, length us, event | category | flops | bytes accessed | tf_op | source)
XLA Modules:
  0.0 133.0 jit_solution(13373531560771400024)
XLA Ops:
  0.6 1.9 %broadcast_in_dim.2 = bf16[128,2,1280]{2,1,0:T(2,128)(2,1)} broadcast(bf16[2,1280]{1,0:T(2,128)(2,1)} %decode_ref.1), dimensions={1,2} | broadcast | bytes 660480 | tf_op jit(solution)/shard_map/broadcast_in_dim | solution.py:627
  2.5 11.1 %all-to-all-start = ((bf16[128,2,1280]{2,1,0:T(2,128)(2,1)}), bf16[128,2,1280]{2,1,0:T(2,128)(2,1)S(1)}, u32[]{:S(2)}, u32[]{:S(2)}) async-start(bf16[128,2,1280]{2,1,0:T(2,128)(2,1)} %broadcast_in_dim.2), calls=%async_computation | async-start | bytes 1310720 | tf_op jit(solution)/shard_map/all_to_all | solution.py:628
  13.7 0.0 copy-start.18
  13.7 0.7 copy-done.18
  14.4 2.6 %prefill_kv.1.own_ref = bf16[256,640]{1,0:T(8,128)(2,1)S(1)} custom-call(s32[1]{0:T(128)S(6)} %select_n.7.rank_ref, bf16[256,1280]{1,0:T(8,128)(2,1)} %hidden_ref.7, f32[1280]{0:T(1024)S(1)} %copy-done.18, bf16[1280,1920]{1,0:T(8,128)(2,1)} %w_ref.7), custom_call_target="tpu_custom_call" | custom-call | flops 3000000000 | bytes 9000000 | tf_op jit(solution)/shard_map/prefill_kv/pallas_call | solution.py:198
  17.0 0.1 collective-permute-start.1
  17.1 1.2 collective-permute-start
  18.3 1.6 %pack.1 = (bf16[336,1280]{1,0:T(8,128)(2,1)S(1)}, bf16[336,1280]{1,0:T(8,128)(2,1)S(1)}) custom-call(bf16[1,448,1280]{2,1,0:T(8,128)(2,1)} %bitcast.6, bf16[1,224,1280]{2,1,0:T(8,128)(2,1)} %down_ref.1), custom_call_target="tpu_custom_call" | custom-call | flops 1500000000 | bytes 4500000 | tf_op jit(solution)/shard_map/pack/pallas_call | solution.py:141
  19.9 0.0 copy-start.24
  19.9 0.0 copy-start.25
  19.9 0.0 copy-start.26
  20.0 0.9 collective-permute-start.2
  20.9 2.4 %collective-permute-start.3 = (bf16[336,1280]{1,0:T(8,128)(2,1)S(1)}, bf16[336,1280]{1,0:T(8,128)(2,1)}, u32[]{:S(2)}, u32[]{:S(2)}) collective-permute-start(bf16[336,1280]{1,0:T(8,128)(2,1)S(1)} %get-tuple-element.55.refs_4_.refs_12_), channel_id=1, source_target_pairs={{0,6},{1,7},{2,0},{3,1},{4,2},{5,3},{6,4},{7,5},{8,14},{9,15},{10,... | collective-permute-start | bytes 2580488 | tf_op jit(solution)/shard_map/ppermute | solution.py:53
  23.3 3.8 %prefill_query.1.query_ref = bf16[256,1280]{1,0:T(8,128)(2,1)S(1)} custom-call(s32[1]{0:T(128)S(6)} %select_n.7.rank_ref, bf16[256,1280]{1,0:T(8,128)(2,1)} %hidden_ref.7, f32[1280]{0:T(1024)S(1)} %copy-done.19, bf16[1280,1920]{1,0:T(8,128)(2,1)} %w_ref.7), custom_call_target="tpu_custom_call" | custom-call | flops 100000000 | bytes 300000 | tf_op jit(solution)/shard_map/prefill_query/pallas_call | solution.py:198
  27.1 0.0 copy-start.1
  27.1 0.8 copy-done.1
  27.9 1.1 collective-permute-start.13
  29.7 0.2 reshape.23.rows_ref
  30.0 0.0 collective-permute-done.1.core_ref
  30.0 1.0 collective-permute-start.12
  30.9 15.3 %decode.1 = bf16[256,1280]{1,0:T(8,128)(2,1)S(1)} custom-call(s32[1]{0:T(128)} %bitcast.device_ref, s32[4]{0:T(128)S(1)} %copy-done.26, s32[1]{0:T(128)S(6)} %copy.16.count_ref, s32[1,256]{1,0:T(1,128)S(1)} %bitcast.5, s32[8,128]{1,0:T(8,128)S(1)} %bitcast.4, bf16[256,1280]{1,0:T(8,128)(2,1)S(1)} %reshape.23.rows_ref, f32[1280]{0:T(1024)S(1)} %copy-done.19, ...), custom_call_target="tpu_custom_call" | custom-call | flops 16999999488 | bytes 51000000 | tf_op jit(solution)/shard_map/decode/pallas_call | solution.py:366
  46.2 0.9 copy-done.16
  47.1 0.6 collective-permute-done.2.refs_6_.refs_2_
  47.6 2.3 %collective-permute-done.3.refs_16_.refs_10_ = bf16[336,1280]{1,0:T(8,128)(2,1)} collective-permute-done((bf16[336,1280]{1,0:T(8,128)(2,1)S(1)}, bf16[336,1280]{1,0:T(8,128)(2,1)}, u32[]{:S(2)}, u32[]{:S(2)}) %collective-permute-start.3) | collective-permute-done | bytes 860192 | tf_op jit(solution)/shard_map/ppermute | solution.py:53
  49.9 0.0 collective-permute-start.6
  49.9 0.5 collective-permute-start.7
  50.4 0.1 collective-permute-start.4
  50.5 2.6 %reshape.26 = bf16[128,2,1280]{2,1,0:T(2,128)(2,1)} reshape(bf16[256,1280]{1,0:T(8,128)(2,1)} %copy-done.16) | data formatting | bytes 1310720 | tf_op jit(solution)/shard_map/reshape | solution.py:665
  53.1 8.4 %all-to-all-start.1 = ((bf16[128,2,1280]{2,1,0:T(2,128)(2,1)}), bf16[128,2,1280]{2,1,0:T(2,128)(2,1)}, u32[]{:S(2)}, u32[]{:S(2)}) async-start(bf16[128,2,1280]{2,1,0:T(2,128)(2,1)} %reshape.26), calls=%async_computation.1 | async-start | bytes 1310720 | tf_op jit(solution)/shard_map/all_to_all | solution.py:665
  61.6 13.4 %collective-permute-done.13.refs_8_.refs_4_ = bf16[336,1280]{1,0:T(8,128)(2,1)} collective-permute-done((bf16[336,1280]{1,0:T(8,128)(2,1)S(1)}, bf16[336,1280]{1,0:T(8,128)(2,1)}, u32[]{:S(2)}, u32[]{:S(2)}) %collective-permute-start.13) | collective-permute-done | bytes 860192 | tf_op jit(solution)/shard_map/ppermute | solution.py:53
  74.9 0.0 collective-permute-start.8
  75.0 0.0 collective-permute-done.12.refs_14_.refs_8_
  75.0 3.2 %collective-permute-start.9 = (bf16[336,1280]{1,0:T(8,128)(2,1)}, bf16[336,1280]{1,0:T(8,128)(2,1)}, u32[]{:S(2)}, u32[]{:S(2)}) collective-permute-start(bf16[336,1280]{1,0:T(8,128)(2,1)} %collective-permute-done.3.refs_16_.refs_10_), channel_id=1, source_target_pairs={{0,6},{1,7},{2,0},{3,1},{4,2},{5,3},{6,4},{7,5},{8,14},{9,15},{10,... | collective-permute-start | bytes 2580488 | tf_op jit(solution)/shard_map/ppermute | solution.py:53
  78.2 0.0 collective-permute-done.4.far_ref
  78.2 0.0 collective-permute-start.5
  78.2 12.4 %attention.1 = (bf16[256,1280]{1,0:T(8,128)(2,1)S(1)}, bf16[128,1280]{1,0:T(8,128)(2,1)}, bf16[128,1280]{1,0:T(8,128)(2,1)}) custom-call(s32[1]{0:T(128)S(6)} %select_n.7.rank_ref, bf16[256,1280]{1,0:T(8,128)(2,1)} %copy-done.1, bf16[256,640]{1,0:T(8,128)(2,1)} %copy-done.17, bf16[256,640]{1,0:T(8,128)(2,1)} %collective-permute-done.1.core_ref, ...), custom_call_target="tpu_custom_call" | custom-call | flops 100000000 | bytes 300000 | tf_op jit(solution)/shard_map/attention/pallas_call | solution.py:478
  90.6 0.8 copy-done.22
  91.4 0.9 copy-done.10
  92.3 0.6 collective-permute-start.10
  92.9 0.9 copy-done.13
  93.8 2.7 %collective-permute-start.11 = (bf16[128,1280]{1,0:T(8,128)(2,1)}, bf16[128,1280]{1,0:T(8,128)(2,1)}, u32[]{:S(2)}, u32[]{:S(2)}) collective-permute-start(bf16[128,1280]{1,0:T(8,128)(2,1)} %get-tuple-element.52.refs_1_), channel_id=1, source_target_pairs={{0,24},{1,25},{2,26},{3,27},{4,28},{5,29},{6,30},{7,31},{8,0},{9,1... | collective-permute-start | bytes 983048 | tf_op jit(solution)/shard_map/ppermute | solution.py:53
  96.5 1.2 copy-done.11
  97.7 1.2 copy-done.14
  98.8 2.6 %feed_first.1.refs_14_ = f32[256,1280]{1,0:T(8,128)S(1)} custom-call(bf16[128,1280]{1,0:T(8,128)(2,1)} %get-tuple-element.51.refs_0_, bf16[128,1280]{1,0:T(8,128)(2,1)} %get-tuple-element.52.refs_1_, bf16[336,1280]{1,0:T(8,128)(2,1)S(1)} %copy-done.5, bf16[336,1280]{1,0:T(8,128)(2,1)S(1)} %copy-done.11, bf16[336,1280]{1,0:T(8,128)(2,1)S(1)} %copy-done.8, ...), custom_call_target="tpu_custom_call" | custom-call | flops 100000000 | bytes 300000 | tf_op jit(solution)/shard_map/feed_first/pallas_call | solution.py:567
  101.4 1.1 copy-done.2
  102.6 0.0 all-to-all-done.1.back_ref
  102.6 1.4 %collective-permute-done.10.refs_0_ = bf16[128,1280]{1,0:T(8,128)(2,1)} collective-permute-done((bf16[128,1280]{1,0:T(8,128)(2,1)}, bf16[128,1280]{1,0:T(8,128)(2,1)}, u32[]{:S(2)}, u32[]{:S(2)}) %collective-permute-start.10) | collective-permute-done | bytes 327712 | tf_op jit(solution)/shard_map/ppermute | solution.py:53
  104.0 0.0 collective-permute-start.17
  104.0 2.3 %decode_rows.1 = (bf16[16,1280]{1,0:T(8,128)(2,1)S(1)}, bf16[16,1280]{1,0:T(8,128)(2,1)S(1)}) custom-call(bf16[128,2,1280]{2,1,0:T(2,128)(2,1)} %all-to-all-done.1.back_ref, bf16[1280,1280]{1,0:T(8,128)(2,1)S(1)} %copy-done, bf16[2,1280]{1,0:T(2,128)(2,1)S(1)} %copy-done.21, f32[1280]{0:T(1024)S(1)} %copy-done.20), custom_call_target="tpu_custom_call" | custom-call | flops 3000000000 | bytes 9000000 | tf_op jit(solution)/shard_map/decode_rows/pallas_call | solution.py:524
  106.3 0.0 collective-permute-done.11.refs_2_
  106.4 0.0 copy-start.23
  106.4 0.6 collective-permute-start.14
  106.9 0.1 collective-permute-start.15
  107.0 0.4 collective-permute-start.16
  107.5 0.1 collective-permute-start.18
  107.6 5.2 %collective-permute-done.19.refs_1_ = bf16[16,1280]{1,0:T(8,128)(2,1)S(1)} collective-permute-done((bf16[16,1280]{1,0:T(8,128)(2,1)S(1)}, bf16[16,1280]{1,0:T(8,128)(2,1)S(1)}, u32[]{:S(2)}, u32[]{:S(2)}) %collective-permute-start.19) | collective-permute-done | bytes 40992 | tf_op jit(solution)/shard_map/ppermute | solution.py:53
  112.8 0.1 collective-permute-done.18.refs_19_.refs_13_
  112.9 7.7 %feed_guest.1 = (bf16[144,1280]{1,0:T(8,128)(2,1)S(1)}, bf16[128,1280]{1,0:T(8,128)(2,1)S(1)}, bf16[16,1280]{1,0:T(8,128)(2,1)S(1)}) custom-call(bf16[128,1280]{1,0:T(8,128)(2,1)} %collective-permute-done.10.refs_0_, bf16[16,1280]{1,0:T(8,128)(2,1)S(1)} %collective-permute-done.19.refs_1_, bf16[128,1280]{1,0:T(8,128)(2,1)} %collective-permute-done.11.refs_2_, ...), custom_call_target="tpu_custom_call" | custom-call | flops 8000000000 | bytes 24000000 | tf_op jit(solution)/shard_map/feed_guest/pallas_call | solution.py:567
  120.6 0.1 collective-permute-start.21
  120.7 3.2 %collective-permute-start.20 = (bf16[144,1280]{1,0:T(8,128)(2,1)S(1)}, bf16[144,1280]{1,0:T(8,128)(2,1)S(1)}, u32[]{:S(2)}, u32[]{:S(2)}) collective-permute-start(bf16[144,1280]{1,0:T(8,128)(2,1)S(1)} %get-tuple-element.74), channel_id=1, source_target_pairs={{0,24},{1,25},{2,26},{3,27},{4,28},{5,29},{6,30},{7,31},{8,0},{9,1... | collective-permute-start | bytes 1105928 | tf_op jit(solution)/shard_map/ppermute | solution.py:53
  124.0 6.5 %feed_second.1.start_ref = f32[256,1280]{1,0:T(8,128)S(1)} custom-call(bf16[128,1280]{1,0:T(8,128)(2,1)} %get-tuple-element.51.refs_0_, bf16[128,1280]{1,0:T(8,128)(2,1)} %get-tuple-element.52.refs_1_, bf16[336,1280]{1,0:T(8,128)(2,1)} %collective-permute-done.2.refs_6_.refs_2_, bf16[336,1280]{1,0:T(8,128)(2,1)} %collective-permute-done.5.refs_7_.refs_3_, ...), custom_call_target="tpu_custom_call" | custom-call | flops 6000000000 | bytes 18000000 | tf_op jit(solution)/shard_map/feed_second/pallas_call | solution.py:567
  130.4 1.5 %collective-permute-done.21.second_ref = bf16[128,1280]{1,0:T(8,128)(2,1)S(1)} collective-permute-done((bf16[128,1280]{1,0:T(8,128)(2,1)S(1)}, bf16[128,1280]{1,0:T(8,128)(2,1)S(1)}, u32[]{:S(2)}, u32[]{:S(2)}) %collective-permute-start.21) | collective-permute-done | bytes 327712 | tf_op jit(solution)/shard_map/ppermute | solution.py:53
  131.9 0.1 collective-permute-done.20.first_ref
  132.0 1.0 final.1
  (51 shorter events, 0.1 us)
Async XLA Ops:
  2.5 27.2 %all-to-all-start = ((bf16[128,2,1280]{2,1,0:T(2,128)(2,1)}), bf16[128,2,1280]{2,1,0:T(2,128)(2,1)S(1)}, u32[]{:S(2)}, u32[]{:S(2)}) async-start(bf16[128,2,1280]{2,1,0:T(2,128)(2,1)} %broadcast_in_dim.2), calls=%async_computation | async-start | bytes 1310720 | tf_op jit(solution)/shard_map/all_to_all | solution.py:628
  13.7 0.7 copy-start.18
  17.0 2.9 %copy-start.17 = (bf16[256,640]{1,0:T(8,128)(2,1)}, bf16[256,640]{1,0:T(8,128)(2,1)S(1)}, u32[]{:S(2)}) copy-start(bf16[256,640]{1,0:T(8,128)(2,1)S(1)} %prefill_kv.1.own_ref) | copy-start | bytes 983044
  17.0 13.0 %collective-permute-start.1 = (bf16[256,640]{1,0:T(8,128)(2,1)S(1)}, bf16[256,640]{1,0:T(8,128)(2,1)}, u32[]{:S(2)}, u32[]{:S(2)}) collective-permute-start(bf16[256,640]{1,0:T(8,128)(2,1)S(1)} %prefill_kv.1.own_ref), channel_id=1, source_target_pairs={{0,1},{1,0},{2,3},{3,2},{4,5},{5,4},{6,7},{7,6},{8,9},{9,8},{10,11... | collective-permute-start | bytes 983048 | tf_op jit(solution)/shard_map/ppermute | solution.py:53
  17.1 30.0 %collective-permute-start = (bf16[256,640]{1,0:T(8,128)(2,1)S(1)}, bf16[256,640]{1,0:T(8,128)(2,1)}, u32[]{:S(2)}, u32[]{:S(2)}) collective-permute-start(bf16[256,640]{1,0:T(8,128)(2,1)S(1)} %prefill_kv.1.own_ref), channel_id=1, source_target_pairs={{0,2},{1,3},{2,0},{3,1},{4,6},{5,7},{6,4},{7,5},{8,10},{9,11},{10,... | collective-permute-start | bytes 983048 | tf_op jit(solution)/shard_map/ppermute | solution.py:53
  18.3 4.9 %copy-start.19 = (f32[1280]{0:T(1024)S(1)}, f32[1280]{0:T(1024)}, u32[]{:S(2)}) copy-start(f32[1280]{0:T(1024)} %gain_ref.7) | copy-start | bytes 15364
  19.9 30.0 %copy-start.4 = (bf16[336,1280]{1,0:T(8,128)(2,1)}, bf16[336,1280]{1,0:T(8,128)(2,1)S(1)}, u32[]{:S(2)}) copy-start(bf16[336,1280]{1,0:T(8,128)(2,1)S(1)} %get-tuple-element.54.refs_2_.refs_4_) | copy-start | bytes 2580484
  19.9 30.0 %copy-start.7 = (bf16[336,1280]{1,0:T(8,128)(2,1)}, bf16[336,1280]{1,0:T(8,128)(2,1)S(1)}, u32[]{:S(2)}) copy-start(bf16[336,1280]{1,0:T(8,128)(2,1)S(1)} %get-tuple-element.55.refs_4_.refs_12_) | copy-start | bytes 2580484
  19.9 11.0 %copy-start.24 = (s32[1024]{0:T(1024)S(1)}, s32[1024]{0:T(1024)}, u32[]{:S(2)}) copy-start(s32[1024]{0:T(1024)} %param.26) | copy-start | bytes 12292
  19.9 11.0 %copy-start.25 = (s32[256]{0:T(256)S(1)}, s32[256]{0:T(256)}, u32[]{:S(2)}) copy-start(s32[256]{0:T(256)} %param.24) | copy-start | bytes 3076
  19.9 11.0 %copy-start.26 = (s32[4]{0:T(128)S(1)}, s32[4]{0:T(128)}, u32[]{:S(2)}) copy-start(s32[4]{0:T(128)} %length_ref.1) | copy-start | bytes 52
  20.0 27.7 %collective-permute-start.2 = (bf16[336,1280]{1,0:T(8,128)(2,1)S(1)}, bf16[336,1280]{1,0:T(8,128)(2,1)}, u32[]{:S(2)}, u32[]{:S(2)}) collective-permute-start(bf16[336,1280]{1,0:T(8,128)(2,1)S(1)} %get-tuple-element.54.refs_2_.refs_4_), channel_id=1, source_target_pairs={{0,2},{1,3},{2,4},{3,5},{4,6},{5,7},{6,0},{7,1},{8,10},{9,11},{10,... | collective-permute-start | bytes 2580488 | tf_op jit(solution)/shard_map/ppermute | solution.py:53
  20.9 29.0 %collective-permute-start.3 = (bf16[336,1280]{1,0:T(8,128)(2,1)S(1)}, bf16[336,1280]{1,0:T(8,128)(2,1)}, u32[]{:S(2)}, u32[]{:S(2)}) collective-permute-start(bf16[336,1280]{1,0:T(8,128)(2,1)S(1)} %get-tuple-element.55.refs_4_.refs_12_), channel_id=1, source_target_pairs={{0,6},{1,7},{2,0},{3,1},{4,2},{5,3},{6,4},{7,5},{8,14},{9,15},{10,... | collective-permute-start | bytes 2580488 | tf_op jit(solution)/shard_map/ppermute | solution.py:53
  27.1 0.8 copy-start.1
  27.9 47.0 %collective-permute-start.13 = (bf16[336,1280]{1,0:T(8,128)(2,1)S(1)}, bf16[336,1280]{1,0:T(8,128)(2,1)}, u32[]{:S(2)}, u32[]{:S(2)}) collective-permute-start(bf16[336,1280]{1,0:T(8,128)(2,1)S(1)} %get-tuple-element.54.refs_2_.refs_4_), channel_id=1, source_target_pairs={{0,6},{1,7},{2,0},{3,1},{4,2},{5,3},{6,4},{7,5},{8,14},{9,15},{10,... | collective-permute-start | bytes 2580488 | tf_op jit(solution)/shard_map/ppermute | solution.py:53
  30.0 45.0 %collective-permute-start.12 = (bf16[336,1280]{1,0:T(8,128)(2,1)S(1)}, bf16[336,1280]{1,0:T(8,128)(2,1)}, u32[]{:S(2)}, u32[]{:S(2)}) collective-permute-start(bf16[336,1280]{1,0:T(8,128)(2,1)S(1)} %get-tuple-element.55.refs_4_.refs_12_), channel_id=1, source_target_pairs={{0,2},{1,3},{2,4},{3,5},{4,6},{5,7},{6,0},{7,1},{8,10},{9,11},{10,... | collective-permute-start | bytes 2580488 | tf_op jit(solution)/shard_map/ppermute | solution.py:53
  46.2 0.9 copy-start.16
  47.1 31.1 %copy-start.20 = (f32[1280]{0:T(1024)S(1)}, f32[1280]{0:T(1024)}, u32[]{:S(2)}) copy-start(f32[1280]{0:T(1024)} %gain_ref.9) | copy-start | bytes 15364
  49.9 41.5 %collective-permute-start.6 = (bf16[336,1280]{1,0:T(8,128)(2,1)S(1)}, bf16[336,1280]{1,0:T(8,128)(2,1)S(1)}, u32[]{:S(2)}, u32[]{:S(2)}) collective-permute-start(bf16[336,1280]{1,0:T(8,128)(2,1)S(1)} %get-tuple-element.54.refs_2_.refs_4_), channel_id=1, source_target_pairs={{0,1},{1,0},{2,3},{3,2},{4,5},{5,4},{6,7},{7,6},{8,9},{9,8},{10,11... | collective-permute-start | bytes 2580488 | tf_op jit(solution)/shard_map/ppermute | solution.py:53
  49.9 43.0 %collective-permute-start.7 = (bf16[336,1280]{1,0:T(8,128)(2,1)S(1)}, bf16[336,1280]{1,0:T(8,128)(2,1)S(1)}, u32[]{:S(2)}, u32[]{:S(2)}) collective-permute-start(bf16[336,1280]{1,0:T(8,128)(2,1)S(1)} %get-tuple-element.55.refs_4_.refs_12_), channel_id=1, source_target_pairs={{0,1},{1,0},{2,3},{3,2},{4,5},{5,4},{6,7},{7,6},{8,9},{9,8},{10,11... | collective-permute-start | bytes 2580488 | tf_op jit(solution)/shard_map/ppermute | solution.py:53
  50.4 27.7 %collective-permute-start.4 = (bf16[256,640]{1,0:T(8,128)(2,1)}, bf16[256,640]{1,0:T(8,128)(2,1)}, u32[]{:S(2)}, u32[]{:S(2)}) collective-permute-start(bf16[256,640]{1,0:T(8,128)(2,1)} %collective-permute-done.zed_ref), channel_id=1, source_target_pairs={{0,1},{1,0},{2,3},{3,2},{4,5},{5,4},{6,7},{7,6},{8,9},{9,8},{10,11... | collective-permute-start | bytes 983048 | tf_op jit(solution)/shard_map/ppermute | solution.py:53
  53.1 49.4 %all-to-all-start.1 = ((bf16[128,2,1280]{2,1,0:T(2,128)(2,1)}), bf16[128,2,1280]{2,1,0:T(2,128)(2,1)}, u32[]{:S(2)}, u32[]{:S(2)}) async-start(bf16[128,2,1280]{2,1,0:T(2,128)(2,1)} %reshape.26), calls=%async_computation.1 | async-start | bytes 1310720 | tf_op jit(solution)/shard_map/all_to_all | solution.py:665
  61.6 34.9 %copy-start.5 = (bf16[336,1280]{1,0:T(8,128)(2,1)S(1)}, bf16[336,1280]{1,0:T(8,128)(2,1)}, u32[]{:S(2)}) copy-start(bf16[336,1280]{1,0:T(8,128)(2,1)} %copy-done.4) | copy-start | bytes 2580484
  61.6 34.9 %copy-start.8 = (bf16[336,1280]{1,0:T(8,128)(2,1)S(1)}, bf16[336,1280]{1,0:T(8,128)(2,1)}, u32[]{:S(2)}) copy-start(bf16[336,1280]{1,0:T(8,128)(2,1)} %copy-done.7) | copy-start | bytes 2580484
  74.9 31.4 %collective-permute-start.8 = (bf16[336,1280]{1,0:T(8,128)(2,1)}, bf16[336,1280]{1,0:T(8,128)(2,1)}, u32[]{:S(2)}, u32[]{:S(2)}) collective-permute-start(bf16[336,1280]{1,0:T(8,128)(2,1)} %collective-permute-done.2.refs_6_.refs_2_), channel_id=1, source_target_pairs={{0,2},{1,3},{2,4},{3,5},{4,6},{5,7},{6,0},{7,1},{8,10},{9,11},{10,... | collective-permute-start | bytes 2580488 | tf_op jit(solution)/shard_map/ppermute | solution.py:53
  75.0 31.4 %collective-permute-start.9 = (bf16[336,1280]{1,0:T(8,128)(2,1)}, bf16[336,1280]{1,0:T(8,128)(2,1)}, u32[]{:S(2)}, u32[]{:S(2)}) collective-permute-start(bf16[336,1280]{1,0:T(8,128)(2,1)} %collective-permute-done.3.refs_16_.refs_10_), channel_id=1, source_target_pairs={{0,6},{1,7},{2,0},{3,1},{4,2},{5,3},{6,4},{7,5},{8,14},{9,15},{10,... | collective-permute-start | bytes 2580488 | tf_op jit(solution)/shard_map/ppermute | solution.py:53
  78.2 29.3 %collective-permute-start.5 = (bf16[336,1280]{1,0:T(8,128)(2,1)}, bf16[336,1280]{1,0:T(8,128)(2,1)}, u32[]{:S(2)}, u32[]{:S(2)}) collective-permute-start(bf16[336,1280]{1,0:T(8,128)(2,1)} %collective-permute-done.2.refs_6_.refs_2_), channel_id=1, source_target_pairs={{0,1},{1,0},{2,3},{3,2},{4,5},{5,4},{6,7},{7,6},{8,9},{9,8},{10,11... | collective-permute-start | bytes 2580488 | tf_op jit(solution)/shard_map/ppermute | solution.py:53
  90.6 0.8 copy-start.22
  91.4 0.9 copy-start.10
  92.3 11.6 %collective-permute-start.10 = (bf16[128,1280]{1,0:T(8,128)(2,1)}, bf16[128,1280]{1,0:T(8,128)(2,1)}, u32[]{:S(2)}, u32[]{:S(2)}) collective-permute-start(bf16[128,1280]{1,0:T(8,128)(2,1)} %get-tuple-element.51.refs_0_), channel_id=1, source_target_pairs={{0,8},{1,9},{2,10},{3,11},{4,12},{5,13},{6,14},{7,15},{8,16},{9,17... | collective-permute-start | bytes 983048 | tf_op jit(solution)/shard_map/ppermute | solution.py:53
  92.9 0.9 copy-start.13
  93.8 10.1 %copy-start = (bf16[1280,1280]{1,0:T(8,128)(2,1)S(1)}, bf16[1280,1280]{1,0:T(8,128)(2,1)}, u32[]{:S(2)}) copy-start(bf16[1280,1280]{1,0:T(8,128)(2,1)} %w_ref.9) | copy-start | bytes 9830404
  93.8 12.5 %collective-permute-start.11 = (bf16[128,1280]{1,0:T(8,128)(2,1)}, bf16[128,1280]{1,0:T(8,128)(2,1)}, u32[]{:S(2)}, u32[]{:S(2)}) collective-permute-start(bf16[128,1280]{1,0:T(8,128)(2,1)} %get-tuple-element.52.refs_1_), channel_id=1, source_target_pairs={{0,24},{1,25},{2,26},{3,27},{4,28},{5,29},{6,30},{7,31},{8,0},{9,1... | collective-permute-start | bytes 983048 | tf_op jit(solution)/shard_map/ppermute | solution.py:53
  96.5 1.2 copy-start.11
  97.7 1.2 copy-start.14
  98.8 5.1 %copy-start.21 = (bf16[2,1280]{1,0:T(2,128)(2,1)S(1)}, bf16[2,1280]{1,0:T(2,128)(2,1)}, u32[]{:S(2)}) copy-start(bf16[2,1280]{1,0:T(2,128)(2,1)} %decode_ref.1) | copy-start | bytes 15364
  101.4 1.1 copy-start.2
  102.6 10.3 %copy-start.6 = (bf16[336,1280]{1,0:T(8,128)(2,1)S(1)}, bf16[336,1280]{1,0:T(8,128)(2,1)}, u32[]{:S(2)}) copy-start(bf16[336,1280]{1,0:T(8,128)(2,1)} %copy-done.4) | copy-start | bytes 2580484
  102.6 10.3 %copy-start.9 = (bf16[336,1280]{1,0:T(8,128)(2,1)S(1)}, bf16[336,1280]{1,0:T(8,128)(2,1)}, u32[]{:S(2)}) copy-start(bf16[336,1280]{1,0:T(8,128)(2,1)} %copy-done.7) | copy-start | bytes 2580484
  102.6 10.3 %copy-start.12 = (bf16[336,1280]{1,0:T(8,128)(2,1)S(1)}, bf16[336,1280]{1,0:T(8,128)(2,1)}, u32[]{:S(2)}) copy-start(bf16[336,1280]{1,0:T(8,128)(2,1)} %copy-done.10) | copy-start | bytes 2580484
  102.6 10.3 %copy-start.15 = (bf16[336,1280]{1,0:T(8,128)(2,1)S(1)}, bf16[336,1280]{1,0:T(8,128)(2,1)}, u32[]{:S(2)}) copy-start(bf16[336,1280]{1,0:T(8,128)(2,1)} %copy-done.13) | copy-start | bytes 2580484
  104.0 3.6 %collective-permute-start.17 = (bf16[336,1280]{1,0:T(8,128)(2,1)}, bf16[336,1280]{1,0:T(8,128)(2,1)S(1)}, u32[]{:S(2)}, u32[]{:S(2)}) collective-permute-start(bf16[336,1280]{1,0:T(8,128)(2,1)} %collective-permute-done.3.refs_16_.refs_10_), channel_id=1, source_target_pairs={{0,1},{1,0},{2,3},{3,2},{4,5},{5,4},{6,7},{7,6},{8,9},{9,8},{10,11... | collective-permute-start | bytes 2580488 | tf_op jit(solution)/shard_map/ppermute | solution.py:53
  106.3 17.6 %copy-start.3 = (f32[256,1280]{1,0:T(8,128)S(1)}, f32[256,1280]{1,0:T(8,128)}, u32[]{:S(2)}) copy-start(f32[256,1280]{1,0:T(8,128)} %copy-done.2) | copy-start | bytes 3932164
  106.4 17.6 %copy-start.23 = (bf16[256,1280]{1,0:T(8,128)(2,1)S(1)}, bf16[256,1280]{1,0:T(8,128)(2,1)}, u32[]{:S(2)}) copy-start(bf16[256,1280]{1,0:T(8,128)(2,1)} %copy-done.22) | copy-start | bytes 1966084
  106.4 6.4 %collective-permute-start.14 = (bf16[336,1280]{1,0:T(8,128)(2,1)}, bf16[336,1280]{1,0:T(8,128)(2,1)S(1)}, u32[]{:S(2)}, u32[]{:S(2)}) collective-permute-start(bf16[336,1280]{1,0:T(8,128)(2,1)} %collective-permute-done.13.refs_8_.refs_4_), channel_id=1, source_target_pairs={{0,1},{1,0},{2,3},{3,2},{4,5},{5,4},{6,7},{7,6},{8,9},{9,8},{10,11... | collective-permute-start | bytes 2580488 | tf_op jit(solution)/shard_map/ppermute | solution.py:53
  106.9 5.8 %collective-permute-start.15 = (bf16[336,1280]{1,0:T(8,128)(2,1)}, bf16[336,1280]{1,0:T(8,128)(2,1)S(1)}, u32[]{:S(2)}, u32[]{:S(2)}) collective-permute-start(bf16[336,1280]{1,0:T(8,128)(2,1)} %collective-permute-done.8.refs_10_.refs_6_), channel_id=1, source_target_pairs={{0,1},{1,0},{2,3},{3,2},{4,5},{5,4},{6,7},{7,6},{8,9},{9,8},{10,11... | collective-permute-start | bytes 2580488 | tf_op jit(solution)/shard_map/ppermute | solution.py:53
  107.0 5.7 %collective-permute-start.16 = (bf16[336,1280]{1,0:T(8,128)(2,1)}, bf16[336,1280]{1,0:T(8,128)(2,1)S(1)}, u32[]{:S(2)}, u32[]{:S(2)}) collective-permute-start(bf16[336,1280]{1,0:T(8,128)(2,1)} %collective-permute-done.12.refs_14_.refs_8_), channel_id=1, source_target_pairs={{0,1},{1,0},{2,3},{3,2},{4,5},{5,4},{6,7},{7,6},{8,9},{9,8},{10,11... | collective-permute-start | bytes 2580488 | tf_op jit(solution)/shard_map/ppermute | solution.py:53
  107.5 5.4 %collective-permute-start.18 = (bf16[336,1280]{1,0:T(8,128)(2,1)}, bf16[336,1280]{1,0:T(8,128)(2,1)S(1)}, u32[]{:S(2)}, u32[]{:S(2)}) collective-permute-start(bf16[336,1280]{1,0:T(8,128)(2,1)} %collective-permute-done.9.refs_18_.refs_12_), channel_id=1, source_target_pairs={{0,1},{1,0},{2,3},{3,2},{4,5},{5,4},{6,7},{7,6},{8,9},{9,8},{10,11... | collective-permute-start | bytes 2580488 | tf_op jit(solution)/shard_map/ppermute | solution.py:53
  107.6 5.2 %collective-permute-start.19 = (bf16[16,1280]{1,0:T(8,128)(2,1)S(1)}, bf16[16,1280]{1,0:T(8,128)(2,1)S(1)}, u32[]{:S(2)}, u32[]{:S(2)}) collective-permute-start(bf16[16,1280]{1,0:T(8,128)(2,1)S(1)} %get-tuple-element.65.refs_3_), channel_id=1, source_target_pairs={{0,8},{1,9},{2,10},{3,11},{4,12},{5,13},{6,14},{7,15},{8,16},{9,17... | collective-permute-start | bytes 122888 | tf_op jit(solution)/shard_map/ppermute | solution.py:53
  120.6 11.3 %collective-permute-start.21 = (bf16[128,1280]{1,0:T(8,128)(2,1)S(1)}, bf16[128,1280]{1,0:T(8,128)(2,1)S(1)}, u32[]{:S(2)}, u32[]{:S(2)}) collective-permute-start(bf16[128,1280]{1,0:T(8,128)(2,1)S(1)} %get-tuple-element.75), channel_id=1, source_target_pairs={{0,8},{1,9},{2,10},{3,11},{4,12},{5,13},{6,14},{7,15},{8,16},{9,17... | collective-permute-start | bytes 983048 | tf_op jit(solution)/shard_map/ppermute | solution.py:53
  120.7 11.3 %collective-permute-start.20 = (bf16[144,1280]{1,0:T(8,128)(2,1)S(1)}, bf16[144,1280]{1,0:T(8,128)(2,1)S(1)}, u32[]{:S(2)}, u32[]{:S(2)}) collective-permute-start(bf16[144,1280]{1,0:T(8,128)(2,1)S(1)} %get-tuple-element.74), channel_id=1, source_target_pairs={{0,24},{1,25},{2,26},{3,27},{4,28},{5,29},{6,30},{7,31},{8,0},{9,1... | collective-permute-start | bytes 1105928 | tf_op jit(solution)/shard_map/ppermute | solution.py:53

commit v7 on v6

--- a/solution.py
+++ b/solution.py
@@ -129,28 +129,43 @@
     return chunk * cosine + other * sine
 
 
-def pack_kernel(gate_up_ref, down_ref, low_ref, high_ref):
-    low_ref[...] = gate_up_ref[:PART, :]
-    high_ref[: 2 * SHARE - PART, :] = gate_up_ref[PART:, :]
-    high_ref[2 * SHARE - PART :, :] = down_ref[...]
+def pack_kernel(gate_up_ref, down_ref, packed_ref):
+    packed_ref[: 2 * SHARE, :] = gate_up_ref[...]
+    packed_ref[2 * SHARE :, :] = down_ref[...]
 
 
 def pack_weights(gate_up, down):
-    half = jax.ShapeDtypeStruct((PART, WIDTH), BF)
-    block = pl.BlockSpec((PART, WIDTH // 2), lambda i: (0, i))
     return pl.pallas_call(
         pack_kernel,
-        out_shape=(half, half),
+        out_shape=jax.ShapeDtypeStruct((3 * SHARE, WIDTH), BF),
         grid=(2,),
         in_specs=[
             pl.BlockSpec((None, 2 * SHARE, WIDTH // 2), lambda i: (0, 0, i)),
             pl.BlockSpec((None, SHARE, WIDTH // 2), lambda i: (0, 0, i)),
         ],
-        out_specs=(block, block),
+        out_specs=pl.BlockSpec((3 * SHARE, WIDTH // 2), lambda i: (0, i)),
         compiler_params=pltpu.CompilerParams(vmem_limit_bytes=VMEM_LIMIT),
         cost_estimate=cost(1.5),
         name="pack",
     )(gate_up, down)
+
+
+def cut_kernel(below_ref, above_ref, low_ref, high_ref):
+    low_ref[...] = below_ref[:PART, :]
+    high_ref[...] = above_ref[PART:, :]
+
+
+def cut_halves(below, above):
+    vmem = pl.BlockSpec(memory_space=pltpu.VMEM)
+    return pl.pallas_call(
+        cut_kernel,
+        out_shape=(jax.ShapeDtypeStruct((PART, WIDTH), BF),) * 2,
+        in_specs=[vmem] * 2,
+        out_specs=(vmem,) * 2,
+        compiler_params=pltpu.CompilerParams(vmem_limit_bytes=VMEM_LIMIT),
+        cost_estimate=cost(0.5),
+        name="cut",
+    )(below, above)
 
 
 def kv_kernel(rank_ref, hidden_ref, gain_ref, w_ref, kv_ref):
@@ -527,38 +542,40 @@
         in_specs=[vmem] * 4,
         out_specs=(vmem,) * 2,
         compiler_params=pltpu.CompilerParams(vmem_limit_bytes=VMEM_LIMIT),
-        cost_estimate=cost(3),
+        cost_estimate=cost(0.1),
         name="decode_rows",
     )(back, w_out, decode, gain)
 
 
-def hidden_units(rows, lows, highs, act):
+def hidden_units(rows, packs, lows, highs, act):
     cut = 2 * SHARE - PART
-    for k in range(len(lows)):
-        gate_rows = lows[k][:SHARE, :]
-        up_rows = jnp.concatenate([lows[k][SHARE:, :], highs[k][:cut, :]], axis=0)
+    weights = [(ref[:SHARE, :], ref[SHARE : 2 * SHARE, :], ref[2 * SHARE :, :]) for ref in packs]
+    for low, high in zip(lows, highs):
+        up_rows = jnp.concatenate([low[SHARE:, :], high[:cut, :]], axis=0)
+        weights.append((low[:SHARE, :], up_rows, high[cut:, :]))
+    for k, (gate_rows, up_rows, _) in enumerate(weights):
         gate = lax.dot_general(rows, gate_rows, NT, preferred_element_type=F32)
         up = lax.dot_general(rows, up_rows, NT, preferred_element_type=F32)
         act[:, k * SHARE : (k + 1) * SHARE] = (gate / (1.0 + jnp.exp(-gate)) * up).astype(BF)
-    down = jnp.concatenate([ref[cut:, :] for ref in highs], axis=0)
+    down = jnp.concatenate([down_rows for _, _, down_rows in weights], axis=0)
     return jnp.dot(act[...], down, preferred_element_type=F32)
 
 
 def first_kernel(*refs):
     rows = jnp.concatenate([refs[0][...], refs[1][...]], axis=0)
-    refs[6][...] = hidden_units(rows, refs[2:4], refs[4:6], refs[7])
+    refs[4][...] = hidden_units(rows, refs[2:4], (), (), refs[5])
 
 
 def second_kernel(*refs):
     rows = jnp.concatenate([refs[0][...], refs[1][...]], axis=0)
-    down = hidden_units(rows, refs[2:8], refs[8:14], refs[17])
-    refs[16][...] = refs[15][...].astype(F32) + (refs[14][...] + down)
+    down = hidden_units(rows, refs[2:6], refs[6:8], refs[8:10], refs[13])
+    refs[12][...] = refs[11][...].astype(F32) + (refs[10][...] + down)
 
 
 def guest_kernel(*refs):
     rows = jnp.concatenate([ref[...] for ref in refs[:4]], axis=0)
-    down = hidden_units(rows, refs[4:12], refs[12:20], refs[23]).astype(BF)
-    for ref, start, stop in zip(refs[20:23], (0, 144, 272), (144, 272, 288)):
+    down = hidden_units(rows, refs[4:10], refs[10:12], refs[12:14], refs[17]).astype(BF)
+    for ref, start, stop in zip(refs[14:17], (0, 144, 272), (144, 272, 288)):
         ref[...] = down[start:stop]
 
 
@@ -627,17 +644,15 @@
     spread = jnp.broadcast_to(decode_hidden[None], (total, 2, WIDTH))
     every_row = lax.all_to_all(spread, "req", 0, 0).reshape(256, WIDTH)
 
-    low, high = pack_weights(*in_hbm(jnp.swapaxes(w_gate_up, 1, 2), w_down))
+    packed = pack_weights(*in_hbm(jnp.swapaxes(w_gate_up, 1, 2), w_down))
     (kv,) = in_hbm(project(rank, prefill_hidden, gain, w_qkv, True))
     zed = send(kv, pair_z)
     core = send(kv, other_core)
-    low, high, kv = lax.optimization_barrier((low, high, kv))
-    below_low = send(low, next_z)
-    above_high = send(high, last_z)
+    packed, kv = lax.optimization_barrier((packed, kv))
+    below = send(packed, next_z)
+    above = send(packed, last_z)
+    packed_core = send(packed, other_core)
     (query,) = in_hbm(project(rank, prefill_hidden, gain, w_qkv, False))
-    low, high, query = lax.optimization_barrier((low, high, query))
-    below_high = send(high, next_z)
-    above_low = send(low, last_z)
     every_row, query = lax.optimization_barrier((every_row, query))
     outgoing = decode_attention(
         device,
@@ -651,17 +666,15 @@
         key_value_cache,
         held_hidden,
     )
-    outgoing, zed, core, below_low, above_high, low, high = lax.optimization_barrier(
-        (outgoing, zed, core, below_low, above_high, low, high)
-    )
-    low_core = send(low, other_core)
-    high_core = send(high, other_core)
+    outgoing, zed, core, packed_core = lax.optimization_barrier(
+        (outgoing, zed, core, packed_core)
+    )
     far = send(zed, other_core)
     core, zed, far = in_hbm(core, zed, far)
-    far_low = send(below_low, next_z)
-    far_high = send(above_high, last_z)
-    below_low_core = send(below_low, other_core)
-    above_high_core = send(above_high, other_core)
+    below, above, packed_core = lax.optimization_barrier((below, above, packed_core))
+    far_low, far_high = cut_halves(below, above)
+    far_low = send(far_low, next_z)
+    far_high = send(far_high, last_z)
     back = lax.all_to_all(outgoing.reshape(total, 2, WIDTH), "req", 0, 0)
 
     resid, lower, upper = attention(
@@ -671,7 +684,7 @@
     from_next = send(upper, last_x)
     (mine,) = feed_forward(
         first_kernel,
-        (lower, upper, low, low_core, high, high_core),
+        (lower, upper, packed, packed_core),
         (jax.ShapeDtypeStruct((ROWS, WIDTH), F32),),
         ROWS,
         2,
@@ -679,24 +692,21 @@
         "feed_first",
     )
     mine, back = lax.optimization_barrier((mine, back))
+    below, above, back, from_last, from_next = lax.optimization_barrier(
+        (below, above, back, from_last, from_next)
+    )
+    below_core = send(below, other_core)
+    above_core = send(above, other_core)
     extra, alone = decode_rows(back, w_all, decode_hidden, gain2)
-    alone, far_low, far_high, from_last, from_next, below_high, above_low = (
-        lax.optimization_barrier(
-            (alone, far_low, far_high, from_last, from_next, below_high, above_low)
-        )
-    )
+    guest = send(alone, next_x)
+    alone, far_low, far_high = lax.optimization_barrier((alone, far_low, far_high))
     far_low_core = send(far_low, other_core)
     far_high_core = send(far_high, other_core)
-    below_high_core = send(below_high, other_core)
-    above_low_core = send(above_low, other_core)
-    guest = send(alone, next_x)
-    lows = (low, low_core)
-    highs = (high, high_core)
-    lows_far = (below_low, below_low_core, above_low, above_low_core, far_low, far_low_core)
-    highs_far = (below_high, below_high_core, above_high, above_high_core, far_high, far_high_core)
+    gathered = (below, below_core, above, above_core)
+    distant = (far_low, far_low_core, far_high, far_high_core)
     to_last, to_next, alone = feed_forward(
         guest_kernel,
-        (from_last, guest, from_next, alone) + lows + lows_far + highs + highs_far,
+        (from_last, guest, from_next, alone, packed, packed_core) + gathered + distant,
         tuple(jax.ShapeDtypeStruct((n, WIDTH), BF) for n in (144, 128, 16)),
         ROWS + 32,
         8,
@@ -708,7 +718,7 @@
     second = send(to_next, next_x)
     (start,) = feed_forward(
         second_kernel,
-        (lower, upper) + lows_far + highs_far + (mine, resid),
+        (lower, upper) + gathered + distant + (mine, resid),
         (jax.ShapeDtypeStruct((ROWS, WIDTH), F32),),
         ROWS,
         6,

time: 134 us -> 129 us (0.963)
  waiting for transfers between devices: 24.5 us -> 16.9 us
  Pallas kernels: 55.7 us -> 58.4 us
    ppermute x22 -> x17, waiting for transfers between devices: 24.5 us -> 16.9 us  [send(): return lax.ppermute(array, 'req', moves(step))]
    ppermute x22 -> x17, starting transfers between devices: 18.3 us -> 15.2 us  [send(): return lax.ppermute(array, 'req', moves(step))]
    unnamed x54 -> x36, local copies, waits for them, and re-layouts: 8.58 us -> 5.61 us
    reshape x1, local copies, waits for them, and re-layouts: 0.25 us -> 2.71 us  [body(): every_row = lax.all_to_all(spread, 'req', 0, 0).reshape(256, WIDTH)]
    all_to_all x1, starting transfers between devices: 8.43 us -> 10.9 us  [body(): back = lax.all_to_all(outgoing.reshape(total, 2, WIDTH), 'req', 0, 0)]
    pallas_call x1 -> x2, Pallas kernels: 1.56 us -> 3.87 us  [the longest x1 2.46 us: pack_weights(): pl.pallas_call(pack_kernel, out_shape=jax.ShapeDtypeStruct((3 * SHARE, WI...]
  transfers between devices with their start and end apart: 24 -> 19, of which waited for: 8 -> 4; matrix products, arithmetic and copies ran while one was open for 2% -> 4% of each run, Pallas kernels for 35% -> 39%
where the time goes in v7:
time: 129 us; the launch traced here: 127 us
  Pallas kernels  58.4 us (45%)
  starting transfers between devices  37.6 us (29%)
  waiting for transfers between devices  16.9 us (13%)
  local copies, waits for them, and re-layouts  12.8 us (10%)
  between operations  1.56 us (1%)
    ppermute x17, waiting for transfers between devices, send(): return lax.ppermute(array, 'req', moves(step))  16.9 us
    pallas_call x3, Pallas kernels, feed_forward(): pl.pallas_call(kernel, out_shape=outputs, in_specs=[vmem] * len(inputs),...  16.3 us
    pallas_call x1, Pallas kernels, decode_attention(): pl.pallas_call(decode_kernel, out_shape=jax.ShapeDtypeStruct((256, QW), B...  15.2 us
    ppermute x17, starting transfers between devices, send(): return lax.ppermute(array, 'req', moves(step))  15.2 us
    pallas_call x1, Pallas kernels, attention(): pl.pallas_call(attention_kernel, out_shape=(jax.ShapeDtypeStruct((ROWS, W...  12.3 us
    all_to_all x1, starting transfers between devices, body(): every_row = lax.all_to_all(spread, 'req', 0, 0).reshape(256, WIDTH)  11.6 us
    all_to_all x1, starting transfers between devices, body(): back = lax.all_to_all(outgoing.reshape(total, 2, WIDTH), 'req', 0, 0)  10.9 us
    pallas_call x2, Pallas kernels, project(): pl.pallas_call(kv_kernel if keys else query_kernel, out_shape=jax.ShapeDt...  7.14 us
  transfers between devices with their start and end apart: 19, of which 4 were waited for; matrix products, arithmetic and copies ran while one was open for 4% of the time, Pallas kernels for 39%

profile of v7, /device:TPU:0, one launch (start us, length us, event | category | flops | bytes accessed | tf_op | source)
XLA Modules:
  0.0 127.4 jit_solution(2872987971191379749)
XLA Ops:
  0.6 1.9 %broadcast_in_dim.2 = bf16[128,2,1280]{2,1,0:T(2,128)(2,1)} broadcast(bf16[2,1280]{1,0:T(2,128)(2,1)} %decode_ref.1), dimensions={1,2} | broadcast | bytes 660480 | tf_op jit(solution)/shard_map/broadcast_in_dim | solution.py:644
  2.5 11.6 %all-to-all-start = ((bf16[128,2,1280]{2,1,0:T(2,128)(2,1)}), bf16[128,2,1280]{2,1,0:T(2,128)(2,1)}, u32[]{:S(2)}, u32[]{:S(2)}) async-start(bf16[128,2,1280]{2,1,0:T(2,128)(2,1)} %broadcast_in_dim.2), calls=%async_computation | async-start | bytes 1310720 | tf_op jit(solution)/shard_map/all_to_all | solution.py:645
  14.1 0.0 copy-start.12
  14.2 2.5 %pack.1.refs_2_.refs_4_ = bf16[672,1280]{1,0:T(8,128)(2,1)} custom-call(bf16[1,448,1280]{2,1,0:T(8,128)(2,1)} %bitcast.6, bf16[1,224,1280]{2,1,0:T(8,128)(2,1)} %down_ref.1), custom_call_target="tpu_custom_call" | custom-call | flops 1500000000 | bytes 4500000 | tf_op jit(solution)/shard_map/pack/pallas_call | solution.py:138
  16.6 3.3 %prefill_kv.1.own_ref = bf16[256,640]{1,0:T(8,128)(2,1)} custom-call(s32[1]{0:T(128)S(6)} %select_n.7.rank_ref, bf16[256,1280]{1,0:T(8,128)(2,1)} %hidden_ref.7, f32[1280]{0:T(1024)S(1)} %copy-done.12, bf16[1280,1920]{1,0:T(8,128)(2,1)} %w_ref.7), custom_call_target="tpu_custom_call" | custom-call | flops 3000000000 | bytes 9000000 | tf_op jit(solution)/shard_map/prefill_kv/pallas_call | solution.py:213
  19.9 0.0 collective-permute-start.2
  19.9 0.5 collective-permute-start.1
  20.4 1.0 collective-permute-start
  21.5 2.3 %collective-permute-start.5 = (bf16[672,1280]{1,0:T(8,128)(2,1)}, bf16[672,1280]{1,0:T(8,128)(2,1)S(1)}, u32[]{:S(2)}, u32[]{:S(2)}) collective-permute-start(bf16[672,1280]{1,0:T(8,128)(2,1)} %pack.1.refs_2_.refs_4_), channel_id=1, source_target_pairs={{0,6},{1,7},{2,0},{3,1},{4,2},{5,3},{6,4},{7,5},{8,14},{9,15},{10,... | collective-permute-start | bytes 5160968 | tf_op jit(solution)/shard_map/ppermute | solution.py:53
  23.8 0.0 collective-permute-start.4
  24.4 0.0 copy-start.15
  24.5 0.0 copy-start.16
  24.5 0.0 copy-start.17
  24.5 3.8 %prefill_query.1.query_ref = bf16[256,1280]{1,0:T(8,128)(2,1)S(1)} custom-call(s32[1]{0:T(128)S(6)} %select_n.7.rank_ref, bf16[256,1280]{1,0:T(8,128)(2,1)} %hidden_ref.7, f32[1280]{0:T(1024)S(1)} %copy-done.12, bf16[1280,1920]{1,0:T(8,128)(2,1)} %w_ref.7), custom_call_target="tpu_custom_call" | custom-call | flops 100000000 | bytes 300000 | tf_op jit(solution)/shard_map/prefill_query/pallas_call | solution.py:213
  28.3 0.0 copy-start.1
  28.3 0.8 copy-done.1
  29.2 0.0 all-to-all-done
  29.2 2.7 %reshape.23.rows_ref = bf16[256,1280]{1,0:T(8,128)(2,1)} reshape(bf16[128,2,1280]{2,1,0:T(2,128)(2,1)} %all-to-all-done) | data formatting | bytes 1310720 | tf_op jit(solution)/shard_map/reshape | solution.py:645
  31.9 1.1 copy-done.9
  33.0 15.2 %decode.1 = bf16[256,1280]{1,0:T(8,128)(2,1)S(1)} custom-call(s32[1]{0:T(128)} %bitcast.device_ref, s32[4]{0:T(128)S(1)} %copy-done.17, s32[1]{0:T(128)S(6)} %copy.16.count_ref, s32[1,256]{1,0:T(1,128)S(1)} %bitcast.5, s32[8,128]{1,0:T(8,128)S(1)} %bitcast.4, bf16[256,1280]{1,0:T(8,128)(2,1)S(1)} %copy-done.9, f32[1280]{0:T(1024)S(1)} %copy-done.12, ...), custom_call_target="tpu_custom_call" | custom-call | flops 16999999488 | bytes 51000000 | tf_op jit(solution)/shard_map/decode/pallas_call | solution.py:381
  48.2 0.8 copy-done.8
  49.1 0.0 collective-permute-done.1.core_ref
  49.1 0.0 collective-permute-done.zed_ref
  49.1 0.0 collective-permute-done.2.refs_3_.refs_5_
  49.1 0.1 collective-permute-start.3
  49.2 2.6 %reshape.26 = bf16[128,2,1280]{2,1,0:T(2,128)(2,1)} reshape(bf16[256,1280]{1,0:T(8,128)(2,1)} %copy-done.8) | data formatting | bytes 1310720 | tf_op jit(solution)/shard_map/reshape | solution.py:678
  51.8 10.9 %all-to-all-start.1 = ((bf16[128,2,1280]{2,1,0:T(2,128)(2,1)}), bf16[128,2,1280]{2,1,0:T(2,128)(2,1)}, u32[]{:S(2)}, u32[]{:S(2)}) async-start(bf16[128,2,1280]{2,1,0:T(2,128)(2,1)} %reshape.26), calls=%async_computation.1 | async-start | bytes 1310720 | tf_op jit(solution)/shard_map/all_to_all | solution.py:678
  62.7 0.0 collective-permute-done.3.far_ref
  62.7 12.3 %attention.1 = (bf16[256,1280]{1,0:T(8,128)(2,1)S(1)}, bf16[128,1280]{1,0:T(8,128)(2,1)}, bf16[128,1280]{1,0:T(8,128)(2,1)}) custom-call(s32[1]{0:T(128)S(6)} %select_n.7.rank_ref, bf16[256,1280]{1,0:T(8,128)(2,1)} %copy-done.1, bf16[256,640]{1,0:T(8,128)(2,1)} %prefill_kv.1.own_ref, bf16[256,640]{1,0:T(8,128)(2,1)} %collective-permute-done.1.core_ref, ...), custom_call_target="tpu_custom_call" | custom-call | flops 100000000 | bytes 300000 | tf_op jit(solution)/shard_map/attention/pallas_call | solution.py:493
  75.1 0.8 copy-done.13
  75.9 0.7 collective-permute-start.6
  76.6 2.5 %collective-permute-start.7 = (bf16[128,1280]{1,0:T(8,128)(2,1)}, bf16[128,1280]{1,0:T(8,128)(2,1)}, u32[]{:S(2)}, u32[]{:S(2)}) collective-permute-start(bf16[128,1280]{1,0:T(8,128)(2,1)} %get-tuple-element.43.refs_1_), channel_id=1, source_target_pairs={{0,24},{1,25},{2,26},{3,27},{4,28},{5,29},{6,30},{7,31},{8,0},{9,1... | collective-permute-start | bytes 983048 | tf_op jit(solution)/shard_map/ppermute | solution.py:53
  79.1 0.0 collective-permute-done.5.above_ref.refs_8_.refs_4_
  79.1 0.0 collective-permute-done.4.below_ref.refs_6_.refs_2_
  79.2 1.4 %cut.1 = (bf16[336,1280]{1,0:T(8,128)(2,1)}, bf16[336,1280]{1,0:T(8,128)(2,1)}) custom-call(bf16[672,1280]{1,0:T(8,128)(2,1)S(1)} %collective-permute-done.4.below_ref.refs_6_.refs_2_, bf16[672,1280]{1,0:T(8,128)(2,1)S(1)} %collective-permute-done.5.above_ref.refs_8_.refs_4_), custom_call_target="tpu_custom_call" | custom-call | flops 500000000 | bytes 1500000 | tf_op jit(solution)/shard_map/cut/pallas_call | solution.py:160
  80.6 0.3 copy-done.2
  80.9 0.5 copy-done.4
  81.4 0.8 collective-permute-start.10
  82.3 2.4 %collective-permute-start.11 = (bf16[336,1280]{1,0:T(8,128)(2,1)}, bf16[336,1280]{1,0:T(8,128)(2,1)}, u32[]{:S(2)}, u32[]{:S(2)}) collective-permute-start(bf16[336,1280]{1,0:T(8,128)(2,1)} %get-tuple-element.55), channel_id=1, source_target_pairs={{0,6},{1,7},{2,0},{3,1},{4,2},{5,3},{6,4},{7,5},{8,14},{9,15},{10,... | collective-permute-start | bytes 2580488 | tf_op jit(solution)/shard_map/ppermute | solution.py:53
  84.7 3.7 %feed_first.1.refs_10_ = f32[256,1280]{1,0:T(8,128)S(1)} custom-call(bf16[128,1280]{1,0:T(8,128)(2,1)} %get-tuple-element.42.refs_0_, bf16[128,1280]{1,0:T(8,128)(2,1)} %get-tuple-element.43.refs_1_, bf16[672,1280]{1,0:T(8,128)(2,1)} %pack.1.refs_2_.refs_4_, bf16[672,1280]{1,0:T(8,128)(2,1)} %collective-permute-done.2.refs_3_.refs_5_), custom_call_target="tpu_custom_call" | custom-call | flops 100000000 | bytes 300000 | tf_op jit(solution)/shard_map/feed_first/pallas_call | solution.py:584
  88.4 1.1 copy-done.6
  89.5 0.0 all-to-all-done.1.back_ref
  89.5 0.0 collective-permute-done.6.refs_0_
  89.5 0.0 collective-permute-done.7.refs_2_
  89.5 0.1 collective-permute-start.8
  89.6 0.5 collective-permute-start.9
  90.1 2.6 %decode_rows.1 = (bf16[16,1280]{1,0:T(8,128)(2,1)S(1)}, bf16[16,1280]{1,0:T(8,128)(2,1)S(1)}) custom-call(bf16[128,2,1280]{2,1,0:T(2,128)(2,1)} %all-to-all-done.1.back_ref, bf16[1280,1280]{1,0:T(8,128)(2,1)S(1)} %copy-done, bf16[2,1280]{1,0:T(2,128)(2,1)S(1)} %copy-done.11, f32[1280]{0:T(1024)S(1)} %copy-done.10), custom_call_target="tpu_custom_call" | custom-call | flops 100000000 | bytes 300000 | tf_op jit(solution)/shard_map/decode_rows/pallas_call | solution.py:539
  92.7 10.5 %collective-permute-done.10.refs_10_.refs_6_ = bf16[336,1280]{1,0:T(8,128)(2,1)} collective-permute-done((bf16[336,1280]{1,0:T(8,128)(2,1)}, bf16[336,1280]{1,0:T(8,128)(2,1)}, u32[]{:S(2)}, u32[]{:S(2)}) %collective-permute-start.10) | collective-permute-done | bytes 860192 | tf_op jit(solution)/shard_map/ppermute | solution.py:53
  103.2 0.0 collective-permute-done.11.refs_12_.refs_8_
  103.2 0.1 collective-permute-start.12
  103.3 0.5 collective-permute-start.13
  103.8 0.3 collective-permute-start.14
  104.1 4.9 %collective-permute-done.14.refs_1_ = bf16[16,1280]{1,0:T(8,128)(2,1)S(1)} collective-permute-done((bf16[16,1280]{1,0:T(8,128)(2,1)S(1)}, bf16[16,1280]{1,0:T(8,128)(2,1)S(1)}, u32[]{:S(2)}, u32[]{:S(2)}) %collective-permute-start.14) | collective-permute-done | bytes 40992 | tf_op jit(solution)/shard_map/ppermute | solution.py:53
  109.0 0.0 collective-permute-done.12.refs_11_.refs_7_
  109.0 0.0 collective-permute-done.13.refs_13_.refs_9_
  109.0 0.0 collective-permute-done.8.refs_7_.refs_3_
  109.0 0.0 collective-permute-done.9.refs_9_.refs_5_
  109.0 7.4 %feed_guest.1 = (bf16[144,1280]{1,0:T(8,128)(2,1)S(1)}, bf16[128,1280]{1,0:T(8,128)(2,1)S(1)}, bf16[16,1280]{1,0:T(8,128)(2,1)S(1)}) custom-call(bf16[128,1280]{1,0:T(8,128)(2,1)} %collective-permute-done.6.refs_0_, bf16[16,1280]{1,0:T(8,128)(2,1)S(1)} %collective-permute-done.14.refs_1_, bf16[128,1280]{1,0:T(8,128)(2,1)} %collective-permute-done.7.refs_2_, ...), custom_call_target="tpu_custom_call" | custom-call | flops 8000000000 | bytes 24000000 | tf_op jit(solution)/shard_map/feed_guest/pallas_call | solution.py:584
  116.5 0.1 collective-permute-start.16
  116.5 3.2 %collective-permute-start.15 = (bf16[144,1280]{1,0:T(8,128)(2,1)S(1)}, bf16[144,1280]{1,0:T(8,128)(2,1)S(1)}, u32[]{:S(2)}, u32[]{:S(2)}) collective-permute-start(bf16[144,1280]{1,0:T(8,128)(2,1)S(1)} %get-tuple-element.68), channel_id=1, source_target_pairs={{0,24},{1,25},{2,26},{3,27},{4,28},{5,29},{6,30},{7,31},{8,0},{9,1... | collective-permute-start | bytes 1105928 | tf_op jit(solution)/shard_map/ppermute | solution.py:53
  119.8 5.2 %feed_second.1.start_ref = f32[256,1280]{1,0:T(8,128)S(1)} custom-call(bf16[128,1280]{1,0:T(8,128)(2,1)} %get-tuple-element.42.refs_0_, bf16[128,1280]{1,0:T(8,128)(2,1)} %get-tuple-element.43.refs_1_, bf16[672,1280]{1,0:T(8,128)(2,1)S(1)} %copy-done.5, bf16[672,1280]{1,0:T(8,128)(2,1)S(1)} %collective-permute-done.8.refs_7_.refs_3_, ...), custom_call_target="tpu_custom_call" | custom-call | flops 6000000000 | bytes 18000000 | tf_op jit(solution)/shard_map/feed_second/pallas_call | solution.py:584
  124.9 1.3 %collective-permute-done.16.second_ref = bf16[128,1280]{1,0:T(8,128)(2,1)S(1)} collective-permute-done((bf16[128,1280]{1,0:T(8,128)(2,1)S(1)}, bf16[128,1280]{1,0:T(8,128)(2,1)S(1)}, u32[]{:S(2)}, u32[]{:S(2)}) %collective-permute-start.16) | collective-permute-done | bytes 327712 | tf_op jit(solution)/shard_map/ppermute | solution.py:53
  126.3 0.1 collective-permute-done.15.first_ref
  126.4 1.0 final.1
  (24 shorter events, 0.0 us)
Async XLA Ops:
  2.5 26.7 %all-to-all-start = ((bf16[128,2,1280]{2,1,0:T(2,128)(2,1)}), bf16[128,2,1280]{2,1,0:T(2,128)(2,1)}, u32[]{:S(2)}, u32[]{:S(2)}) async-start(bf16[128,2,1280]{2,1,0:T(2,128)(2,1)} %broadcast_in_dim.2), calls=%async_computation | async-start | bytes 1310720 | tf_op jit(solution)/shard_map/all_to_all | solution.py:645
  14.1 2.5 %copy-start.12 = (f32[1280]{0:T(1024)S(1)}, f32[1280]{0:T(1024)}, u32[]{:S(2)}) copy-start(f32[1280]{0:T(1024)} %gain_ref.7) | copy-start | bytes 15364
  19.9 29.2 %collective-permute-start.2 = (bf16[672,1280]{1,0:T(8,128)(2,1)}, bf16[672,1280]{1,0:T(8,128)(2,1)}, u32[]{:S(2)}, u32[]{:S(2)}) collective-permute-start(bf16[672,1280]{1,0:T(8,128)(2,1)} %pack.1.refs_2_.refs_4_), channel_id=1, source_target_pairs={{0,1},{1,0},{2,3},{3,2},{4,5},{5,4},{6,7},{7,6},{8,9},{9,8},{10,11... | collective-permute-start | bytes 5160968 | tf_op jit(solution)/shard_map/ppermute | solution.py:53
  19.9 29.1 %collective-permute-start.1 = (bf16[256,640]{1,0:T(8,128)(2,1)}, bf16[256,640]{1,0:T(8,128)(2,1)}, u32[]{:S(2)}, u32[]{:S(2)}) collective-permute-start(bf16[256,640]{1,0:T(8,128)(2,1)} %prefill_kv.1.own_ref), channel_id=1, source_target_pairs={{0,1},{1,0},{2,3},{3,2},{4,5},{5,4},{6,7},{7,6},{8,9},{9,8},{10,11... | collective-permute-start | bytes 983048 | tf_op jit(solution)/shard_map/ppermute | solution.py:53
  20.4 28.6 %collective-permute-start = (bf16[256,640]{1,0:T(8,128)(2,1)}, bf16[256,640]{1,0:T(8,128)(2,1)}, u32[]{:S(2)}, u32[]{:S(2)}) collective-permute-start(bf16[256,640]{1,0:T(8,128)(2,1)} %prefill_kv.1.own_ref), channel_id=1, source_target_pairs={{0,2},{1,3},{2,0},{3,1},{4,6},{5,7},{6,4},{7,5},{8,10},{9,11},{10,... | collective-permute-start | bytes 983048 | tf_op jit(solution)/shard_map/ppermute | solution.py:53
  21.5 57.7 %collective-permute-start.5 = (bf16[672,1280]{1,0:T(8,128)(2,1)}, bf16[672,1280]{1,0:T(8,128)(2,1)S(1)}, u32[]{:S(2)}, u32[]{:S(2)}) collective-permute-start(bf16[672,1280]{1,0:T(8,128)(2,1)} %pack.1.refs_2_.refs_4_), channel_id=1, source_target_pairs={{0,6},{1,7},{2,0},{3,1},{4,2},{5,3},{6,4},{7,5},{8,14},{9,15},{10,... | collective-permute-start | bytes 5160968 | tf_op jit(solution)/shard_map/ppermute | solution.py:53
  23.8 55.3 %collective-permute-start.4 = (bf16[672,1280]{1,0:T(8,128)(2,1)}, bf16[672,1280]{1,0:T(8,128)(2,1)S(1)}, u32[]{:S(2)}, u32[]{:S(2)}) collective-permute-start(bf16[672,1280]{1,0:T(8,128)(2,1)} %pack.1.refs_2_.refs_4_), channel_id=1, source_target_pairs={{0,2},{1,3},{2,4},{3,5},{4,6},{5,7},{6,0},{7,1},{8,10},{9,11},{10,... | collective-permute-start | bytes 5160968 | tf_op jit(solution)/shard_map/ppermute | solution.py:53
  24.4 7.4 %copy-start.15 = (s32[1024]{0:T(1024)S(1)}, s32[1024]{0:T(1024)}, u32[]{:S(2)}) copy-start(s32[1024]{0:T(1024)} %param.26) | copy-start | bytes 12292
  24.5 7.4 %copy-start.16 = (s32[256]{0:T(256)S(1)}, s32[256]{0:T(256)}, u32[]{:S(2)}) copy-start(s32[256]{0:T(256)} %param.24) | copy-start | bytes 3076
  24.5 7.4 %copy-start.17 = (s32[4]{0:T(128)S(1)}, s32[4]{0:T(128)}, u32[]{:S(2)}) copy-start(s32[4]{0:T(128)} %length_ref.1) | copy-start | bytes 52
  28.3 0.8 copy-start.1
  31.9 1.1 copy-start.9
  48.2 0.9 copy-start.8
  49.1 13.6 %copy-start.10 = (f32[1280]{0:T(1024)S(1)}, f32[1280]{0:T(1024)}, u32[]{:S(2)}) copy-start(f32[1280]{0:T(1024)} %gain_ref.9) | copy-start | bytes 15364
  49.1 13.6 %collective-permute-start.3 = (bf16[256,640]{1,0:T(8,128)(2,1)}, bf16[256,640]{1,0:T(8,128)(2,1)}, u32[]{:S(2)}, u32[]{:S(2)}) collective-permute-start(bf16[256,640]{1,0:T(8,128)(2,1)} %collective-permute-done.zed_ref), channel_id=1, source_target_pairs={{0,1},{1,0},{2,3},{3,2},{4,5},{5,4},{6,7},{7,6},{8,9},{9,8},{10,11... | collective-permute-start | bytes 983048 | tf_op jit(solution)/shard_map/ppermute | solution.py:53
  51.8 37.7 %all-to-all-start.1 = ((bf16[128,2,1280]{2,1,0:T(2,128)(2,1)}), bf16[128,2,1280]{2,1,0:T(2,128)(2,1)}, u32[]{:S(2)}, u32[]{:S(2)}) async-start(bf16[128,2,1280]{2,1,0:T(2,128)(2,1)} %reshape.26), calls=%async_computation.1 | async-start | bytes 1310720 | tf_op jit(solution)/shard_map/all_to_all | solution.py:678
  75.1 0.8 copy-start.13
  75.9 13.6 %collective-permute-start.6 = (bf16[128,1280]{1,0:T(8,128)(2,1)}, bf16[128,1280]{1,0:T(8,128)(2,1)}, u32[]{:S(2)}, u32[]{:S(2)}) collective-permute-start(bf16[128,1280]{1,0:T(8,128)(2,1)} %get-tuple-element.42.refs_0_), channel_id=1, source_target_pairs={{0,8},{1,9},{2,10},{3,11},{4,12},{5,13},{6,14},{7,15},{8,16},{9,17... | collective-permute-start | bytes 983048 | tf_op jit(solution)/shard_map/ppermute | solution.py:53
  76.6 12.9 %collective-permute-start.7 = (bf16[128,1280]{1,0:T(8,128)(2,1)}, bf16[128,1280]{1,0:T(8,128)(2,1)}, u32[]{:S(2)}, u32[]{:S(2)}) collective-permute-start(bf16[128,1280]{1,0:T(8,128)(2,1)} %get-tuple-element.43.refs_1_), channel_id=1, source_target_pairs={{0,24},{1,25},{2,26},{3,27},{4,28},{5,29},{6,30},{7,31},{8,0},{9,1... | collective-permute-start | bytes 983048 | tf_op jit(solution)/shard_map/ppermute | solution.py:53
  79.1 1.7 %copy-start.2 = (bf16[672,1280]{1,0:T(8,128)(2,1)}, bf16[672,1280]{1,0:T(8,128)(2,1)S(1)}, u32[]{:S(2)}) copy-start(bf16[672,1280]{1,0:T(8,128)(2,1)S(1)} %collective-permute-done.5.above_ref.refs_8_.refs_4_) | copy-start | bytes 5160964
  79.1 2.3 %copy-start.4 = (bf16[672,1280]{1,0:T(8,128)(2,1)}, bf16[672,1280]{1,0:T(8,128)(2,1)S(1)}, u32[]{:S(2)}) copy-start(bf16[672,1280]{1,0:T(8,128)(2,1)S(1)} %collective-permute-done.4.below_ref.refs_6_.refs_2_) | copy-start | bytes 5160964
  81.4 21.8 %collective-permute-start.10 = (bf16[336,1280]{1,0:T(8,128)(2,1)}, bf16[336,1280]{1,0:T(8,128)(2,1)}, u32[]{:S(2)}, u32[]{:S(2)}) collective-permute-start(bf16[336,1280]{1,0:T(8,128)(2,1)} %get-tuple-element.54), channel_id=1, source_target_pairs={{0,2},{1,3},{2,4},{3,5},{4,6},{5,7},{6,0},{7,1},{8,10},{9,11},{10,... | collective-permute-start | bytes 2580488 | tf_op jit(solution)/shard_map/ppermute | solution.py:53
  82.3 7.8 %copy-start = (bf16[1280,1280]{1,0:T(8,128)(2,1)S(1)}, bf16[1280,1280]{1,0:T(8,128)(2,1)}, u32[]{:S(2)}) copy-start(bf16[1280,1280]{1,0:T(8,128)(2,1)} %w_ref.9) | copy-start | bytes 9830404
  82.3 7.8 %copy-start.11 = (bf16[2,1280]{1,0:T(2,128)(2,1)S(1)}, bf16[2,1280]{1,0:T(2,128)(2,1)}, u32[]{:S(2)}) copy-start(bf16[2,1280]{1,0:T(2,128)(2,1)} %decode_ref.1) | copy-start | bytes 15364
  82.3 20.9 %collective-permute-start.11 = (bf16[336,1280]{1,0:T(8,128)(2,1)}, bf16[336,1280]{1,0:T(8,128)(2,1)}, u32[]{:S(2)}, u32[]{:S(2)}) collective-permute-start(bf16[336,1280]{1,0:T(8,128)(2,1)} %get-tuple-element.55), channel_id=1, source_target_pairs={{0,6},{1,7},{2,0},{3,1},{4,2},{5,3},{6,4},{7,5},{8,14},{9,15},{10,... | collective-permute-start | bytes 2580488 | tf_op jit(solution)/shard_map/ppermute | solution.py:53
  88.4 1.1 copy-start.6
  89.5 19.6 %copy-start.3 = (bf16[672,1280]{1,0:T(8,128)(2,1)S(1)}, bf16[672,1280]{1,0:T(8,128)(2,1)}, u32[]{:S(2)}) copy-start(bf16[672,1280]{1,0:T(8,128)(2,1)} %copy-done.2) | copy-start | bytes 5160964
  89.5 19.6 %copy-start.5 = (bf16[672,1280]{1,0:T(8,128)(2,1)S(1)}, bf16[672,1280]{1,0:T(8,128)(2,1)}, u32[]{:S(2)}) copy-start(bf16[672,1280]{1,0:T(8,128)(2,1)} %copy-done.4) | copy-start | bytes 5160964
  89.5 19.5 %collective-permute-start.8 = (bf16[672,1280]{1,0:T(8,128)(2,1)}, bf16[672,1280]{1,0:T(8,128)(2,1)S(1)}, u32[]{:S(2)}, u32[]{:S(2)}) collective-permute-start(bf16[672,1280]{1,0:T(8,128)(2,1)} %copy-done.4), channel_id=1, source_target_pairs={{0,1},{1,0},{2,3},{3,2},{4,5},{5,4},{6,7},{7,6},{8,9},{9,8},{10,11... | collective-permute-start | bytes 5160968 | tf_op jit(solution)/shard_map/ppermute | solution.py:53
  89.6 19.4 %collective-permute-start.9 = (bf16[672,1280]{1,0:T(8,128)(2,1)}, bf16[672,1280]{1,0:T(8,128)(2,1)S(1)}, u32[]{:S(2)}, u32[]{:S(2)}) collective-permute-start(bf16[672,1280]{1,0:T(8,128)(2,1)} %copy-done.2), channel_id=1, source_target_pairs={{0,1},{1,0},{2,3},{3,2},{4,5},{5,4},{6,7},{7,6},{8,9},{9,8},{10,11... | collective-permute-start | bytes 5160968 | tf_op jit(solution)/shard_map/ppermute | solution.py:53
  103.2 16.6 %copy-start.7 = (f32[256,1280]{1,0:T(8,128)S(1)}, f32[256,1280]{1,0:T(8,128)}, u32[]{:S(2)}) copy-start(f32[256,1280]{1,0:T(8,128)} %copy-done.6) | copy-start | bytes 3932164
  103.2 16.6 %copy-start.14 = (bf16[256,1280]{1,0:T(8,128)(2,1)S(1)}, bf16[256,1280]{1,0:T(8,128)(2,1)}, u32[]{:S(2)}) copy-start(bf16[256,1280]{1,0:T(8,128)(2,1)} %copy-done.13) | copy-start | bytes 1966084
  103.2 5.8 %collective-permute-start.12 = (bf16[336,1280]{1,0:T(8,128)(2,1)}, bf16[336,1280]{1,0:T(8,128)(2,1)S(1)}, u32[]{:S(2)}, u32[]{:S(2)}) collective-permute-start(bf16[336,1280]{1,0:T(8,128)(2,1)} %collective-permute-done.10.refs_10_.refs_6_), channel_id=1, source_target_pairs={{0,1},{1,0},{2,3},{3,2},{4,5},{5,4},{6,7},{7,6},{8,9},{9,8},{10,11... | collective-permute-start | bytes 2580488 | tf_op jit(solution)/shard_map/ppermute | solution.py:53
  103.3 5.7 %collective-permute-start.13 = (bf16[336,1280]{1,0:T(8,128)(2,1)}, bf16[336,1280]{1,0:T(8,128)(2,1)S(1)}, u32[]{:S(2)}, u32[]{:S(2)}) collective-permute-start(bf16[336,1280]{1,0:T(8,128)(2,1)} %collective-permute-done.11.refs_12_.refs_8_), channel_id=1, source_target_pairs={{0,1},{1,0},{2,3},{3,2},{4,5},{5,4},{6,7},{7,6},{8,9},{9,8},{10,11... | collective-permute-start | bytes 2580488 | tf_op jit(solution)/shard_map/ppermute | solution.py:53
  103.8 5.2 %collective-permute-start.14 = (bf16[16,1280]{1,0:T(8,128)(2,1)S(1)}, bf16[16,1280]{1,0:T(8,128)(2,1)S(1)}, u32[]{:S(2)}, u32[]{:S(2)}) collective-permute-start(bf16[16,1280]{1,0:T(8,128)(2,1)S(1)} %get-tuple-element.60.refs_3_), channel_id=1, source_target_pairs={{0,8},{1,9},{2,10},{3,11},{4,12},{5,13},{6,14},{7,15},{8,16},{9,17... | collective-permute-start | bytes 122888 | tf_op jit(solution)/shard_map/ppermute | solution.py:53
  116.5 9.8 %collective-permute-start.16 = (bf16[128,1280]{1,0:T(8,128)(2,1)S(1)}, bf16[128,1280]{1,0:T(8,128)(2,1)S(1)}, u32[]{:S(2)}, u32[]{:S(2)}) collective-permute-start(bf16[128,1280]{1,0:T(8,128)(2,1)S(1)} %get-tuple-element.69), channel_id=1, source_target_pairs={{0,8},{1,9},{2,10},{3,11},{4,12},{5,13},{6,14},{7,15},{8,16},{9,17... | collective-permute-start | bytes 983048 | tf_op jit(solution)/shard_map/ppermute | solution.py:53
  116.5 9.9 %collective-permute-start.15 = (bf16[144,1280]{1,0:T(8,128)(2,1)S(1)}, bf16[144,1280]{1,0:T(8,128)(2,1)S(1)}, u32[]{:S(2)}, u32[]{:S(2)}) collective-permute-start(bf16[144,1280]{1,0:T(8,128)(2,1)S(1)} %get-tuple-element.68), channel_id=1, source_target_pairs={{0,24},{1,25},{2,26},{3,27},{4,28},{5,29},{6,30},{7,31},{8,0},{9,1... | collective-permute-start | bytes 1105928 | tf_op jit(solution)/shard_map/ppermute | solution.py:53

commit v8 on v7

--- a/solution.py
+++ b/solution.py
@@ -251,6 +251,10 @@
     fresh_value,
     over,
     result,
+    held_score,
+    held_weight,
+    mixture,
+    totals,
 ):
     tick = pl.program_id(0)
     step = tick - SLOTS
@@ -316,51 +320,72 @@
             counts = counts + lax.dot_general(upper, lower, NT, preferred_element_type=F32)
         over[...] = counts
 
+    index = jnp.concatenate(index_rows, axis=1)
+
+    @pl.when(step == 0)
+    def _():
+        score = lax.dot_general(query[...], held_ref[:, :384], NT, preferred_element_type=F32)
+        slot = sublanes((128, 1)) // 32
+        length = jnp.zeros((128, 1), jnp.int32)
+        for j in range(SLOTS):
+            length = jnp.where(slot == j, length_ref[j], length)
+        live = lanes((128, 1024)) < count_ref[0]
+        live &= jnp.broadcast_to(index // POSITIONS, (128, 1024)) == slot
+        live &= jnp.broadcast_to(index % POSITIONS, (128, 1024)) < length
+        held_score[...] = jnp.where(live, score, NEG)
+
     @pl.when(step >= 0)
     def _():
         length = length_ref[step]
-        queries = query[pl.ds(pl.multiple_of(step * 32, 32), 32), :]
+        part = pl.ds(pl.multiple_of(step * 32, 32), 32)
+        queries = query[part, :]
         taken = over[pl.ds(pl.multiple_of(step * 8, 8), 8), :]
         taken = jnp.concatenate([taken[i : i + 1, :] for i in range(8)], axis=1)
         cache_live = (lanes((1, POSITIONS)) < length) & (taken < 0.5)
-        index = jnp.concatenate(index_rows, axis=1)
-        held_live = (
-            (lanes((1, 1024)) < count_ref[0])
-            & (index // POSITIONS == step)
-            & (index % POSITIONS < length)
-        )
         cache_score = lax.dot_general(queries, cache_ref[:, :384], NT, preferred_element_type=F32)
-        held_score = lax.dot_general(queries, held_ref[:, :384], NT, preferred_element_type=F32)
         own_score = jnp.sum(
             queries.astype(F32) * fresh_key[pl.ds(step, 1), :], axis=-1, keepdims=True
         )
         cache_live = jnp.broadcast_to(cache_live, cache_score.shape)
-        held_live = jnp.broadcast_to(held_live, held_score.shape)
         cache_score = jnp.where(cache_live, cache_score, NEG)
-        held_score = jnp.where(held_live, held_score, NEG)
+        kept_score = held_score[part, :]
         top = jnp.maximum(
             jnp.maximum(
-                jnp.max(cache_score, axis=-1, keepdims=True), jnp.max(held_score, axis=-1, keepdims=True)
+                jnp.max(cache_score, axis=-1, keepdims=True),
+                jnp.max(kept_score, axis=-1, keepdims=True),
             ),
             own_score,
         )
         cache_weight = jnp.where(cache_live, jnp.exp(cache_score - top), 0.0)
-        held_weight = jnp.where(held_live, jnp.exp(held_score - top), 0.0)
+        kept_weight = jnp.where(kept_score > NEG, jnp.exp(kept_score - top), 0.0)
         own_weight = jnp.exp(own_score - top)
         total = (
             jnp.sum(cache_weight, axis=-1, keepdims=True)
-            + jnp.sum(held_weight, axis=-1, keepdims=True)
+            + jnp.sum(kept_weight, axis=-1, keepdims=True)
             + own_weight
         )
+        held_weight[part, :] = kept_weight.astype(BF)
         mixed = jnp.dot(cache_weight.astype(BF), cache_ref[:, 256:], preferred_element_type=F32)
-        mixed += jnp.dot(held_weight.astype(BF), held_ref[:, 256:], preferred_element_type=F32)
         mixed += own_weight.astype(BF).astype(F32) * fresh_value[pl.ds(step, 1), :]
-        group = sublanes((32, 384))
-        block = (lanes((32, 384)) // HEAD == group // 4 + 1) & (group < QUERY_HEADS)
+        mixture[part, :] = mixed
+        totals[part, :] = jnp.broadcast_to(total, (32, 128))
+
+    @pl.when(step == SLOTS - 1)
+    def _():
+        mixed = mixture[...] + jnp.dot(
+            held_weight[...], held_ref[:, 256:], preferred_element_type=F32
+        )
+        total = jnp.concatenate([totals[...]] * 3, axis=1)
+        head = sublanes((128, 384)) % 32
+        block = (lanes((128, 384)) // HEAD == head // 4 + 1) & (head < QUERY_HEADS)
         mixed = jnp.where(block, mixed / total, 0.0).astype(BF)
         turned = lax.dot_general(mixed, spread[...], NT, preferred_element_type=F32)
         keep = lanes((32, QW)) // HEAD == sublanes((32, QW))
-        result[pl.ds(step, 1), :] = jnp.sum(jnp.where(keep, turned, 0.0), axis=0, keepdims=True)
+        rows = [
+            jnp.sum(jnp.where(keep, turned[j * 32 : (j + 1) * 32], 0.0), axis=0, keepdims=True)
+            for j in range(SLOTS)
+        ]
+        result[:SLOTS, :] = jnp.concatenate(rows, axis=0)
 
     @pl.when(step == SLOTS - 1)
     def _():
@@ -405,6 +430,10 @@
             pltpu.VMEM((8, 384), F32),
             pltpu.VMEM((32, 128), F32),
             pltpu.VMEM((8, QW), F32),
+            pltpu.VMEM((128, 1024), F32),
+            pltpu.VMEM((128, 1024), BF),
+            pltpu.VMEM((128, 384), F32),
+            pltpu.VMEM((128, 128), F32),
         ],
         compiler_params=pltpu.CompilerParams(vmem_limit_bytes=VMEM_LIMIT),
         cost_estimate=cost(17),

time: 129 us -> 127 us (0.984)
  Pallas kernels: 58.4 us -> 56.6 us
    pallas_call x1, Pallas kernels: 15.2 us -> 13.4 us  [decode_attention(): pl.pallas_call(decode_kernel, out_shape=jax.ShapeDtypeStruct((256, QW), B...]
  transfers between devices with their start and end apart: 19 -> 19, of which waited for: 4 -> 4; matrix products, arithmetic and copies ran while one was open for 4% -> 4% of each run, Pallas kernels for 39% -> 38%
where the time goes in v8:
time: 127 us; the launch traced here: 126 us
  Pallas kernels  56.6 us (45%)
  starting transfers between devices  37.6 us (30%)
  waiting for transfers between devices  16.9 us (13%)
  local copies, waits for them, and re-layouts  12.8 us (10%)
  between operations  1.56 us (1%)
    ppermute x17, waiting for transfers between devices, send(): return lax.ppermute(array, 'req', moves(step))  16.9 us
    pallas_call x3, Pallas kernels, feed_forward(): pl.pallas_call(kernel, out_shape=outputs, in_specs=[vmem] * len(inputs),...  16.3 us
    ppermute x17, starting transfers between devices, send(): return lax.ppermute(array, 'req', moves(step))  15.2 us
    pallas_call x1, Pallas kernels, decode_attention(): pl.pallas_call(decode_kernel, out_shape=jax.ShapeDtypeStruct((256, QW), B...  13.4 us
    pallas_call x1, Pallas kernels, attention(): pl.pallas_call(attention_kernel, out_shape=(jax.ShapeDtypeStruct((ROWS, W...  12.3 us
    all_to_all x1, starting transfers between devices, body(): every_row = lax.all_to_all(spread, 'req', 0, 0).reshape(256, WIDTH)  11.6 us
    all_to_all x1, starting transfers between devices, body(): back = lax.all_to_all(outgoing.reshape(total, 2, WIDTH), 'req', 0, 0)  10.9 us
    pallas_call x2, Pallas kernels, project(): pl.pallas_call(kv_kernel if keys else query_kernel, out_shape=jax.ShapeDt...  7.14 us
  transfers between devices with their start and end apart: 19, of which 4 were waited for; matrix products, arithmetic and copies ran while one was open for 4% of the time, Pallas kernels for 38%

profile of v8, /device:TPU:0, one launch (start us, length us, event | category | flops | bytes accessed | tf_op | source)
XLA Modules:
  0.0 125.6 jit_solution(14245854987740154681)
XLA Ops:
  0.6 1.9 %broadcast_in_dim.2 = bf16[128,2,1280]{2,1,0:T(2,128)(2,1)} broadcast(bf16[2,1280]{1,0:T(2,128)(2,1)} %decode_ref.1), dimensions={1,2} | broadcast | bytes 660480 | tf_op jit(solution)/shard_map/broadcast_in_dim | solution.py:673
  2.5 11.6 %all-to-all-start = ((bf16[128,2,1280]{2,1,0:T(2,128)(2,1)}), bf16[128,2,1280]{2,1,0:T(2,128)(2,1)}, u32[]{:S(2)}, u32[]{:S(2)}) async-start(bf16[128,2,1280]{2,1,0:T(2,128)(2,1)} %broadcast_in_dim.2), calls=%async_computation | async-start | bytes 1310720 | tf_op jit(solution)/shard_map/all_to_all | solution.py:674
  14.1 0.0 copy-start.12
  14.2 2.5 %pack.1.refs_2_.refs_4_ = bf16[672,1280]{1,0:T(8,128)(2,1)} custom-call(bf16[1,448,1280]{2,1,0:T(8,128)(2,1)} %bitcast.6, bf16[1,224,1280]{2,1,0:T(8,128)(2,1)} %down_ref.1), custom_call_target="tpu_custom_call" | custom-call | flops 1500000000 | bytes 4500000 | tf_op jit(solution)/shard_map/pack/pallas_call | solution.py:138
  16.6 3.3 %prefill_kv.1.own_ref = bf16[256,640]{1,0:T(8,128)(2,1)} custom-call(s32[1]{0:T(128)S(6)} %select_n.7.rank_ref, bf16[256,1280]{1,0:T(8,128)(2,1)} %hidden_ref.7, f32[1280]{0:T(1024)S(1)} %copy-done.12, bf16[1280,1920]{1,0:T(8,128)(2,1)} %w_ref.7), custom_call_target="tpu_custom_call" | custom-call | flops 3000000000 | bytes 9000000 | tf_op jit(solution)/shard_map/prefill_kv/pallas_call | solution.py:213
  19.9 0.0 collective-permute-start.2
  19.9 0.5 collective-permute-start.1
  20.4 1.0 collective-permute-start
  21.5 2.3 %collective-permute-start.5 = (bf16[672,1280]{1,0:T(8,128)(2,1)}, bf16[672,1280]{1,0:T(8,128)(2,1)S(1)}, u32[]{:S(2)}, u32[]{:S(2)}) collective-permute-start(bf16[672,1280]{1,0:T(8,128)(2,1)} %pack.1.refs_2_.refs_4_), channel_id=1, source_target_pairs={{0,6},{1,7},{2,0},{3,1},{4,2},{5,3},{6,4},{7,5},{8,14},{9,15},{10,... | collective-permute-start | bytes 5160968 | tf_op jit(solution)/shard_map/ppermute | solution.py:53
  23.8 0.0 collective-permute-start.4
  24.4 0.0 copy-start.15
  24.5 0.0 copy-start.16
  24.5 0.0 copy-start.17
  24.5 3.8 %prefill_query.1.query_ref = bf16[256,1280]{1,0:T(8,128)(2,1)S(1)} custom-call(s32[1]{0:T(128)S(6)} %select_n.7.rank_ref, bf16[256,1280]{1,0:T(8,128)(2,1)} %hidden_ref.7, f32[1280]{0:T(1024)S(1)} %copy-done.12, bf16[1280,1920]{1,0:T(8,128)(2,1)} %w_ref.7), custom_call_target="tpu_custom_call" | custom-call | flops 100000000 | bytes 300000 | tf_op jit(solution)/shard_map/prefill_query/pallas_call | solution.py:213
  28.3 0.0 copy-start.1
  28.3 0.8 copy-done.1
  29.2 0.0 all-to-all-done
  29.2 2.7 %reshape.23.rows_ref = bf16[256,1280]{1,0:T(8,128)(2,1)} reshape(bf16[128,2,1280]{2,1,0:T(2,128)(2,1)} %all-to-all-done) | data formatting | bytes 1310720 | tf_op jit(solution)/shard_map/reshape | solution.py:674
  31.9 1.1 copy-done.9
  33.0 13.4 %decode.1 = bf16[256,1280]{1,0:T(8,128)(2,1)S(1)} custom-call(s32[1]{0:T(128)} %bitcast.device_ref, s32[4]{0:T(128)S(1)} %copy-done.17, s32[1]{0:T(128)S(6)} %copy.16.count_ref, s32[1,256]{1,0:T(1,128)S(1)} %bitcast.5, s32[8,128]{1,0:T(8,128)S(1)} %bitcast.4, bf16[256,1280]{1,0:T(8,128)(2,1)S(1)} %copy-done.9, f32[1280]{0:T(1024)S(1)} %copy-done.12, ...), custom_call_target="tpu_custom_call" | custom-call | flops 16999999488 | bytes 51000000 | tf_op jit(solution)/shard_map/decode/pallas_call | solution.py:406
  46.4 0.8 copy-done.8
  47.3 0.0 collective-permute-done.1.core_ref
  47.3 0.0 collective-permute-done.zed_ref
  47.3 0.0 collective-permute-done.2.refs_3_.refs_5_
  47.3 0.1 collective-permute-start.3
  47.4 2.6 %reshape.26 = bf16[128,2,1280]{2,1,0:T(2,128)(2,1)} reshape(bf16[256,1280]{1,0:T(8,128)(2,1)} %copy-done.8) | data formatting | bytes 1310720 | tf_op jit(solution)/shard_map/reshape | solution.py:707
  50.0 10.9 %all-to-all-start.1 = ((bf16[128,2,1280]{2,1,0:T(2,128)(2,1)}), bf16[128,2,1280]{2,1,0:T(2,128)(2,1)}, u32[]{:S(2)}, u32[]{:S(2)}) async-start(bf16[128,2,1280]{2,1,0:T(2,128)(2,1)} %reshape.26), calls=%async_computation.1 | async-start | bytes 1310720 | tf_op jit(solution)/shard_map/all_to_all | solution.py:707
  60.9 0.0 collective-permute-done.3.far_ref
  60.9 12.3 %attention.1 = (bf16[256,1280]{1,0:T(8,128)(2,1)S(1)}, bf16[128,1280]{1,0:T(8,128)(2,1)}, bf16[128,1280]{1,0:T(8,128)(2,1)}) custom-call(s32[1]{0:T(128)S(6)} %select_n.7.rank_ref, bf16[256,1280]{1,0:T(8,128)(2,1)} %copy-done.1, bf16[256,640]{1,0:T(8,128)(2,1)} %prefill_kv.1.own_ref, bf16[256,640]{1,0:T(8,128)(2,1)} %collective-permute-done.1.core_ref, ...), custom_call_target="tpu_custom_call" | custom-call | flops 100000000 | bytes 300000 | tf_op jit(solution)/shard_map/attention/pallas_call | solution.py:522
  73.3 0.8 copy-done.13
  74.1 0.7 collective-permute-start.6
  74.8 2.5 %collective-permute-start.7 = (bf16[128,1280]{1,0:T(8,128)(2,1)}, bf16[128,1280]{1,0:T(8,128)(2,1)}, u32[]{:S(2)}, u32[]{:S(2)}) collective-permute-start(bf16[128,1280]{1,0:T(8,128)(2,1)} %get-tuple-element.43.refs_1_), channel_id=1, source_target_pairs={{0,24},{1,25},{2,26},{3,27},{4,28},{5,29},{6,30},{7,31},{8,0},{9,1... | collective-permute-start | bytes 983048 | tf_op jit(solution)/shard_map/ppermute | solution.py:53
  77.3 0.0 collective-permute-done.5.above_ref.refs_8_.refs_4_
  77.4 0.0 collective-permute-done.4.below_ref.refs_6_.refs_2_
  77.4 1.4 %cut.1 = (bf16[336,1280]{1,0:T(8,128)(2,1)}, bf16[336,1280]{1,0:T(8,128)(2,1)}) custom-call(bf16[672,1280]{1,0:T(8,128)(2,1)S(1)} %collective-permute-done.4.below_ref.refs_6_.refs_2_, bf16[672,1280]{1,0:T(8,128)(2,1)S(1)} %collective-permute-done.5.above_ref.refs_8_.refs_4_), custom_call_target="tpu_custom_call" | custom-call | flops 500000000 | bytes 1500000 | tf_op jit(solution)/shard_map/cut/pallas_call | solution.py:160
  78.8 0.3 copy-done.2
  79.1 0.5 copy-done.4
  79.6 0.8 collective-permute-start.10
  80.5 2.4 %collective-permute-start.11 = (bf16[336,1280]{1,0:T(8,128)(2,1)}, bf16[336,1280]{1,0:T(8,128)(2,1)}, u32[]{:S(2)}, u32[]{:S(2)}) collective-permute-start(bf16[336,1280]{1,0:T(8,128)(2,1)} %get-tuple-element.55), channel_id=1, source_target_pairs={{0,6},{1,7},{2,0},{3,1},{4,2},{5,3},{6,4},{7,5},{8,14},{9,15},{10,... | collective-permute-start | bytes 2580488 | tf_op jit(solution)/shard_map/ppermute | solution.py:53
  82.9 3.7 %feed_first.1.refs_10_ = f32[256,1280]{1,0:T(8,128)S(1)} custom-call(bf16[128,1280]{1,0:T(8,128)(2,1)} %get-tuple-element.42.refs_0_, bf16[128,1280]{1,0:T(8,128)(2,1)} %get-tuple-element.43.refs_1_, bf16[672,1280]{1,0:T(8,128)(2,1)} %pack.1.refs_2_.refs_4_, bf16[672,1280]{1,0:T(8,128)(2,1)} %collective-permute-done.2.refs_3_.refs_5_), custom_call_target="tpu_custom_call" | custom-call | flops 100000000 | bytes 300000 | tf_op jit(solution)/shard_map/feed_first/pallas_call | solution.py:613
  86.6 1.1 copy-done.6
  87.7 0.0 all-to-all-done.1.back_ref
  87.7 0.0 collective-permute-done.6.refs_0_
  87.7 0.0 collective-permute-done.7.refs_2_
  87.7 0.1 collective-permute-start.8
  87.8 0.5 collective-permute-start.9
  88.3 2.6 %decode_rows.1 = (bf16[16,1280]{1,0:T(8,128)(2,1)S(1)}, bf16[16,1280]{1,0:T(8,128)(2,1)S(1)}) custom-call(bf16[128,2,1280]{2,1,0:T(2,128)(2,1)} %all-to-all-done.1.back_ref, bf16[1280,1280]{1,0:T(8,128)(2,1)S(1)} %copy-done, bf16[2,1280]{1,0:T(2,128)(2,1)S(1)} %copy-done.11, f32[1280]{0:T(1024)S(1)} %copy-done.10), custom_call_target="tpu_custom_call" | custom-call | flops 100000000 | bytes 300000 | tf_op jit(solution)/shard_map/decode_rows/pallas_call | solution.py:568
  90.9 10.5 %collective-permute-done.10.refs_10_.refs_6_ = bf16[336,1280]{1,0:T(8,128)(2,1)} collective-permute-done((bf16[336,1280]{1,0:T(8,128)(2,1)}, bf16[336,1280]{1,0:T(8,128)(2,1)}, u32[]{:S(2)}, u32[]{:S(2)}) %collective-permute-start.10) | collective-permute-done | bytes 860192 | tf_op jit(solution)/shard_map/ppermute | solution.py:53
  101.4 0.0 collective-permute-done.11.refs_12_.refs_8_
  101.4 0.1 collective-permute-start.12
  101.5 0.5 collective-permute-start.13
  102.0 0.3 collective-permute-start.14
  102.3 4.9 %collective-permute-done.14.refs_1_ = bf16[16,1280]{1,0:T(8,128)(2,1)S(1)} collective-permute-done((bf16[16,1280]{1,0:T(8,128)(2,1)S(1)}, bf16[16,1280]{1,0:T(8,128)(2,1)S(1)}, u32[]{:S(2)}, u32[]{:S(2)}) %collective-permute-start.14) | collective-permute-done | bytes 40992 | tf_op jit(solution)/shard_map/ppermute | solution.py:53
  107.2 0.0 collective-permute-done.12.refs_11_.refs_7_
  107.2 0.0 collective-permute-done.13.refs_13_.refs_9_
  107.2 0.0 collective-permute-done.8.refs_7_.refs_3_
  107.2 0.0 collective-permute-done.9.refs_9_.refs_5_
  107.3 7.4 %feed_guest.1 = (bf16[144,1280]{1,0:T(8,128)(2,1)S(1)}, bf16[128,1280]{1,0:T(8,128)(2,1)S(1)}, bf16[16,1280]{1,0:T(8,128)(2,1)S(1)}) custom-call(bf16[128,1280]{1,0:T(8,128)(2,1)} %collective-permute-done.6.refs_0_, bf16[16,1280]{1,0:T(8,128)(2,1)S(1)} %collective-permute-done.14.refs_1_, bf16[128,1280]{1,0:T(8,128)(2,1)} %collective-permute-done.7.refs_2_, ...), custom_call_target="tpu_custom_call" | custom-call | flops 8000000000 | bytes 24000000 | tf_op jit(solution)/shard_map/feed_guest/pallas_call | solution.py:613
  114.7 0.1 collective-permute-start.16
  114.7 3.2 %collective-permute-start.15 = (bf16[144,1280]{1,0:T(8,128)(2,1)S(1)}, bf16[144,1280]{1,0:T(8,128)(2,1)S(1)}, u32[]{:S(2)}, u32[]{:S(2)}) collective-permute-start(bf16[144,1280]{1,0:T(8,128)(2,1)S(1)} %get-tuple-element.68), channel_id=1, source_target_pairs={{0,24},{1,25},{2,26},{3,27},{4,28},{5,29},{6,30},{7,31},{8,0},{9,1... | collective-permute-start | bytes 1105928 | tf_op jit(solution)/shard_map/ppermute | solution.py:53
  118.0 5.2 %feed_second.1.start_ref = f32[256,1280]{1,0:T(8,128)S(1)} custom-call(bf16[128,1280]{1,0:T(8,128)(2,1)} %get-tuple-element.42.refs_0_, bf16[128,1280]{1,0:T(8,128)(2,1)} %get-tuple-element.43.refs_1_, bf16[672,1280]{1,0:T(8,128)(2,1)S(1)} %copy-done.5, bf16[672,1280]{1,0:T(8,128)(2,1)S(1)} %collective-permute-done.8.refs_7_.refs_3_, ...), custom_call_target="tpu_custom_call" | custom-call | flops 6000000000 | bytes 18000000 | tf_op jit(solution)/shard_map/feed_second/pallas_call | solution.py:613
  123.2 1.3 %collective-permute-done.16.second_ref = bf16[128,1280]{1,0:T(8,128)(2,1)S(1)} collective-permute-done((bf16[128,1280]{1,0:T(8,128)(2,1)S(1)}, bf16[128,1280]{1,0:T(8,128)(2,1)S(1)}, u32[]{:S(2)}, u32[]{:S(2)}) %collective-permute-start.16) | collective-permute-done | bytes 327712 | tf_op jit(solution)/shard_map/ppermute | solution.py:53
  124.5 0.1 collective-permute-done.15.first_ref
  124.6 1.0 final.1
  (24 shorter events, 0.0 us)
Async XLA Ops:
  2.5 26.7 %all-to-all-start = ((bf16[128,2,1280]{2,1,0:T(2,128)(2,1)}), bf16[128,2,1280]{2,1,0:T(2,128)(2,1)}, u32[]{:S(2)}, u32[]{:S(2)}) async-start(bf16[128,2,1280]{2,1,0:T(2,128)(2,1)} %broadcast_in_dim.2), calls=%async_computation | async-start | bytes 1310720 | tf_op jit(solution)/shard_map/all_to_all | solution.py:674
  14.1 2.5 %copy-start.12 = (f32[1280]{0:T(1024)S(1)}, f32[1280]{0:T(1024)}, u32[]{:S(2)}) copy-start(f32[1280]{0:T(1024)} %gain_ref.7) | copy-start | bytes 15364
  19.9 27.4 %collective-permute-start.2 = (bf16[672,1280]{1,0:T(8,128)(2,1)}, bf16[672,1280]{1,0:T(8,128)(2,1)}, u32[]{:S(2)}, u32[]{:S(2)}) collective-permute-start(bf16[672,1280]{1,0:T(8,128)(2,1)} %pack.1.refs_2_.refs_4_), channel_id=1, source_target_pairs={{0,1},{1,0},{2,3},{3,2},{4,5},{5,4},{6,7},{7,6},{8,9},{9,8},{10,11... | collective-permute-start | bytes 5160968 | tf_op jit(solution)/shard_map/ppermute | solution.py:53
  19.9 27.4 %collective-permute-start.1 = (bf16[256,640]{1,0:T(8,128)(2,1)}, bf16[256,640]{1,0:T(8,128)(2,1)}, u32[]{:S(2)}, u32[]{:S(2)}) collective-permute-start(bf16[256,640]{1,0:T(8,128)(2,1)} %prefill_kv.1.own_ref), channel_id=1, source_target_pairs={{0,1},{1,0},{2,3},{3,2},{4,5},{5,4},{6,7},{7,6},{8,9},{9,8},{10,11... | collective-permute-start | bytes 983048 | tf_op jit(solution)/shard_map/ppermute | solution.py:53
  20.4 26.9 %collective-permute-start = (bf16[256,640]{1,0:T(8,128)(2,1)}, bf16[256,640]{1,0:T(8,128)(2,1)}, u32[]{:S(2)}, u32[]{:S(2)}) collective-permute-start(bf16[256,640]{1,0:T(8,128)(2,1)} %prefill_kv.1.own_ref), channel_id=1, source_target_pairs={{0,2},{1,3},{2,0},{3,1},{4,6},{5,7},{6,4},{7,5},{8,10},{9,11},{10,... | collective-permute-start | bytes 983048 | tf_op jit(solution)/shard_map/ppermute | solution.py:53
  21.5 55.9 %collective-permute-start.5 = (bf16[672,1280]{1,0:T(8,128)(2,1)}, bf16[672,1280]{1,0:T(8,128)(2,1)S(1)}, u32[]{:S(2)}, u32[]{:S(2)}) collective-permute-start(bf16[672,1280]{1,0:T(8,128)(2,1)} %pack.1.refs_2_.refs_4_), channel_id=1, source_target_pairs={{0,6},{1,7},{2,0},{3,1},{4,2},{5,3},{6,4},{7,5},{8,14},{9,15},{10,... | collective-permute-start | bytes 5160968 | tf_op jit(solution)/shard_map/ppermute | solution.py:53
  23.8 53.6 %collective-permute-start.4 = (bf16[672,1280]{1,0:T(8,128)(2,1)}, bf16[672,1280]{1,0:T(8,128)(2,1)S(1)}, u32[]{:S(2)}, u32[]{:S(2)}) collective-permute-start(bf16[672,1280]{1,0:T(8,128)(2,1)} %pack.1.refs_2_.refs_4_), channel_id=1, source_target_pairs={{0,2},{1,3},{2,4},{3,5},{4,6},{5,7},{6,0},{7,1},{8,10},{9,11},{10,... | collective-permute-start | bytes 5160968 | tf_op jit(solution)/shard_map/ppermute | solution.py:53
  24.4 7.4 %copy-start.15 = (s32[1024]{0:T(1024)S(1)}, s32[1024]{0:T(1024)}, u32[]{:S(2)}) copy-start(s32[1024]{0:T(1024)} %param.26) | copy-start | bytes 12292
  24.5 7.4 %copy-start.16 = (s32[256]{0:T(256)S(1)}, s32[256]{0:T(256)}, u32[]{:S(2)}) copy-start(s32[256]{0:T(256)} %param.24) | copy-start | bytes 3076
  24.5 7.4 %copy-start.17 = (s32[4]{0:T(128)S(1)}, s32[4]{0:T(128)}, u32[]{:S(2)}) copy-start(s32[4]{0:T(128)} %length_ref.1) | copy-start | bytes 52
  28.3 0.8 copy-start.1
  31.9 1.1 copy-start.9
  46.4 0.9 copy-start.8
  47.3 13.6 %copy-start.10 = (f32[1280]{0:T(1024)S(1)}, f32[1280]{0:T(1024)}, u32[]{:S(2)}) copy-start(f32[1280]{0:T(1024)} %gain_ref.9) | copy-start | bytes 15364
  47.3 13.6 %collective-permute-start.3 = (bf16[256,640]{1,0:T(8,128)(2,1)}, bf16[256,640]{1,0:T(8,128)(2,1)}, u32[]{:S(2)}, u32[]{:S(2)}) collective-permute-start(bf16[256,640]{1,0:T(8,128)(2,1)} %collective-permute-done.zed_ref), channel_id=1, source_target_pairs={{0,1},{1,0},{2,3},{3,2},{4,5},{5,4},{6,7},{7,6},{8,9},{9,8},{10,11... | collective-permute-start | bytes 983048 | tf_op jit(solution)/shard_map/ppermute | solution.py:53
  50.0 37.7 %all-to-all-start.1 = ((bf16[128,2,1280]{2,1,0:T(2,128)(2,1)}), bf16[128,2,1280]{2,1,0:T(2,128)(2,1)}, u32[]{:S(2)}, u32[]{:S(2)}) async-start(bf16[128,2,1280]{2,1,0:T(2,128)(2,1)} %reshape.26), calls=%async_computation.1 | async-start | bytes 1310720 | tf_op jit(solution)/shard_map/all_to_all | solution.py:707
  73.3 0.8 copy-start.13
  74.1 13.6 %collective-permute-start.6 = (bf16[128,1280]{1,0:T(8,128)(2,1)}, bf16[128,1280]{1,0:T(8,128)(2,1)}, u32[]{:S(2)}, u32[]{:S(2)}) collective-permute-start(bf16[128,1280]{1,0:T(8,128)(2,1)} %get-tuple-element.42.refs_0_), channel_id=1, source_target_pairs={{0,8},{1,9},{2,10},{3,11},{4,12},{5,13},{6,14},{7,15},{8,16},{9,17... | collective-permute-start | bytes 983048 | tf_op jit(solution)/shard_map/ppermute | solution.py:53
  74.8 12.9 %collective-permute-start.7 = (bf16[128,1280]{1,0:T(8,128)(2,1)}, bf16[128,1280]{1,0:T(8,128)(2,1)}, u32[]{:S(2)}, u32[]{:S(2)}) collective-permute-start(bf16[128,1280]{1,0:T(8,128)(2,1)} %get-tuple-element.43.refs_1_), channel_id=1, source_target_pairs={{0,24},{1,25},{2,26},{3,27},{4,28},{5,29},{6,30},{7,31},{8,0},{9,1... | collective-permute-start | bytes 983048 | tf_op jit(solution)/shard_map/ppermute | solution.py:53
  77.3 1.7 %copy-start.2 = (bf16[672,1280]{1,0:T(8,128)(2,1)}, bf16[672,1280]{1,0:T(8,128)(2,1)S(1)}, u32[]{:S(2)}) copy-start(bf16[672,1280]{1,0:T(8,128)(2,1)S(1)} %collective-permute-done.5.above_ref.refs_8_.refs_4_) | copy-start | bytes 5160964
  77.4 2.3 %copy-start.4 = (bf16[672,1280]{1,0:T(8,128)(2,1)}, bf16[672,1280]{1,0:T(8,128)(2,1)S(1)}, u32[]{:S(2)}) copy-start(bf16[672,1280]{1,0:T(8,128)(2,1)S(1)} %collective-permute-done.4.below_ref.refs_6_.refs_2_) | copy-start | bytes 5160964
  79.6 21.8 %collective-permute-start.10 = (bf16[336,1280]{1,0:T(8,128)(2,1)}, bf16[336,1280]{1,0:T(8,128)(2,1)}, u32[]{:S(2)}, u32[]{:S(2)}) collective-permute-start(bf16[336,1280]{1,0:T(8,128)(2,1)} %get-tuple-element.54), channel_id=1, source_target_pairs={{0,2},{1,3},{2,4},{3,5},{4,6},{5,7},{6,0},{7,1},{8,10},{9,11},{10,... | collective-permute-start | bytes 2580488 | tf_op jit(solution)/shard_map/ppermute | solution.py:53
  80.5 7.8 %copy-start = (bf16[1280,1280]{1,0:T(8,128)(2,1)S(1)}, bf16[1280,1280]{1,0:T(8,128)(2,1)}, u32[]{:S(2)}) copy-start(bf16[1280,1280]{1,0:T(8,128)(2,1)} %w_ref.9) | copy-start | bytes 9830404
  80.5 7.8 %copy-start.11 = (bf16[2,1280]{1,0:T(2,128)(2,1)S(1)}, bf16[2,1280]{1,0:T(2,128)(2,1)}, u32[]{:S(2)}) copy-start(bf16[2,1280]{1,0:T(2,128)(2,1)} %decode_ref.1) | copy-start | bytes 15364
  80.5 20.9 %collective-permute-start.11 = (bf16[336,1280]{1,0:T(8,128)(2,1)}, bf16[336,1280]{1,0:T(8,128)(2,1)}, u32[]{:S(2)}, u32[]{:S(2)}) collective-permute-start(bf16[336,1280]{1,0:T(8,128)(2,1)} %get-tuple-element.55), channel_id=1, source_target_pairs={{0,6},{1,7},{2,0},{3,1},{4,2},{5,3},{6,4},{7,5},{8,14},{9,15},{10,... | collective-permute-start | bytes 2580488 | tf_op jit(solution)/shard_map/ppermute | solution.py:53
  86.6 1.1 copy-start.6
  87.7 19.5 %copy-start.3 = (bf16[672,1280]{1,0:T(8,128)(2,1)S(1)}, bf16[672,1280]{1,0:T(8,128)(2,1)}, u32[]{:S(2)}) copy-start(bf16[672,1280]{1,0:T(8,128)(2,1)} %copy-done.2) | copy-start | bytes 5160964
  87.7 19.6 %copy-start.5 = (bf16[672,1280]{1,0:T(8,128)(2,1)S(1)}, bf16[672,1280]{1,0:T(8,128)(2,1)}, u32[]{:S(2)}) copy-start(bf16[672,1280]{1,0:T(8,128)(2,1)} %copy-done.4) | copy-start | bytes 5160964
  87.7 19.5 %collective-permute-start.8 = (bf16[672,1280]{1,0:T(8,128)(2,1)}, bf16[672,1280]{1,0:T(8,128)(2,1)S(1)}, u32[]{:S(2)}, u32[]{:S(2)}) collective-permute-start(bf16[672,1280]{1,0:T(8,128)(2,1)} %copy-done.4), channel_id=1, source_target_pairs={{0,1},{1,0},{2,3},{3,2},{4,5},{5,4},{6,7},{7,6},{8,9},{9,8},{10,11... | collective-permute-start | bytes 5160968 | tf_op jit(solution)/shard_map/ppermute | solution.py:53
  87.8 19.4 %collective-permute-start.9 = (bf16[672,1280]{1,0:T(8,128)(2,1)}, bf16[672,1280]{1,0:T(8,128)(2,1)S(1)}, u32[]{:S(2)}, u32[]{:S(2)}) collective-permute-start(bf16[672,1280]{1,0:T(8,128)(2,1)} %copy-done.2), channel_id=1, source_target_pairs={{0,1},{1,0},{2,3},{3,2},{4,5},{5,4},{6,7},{7,6},{8,9},{9,8},{10,11... | collective-permute-start | bytes 5160968 | tf_op jit(solution)/shard_map/ppermute | solution.py:53
  101.4 16.6 %copy-start.7 = (f32[256,1280]{1,0:T(8,128)S(1)}, f32[256,1280]{1,0:T(8,128)}, u32[]{:S(2)}) copy-start(f32[256,1280]{1,0:T(8,128)} %copy-done.6) | copy-start | bytes 3932164
  101.4 16.6 %copy-start.14 = (bf16[256,1280]{1,0:T(8,128)(2,1)S(1)}, bf16[256,1280]{1,0:T(8,128)(2,1)}, u32[]{:S(2)}) copy-start(bf16[256,1280]{1,0:T(8,128)(2,1)} %copy-done.13) | copy-start | bytes 1966084
  101.4 5.8 %collective-permute-start.12 = (bf16[336,1280]{1,0:T(8,128)(2,1)}, bf16[336,1280]{1,0:T(8,128)(2,1)S(1)}, u32[]{:S(2)}, u32[]{:S(2)}) collective-permute-start(bf16[336,1280]{1,0:T(8,128)(2,1)} %collective-permute-done.10.refs_10_.refs_6_), channel_id=1, source_target_pairs={{0,1},{1,0},{2,3},{3,2},{4,5},{5,4},{6,7},{7,6},{8,9},{9,8},{10,11... | collective-permute-start | bytes 2580488 | tf_op jit(solution)/shard_map/ppermute | solution.py:53
  101.5 5.7 %collective-permute-start.13 = (bf16[336,1280]{1,0:T(8,128)(2,1)}, bf16[336,1280]{1,0:T(8,128)(2,1)S(1)}, u32[]{:S(2)}, u32[]{:S(2)}) collective-permute-start(bf16[336,1280]{1,0:T(8,128)(2,1)} %collective-permute-done.11.refs_12_.refs_8_), channel_id=1, source_target_pairs={{0,1},{1,0},{2,3},{3,2},{4,5},{5,4},{6,7},{7,6},{8,9},{9,8},{10,11... | collective-permute-start | bytes 2580488 | tf_op jit(solution)/shard_map/ppermute | solution.py:53
  102.0 5.2 %collective-permute-start.14 = (bf16[16,1280]{1,0:T(8,128)(2,1)S(1)}, bf16[16,1280]{1,0:T(8,128)(2,1)S(1)}, u32[]{:S(2)}, u32[]{:S(2)}) collective-permute-start(bf16[16,1280]{1,0:T(8,128)(2,1)S(1)} %get-tuple-element.60.refs_3_), channel_id=1, source_target_pairs={{0,8},{1,9},{2,10},{3,11},{4,12},{5,13},{6,14},{7,15},{8,16},{9,17... | collective-permute-start | bytes 122888 | tf_op jit(solution)/shard_map/ppermute | solution.py:53
  114.7 9.8 %collective-permute-start.16 = (bf16[128,1280]{1,0:T(8,128)(2,1)S(1)}, bf16[128,1280]{1,0:T(8,128)(2,1)S(1)}, u32[]{:S(2)}, u32[]{:S(2)}) collective-permute-start(bf16[128,1280]{1,0:T(8,128)(2,1)S(1)} %get-tuple-element.69), channel_id=1, source_target_pairs={{0,8},{1,9},{2,10},{3,11},{4,12},{5,13},{6,14},{7,15},{8,16},{9,17... | collective-permute-start | bytes 983048 | tf_op jit(solution)/shard_map/ppermute | solution.py:53
  114.7 9.9 %collective-permute-start.15 = (bf16[144,1280]{1,0:T(8,128)(2,1)S(1)}, bf16[144,1280]{1,0:T(8,128)(2,1)S(1)}, u32[]{:S(2)}, u32[]{:S(2)}) collective-permute-start(bf16[144,1280]{1,0:T(8,128)(2,1)S(1)} %get-tuple-element.68), channel_id=1, source_target_pairs={{0,24},{1,25},{2,26},{3,27},{4,28},{5,29},{6,30},{7,31},{8,0},{9,1... | collective-permute-start | bytes 1105928 | tf_op jit(solution)/shard_map/ppermute | solution.py:53

commit v9 on v8

--- a/solution.py
+++ b/solution.py
@@ -279,15 +279,18 @@
 
     index_rows = [index_ref[i : i + 1, :] for i in range(8)]
 
+    def chosen(k):
+        wanted = jnp.broadcast_to(slot_ref[k : k + 1, :], (8, 128))
+        slot = sublanes((8, 128))
+        return ((wanted == first_slot + slot) & (slot < SLOTS)).astype(F32).astype(BF)
+
     @pl.when(step == 0)
     def _():
         spread[...] = (
             sublanes((QW, 384)) % HEAD == lanes((QW, 384)) % HEAD
         ).astype(F32).astype(BF)
-        wanted = jnp.broadcast_to(slot_ref[...], (8, 256))
-        slot = sublanes((8, 256))
-        chosen = ((wanted == first_slot + slot) & (slot < SLOTS)).astype(F32).astype(BF)
-        rows = jnp.dot(chosen, rows_ref[...], preferred_element_type=F32)
+        rows = jnp.dot(chosen(0), rows_ref[:, 0, :], preferred_element_type=F32)
+        rows += jnp.dot(chosen(1), rows_ref[:, 1, :], preferred_element_type=F32)
         normed = norm_rows(rows, gain_ref[...])
         projected = jnp.dot(normed, w_ref[...], preferred_element_type=F32)
         projected = projected.astype(BF).astype(F32)
@@ -389,13 +392,11 @@
 
     @pl.when(step == SLOTS - 1)
     def _():
-        wanted = jnp.broadcast_to(slot_ref[...], (8, 256))
-        slot = sublanes((8, 256))
-        chosen = ((wanted == first_slot + slot) & (slot < SLOTS)).astype(F32).astype(BF)
         good = jnp.where(sublanes((8, QW)) < SLOTS, result[...], 0.0).astype(BF)
-        out_ref[...] = lax.dot_general(
-            chosen, good, (((0,), (0,)), ((), ())), preferred_element_type=F32
-        ).astype(BF)
+        for k in range(2):
+            out_ref[:, k, :] = lax.dot_general(
+                chosen(k), good, (((0,), (0,)), ((), ())), preferred_element_type=F32
+            ).astype(BF)
 
 
 def decode_attention(
@@ -405,15 +406,15 @@
     full = lambda shape: pl.BlockSpec(shape, lambda j: (0,) * len(shape))
     return pl.pallas_call(
         decode_kernel,
-        out_shape=jax.ShapeDtypeStruct((256, QW), BF),
+        out_shape=jax.ShapeDtypeStruct((128, 2, QW), BF),
         grid=(2 * SLOTS,),
         in_specs=[
             smem,
             smem,
             smem,
-            full((1, 256)),
+            full((2, 128)),
             full((8, 128)),
-            full((256, WIDTH)),
+            full((128, 2, WIDTH)),
             full((WIDTH,)),
             pl.BlockSpec(
                 (WIDTH, QW + KVW), lambda j: (0, 0), pipeline_mode=pl.Buffered(1)
@@ -421,7 +422,7 @@
             pl.BlockSpec((None, POSITIONS, KVW), lambda j: (jnp.maximum(j - SLOTS, 0), 0, 0)),
             pl.BlockSpec((256, WIDTH), lambda j: (jnp.minimum(j, SLOTS - 1), 0)),
         ],
-        out_specs=full((256, QW)),
+        out_specs=full((128, 2, QW)),
         scratch_shapes=[
             pltpu.VMEM((1024, KVW), BF),
             pltpu.VMEM((QW, 384), BF),
@@ -671,7 +672,7 @@
     )
     total = 2 * SIDE**3
     spread = jnp.broadcast_to(decode_hidden[None], (total, 2, WIDTH))
-    every_row = lax.all_to_all(spread, "req", 0, 0).reshape(256, WIDTH)
+    every_row = lax.all_to_all(spread, "req", 0, 0)
 
     packed = pack_weights(*in_hbm(jnp.swapaxes(w_gate_up, 1, 2), w_down))
     (kv,) = in_hbm(project(rank, prefill_hidden, gain, w_qkv, True))
@@ -687,7 +688,7 @@
         device,
         cache_len,
         recomp_count,
-        slot_of_request.reshape(1, 256),
+        slot_of_request.reshape(128, 2).T,
         index,
         every_row,
         gain,
@@ -704,7 +705,7 @@
     far_low, far_high = cut_halves(below, above)
     far_low = send(far_low, next_z)
     far_high = send(far_high, last_z)
-    back = lax.all_to_all(outgoing.reshape(total, 2, WIDTH), "req", 0, 0)
+    back = lax.all_to_all(outgoing, "req", 0, 0)
 
     resid, lower, upper = attention(
         rank, query, kv, core, zed, far, w_out, prefill_hidden, gain2

time: 127 us -> 125 us (0.984)
  local copies, waits for them, and re-layouts: 12.8 us -> 6.53 us
  waiting for transfers between devices: 16.9 us -> 20 us
  Pallas kernels: 56.6 us -> 58.3 us
    reshape x2, local copies, waits for them, and re-layouts: 5.34 us -> 0.19 us  [body(): slot_of_request.reshape(128, 2)]
    ppermute x17, waiting for transfers between devices: 16.9 us -> 20 us  [send(): return lax.ppermute(array, 'req', moves(step))]
    pallas_call x1, Pallas kernels: 13.4 us -> 15.1 us  [decode_attention(): pl.pallas_call(decode_kernel, out_shape=jax.ShapeDtypeStruct((128, 2, QW)...]
    unnamed x36 -> x34, local copies, waits for them, and re-layouts: 5.61 us -> 4.45 us
  transfers between devices with their start and end apart: 19 -> 19, of which waited for: 4 -> 5; matrix products, arithmetic and copies ran while one was open for 4% -> 0% of each run, Pallas kernels for 38% -> 40%
where the time goes in v9:
time: 125 us; the launch traced here: 124 us
  Pallas kernels  58.3 us (47%)
  starting transfers between devices  37.3 us (30%)
  waiting for transfers between devices  20 us (16%)
  local copies, waits for them, and re-layouts  6.53 us (5%)
  between operations  1.55 us (1%)
    ppermute x17, waiting for transfers between devices, send(): return lax.ppermute(array, 'req', moves(step))  20 us
    pallas_call x3, Pallas kernels, feed_forward(): pl.pallas_call(kernel, out_shape=outputs, in_specs=[vmem] * len(inputs),...  16.3 us
    pallas_call x1, Pallas kernels, decode_attention(): pl.pallas_call(decode_kernel, out_shape=jax.ShapeDtypeStruct((128, 2, QW)...  15.1 us
    ppermute x17, starting transfers between devices, send(): return lax.ppermute(array, 'req', moves(step))  14.8 us
    pallas_call x1, Pallas kernels, attention(): pl.pallas_call(attention_kernel, out_shape=(jax.ShapeDtypeStruct((ROWS, W...  12.3 us
    all_to_all x1, starting transfers between devices, body(): every_row = lax.all_to_all(spread, 'req', 0, 0)  11.6 us
    all_to_all x1, starting transfers between devices, body(): back = lax.all_to_all(outgoing, 'req', 0, 0)  10.9 us
    pallas_call x2, Pallas kernels, project(): pl.pallas_call(kv_kernel if keys else query_kernel, out_shape=jax.ShapeDt...  7.19 us
  transfers between devices with their start and end apart: 19, of which 5 were waited for; matrix products, arithmetic and copies ran while one was open for 0% of the time, Pallas kernels for 40%

profile of v9, /device:TPU:0, one launch (start us, length us, event | category | flops | bytes accessed | tf_op | source)
XLA Modules:
  0.0 123.7 jit_solution(4126620391112133358)
XLA Ops:
  0.6 1.9 %broadcast_in_dim.2 = bf16[128,2,1280]{2,1,0:T(2,128)(2,1)} broadcast(bf16[2,1280]{1,0:T(2,128)(2,1)} %decode_ref.1), dimensions={1,2} | broadcast | bytes 660480 | tf_op jit(solution)/shard_map/broadcast_in_dim | solution.py:674
  2.5 11.6 %all-to-all-start = ((bf16[128,2,1280]{2,1,0:T(2,128)(2,1)}), bf16[128,2,1280]{2,1,0:T(2,128)(2,1)}, u32[]{:S(2)}, u32[]{:S(2)}) async-start(bf16[128,2,1280]{2,1,0:T(2,128)(2,1)} %broadcast_in_dim.2), calls=%async_computation | async-start | bytes 1310720 | tf_op jit(solution)/shard_map/all_to_all | solution.py:675
  14.1 0.0 copy-start.11
  14.2 2.5 %pack.1.refs_2_.refs_4_ = bf16[672,1280]{1,0:T(8,128)(2,1)} custom-call(bf16[1,448,1280]{2,1,0:T(8,128)(2,1)} %bitcast.6, bf16[1,224,1280]{2,1,0:T(8,128)(2,1)} %down_ref.1), custom_call_target="tpu_custom_call" | custom-call | flops 1500000000 | bytes 4500000 | tf_op jit(solution)/shard_map/pack/pallas_call | solution.py:138
  16.6 0.0 copy-done.11
  16.6 3.3 %prefill_kv.1.own_ref = bf16[256,640]{1,0:T(8,128)(2,1)} custom-call(s32[1]{0:T(128)S(6)} %select_n.7.rank_ref, bf16[256,1280]{1,0:T(8,128)(2,1)} %hidden_ref.7, f32[1280]{0:T(1024)S(1)} %copy-done.11, bf16[1280,1920]{1,0:T(8,128)(2,1)} %w_ref.7), custom_call_target="tpu_custom_call" | custom-call | flops 3000000000 | bytes 9000000 | tf_op jit(solution)/shard_map/prefill_kv/pallas_call | solution.py:213
  20.0 0.0 collective-permute-start.2
  20.0 0.5 collective-permute-start.1
  20.5 1.0 collective-permute-start
  21.5 2.3 %collective-permute-start.5 = (bf16[672,1280]{1,0:T(8,128)(2,1)}, bf16[672,1280]{1,0:T(8,128)(2,1)S(1)}, u32[]{:S(2)}, u32[]{:S(2)}) collective-permute-start(bf16[672,1280]{1,0:T(8,128)(2,1)} %pack.1.refs_2_.refs_4_), channel_id=1, source_target_pairs={{0,6},{1,7},{2,0},{3,1},{4,2},{5,3},{6,4},{7,5},{8,14},{9,15},{10,... | collective-permute-start | bytes 5160968 | tf_op jit(solution)/shard_map/ppermute | solution.py:53
  23.8 0.0 collective-permute-start.4
  24.5 0.1 reshape.17
  24.6 0.1 copy.16
  24.7 3.9 %prefill_query.1.query_ref = bf16[256,1280]{1,0:T(8,128)(2,1)S(1)} custom-call(s32[1]{0:T(128)S(6)} %select_n.7.rank_ref, bf16[256,1280]{1,0:T(8,128)(2,1)} %hidden_ref.7, f32[1280]{0:T(1024)S(1)} %copy-done.11, bf16[1280,1920]{1,0:T(8,128)(2,1)} %w_ref.7), custom_call_target="tpu_custom_call" | custom-call | flops 100000000 | bytes 300000 | tf_op jit(solution)/shard_map/prefill_query/pallas_call | solution.py:213
  28.6 0.0 copy-start.1
  28.6 0.8 copy-done.1
  29.4 0.0 all-to-all-done.rows_ref
  29.4 0.0 copy-done.14
  29.4 0.0 copy-start.9
  29.4 15.1 %decode.1 = bf16[128,2,1280]{2,1,0:T(2,128)(2,1)S(1)} custom-call(s32[1]{0:T(128)} %bitcast.device_ref, s32[4]{0:T(128)S(1)} %copy-done.15, s32[1]{0:T(128)S(6)} %copy.17.count_ref, s32[2,128]{1,0:T(2,128)S(1)} %bitcast.4, s32[8,128]{1,0:T(8,128)S(1)} %bitcast.5, bf16[128,2,1280]{2,1,0:T(2,128)(2,1)} %all-to-all-done.rows_ref, f32[1280]{0:T(1024)S(1)} %copy-done.11, ...), custom_call_target="tpu_custom_call" | custom-call | flops 16999999488 | bytes 51000000 | tf_op jit(solution)/shard_map/decode/pallas_call | solution.py:407
  44.5 0.0 collective-permute-done.1.core_ref
  44.5 0.0 collective-permute-done.zed_ref
  44.5 0.0 collective-permute-done.2.refs_3_.refs_5_
  44.5 0.8 copy-done.8
  45.4 0.0 collective-permute-start.3
  45.4 10.9 %all-to-all-start.1 = ((bf16[128,2,1280]{2,1,0:T(2,128)(2,1)}), bf16[128,2,1280]{2,1,0:T(2,128)(2,1)}, u32[]{:S(2)}, u32[]{:S(2)}) async-start(bf16[128,2,1280]{2,1,0:T(2,128)(2,1)} %copy-done.8), calls=%async_computation.1 | async-start | bytes 1310720 | tf_op jit(solution)/shard_map/all_to_all | solution.py:708
  56.3 0.0 collective-permute-done.3.far_ref
  56.3 0.0 copy-done.9
  56.3 12.3 %attention.1 = (bf16[256,1280]{1,0:T(8,128)(2,1)S(1)}, bf16[128,1280]{1,0:T(8,128)(2,1)}, bf16[128,1280]{1,0:T(8,128)(2,1)}) custom-call(s32[1]{0:T(128)S(6)} %select_n.7.rank_ref, bf16[256,1280]{1,0:T(8,128)(2,1)} %copy-done.1, bf16[256,640]{1,0:T(8,128)(2,1)} %prefill_kv.1.own_ref, bf16[256,640]{1,0:T(8,128)(2,1)} %collective-permute-done.1.core_ref, ...), custom_call_target="tpu_custom_call" | custom-call | flops 100000000 | bytes 300000 | tf_op jit(solution)/shard_map/attention/pallas_call | solution.py:523
  68.6 0.8 copy-done.12
  69.4 0.7 collective-permute-start.6
  70.2 2.5 %collective-permute-start.7 = (bf16[128,1280]{1,0:T(8,128)(2,1)}, bf16[128,1280]{1,0:T(8,128)(2,1)}, u32[]{:S(2)}, u32[]{:S(2)}) collective-permute-start(bf16[128,1280]{1,0:T(8,128)(2,1)} %get-tuple-element.43.refs_1_), channel_id=1, source_target_pairs={{0,24},{1,25},{2,26},{3,27},{4,28},{5,29},{6,30},{7,31},{8,0},{9,1... | collective-permute-start | bytes 983048 | tf_op jit(solution)/shard_map/ppermute | solution.py:53
  72.7 2.9 %collective-permute-done.5.above_ref.refs_8_.refs_4_ = bf16[672,1280]{1,0:T(8,128)(2,1)S(1)} collective-permute-done((bf16[672,1280]{1,0:T(8,128)(2,1)}, bf16[672,1280]{1,0:T(8,128)(2,1)S(1)}, u32[]{:S(2)}, u32[]{:S(2)}) %collective-permute-start.5) | collective-permute-done | bytes 1720352 | tf_op jit(solution)/shard_map/ppermute | solution.py:53
  75.6 0.0 collective-permute-done.4.below_ref.refs_6_.refs_2_
  75.6 1.4 %cut.1 = (bf16[336,1280]{1,0:T(8,128)(2,1)}, bf16[336,1280]{1,0:T(8,128)(2,1)}) custom-call(bf16[672,1280]{1,0:T(8,128)(2,1)S(1)} %collective-permute-done.4.below_ref.refs_6_.refs_2_, bf16[672,1280]{1,0:T(8,128)(2,1)S(1)} %collective-permute-done.5.above_ref.refs_8_.refs_4_), custom_call_target="tpu_custom_call" | custom-call | flops 500000000 | bytes 1500000 | tf_op jit(solution)/shard_map/cut/pallas_call | solution.py:160
  77.0 0.3 copy-done.2
  77.3 0.1 collective-permute-start.10
  77.4 0.5 copy-done.4
  77.8 2.7 %collective-permute-start.11 = (bf16[336,1280]{1,0:T(8,128)(2,1)}, bf16[336,1280]{1,0:T(8,128)(2,1)}, u32[]{:S(2)}, u32[]{:S(2)}) collective-permute-start(bf16[336,1280]{1,0:T(8,128)(2,1)} %get-tuple-element.55), channel_id=1, source_target_pairs={{0,6},{1,7},{2,0},{3,1},{4,2},{5,3},{6,4},{7,5},{8,14},{9,15},{10,... | collective-permute-start | bytes 2580488 | tf_op jit(solution)/shard_map/ppermute | solution.py:53
  80.6 3.7 %feed_first.1.refs_10_ = f32[256,1280]{1,0:T(8,128)S(1)} custom-call(bf16[128,1280]{1,0:T(8,128)(2,1)} %get-tuple-element.42.refs_0_, bf16[128,1280]{1,0:T(8,128)(2,1)} %get-tuple-element.43.refs_1_, bf16[672,1280]{1,0:T(8,128)(2,1)} %pack.1.refs_2_.refs_4_, bf16[672,1280]{1,0:T(8,128)(2,1)} %collective-permute-done.2.refs_3_.refs_5_), custom_call_target="tpu_custom_call" | custom-call | flops 100000000 | bytes 300000 | tf_op jit(solution)/shard_map/feed_first/pallas_call | solution.py:614
  84.3 1.1 copy-done.6
  85.4 0.0 all-to-all-done.1.back_ref
  85.4 0.0 collective-permute-done.6.refs_0_
  85.4 0.0 collective-permute-done.7.refs_2_
  85.4 0.1 collective-permute-start.8
  85.5 0.5 collective-permute-start.9
  86.0 2.6 %decode_rows.1 = (bf16[16,1280]{1,0:T(8,128)(2,1)S(1)}, bf16[16,1280]{1,0:T(8,128)(2,1)S(1)}) custom-call(bf16[128,2,1280]{2,1,0:T(2,128)(2,1)} %all-to-all-done.1.back_ref, bf16[1280,1280]{1,0:T(8,128)(2,1)S(1)} %copy-done, bf16[2,1280]{1,0:T(2,128)(2,1)S(1)} %copy-done.10, f32[1280]{0:T(1024)S(1)} %copy-done.9), custom_call_target="tpu_custom_call" | custom-call | flops 100000000 | bytes 300000 | tf_op jit(solution)/shard_map/decode_rows/pallas_call | solution.py:569
  88.6 10.9 %collective-permute-done.10.refs_10_.refs_6_ = bf16[336,1280]{1,0:T(8,128)(2,1)} collective-permute-done((bf16[336,1280]{1,0:T(8,128)(2,1)}, bf16[336,1280]{1,0:T(8,128)(2,1)}, u32[]{:S(2)}, u32[]{:S(2)}) %collective-permute-start.10) | collective-permute-done | bytes 860192 | tf_op jit(solution)/shard_map/ppermute | solution.py:53
  99.5 0.0 collective-permute-done.11.refs_12_.refs_8_
  99.5 0.1 collective-permute-start.12
  99.6 0.5 collective-permute-start.13
  100.1 0.5 collective-permute-start.14
  100.6 4.7 %collective-permute-done.14.refs_1_ = bf16[16,1280]{1,0:T(8,128)(2,1)S(1)} collective-permute-done((bf16[16,1280]{1,0:T(8,128)(2,1)S(1)}, bf16[16,1280]{1,0:T(8,128)(2,1)S(1)}, u32[]{:S(2)}, u32[]{:S(2)}) %collective-permute-start.14) | collective-permute-done | bytes 40992 | tf_op jit(solution)/shard_map/ppermute | solution.py:53
  105.3 0.0 collective-permute-done.12.refs_11_.refs_7_
  105.4 0.0 collective-permute-done.13.refs_13_.refs_9_
  105.4 0.0 collective-permute-done.8.refs_7_.refs_3_
  105.4 0.0 collective-permute-done.9.refs_9_.refs_5_
  105.4 7.4 %feed_guest.1 = (bf16[144,1280]{1,0:T(8,128)(2,1)S(1)}, bf16[128,1280]{1,0:T(8,128)(2,1)S(1)}, bf16[16,1280]{1,0:T(8,128)(2,1)S(1)}) custom-call(bf16[128,1280]{1,0:T(8,128)(2,1)} %collective-permute-done.6.refs_0_, bf16[16,1280]{1,0:T(8,128)(2,1)S(1)} %collective-permute-done.14.refs_1_, bf16[128,1280]{1,0:T(8,128)(2,1)} %collective-permute-done.7.refs_2_, ...), custom_call_target="tpu_custom_call" | custom-call | flops 8000000000 | bytes 24000000 | tf_op jit(solution)/shard_map/feed_guest/pallas_call | solution.py:614
  112.8 0.1 collective-permute-start.16
  112.9 3.2 %collective-permute-start.15 = (bf16[144,1280]{1,0:T(8,128)(2,1)S(1)}, bf16[144,1280]{1,0:T(8,128)(2,1)S(1)}, u32[]{:S(2)}, u32[]{:S(2)}) collective-permute-start(bf16[144,1280]{1,0:T(8,128)(2,1)S(1)} %get-tuple-element.68), channel_id=1, source_target_pairs={{0,24},{1,25},{2,26},{3,27},{4,28},{5,29},{6,30},{7,31},{8,0},{9,1... | collective-permute-start | bytes 1105928 | tf_op jit(solution)/shard_map/ppermute | solution.py:53
  116.1 5.2 %feed_second.1.start_ref = f32[256,1280]{1,0:T(8,128)S(1)} custom-call(bf16[128,1280]{1,0:T(8,128)(2,1)} %get-tuple-element.42.refs_0_, bf16[128,1280]{1,0:T(8,128)(2,1)} %get-tuple-element.43.refs_1_, bf16[672,1280]{1,0:T(8,128)(2,1)S(1)} %copy-done.5, bf16[672,1280]{1,0:T(8,128)(2,1)S(1)} %collective-permute-done.8.refs_7_.refs_3_, ...), custom_call_target="tpu_custom_call" | custom-call | flops 6000000000 | bytes 18000000 | tf_op jit(solution)/shard_map/feed_second/pallas_call | solution.py:614
  121.3 1.3 %collective-permute-done.16.second_ref = bf16[128,1280]{1,0:T(8,128)(2,1)S(1)} collective-permute-done((bf16[128,1280]{1,0:T(8,128)(2,1)S(1)}, bf16[128,1280]{1,0:T(8,128)(2,1)S(1)}, u32[]{:S(2)}, u32[]{:S(2)}) %collective-permute-start.16) | collective-permute-done | bytes 327712 | tf_op jit(solution)/shard_map/ppermute | solution.py:53
  122.6 0.1 collective-permute-done.15.first_ref
  122.8 1.0 final.1
  (22 shorter events, 0.0 us)
Async XLA Ops:
  2.5 26.9 %all-to-all-start = ((bf16[128,2,1280]{2,1,0:T(2,128)(2,1)}), bf16[128,2,1280]{2,1,0:T(2,128)(2,1)}, u32[]{:S(2)}, u32[]{:S(2)}) async-start(bf16[128,2,1280]{2,1,0:T(2,128)(2,1)} %broadcast_in_dim.2), calls=%async_computation | async-start | bytes 1310720 | tf_op jit(solution)/shard_map/all_to_all | solution.py:675
  14.1 2.5 %copy-start.11 = (f32[1280]{0:T(1024)S(1)}, f32[1280]{0:T(1024)}, u32[]{:S(2)}) copy-start(f32[1280]{0:T(1024)} %gain_ref.7) | copy-start | bytes 15364
  16.6 7.9 %copy-start.16 = (s32[256]{0:T(256)S(1)}, s32[256]{0:T(256)}, u32[]{:S(2)}) copy-start(s32[256]{0:T(256)} %param.24) | copy-start | bytes 3076
  20.0 24.6 %collective-permute-start.2 = (bf16[672,1280]{1,0:T(8,128)(2,1)}, bf16[672,1280]{1,0:T(8,128)(2,1)}, u32[]{:S(2)}, u32[]{:S(2)}) collective-permute-start(bf16[672,1280]{1,0:T(8,128)(2,1)} %pack.1.refs_2_.refs_4_), channel_id=1, source_target_pairs={{0,1},{1,0},{2,3},{3,2},{4,5},{5,4},{6,7},{7,6},{8,9},{9,8},{10,11... | collective-permute-start | bytes 5160968 | tf_op jit(solution)/shard_map/ppermute | solution.py:53
  20.0 24.6 %collective-permute-start.1 = (bf16[256,640]{1,0:T(8,128)(2,1)}, bf16[256,640]{1,0:T(8,128)(2,1)}, u32[]{:S(2)}, u32[]{:S(2)}) collective-permute-start(bf16[256,640]{1,0:T(8,128)(2,1)} %prefill_kv.1.own_ref), channel_id=1, source_target_pairs={{0,1},{1,0},{2,3},{3,2},{4,5},{5,4},{6,7},{7,6},{8,9},{9,8},{10,11... | collective-permute-start | bytes 983048 | tf_op jit(solution)/shard_map/ppermute | solution.py:53
  20.5 24.1 %collective-permute-start = (bf16[256,640]{1,0:T(8,128)(2,1)}, bf16[256,640]{1,0:T(8,128)(2,1)}, u32[]{:S(2)}, u32[]{:S(2)}) collective-permute-start(bf16[256,640]{1,0:T(8,128)(2,1)} %prefill_kv.1.own_ref), channel_id=1, source_target_pairs={{0,2},{1,3},{2,0},{3,1},{4,6},{5,7},{6,4},{7,5},{8,10},{9,11},{10,... | collective-permute-start | bytes 983048 | tf_op jit(solution)/shard_map/ppermute | solution.py:53
  21.5 54.1 %collective-permute-start.5 = (bf16[672,1280]{1,0:T(8,128)(2,1)}, bf16[672,1280]{1,0:T(8,128)(2,1)S(1)}, u32[]{:S(2)}, u32[]{:S(2)}) collective-permute-start(bf16[672,1280]{1,0:T(8,128)(2,1)} %pack.1.refs_2_.refs_4_), channel_id=1, source_target_pairs={{0,6},{1,7},{2,0},{3,1},{4,2},{5,3},{6,4},{7,5},{8,14},{9,15},{10,... | collective-permute-start | bytes 5160968 | tf_op jit(solution)/shard_map/ppermute | solution.py:53
  23.8 51.7 %collective-permute-start.4 = (bf16[672,1280]{1,0:T(8,128)(2,1)}, bf16[672,1280]{1,0:T(8,128)(2,1)S(1)}, u32[]{:S(2)}, u32[]{:S(2)}) collective-permute-start(bf16[672,1280]{1,0:T(8,128)(2,1)} %pack.1.refs_2_.refs_4_), channel_id=1, source_target_pairs={{0,2},{1,3},{2,4},{3,5},{4,6},{5,7},{6,0},{7,1},{8,10},{9,11},{10,... | collective-permute-start | bytes 5160968 | tf_op jit(solution)/shard_map/ppermute | solution.py:53
  24.7 4.7 %copy-start.14 = (s32[1024]{0:T(1024)S(1)}, s32[1024]{0:T(1024)}, u32[]{:S(2)}) copy-start(s32[1024]{0:T(1024)} %param.26) | copy-start | bytes 12292
  24.7 4.7 %copy-start.15 = (s32[4]{0:T(128)S(1)}, s32[4]{0:T(128)}, u32[]{:S(2)}) copy-start(s32[4]{0:T(128)} %length_ref.1) | copy-start | bytes 52
  28.6 0.8 copy-start.1
  29.4 26.9 %copy-start.9 = (f32[1280]{0:T(1024)S(1)}, f32[1280]{0:T(1024)}, u32[]{:S(2)}) copy-start(f32[1280]{0:T(1024)} %gain_ref.9) | copy-start | bytes 15364
  44.5 0.9 copy-start.8
  45.4 10.9 %collective-permute-start.3 = (bf16[256,640]{1,0:T(8,128)(2,1)}, bf16[256,640]{1,0:T(8,128)(2,1)}, u32[]{:S(2)}, u32[]{:S(2)}) collective-permute-start(bf16[256,640]{1,0:T(8,128)(2,1)} %collective-permute-done.zed_ref), channel_id=1, source_target_pairs={{0,1},{1,0},{2,3},{3,2},{4,5},{5,4},{6,7},{7,6},{8,9},{9,8},{10,11... | collective-permute-start | bytes 983048 | tf_op jit(solution)/shard_map/ppermute | solution.py:53
  45.4 40.0 %all-to-all-start.1 = ((bf16[128,2,1280]{2,1,0:T(2,128)(2,1)}), bf16[128,2,1280]{2,1,0:T(2,128)(2,1)}, u32[]{:S(2)}, u32[]{:S(2)}) async-start(bf16[128,2,1280]{2,1,0:T(2,128)(2,1)} %copy-done.8), calls=%async_computation.1 | async-start | bytes 1310720 | tf_op jit(solution)/shard_map/all_to_all | solution.py:708
  68.6 0.8 copy-start.12
  69.4 15.9 %collective-permute-start.6 = (bf16[128,1280]{1,0:T(8,128)(2,1)}, bf16[128,1280]{1,0:T(8,128)(2,1)}, u32[]{:S(2)}, u32[]{:S(2)}) collective-permute-start(bf16[128,1280]{1,0:T(8,128)(2,1)} %get-tuple-element.42.refs_0_), channel_id=1, source_target_pairs={{0,8},{1,9},{2,10},{3,11},{4,12},{5,13},{6,14},{7,15},{8,16},{9,17... | collective-permute-start | bytes 983048 | tf_op jit(solution)/shard_map/ppermute | solution.py:53
  70.2 15.2 %collective-permute-start.7 = (bf16[128,1280]{1,0:T(8,128)(2,1)}, bf16[128,1280]{1,0:T(8,128)(2,1)}, u32[]{:S(2)}, u32[]{:S(2)}) collective-permute-start(bf16[128,1280]{1,0:T(8,128)(2,1)} %get-tuple-element.43.refs_1_), channel_id=1, source_target_pairs={{0,24},{1,25},{2,26},{3,27},{4,28},{5,29},{6,30},{7,31},{8,0},{9,1... | collective-permute-start | bytes 983048 | tf_op jit(solution)/shard_map/ppermute | solution.py:53
  75.6 1.8 %copy-start.2 = (bf16[672,1280]{1,0:T(8,128)(2,1)}, bf16[672,1280]{1,0:T(8,128)(2,1)S(1)}, u32[]{:S(2)}) copy-start(bf16[672,1280]{1,0:T(8,128)(2,1)S(1)} %collective-permute-done.5.above_ref.refs_8_.refs_4_) | copy-start | bytes 5160964
  75.6 2.3 %copy-start.4 = (bf16[672,1280]{1,0:T(8,128)(2,1)}, bf16[672,1280]{1,0:T(8,128)(2,1)S(1)}, u32[]{:S(2)}) copy-start(bf16[672,1280]{1,0:T(8,128)(2,1)S(1)} %collective-permute-done.4.below_ref.refs_6_.refs_2_) | copy-start | bytes 5160964
  77.3 22.2 %collective-permute-start.10 = (bf16[336,1280]{1,0:T(8,128)(2,1)}, bf16[336,1280]{1,0:T(8,128)(2,1)}, u32[]{:S(2)}, u32[]{:S(2)}) collective-permute-start(bf16[336,1280]{1,0:T(8,128)(2,1)} %get-tuple-element.54), channel_id=1, source_target_pairs={{0,2},{1,3},{2,4},{3,5},{4,6},{5,7},{6,0},{7,1},{8,10},{9,11},{10,... | collective-permute-start | bytes 2580488 | tf_op jit(solution)/shard_map/ppermute | solution.py:53
  77.8 8.1 %copy-start = (bf16[1280,1280]{1,0:T(8,128)(2,1)S(1)}, bf16[1280,1280]{1,0:T(8,128)(2,1)}, u32[]{:S(2)}) copy-start(bf16[1280,1280]{1,0:T(8,128)(2,1)} %w_ref.9) | copy-start | bytes 9830404
  77.8 8.1 %copy-start.10 = (bf16[2,1280]{1,0:T(2,128)(2,1)S(1)}, bf16[2,1280]{1,0:T(2,128)(2,1)}, u32[]{:S(2)}) copy-start(bf16[2,1280]{1,0:T(2,128)(2,1)} %decode_ref.1) | copy-start | bytes 15364
  77.8 21.7 %collective-permute-start.11 = (bf16[336,1280]{1,0:T(8,128)(2,1)}, bf16[336,1280]{1,0:T(8,128)(2,1)}, u32[]{:S(2)}, u32[]{:S(2)}) collective-permute-start(bf16[336,1280]{1,0:T(8,128)(2,1)} %get-tuple-element.55), channel_id=1, source_target_pairs={{0,6},{1,7},{2,0},{3,1},{4,2},{5,3},{6,4},{7,5},{8,14},{9,15},{10,... | collective-permute-start | bytes 2580488 | tf_op jit(solution)/shard_map/ppermute | solution.py:53
  84.3 1.1 copy-start.6
  85.4 20.0 %copy-start.3 = (bf16[672,1280]{1,0:T(8,128)(2,1)S(1)}, bf16[672,1280]{1,0:T(8,128)(2,1)}, u32[]{:S(2)}) copy-start(bf16[672,1280]{1,0:T(8,128)(2,1)} %copy-done.2) | copy-start | bytes 5160964
  85.4 20.0 %copy-start.5 = (bf16[672,1280]{1,0:T(8,128)(2,1)S(1)}, bf16[672,1280]{1,0:T(8,128)(2,1)}, u32[]{:S(2)}) copy-start(bf16[672,1280]{1,0:T(8,128)(2,1)} %copy-done.4) | copy-start | bytes 5160964
  85.4 20.0 %collective-permute-start.8 = (bf16[672,1280]{1,0:T(8,128)(2,1)}, bf16[672,1280]{1,0:T(8,128)(2,1)S(1)}, u32[]{:S(2)}, u32[]{:S(2)}) collective-permute-start(bf16[672,1280]{1,0:T(8,128)(2,1)} %copy-done.4), channel_id=1, source_target_pairs={{0,1},{1,0},{2,3},{3,2},{4,5},{5,4},{6,7},{7,6},{8,9},{9,8},{10,11... | collective-permute-start | bytes 5160968 | tf_op jit(solution)/shard_map/ppermute | solution.py:53
  85.5 19.9 %collective-permute-start.9 = (bf16[672,1280]{1,0:T(8,128)(2,1)}, bf16[672,1280]{1,0:T(8,128)(2,1)S(1)}, u32[]{:S(2)}, u32[]{:S(2)}) collective-permute-start(bf16[672,1280]{1,0:T(8,128)(2,1)} %copy-done.2), channel_id=1, source_target_pairs={{0,1},{1,0},{2,3},{3,2},{4,5},{5,4},{6,7},{7,6},{8,9},{9,8},{10,11... | collective-permute-start | bytes 5160968 | tf_op jit(solution)/shard_map/ppermute | solution.py:53
  99.5 16.6 %copy-start.7 = (f32[256,1280]{1,0:T(8,128)S(1)}, f32[256,1280]{1,0:T(8,128)}, u32[]{:S(2)}) copy-start(f32[256,1280]{1,0:T(8,128)} %copy-done.6) | copy-start | bytes 3932164
  99.5 16.6 %copy-start.13 = (bf16[256,1280]{1,0:T(8,128)(2,1)S(1)}, bf16[256,1280]{1,0:T(8,128)(2,1)}, u32[]{:S(2)}) copy-start(bf16[256,1280]{1,0:T(8,128)(2,1)} %copy-done.12) | copy-start | bytes 1966084
  99.5 5.8 %collective-permute-start.12 = (bf16[336,1280]{1,0:T(8,128)(2,1)}, bf16[336,1280]{1,0:T(8,128)(2,1)S(1)}, u32[]{:S(2)}, u32[]{:S(2)}) collective-permute-start(bf16[336,1280]{1,0:T(8,128)(2,1)} %collective-permute-done.10.refs_10_.refs_6_), channel_id=1, source_target_pairs={{0,1},{1,0},{2,3},{3,2},{4,5},{5,4},{6,7},{7,6},{8,9},{9,8},{10,11... | collective-permute-start | bytes 2580488 | tf_op jit(solution)/shard_map/ppermute | solution.py:53
  99.6 5.7 %collective-permute-start.13 = (bf16[336,1280]{1,0:T(8,128)(2,1)}, bf16[336,1280]{1,0:T(8,128)(2,1)S(1)}, u32[]{:S(2)}, u32[]{:S(2)}) collective-permute-start(bf16[336,1280]{1,0:T(8,128)(2,1)} %collective-permute-done.11.refs_12_.refs_8_), channel_id=1, source_target_pairs={{0,1},{1,0},{2,3},{3,2},{4,5},{5,4},{6,7},{7,6},{8,9},{9,8},{10,11... | collective-permute-start | bytes 2580488 | tf_op jit(solution)/shard_map/ppermute | solution.py:53
  100.1 5.2 %collective-permute-start.14 = (bf16[16,1280]{1,0:T(8,128)(2,1)S(1)}, bf16[16,1280]{1,0:T(8,128)(2,1)S(1)}, u32[]{:S(2)}, u32[]{:S(2)}) collective-permute-start(bf16[16,1280]{1,0:T(8,128)(2,1)S(1)} %get-tuple-element.60.refs_3_), channel_id=1, source_target_pairs={{0,8},{1,9},{2,10},{3,11},{4,12},{5,13},{6,14},{7,15},{8,16},{9,17... | collective-permute-start | bytes 122888 | tf_op jit(solution)/shard_map/ppermute | solution.py:53
  112.8 9.8 %collective-permute-start.16 = (bf16[128,1280]{1,0:T(8,128)(2,1)S(1)}, bf16[128,1280]{1,0:T(8,128)(2,1)S(1)}, u32[]{:S(2)}, u32[]{:S(2)}) collective-permute-start(bf16[128,1280]{1,0:T(8,128)(2,1)S(1)} %get-tuple-element.69), channel_id=1, source_target_pairs={{0,8},{1,9},{2,10},{3,11},{4,12},{5,13},{6,14},{7,15},{8,16},{9,17... | collective-permute-start | bytes 983048 | tf_op jit(solution)/shard_map/ppermute | solution.py:53
  112.9 9.9 %collective-permute-start.15 = (bf16[144,1280]{1,0:T(8,128)(2,1)S(1)}, bf16[144,1280]{1,0:T(8,128)(2,1)S(1)}, u32[]{:S(2)}, u32[]{:S(2)}) collective-permute-start(bf16[144,1280]{1,0:T(8,128)(2,1)S(1)} %get-tuple-element.68), channel_id=1, source_target_pairs={{0,24},{1,25},{2,26},{3,27},{4,28},{5,29},{6,30},{7,31},{8,0},{9,1... | collective-permute-start | bytes 1105928 | tf_op jit(solution)/shard_map/ppermute | solution.py:53

commit v10 on v9

--- a/solution.py
+++ b/solution.py
@@ -682,7 +682,7 @@
     below = send(packed, next_z)
     above = send(packed, last_z)
     packed_core = send(packed, other_core)
-    (query,) = in_hbm(project(rank, prefill_hidden, gain, w_qkv, False))
+    query = project(rank, prefill_hidden, gain, w_qkv, False)
     every_row, query = lax.optimization_barrier((every_row, query))
     outgoing = decode_attention(
         device,

time: 125 us -> 127 us (1.016)
  waiting for transfers between devices: 20 us -> 21.9 us
  Pallas kernels: 58.3 us -> 60 us
    pallas_call x1, Pallas kernels: 1.41 us -> 3.39 us  [cut_halves(): pl.pallas_call(cut_kernel, out_shape=(jax.ShapeDtypeStruct((PART, WIDTH),...]
    unnamed x34 -> x32, local copies, waits for them, and re-layouts: 4.45 us -> 3.57 us
  transfers between devices with their start and end apart: 19 -> 19, of which waited for: 5 -> 6; matrix products, arithmetic and copies ran while one was open for 0% -> 0% of each run, Pallas kernels for 40% -> 41%
where the time goes in v10:
time: 127 us; the launch traced here: 126 us
  Pallas kernels  60 us (47%)
  starting transfers between devices  36.6 us (29%)
  waiting for transfers between devices  21.9 us (17%)
  local copies, waits for them, and re-layouts  5.63 us (4%)
  between operations  1.56 us (1%)
    ppermute x17, waiting for transfers between devices, send(): return lax.ppermute(array, 'req', moves(step))  20.6 us
    pallas_call x3, Pallas kernels, feed_forward(): pl.pallas_call(kernel, out_shape=outputs, in_specs=[vmem] * len(inputs),...  17.3 us
    ppermute x17, starting transfers between devices, send(): return lax.ppermute(array, 'req', moves(step))  15.8 us
    pallas_call x1, Pallas kernels, decode_attention(): pl.pallas_call(decode_kernel, out_shape=jax.ShapeDtypeStruct((128, 2, QW)...  14.9 us
    pallas_call x1, Pallas kernels, attention(): pl.pallas_call(attention_kernel, out_shape=(jax.ShapeDtypeStruct((ROWS, W...  12.2 us
    all_to_all x1, starting transfers between devices, body(): every_row = lax.all_to_all(spread, 'req', 0, 0)  11.1 us
    all_to_all x1, starting transfers between devices, body(): back = lax.all_to_all(outgoing, 'req', 0, 0)  9.67 us
    pallas_call x2, Pallas kernels, project(): pl.pallas_call(kv_kernel if keys else query_kernel, out_shape=jax.ShapeDt...  6.47 us
  transfers between devices with their start and end apart: 19, of which 6 were waited for; matrix products, arithmetic and copies ran while one was open for 0% of the time, Pallas kernels for 41%

profile of v10, /device:TPU:0, one launch (start us, length us, event | category | flops | bytes accessed | tf_op | source)
XLA Modules:
  0.0 125.6 jit_solution(15040359061536770618)
XLA Ops:
  0.6 1.9 %broadcast_in_dim.2 = bf16[128,2,1280]{2,1,0:T(2,128)(2,1)} broadcast(bf16[2,1280]{1,0:T(2,128)(2,1)} %decode_ref.1), dimensions={1,2} | broadcast | bytes 660480 | tf_op jit(solution)/shard_map/broadcast_in_dim | solution.py:674
  2.5 11.1 %all-to-all-start = ((bf16[128,2,1280]{2,1,0:T(2,128)(2,1)}), bf16[128,2,1280]{2,1,0:T(2,128)(2,1)S(1)}, u32[]{:S(2)}, u32[]{:S(2)}) async-start(bf16[128,2,1280]{2,1,0:T(2,128)(2,1)} %broadcast_in_dim.2), calls=%async_computation | async-start | bytes 1310720 | tf_op jit(solution)/shard_map/all_to_all | solution.py:675
  13.7 0.0 copy-start.9
  13.7 2.4 %pack.1.refs_2_.refs_4_ = bf16[672,1280]{1,0:T(8,128)(2,1)} custom-call(bf16[1,448,1280]{2,1,0:T(8,128)(2,1)} %bitcast.6, bf16[1,224,1280]{2,1,0:T(8,128)(2,1)} %down_ref.1), custom_call_target="tpu_custom_call" | custom-call | flops 1500000000 | bytes 4500000 | tf_op jit(solution)/shard_map/pack/pallas_call | solution.py:138
  16.1 2.6 %prefill_kv.1.own_ref = bf16[256,640]{1,0:T(8,128)(2,1)S(1)} custom-call(s32[1]{0:T(128)S(6)} %select_n.7.rank_ref, bf16[256,1280]{1,0:T(8,128)(2,1)} %hidden_ref.7, f32[1280]{0:T(1024)S(1)} %copy-done.9, bf16[1280,1920]{1,0:T(8,128)(2,1)} %w_ref.7), custom_call_target="tpu_custom_call" | custom-call | flops 3000000000 | bytes 9000000 | tf_op jit(solution)/shard_map/prefill_kv/pallas_call | solution.py:213
  18.7 0.1 collective-permute-start.2
  18.8 0.5 collective-permute-start.1
  19.3 1.1 collective-permute-start
  20.4 2.3 %collective-permute-start.5 = (bf16[672,1280]{1,0:T(8,128)(2,1)}, bf16[672,1280]{1,0:T(8,128)(2,1)S(1)}, u32[]{:S(2)}, u32[]{:S(2)}) collective-permute-start(bf16[672,1280]{1,0:T(8,128)(2,1)} %pack.1.refs_2_.refs_4_), channel_id=1, source_target_pairs={{0,6},{1,7},{2,0},{3,1},{4,2},{5,3},{6,4},{7,5},{8,14},{9,15},{10,... | collective-permute-start | bytes 5160968 | tf_op jit(solution)/shard_map/ppermute | solution.py:53
  22.7 0.0 collective-permute-start.4
  23.4 0.0 copy-done.15
  23.4 0.1 reshape.17
  23.5 0.1 copy.16
  23.6 3.9 %prefill_query.1.query_ref = bf16[256,1280]{1,0:T(8,128)(2,1)S(1)} custom-call(s32[1]{0:T(128)S(6)} %select_n.7.rank_ref, bf16[256,1280]{1,0:T(8,128)(2,1)} %hidden_ref.7, f32[1280]{0:T(1024)S(1)} %copy-done.9, bf16[1280,1920]{1,0:T(8,128)(2,1)} %w_ref.7), custom_call_target="tpu_custom_call" | custom-call | flops 100000000 | bytes 300000 | tf_op jit(solution)/shard_map/prefill_query/pallas_call | solution.py:213
  27.5 1.3 %all-to-all-done.rows_ref = bf16[128,2,1280]{2,1,0:T(2,128)(2,1)S(1)} async-done(((bf16[128,2,1280]{2,1,0:T(2,128)(2,1)}), bf16[128,2,1280]{2,1,0:T(2,128)(2,1)S(1)}, u32[]{:S(2)}, u32[]{:S(2)}) %all-to-all-start) | async-done | bytes 655392 | tf_op jit(solution)/shard_map/all_to_all | solution.py:675
  28.8 14.9 %decode.1 = bf16[128,2,1280]{2,1,0:T(2,128)(2,1)S(1)} custom-call(s32[1]{0:T(128)} %bitcast.device_ref, s32[4]{0:T(128)S(1)} %copy-done.13, s32[1]{0:T(128)S(6)} %copy.17.count_ref, s32[2,128]{1,0:T(2,128)S(1)} %bitcast.4, s32[8,128]{1,0:T(8,128)S(1)} %bitcast.5, bf16[128,2,1280]{2,1,0:T(2,128)(2,1)S(1)} %all-to-all-done.rows_ref, f32[1280]{0:T(1024)S(1)} %copy-done.9, ...), custom_call_target="tpu_custom_call" | custom-call | flops 16999999488 | bytes 51000000 | tf_op jit(solution)/shard_map/decode/pallas_call | solution.py:407
  43.7 0.0 copy-start.5
  43.7 0.0 collective-permute-done.1.core_ref
  43.7 0.0 collective-permute-done.zed_ref
  43.7 0.0 collective-permute-done.2.refs_3_.refs_5_
  43.7 0.9 copy-done.5
  44.6 0.0 collective-permute-start.3
  44.6 9.7 %all-to-all-start.1 = ((bf16[128,2,1280]{2,1,0:T(2,128)(2,1)}), bf16[128,2,1280]{2,1,0:T(2,128)(2,1)}, u32[]{:S(2)}, u32[]{:S(2)}) async-start(bf16[128,2,1280]{2,1,0:T(2,128)(2,1)} %copy-done.5), calls=%async_computation.1 | async-start | bytes 1310720 | tf_op jit(solution)/shard_map/all_to_all | solution.py:708
  54.2 0.0 collective-permute-done.3.far_ref
  54.2 0.0 copy-start.14
  54.3 0.7 copy-done.14
  55.0 0.0 copy-done.7
  55.0 12.2 %attention.1 = (bf16[256,1280]{1,0:T(8,128)(2,1)S(1)}, bf16[128,1280]{1,0:T(8,128)(2,1)}, bf16[128,1280]{1,0:T(8,128)(2,1)}) custom-call(s32[1]{0:T(128)S(6)} %select_n.7.rank_ref, bf16[256,1280]{1,0:T(8,128)(2,1)S(1)} %prefill_query.1.query_ref, bf16[256,640]{1,0:T(8,128)(2,1)} %copy-done.6, bf16[256,640]{1,0:T(8,128)(2,1)} %collective-permute-done.1.core_ref, ...), custom_call_target="tpu_custom_call" | custom-call | flops 100000000 | bytes 300000 | tf_op jit(solution)/shard_map/attention/pallas_call | solution.py:523
  67.2 0.8 copy-done.10
  68.0 0.7 collective-permute-start.6
  68.8 2.5 %collective-permute-start.7 = (bf16[128,1280]{1,0:T(8,128)(2,1)}, bf16[128,1280]{1,0:T(8,128)(2,1)}, u32[]{:S(2)}, u32[]{:S(2)}) collective-permute-start(bf16[128,1280]{1,0:T(8,128)(2,1)} %get-tuple-element.43.refs_1_), channel_id=1, source_target_pairs={{0,24},{1,25},{2,26},{3,27},{4,28},{5,29},{6,30},{7,31},{8,0},{9,1... | collective-permute-start | bytes 983048 | tf_op jit(solution)/shard_map/ppermute | solution.py:53
  71.3 4.0 %collective-permute-done.5.above_ref.refs_8_.refs_4_ = bf16[672,1280]{1,0:T(8,128)(2,1)S(1)} collective-permute-done((bf16[672,1280]{1,0:T(8,128)(2,1)}, bf16[672,1280]{1,0:T(8,128)(2,1)S(1)}, u32[]{:S(2)}, u32[]{:S(2)}) %collective-permute-start.5) | collective-permute-done | bytes 1720352 | tf_op jit(solution)/shard_map/ppermute | solution.py:53
  75.2 0.0 collective-permute-done.4.below_ref.refs_6_.refs_2_
  75.2 3.4 %cut.1 = (bf16[336,1280]{1,0:T(8,128)(2,1)}, bf16[336,1280]{1,0:T(8,128)(2,1)}) custom-call(bf16[672,1280]{1,0:T(8,128)(2,1)} %collective-permute-done.4.below_ref.refs_6_.refs_2_, bf16[672,1280]{1,0:T(8,128)(2,1)S(1)} %collective-permute-done.5.above_ref.refs_8_.refs_4_), custom_call_target="tpu_custom_call" | custom-call | flops 500000000 | bytes 1500000 | tf_op jit(solution)/shard_map/cut/pallas_call | solution.py:160
  78.6 0.0 copy-done.1
  78.6 0.0 collective-permute-start.10
  78.6 0.0 copy-start.8
  78.7 3.2 %collective-permute-start.11 = (bf16[336,1280]{1,0:T(8,128)(2,1)}, bf16[336,1280]{1,0:T(8,128)(2,1)}, u32[]{:S(2)}, u32[]{:S(2)}) collective-permute-start(bf16[336,1280]{1,0:T(8,128)(2,1)} %get-tuple-element.55), channel_id=1, source_target_pairs={{0,6},{1,7},{2,0},{3,1},{4,2},{5,3},{6,4},{7,5},{8,14},{9,15},{10,... | collective-permute-start | bytes 2580488 | tf_op jit(solution)/shard_map/ppermute | solution.py:53
  81.9 3.7 %feed_first.1.refs_10_ = f32[256,1280]{1,0:T(8,128)S(1)} custom-call(bf16[128,1280]{1,0:T(8,128)(2,1)} %get-tuple-element.42.refs_0_, bf16[128,1280]{1,0:T(8,128)(2,1)} %get-tuple-element.43.refs_1_, bf16[672,1280]{1,0:T(8,128)(2,1)} %pack.1.refs_2_.refs_4_, bf16[672,1280]{1,0:T(8,128)(2,1)} %collective-permute-done.2.refs_3_.refs_5_), custom_call_target="tpu_custom_call" | custom-call | flops 100000000 | bytes 300000 | tf_op jit(solution)/shard_map/feed_first/pallas_call | solution.py:614
  85.6 0.0 copy-start.3
  85.6 1.1 copy-done.3
  86.7 0.0 all-to-all-done.1.back_ref
  86.7 0.0 collective-permute-done.6.refs_0_
  86.7 0.0 collective-permute-done.7.refs_2_
  86.7 0.1 collective-permute-start.8
  86.8 0.5 collective-permute-start.9
  87.3 2.3 %decode_rows.1 = (bf16[16,1280]{1,0:T(8,128)(2,1)S(1)}, bf16[16,1280]{1,0:T(8,128)(2,1)S(1)}) custom-call(bf16[128,2,1280]{2,1,0:T(2,128)(2,1)} %all-to-all-done.1.back_ref, bf16[1280,1280]{1,0:T(8,128)(2,1)S(1)} %copy-done, bf16[2,1280]{1,0:T(2,128)(2,1)S(1)} %copy-done.8, f32[1280]{0:T(1024)S(1)} %copy-done.7), custom_call_target="tpu_custom_call" | custom-call | flops 100000000 | bytes 300000 | tf_op jit(solution)/shard_map/decode_rows/pallas_call | solution.py:569
  89.6 11.3 %collective-permute-done.10.refs_10_.refs_6_ = bf16[336,1280]{1,0:T(8,128)(2,1)} collective-permute-done((bf16[336,1280]{1,0:T(8,128)(2,1)}, bf16[336,1280]{1,0:T(8,128)(2,1)}, u32[]{:S(2)}, u32[]{:S(2)}) %collective-permute-start.10) | collective-permute-done | bytes 860192 | tf_op jit(solution)/shard_map/ppermute | solution.py:53
  100.9 0.0 collective-permute-done.11.refs_12_.refs_8_
  100.9 0.1 collective-permute-start.12
  101.0 0.5 collective-permute-start.13
  101.5 0.9 collective-permute-start.14
  102.4 4.3 %collective-permute-done.14.refs_1_ = bf16[16,1280]{1,0:T(8,128)(2,1)S(1)} collective-permute-done((bf16[16,1280]{1,0:T(8,128)(2,1)S(1)}, bf16[16,1280]{1,0:T(8,128)(2,1)S(1)}, u32[]{:S(2)}, u32[]{:S(2)}) %collective-permute-start.14) | collective-permute-done | bytes 40992 | tf_op jit(solution)/shard_map/ppermute | solution.py:53
  106.7 0.0 collective-permute-done.12.refs_11_.refs_7_
  106.7 0.0 collective-permute-done.13.refs_13_.refs_9_
  106.7 0.0 collective-permute-done.8.refs_7_.refs_3_
  106.7 0.0 collective-permute-done.9.refs_9_.refs_5_
  106.8 7.9 %feed_guest.1 = (bf16[144,1280]{1,0:T(8,128)(2,1)S(1)}, bf16[128,1280]{1,0:T(8,128)(2,1)S(1)}, bf16[16,1280]{1,0:T(8,128)(2,1)S(1)}) custom-call(bf16[128,1280]{1,0:T(8,128)(2,1)} %collective-permute-done.6.refs_0_, bf16[16,1280]{1,0:T(8,128)(2,1)S(1)} %collective-permute-done.14.refs_1_, bf16[128,1280]{1,0:T(8,128)(2,1)} %collective-permute-done.7.refs_2_, ...), custom_call_target="tpu_custom_call" | custom-call | flops 8000000000 | bytes 24000000 | tf_op jit(solution)/shard_map/feed_guest/pallas_call | solution.py:614
  114.7 0.1 collective-permute-start.16
  114.8 3.2 %collective-permute-start.15 = (bf16[144,1280]{1,0:T(8,128)(2,1)S(1)}, bf16[144,1280]{1,0:T(8,128)(2,1)S(1)}, u32[]{:S(2)}, u32[]{:S(2)}) collective-permute-start(bf16[144,1280]{1,0:T(8,128)(2,1)S(1)} %get-tuple-element.68), channel_id=1, source_target_pairs={{0,24},{1,25},{2,26},{3,27},{4,28},{5,29},{6,30},{7,31},{8,0},{9,1... | collective-permute-start | bytes 1105928 | tf_op jit(solution)/shard_map/ppermute | solution.py:53
  118.0 5.7 %feed_second.1.start_ref = f32[256,1280]{1,0:T(8,128)S(1)} custom-call(bf16[128,1280]{1,0:T(8,128)(2,1)} %get-tuple-element.42.refs_0_, bf16[128,1280]{1,0:T(8,128)(2,1)} %get-tuple-element.43.refs_1_, bf16[672,1280]{1,0:T(8,128)(2,1)} %collective-permute-done.4.below_ref.refs_6_.refs_2_, bf16[672,1280]{1,0:T(8,128)(2,1)S(1)} %collective-permute-done.8.refs_7_.refs_3_, ...), custom_call_target="tpu_custom_call" | custom-call | flops 6000000000 | bytes 18000000 | tf_op jit(solution)/shard_map/feed_second/pallas_call | solution.py:614
  123.7 0.8 collective-permute-done.16.second_ref
  124.5 0.1 collective-permute-done.15.first_ref
  124.7 1.0 final.1
  (20 shorter events, 0.0 us)
Async XLA Ops:
  2.5 26.3 %all-to-all-start = ((bf16[128,2,1280]{2,1,0:T(2,128)(2,1)}), bf16[128,2,1280]{2,1,0:T(2,128)(2,1)S(1)}, u32[]{:S(2)}, u32[]{:S(2)}) async-start(bf16[128,2,1280]{2,1,0:T(2,128)(2,1)} %broadcast_in_dim.2), calls=%async_computation | async-start | bytes 1310720 | tf_op jit(solution)/shard_map/all_to_all | solution.py:675
  13.7 2.4 %copy-start.9 = (f32[1280]{0:T(1024)S(1)}, f32[1280]{0:T(1024)}, u32[]{:S(2)}) copy-start(f32[1280]{0:T(1024)} %gain_ref.7) | copy-start | bytes 15364
  16.1 7.3 %copy-start.15 = (s32[256]{0:T(256)S(1)}, s32[256]{0:T(256)}, u32[]{:S(2)}) copy-start(s32[256]{0:T(256)} %param.24) | copy-start | bytes 3076
  18.7 8.8 %copy-start.6 = (bf16[256,640]{1,0:T(8,128)(2,1)}, bf16[256,640]{1,0:T(8,128)(2,1)S(1)}, u32[]{:S(2)}) copy-start(bf16[256,640]{1,0:T(8,128)(2,1)S(1)} %prefill_kv.1.own_ref) | copy-start | bytes 983044
  18.7 25.0 %collective-permute-start.2 = (bf16[672,1280]{1,0:T(8,128)(2,1)}, bf16[672,1280]{1,0:T(8,128)(2,1)}, u32[]{:S(2)}, u32[]{:S(2)}) collective-permute-start(bf16[672,1280]{1,0:T(8,128)(2,1)} %pack.1.refs_2_.refs_4_), channel_id=1, source_target_pairs={{0,1},{1,0},{2,3},{3,2},{4,5},{5,4},{6,7},{7,6},{8,9},{9,8},{10,11... | collective-permute-start | bytes 5160968 | tf_op jit(solution)/shard_map/ppermute | solution.py:53
  18.8 24.8 %collective-permute-start.1 = (bf16[256,640]{1,0:T(8,128)(2,1)S(1)}, bf16[256,640]{1,0:T(8,128)(2,1)}, u32[]{:S(2)}, u32[]{:S(2)}) collective-permute-start(bf16[256,640]{1,0:T(8,128)(2,1)S(1)} %prefill_kv.1.own_ref), channel_id=1, source_target_pairs={{0,1},{1,0},{2,3},{3,2},{4,5},{5,4},{6,7},{7,6},{8,9},{9,8},{10,11... | collective-permute-start | bytes 983048 | tf_op jit(solution)/shard_map/ppermute | solution.py:53
  19.3 24.4 %collective-permute-start = (bf16[256,640]{1,0:T(8,128)(2,1)S(1)}, bf16[256,640]{1,0:T(8,128)(2,1)}, u32[]{:S(2)}, u32[]{:S(2)}) collective-permute-start(bf16[256,640]{1,0:T(8,128)(2,1)S(1)} %prefill_kv.1.own_ref), channel_id=1, source_target_pairs={{0,2},{1,3},{2,0},{3,1},{4,6},{5,7},{6,4},{7,5},{8,10},{9,11},{10,... | collective-permute-start | bytes 983048 | tf_op jit(solution)/shard_map/ppermute | solution.py:53
  20.4 54.8 %collective-permute-start.5 = (bf16[672,1280]{1,0:T(8,128)(2,1)}, bf16[672,1280]{1,0:T(8,128)(2,1)S(1)}, u32[]{:S(2)}, u32[]{:S(2)}) collective-permute-start(bf16[672,1280]{1,0:T(8,128)(2,1)} %pack.1.refs_2_.refs_4_), channel_id=1, source_target_pairs={{0,6},{1,7},{2,0},{3,1},{4,2},{5,3},{6,4},{7,5},{8,14},{9,15},{10,... | collective-permute-start | bytes 5160968 | tf_op jit(solution)/shard_map/ppermute | solution.py:53
  22.7 52.5 %collective-permute-start.4 = (bf16[672,1280]{1,0:T(8,128)(2,1)}, bf16[672,1280]{1,0:T(8,128)(2,1)}, u32[]{:S(2)}, u32[]{:S(2)}) collective-permute-start(bf16[672,1280]{1,0:T(8,128)(2,1)} %pack.1.refs_2_.refs_4_), channel_id=1, source_target_pairs={{0,2},{1,3},{2,4},{3,5},{4,6},{5,7},{6,0},{7,1},{8,10},{9,11},{10,... | collective-permute-start | bytes 5160968 | tf_op jit(solution)/shard_map/ppermute | solution.py:53
  23.6 5.2 %copy-start.12 = (s32[1024]{0:T(1024)S(1)}, s32[1024]{0:T(1024)}, u32[]{:S(2)}) copy-start(s32[1024]{0:T(1024)} %param.26) | copy-start | bytes 12292
  23.6 5.2 %copy-start.13 = (s32[4]{0:T(128)S(1)}, s32[4]{0:T(128)}, u32[]{:S(2)}) copy-start(s32[4]{0:T(128)} %length_ref.1) | copy-start | bytes 52
  28.8 26.2 %copy-start.7 = (f32[1280]{0:T(1024)S(1)}, f32[1280]{0:T(1024)}, u32[]{:S(2)}) copy-start(f32[1280]{0:T(1024)} %gain_ref.9) | copy-start | bytes 15364
  43.7 0.9 copy-start.5
  44.6 9.7 %collective-permute-start.3 = (bf16[256,640]{1,0:T(8,128)(2,1)}, bf16[256,640]{1,0:T(8,128)(2,1)S(1)}, u32[]{:S(2)}, u32[]{:S(2)}) collective-permute-start(bf16[256,640]{1,0:T(8,128)(2,1)} %collective-permute-done.zed_ref), channel_id=1, source_target_pairs={{0,1},{1,0},{2,3},{3,2},{4,5},{5,4},{6,7},{7,6},{8,9},{9,8},{10,11... | collective-permute-start | bytes 983048 | tf_op jit(solution)/shard_map/ppermute | solution.py:53
  44.6 42.1 %all-to-all-start.1 = ((bf16[128,2,1280]{2,1,0:T(2,128)(2,1)}), bf16[128,2,1280]{2,1,0:T(2,128)(2,1)}, u32[]{:S(2)}, u32[]{:S(2)}) async-start(bf16[128,2,1280]{2,1,0:T(2,128)(2,1)} %copy-done.5), calls=%async_computation.1 | async-start | bytes 1310720 | tf_op jit(solution)/shard_map/all_to_all | solution.py:708
  54.2 0.7 copy-start.14
  67.2 0.8 copy-start.10
  68.0 18.7 %collective-permute-start.6 = (bf16[128,1280]{1,0:T(8,128)(2,1)}, bf16[128,1280]{1,0:T(8,128)(2,1)}, u32[]{:S(2)}, u32[]{:S(2)}) collective-permute-start(bf16[128,1280]{1,0:T(8,128)(2,1)} %get-tuple-element.42.refs_0_), channel_id=1, source_target_pairs={{0,8},{1,9},{2,10},{3,11},{4,12},{5,13},{6,14},{7,15},{8,16},{9,17... | collective-permute-start | bytes 983048 | tf_op jit(solution)/shard_map/ppermute | solution.py:53
  68.8 17.9 %collective-permute-start.7 = (bf16[128,1280]{1,0:T(8,128)(2,1)}, bf16[128,1280]{1,0:T(8,128)(2,1)}, u32[]{:S(2)}, u32[]{:S(2)}) collective-permute-start(bf16[128,1280]{1,0:T(8,128)(2,1)} %get-tuple-element.43.refs_1_), channel_id=1, source_target_pairs={{0,24},{1,25},{2,26},{3,27},{4,28},{5,29},{6,30},{7,31},{8,0},{9,1... | collective-permute-start | bytes 983048 | tf_op jit(solution)/shard_map/ppermute | solution.py:53
  75.2 3.4 %copy-start.1 = (bf16[672,1280]{1,0:T(8,128)(2,1)}, bf16[672,1280]{1,0:T(8,128)(2,1)S(1)}, u32[]{:S(2)}) copy-start(bf16[672,1280]{1,0:T(8,128)(2,1)S(1)} %collective-permute-done.5.above_ref.refs_8_.refs_4_) | copy-start | bytes 5160964
  78.6 22.3 %collective-permute-start.10 = (bf16[336,1280]{1,0:T(8,128)(2,1)}, bf16[336,1280]{1,0:T(8,128)(2,1)}, u32[]{:S(2)}, u32[]{:S(2)}) collective-permute-start(bf16[336,1280]{1,0:T(8,128)(2,1)} %get-tuple-element.54), channel_id=1, source_target_pairs={{0,2},{1,3},{2,4},{3,5},{4,6},{5,7},{6,0},{7,1},{8,10},{9,11},{10,... | collective-permute-start | bytes 2580488 | tf_op jit(solution)/shard_map/ppermute | solution.py:53
  78.6 8.7 %copy-start = (bf16[1280,1280]{1,0:T(8,128)(2,1)S(1)}, bf16[1280,1280]{1,0:T(8,128)(2,1)}, u32[]{:S(2)}) copy-start(bf16[1280,1280]{1,0:T(8,128)(2,1)} %w_ref.9) | copy-start | bytes 9830404
  78.6 8.7 %copy-start.8 = (bf16[2,1280]{1,0:T(2,128)(2,1)S(1)}, bf16[2,1280]{1,0:T(2,128)(2,1)}, u32[]{:S(2)}) copy-start(bf16[2,1280]{1,0:T(2,128)(2,1)} %decode_ref.1) | copy-start | bytes 15364
  78.7 22.3 %collective-permute-start.11 = (bf16[336,1280]{1,0:T(8,128)(2,1)}, bf16[336,1280]{1,0:T(8,128)(2,1)}, u32[]{:S(2)}, u32[]{:S(2)}) collective-permute-start(bf16[336,1280]{1,0:T(8,128)(2,1)} %get-tuple-element.55), channel_id=1, source_target_pairs={{0,6},{1,7},{2,0},{3,1},{4,2},{5,3},{6,4},{7,5},{8,14},{9,15},{10,... | collective-permute-start | bytes 2580488 | tf_op jit(solution)/shard_map/ppermute | solution.py:53
  85.6 1.1 copy-start.3
  86.7 20.1 %copy-start.2 = (bf16[672,1280]{1,0:T(8,128)(2,1)S(1)}, bf16[672,1280]{1,0:T(8,128)(2,1)}, u32[]{:S(2)}) copy-start(bf16[672,1280]{1,0:T(8,128)(2,1)} %copy-done.1) | copy-start | bytes 5160964
  86.7 20.0 %collective-permute-start.8 = (bf16[672,1280]{1,0:T(8,128)(2,1)}, bf16[672,1280]{1,0:T(8,128)(2,1)S(1)}, u32[]{:S(2)}, u32[]{:S(2)}) collective-permute-start(bf16[672,1280]{1,0:T(8,128)(2,1)} %collective-permute-done.4.below_ref.refs_6_.refs_2_), channel_id=1, source_target_pairs={{0,1},{1,0},{2,3},{3,2},{4,5},{5,4},{6,7},{7,6},{8,9},{9,8},{10,11... | collective-permute-start | bytes 5160968 | tf_op jit(solution)/shard_map/ppermute | solution.py:53
  86.8 19.9 %collective-permute-start.9 = (bf16[672,1280]{1,0:T(8,128)(2,1)}, bf16[672,1280]{1,0:T(8,128)(2,1)S(1)}, u32[]{:S(2)}, u32[]{:S(2)}) collective-permute-start(bf16[672,1280]{1,0:T(8,128)(2,1)} %copy-done.1), channel_id=1, source_target_pairs={{0,1},{1,0},{2,3},{3,2},{4,5},{5,4},{6,7},{7,6},{8,9},{9,8},{10,11... | collective-permute-start | bytes 5160968 | tf_op jit(solution)/shard_map/ppermute | solution.py:53
  100.9 17.1 %copy-start.4 = (f32[256,1280]{1,0:T(8,128)S(1)}, f32[256,1280]{1,0:T(8,128)}, u32[]{:S(2)}) copy-start(f32[256,1280]{1,0:T(8,128)} %copy-done.3) | copy-start | bytes 3932164
  100.9 17.1 %copy-start.11 = (bf16[256,1280]{1,0:T(8,128)(2,1)S(1)}, bf16[256,1280]{1,0:T(8,128)(2,1)}, u32[]{:S(2)}) copy-start(bf16[256,1280]{1,0:T(8,128)(2,1)} %copy-done.10) | copy-start | bytes 1966084
  100.9 5.8 %collective-permute-start.12 = (bf16[336,1280]{1,0:T(8,128)(2,1)}, bf16[336,1280]{1,0:T(8,128)(2,1)S(1)}, u32[]{:S(2)}, u32[]{:S(2)}) collective-permute-start(bf16[336,1280]{1,0:T(8,128)(2,1)} %collective-permute-done.10.refs_10_.refs_6_), channel_id=1, source_target_pairs={{0,1},{1,0},{2,3},{3,2},{4,5},{5,4},{6,7},{7,6},{8,9},{9,8},{10,11... | collective-permute-start | bytes 2580488 | tf_op jit(solution)/shard_map/ppermute | solution.py:53
  101.0 5.7 %collective-permute-start.13 = (bf16[336,1280]{1,0:T(8,128)(2,1)}, bf16[336,1280]{1,0:T(8,128)(2,1)S(1)}, u32[]{:S(2)}, u32[]{:S(2)}) collective-permute-start(bf16[336,1280]{1,0:T(8,128)(2,1)} %collective-permute-done.11.refs_12_.refs_8_), channel_id=1, source_target_pairs={{0,1},{1,0},{2,3},{3,2},{4,5},{5,4},{6,7},{7,6},{8,9},{9,8},{10,11... | collective-permute-start | bytes 2580488 | tf_op jit(solution)/shard_map/ppermute | solution.py:53
  101.5 5.2 %collective-permute-start.14 = (bf16[16,1280]{1,0:T(8,128)(2,1)S(1)}, bf16[16,1280]{1,0:T(8,128)(2,1)S(1)}, u32[]{:S(2)}, u32[]{:S(2)}) collective-permute-start(bf16[16,1280]{1,0:T(8,128)(2,1)S(1)} %get-tuple-element.60.refs_3_), channel_id=1, source_target_pairs={{0,8},{1,9},{2,10},{3,11},{4,12},{5,13},{6,14},{7,15},{8,16},{9,17... | collective-permute-start | bytes 122888 | tf_op jit(solution)/shard_map/ppermute | solution.py:53
  114.7 9.8 %collective-permute-start.16 = (bf16[128,1280]{1,0:T(8,128)(2,1)S(1)}, bf16[128,1280]{1,0:T(8,128)(2,1)S(1)}, u32[]{:S(2)}, u32[]{:S(2)}) collective-permute-start(bf16[128,1280]{1,0:T(8,128)(2,1)S(1)} %get-tuple-element.69), channel_id=1, source_target_pairs={{0,8},{1,9},{2,10},{3,11},{4,12},{5,13},{6,14},{7,15},{8,16},{9,17... | collective-permute-start | bytes 983048 | tf_op jit(solution)/shard_map/ppermute | solution.py:53
  114.8 9.9 %collective-permute-start.15 = (bf16[144,1280]{1,0:T(8,128)(2,1)S(1)}, bf16[144,1280]{1,0:T(8,128)(2,1)S(1)}, u32[]{:S(2)}, u32[]{:S(2)}) collective-permute-start(bf16[144,1280]{1,0:T(8,128)(2,1)S(1)} %get-tuple-element.68), channel_id=1, source_target_pairs={{0,24},{1,25},{2,26},{3,27},{4,28},{5,29},{6,30},{7,31},{8,0},{9,1... | collective-permute-start | bytes 1105928 | tf_op jit(solution)/shard_map/ppermute | solution.py:53
